TPU v7x, 32 devices: a whole 2x2x4 slice. The times are simulated.
32 devices in a mesh: batch: 4 (over x, core), head: 8 (over z, y).
Axes of the slice: x: 2, y: 2, z: 4, core: 2. Of those that a mesh axis runs over, the one named last changes fastest.
Arguments:
- tokens: bfloat16 [5120, 2048], P('batch'), may hold values from -6 to 6
- segment_ids: int32 [5120], P('batch'), may hold values from 0 to 6, as said below
- norm1_gain: bfloat16 [2048], P('batch'), may hold values from 0.25 to 1.75
- w_query: bfloat16 [2048, 1024], P('batch', 'head'), may hold values from -0.125 to 0.125
- w_key: bfloat16 [2048, 512], P('batch', 'head'), may hold values from -0.125 to 0.125
- w_value: bfloat16 [2048, 512], P('batch', 'head'), may hold values from -0.125 to 0.125
- w_gate: bfloat16 [2048, 1024], P('batch', 'head'), may hold values from -0.125 to 0.125
- w_out: bfloat16 [1024, 2048], P('head', 'batch'), may hold values from -4 to 4
- norm2_gain: bfloat16 [2048], P('batch'), may hold values from 0.25 to 1.75
- w_mlp_gate: bfloat16 [2048, 6144], P('batch', 'head'), may hold values from -0.125 to 0.125
- w_mlp_up: bfloat16 [2048, 6144], P('batch', 'head'), may hold values from -0.125 to 0.125
- w_down: bfloat16 [6144, 2048], P('head', 'batch'), may hold values from -0.078125 to 0.078125
- out_grad: bfloat16 [5120, 2048], P('batch'), may hold values from -6 to 6
Outputs:
- output: bfloat16 [5120, 2048], P('batch')
- d_tokens: bfloat16 [5120, 2048], P('batch')
- d_norm1_gain: float32 [2048], P('batch')
- d_w_query: float32 [2048, 1024], P('batch', 'head')
- d_w_key: float32 [2048, 512], P('batch', 'head')
- d_w_value: float32 [2048, 512], P('batch', 'head')
- d_w_gate: float32 [2048, 1024], P('batch', 'head')
- d_w_out: float32 [1024, 2048], P('head', 'batch')
- d_norm2_gain: float32 [2048], P('batch')
- d_w_mlp_gate: float32 [2048, 6144], P('batch', 'head')
- d_w_mlp_up: float32 [2048, 6144], P('batch', 'head')
- d_w_down: float32 [6144, 2048], P('head', 'batch')
Inputs may be any that keep to these rules, and one draw needn't show every extreme that they name: `segment_ids`: segment ids never fall along the packed batch and every id from 0 to 6 occurs.
All inputs are finite; a program needn't handle non-finite values.
Results may differ from a plain program's by a relative error of at most 0.02.
Values may be sent and summed in bfloat16 or wider, within the bound.
A program may use at most 256 MiB of HBM per device.

v0:
```python
import math

import jax
import jax.numpy as jnp
from jax import lax
from jax.sharding import PartitionSpec as P

EPSILON = 1e-06
MASKED = -1e30


def from_partner(block, axis, stride):
    count = lax.axis_size(axis)
    route = []
    for low in range(count):
        high = low | 1 << stride
        if high != low and high < count:
            route += [(low, high), (high, low)]
    return lax.ppermute(block, axis, route)


def matmul(left, right):
    return jnp.dot(left, right, preferred_element_type=jnp.float32)


def rows_inner(left, right):
    return lax.dot_general(
        left, right, (((0,), (0,)), ((), ())), preferred_element_type=jnp.float32
    )


def cols_inner(left, right):
    return lax.dot_general(
        left, right, (((1,), (1,)), ((), ())), preferred_element_type=jnp.float32
    )


def rms_scale(values):
    return lax.rsqrt(jnp.mean(values * values, axis=1, keepdims=True) + EPSILON)


def keep_same(state):
    return state


def per_device(
    tokens,
    segment_ids,
    norm1_gain,
    w_query,
    w_key,
    w_value,
    w_gate,
    w_out,
    norm2_gain,
    w_mlp_gate,
    w_mlp_up,
    w_down,
    out_grad,
):
    gathered = (
        lax.all_gather(norm1_gain, "batch", axis=0, tiled=True),
        lax.all_gather(w_query, "batch", axis=0, tiled=True),
        lax.all_gather(w_key, "batch", axis=0, tiled=True),
        lax.all_gather(w_value, "batch", axis=0, tiled=True),
        lax.all_gather(w_gate, "batch", axis=0, tiled=True),
        lax.all_gather(w_out, "batch", axis=1, tiled=True),
        lax.all_gather(norm2_gain, "batch", axis=0, tiled=True),
        lax.all_gather(w_mlp_gate, "batch", axis=0, tiled=True),
        lax.all_gather(w_mlp_up, "batch", axis=0, tiled=True),
        lax.all_gather(w_down, "batch", axis=1, tiled=True),
    )
    (
        gain_one,
        query_full,
        key_full,
        value_full,
        gate_full,
        out_full,
        gain_two,
        mgate_full,
        mup_full,
        down_full,
    ) = gathered
    gain_one = gain_one.astype(jnp.float32)
    gain_two = gain_two.astype(jnp.float32)
    row_count = tokens.shape[0]
    head_size = query_full.shape[1]
    half_width = key_full.shape[1]
    scale_factor = 1.0 / math.sqrt(head_size)
    positions = lax.axis_index("batch") * row_count + jnp.arange(row_count, dtype=jnp.int32)
    inputs = tokens.astype(jnp.float32)
    recip_one = rms_scale(inputs)
    normed_one = (inputs * recip_one * gain_one).astype(jnp.bfloat16)
    queries = matmul(normed_one, query_full).astype(jnp.bfloat16)
    kv_half = matmul(normed_one, jnp.concatenate([key_full, value_full], axis=1)).astype(
        jnp.bfloat16
    )
    partner = from_partner(kv_half, "head", 0)
    lower_half = lax.axis_index("head") % 2 == 0
    own_key, own_value = (kv_half[:, :half_width], kv_half[:, half_width:])
    mate_key, mate_value = (partner[:, :half_width], partner[:, half_width:])
    keys_full = jnp.where(
        lower_half, jnp.concatenate([own_key, mate_key], 1), jnp.concatenate([mate_key, own_key], 1)
    )
    values_full = jnp.where(
        lower_half,
        jnp.concatenate([own_value, mate_value], 1),
        jnp.concatenate([mate_value, own_value], 1),
    )
    kv_local = jnp.concatenate([keys_full, values_full], axis=1)
    kv_all, seg_all = (
        lax.all_gather(kv_local, "batch", axis=0, tiled=True),
        lax.all_gather(segment_ids, "batch", axis=0, tiled=True),
    )
    group_total = kv_all.shape[0] // row_count
    per_block = max(
        (
            step
            for step in range(1, group_total + 1)
            if group_total % step == 0 and step * row_count <= max(row_count, 1024)
        )
    )
    block_rows = per_block * row_count
    block_total = group_total // per_block

    def block_parts(block_index):
        first_row = block_index * block_rows
        key_block = kv_all[first_row : first_row + block_rows, :head_size]
        value_block = kv_all[first_row : first_row + block_rows, head_size:]
        seg_block = seg_all[first_row : first_row + block_rows]
        key_pos = first_row + jnp.arange(block_rows, dtype=jnp.int32)
        allowed = (segment_ids[:, None] == seg_block[None, :]) & (
            key_pos[None, :] <= positions[:, None]
        )
        scores = cols_inner(queries, key_block) * scale_factor
        return (scores, allowed, key_block, value_block)

    def is_live(block_index):
        first_row = block_index * block_rows
        return (first_row <= positions[-1]) & (
            seg_all[first_row + block_rows - 1] >= segment_ids[0]
        )

    run_max = jnp.full((row_count,), MASKED, jnp.float32)
    run_sum = jnp.zeros((row_count,), jnp.float32)
    for block_index in range(block_total):

        def grow(state, block_index=block_index):
            old_max, old_sum = state
            scores, allowed, key_block, value_block = block_parts(block_index)
            new_max = jnp.maximum(old_max, jnp.max(jnp.where(allowed, scores, MASKED), axis=1))
            weights = jnp.where(allowed, jnp.exp(scores - new_max[:, None]), 0.0)
            return (new_max, old_sum * jnp.exp(old_max - new_max) + jnp.sum(weights, axis=1))

        run_max, run_sum = lax.cond(is_live(block_index), grow, keep_same, (run_max, run_sum))
    log_total = run_max + jnp.log(run_sum)

    def probs_of(block_index):
        scores, allowed, key_block, value_block = block_parts(block_index)
        return (
            jnp.where(allowed, jnp.exp(scores - log_total[:, None]), 0.0),
            key_block,
            value_block,
        )

    attended = jnp.zeros((row_count, head_size), jnp.float32)
    for block_index in range(block_total):

        def accumulate(running, block_index=block_index):
            probs, key_block, value_block = probs_of(block_index)
            return running + matmul(probs.astype(jnp.bfloat16), value_block)

        attended = lax.cond(is_live(block_index), accumulate, keep_same, attended)
    gate_vals = jax.nn.sigmoid(matmul(normed_one, gate_full))
    mixed = (attended * gate_vals).astype(jnp.bfloat16)
    attn_part = matmul(mixed, out_full)
    resid = inputs + lax.psum(attn_part, "head")
    recip_two = rms_scale(resid)
    normed_two = (resid * recip_two * gain_two).astype(jnp.bfloat16)
    gate_pre = matmul(normed_two, mgate_full)
    up_pre = matmul(normed_two, mup_full)
    sig_gate = jax.nn.sigmoid(gate_pre)
    silu_gate = gate_pre * sig_gate
    hidden = (silu_gate * up_pre).astype(jnp.bfloat16)
    mlp_part = matmul(hidden, down_full)
    d_down = rows_inner(hidden, out_grad)
    d_hidden = cols_inner(out_grad, down_full)
    d_gate_pre = (d_hidden * up_pre * sig_gate * (1.0 + gate_pre * (1.0 - sig_gate))).astype(
        jnp.bfloat16
    )
    d_up_pre = (d_hidden * silu_gate).astype(jnp.bfloat16)
    d_mgate = rows_inner(normed_two, d_gate_pre)
    d_mup = rows_inner(normed_two, d_up_pre)
    dn2_part = cols_inner(d_gate_pre, mgate_full) + cols_inner(d_up_pre, mup_full)
    mlp_total = lax.psum(mlp_part.astype(jnp.bfloat16), "head").astype(jnp.float32)
    output = (resid + mlp_total).astype(jnp.bfloat16)
    d_normed_two = lax.psum(dn2_part.astype(jnp.bfloat16), "head").astype(jnp.float32)
    gain_two_full = jnp.sum(d_normed_two * resid * recip_two, axis=0)
    gain_two_term = jnp.where(
        lax.axis_index("head") == 0, gain_two_full, jnp.zeros_like(gain_two_full)
    )
    weighted_two = gain_two * d_normed_two
    d_resid = (
        out_grad.astype(jnp.float32)
        + recip_two * weighted_two
        - resid * recip_two**3 * jnp.mean(weighted_two * resid, axis=1, keepdims=True)
    )
    d_resid_low = d_resid.astype(jnp.bfloat16)
    d_out = rows_inner(mixed, d_resid_low)
    d_mixed = cols_inner(d_resid_low, out_full)
    d_attended = (d_mixed * gate_vals).astype(jnp.bfloat16)
    d_gate_logit = (d_mixed * attended * gate_vals * (1.0 - gate_vals)).astype(jnp.bfloat16)
    delta = jnp.zeros((row_count,), jnp.float32)
    for block_index in range(block_total):

        def delta_add(running, block_index=block_index):
            probs, key_block, value_block = probs_of(block_index)
            return running + jnp.sum(probs * cols_inner(d_attended, value_block), axis=1)

        delta = lax.cond(is_live(block_index), delta_add, keep_same, delta)
    d_queries = jnp.zeros((row_count, head_size), jnp.float32)
    grad_pieces = []
    for block_index in range(block_total):

        def block_grads(running, block_index=block_index):
            probs, key_block, value_block = probs_of(block_index)
            d_probs = cols_inner(d_attended, value_block)
            d_scores = (probs * (d_probs - delta[:, None]) * scale_factor).astype(jnp.bfloat16)
            d_key_block = rows_inner(d_scores, queries)
            d_value_block = rows_inner(probs.astype(jnp.bfloat16), d_attended)
            return (
                running + matmul(d_scores, key_block),
                jnp.concatenate([d_key_block, d_value_block], axis=1),
            )

        def block_empty(running):
            return (running, jnp.zeros((block_rows, 2 * head_size), jnp.float32))

        d_queries, grad_piece = lax.cond(is_live(block_index), block_grads, block_empty, d_queries)
        grad_pieces.append(grad_piece)
    d_kv_all = jnp.concatenate(grad_pieces, axis=0)
    d_kv_own = lax.psum_scatter(
        d_kv_all.astype(jnp.bfloat16), "batch", scatter_dimension=0, tiled=True
    ).astype(jnp.float32)
    d_kv_mate = from_partner(d_kv_own.astype(jnp.bfloat16), "head", 0).astype(d_kv_own.dtype)
    d_kv_low = (d_kv_own + d_kv_mate).astype(jnp.bfloat16)
    d_key_half = jnp.where(lower_half, d_kv_low[:, :half_width], d_kv_low[:, half_width:head_size])
    d_value_half = jnp.where(
        lower_half,
        d_kv_low[:, head_size : head_size + half_width],
        d_kv_low[:, head_size + half_width :],
    )
    d_queries_low = d_queries.astype(jnp.bfloat16)
    d_query_w = rows_inner(normed_one, d_queries_low)
    d_key_w = rows_inner(normed_one, d_key_half)
    d_value_w = rows_inner(normed_one, d_value_half)
    d_gate_w = rows_inner(normed_one, d_gate_logit)
    dn1_part = (
        cols_inner(d_queries_low, query_full)
        + cols_inner(d_key_half, key_full)
        + cols_inner(d_value_half, value_full)
        + cols_inner(d_gate_logit, gate_full)
    )
    d_normed_one, d_gain_two = (
        lax.psum(dn1_part.astype(jnp.bfloat16), "head").astype(jnp.float32),
        lax.psum(gain_two_term.astype(jnp.bfloat16), "head").astype(jnp.float32),
    )
    d_gain_one = jnp.sum(d_normed_one * inputs * recip_one, axis=0)
    weighted_one = gain_one * d_normed_one
    d_tokens = (
        d_resid
        + recip_one * weighted_one
        - inputs * recip_one**3 * jnp.mean(weighted_one * inputs, axis=1, keepdims=True)
    ).astype(jnp.bfloat16)
    summed = (
        lax.psum_scatter(
            d_gain_one.astype(jnp.bfloat16), "batch", scatter_dimension=0, tiled=True
        ).astype(jnp.float32),
        lax.psum_scatter(
            d_query_w.astype(jnp.bfloat16), "batch", scatter_dimension=0, tiled=True
        ).astype(jnp.float32),
        lax.psum_scatter(
            d_key_w.astype(jnp.bfloat16), "batch", scatter_dimension=0, tiled=True
        ).astype(jnp.float32),
        lax.psum_scatter(
            d_value_w.astype(jnp.bfloat16), "batch", scatter_dimension=0, tiled=True
        ).astype(jnp.float32),
        lax.psum_scatter(
            d_gate_w.astype(jnp.bfloat16), "batch", scatter_dimension=0, tiled=True
        ).astype(jnp.float32),
        lax.psum_scatter(
            d_out.astype(jnp.bfloat16), "batch", scatter_dimension=1, tiled=True
        ).astype(jnp.float32),
        lax.psum_scatter(
            d_gain_two.astype(jnp.bfloat16), "batch", scatter_dimension=0, tiled=True
        ).astype(jnp.float32),
        lax.psum_scatter(
            d_mgate.astype(jnp.bfloat16), "batch", scatter_dimension=0, tiled=True
        ).astype(jnp.float32),
        lax.psum_scatter(
            d_mup.astype(jnp.bfloat16), "batch", scatter_dimension=0, tiled=True
        ).astype(jnp.float32),
        lax.psum_scatter(
            d_down.astype(jnp.bfloat16), "batch", scatter_dimension=1, tiled=True
        ).astype(jnp.float32),
    )
    return (
        output,
        d_tokens,
        summed[0],
        summed[1],
        summed[2],
        summed[3],
        summed[4],
        summed[5],
        summed[6],
        summed[7],
        summed[8],
        summed[9],
    )


def solution(mesh):
    return jax.shard_map(
        per_device,
        mesh=mesh,
        in_specs=(
            P("batch", None),
            P("batch"),
            P("batch"),
            P("batch", "head"),
            P("batch", "head"),
            P("batch", "head"),
            P("batch", "head"),
            P("head", "batch"),
            P("batch"),
            P("batch", "head"),
            P("batch", "head"),
            P("head", "batch"),
            P("batch", None),
        ),
        out_specs=(
            P("batch", None),
            P("batch", None),
            P("batch"),
            P("batch", "head"),
            P("batch", "head"),
            P("batch", "head"),
            P("batch", "head"),
            P("head", "batch"),
            P("batch"),
            P("batch", "head"),
            P("batch", "head"),
            P("head", "batch"),
        ),
        check_vma=False,
    )
```

profile of v0, /device:TPU:0, one launch (start us, length us, event | category | flops | bytes accessed | tf_op | source)
XLA Modules:
  0.0 1581.4 jit_solution(1215481020769771091)
XLA Ops:
  62.4 10.5 all_gather.41
  124.7 57.2 %all-gather.2 = bf16[4,1,512]{2,1,0:T(2,128)(2,1)S(1)} all-gather(bf16[1,1,512]{2,1,0:T(2,128)(2,1)S(1)} %reshape.212), channel_id=1, replica_groups=mesh['batch'=4,'head'=8] {'batch'}, dimensions={0}, use_global_device_ids=true | all-gather | bytes 5120 | tf_op jit(solution)/shard_map/all_gather | solution.py:68
  181.9 321.6 %all-reduce.8.cloned.1.call-done = f32[1280,2048]{1,0:T(8,128)} async-done(((f32[1280,2048]{1,0:T(8,128)}), f32[1280,2048]{1,0:T(8,128)}) %all-reduce.8.cloned.1.call-update) | async-done | bytes 10485776 | tf_op jit(solution)/shard_map/psum | solution.py:178
  503.6 11.1 multiply_reduce_fusion
  522.0 10.8 all-gather.12.cloned.1.call-done
  542.4 20.5 %all-gather.10.cloned.1.call-done = bf16[2048,768]{1,0:T(8,128)(2,1)} async-done(((bf16[512,768]{1,0:T(8,128)(2,1)}), bf16[2048,768]{1,0:T(8,128)(2,1)}) %all-gather.10.cloned.1.call-update) | async-done | bytes 3145744 | tf_op jit(solution)/shard_map/all_gather | solution.py:69
  562.9 9.7 fusion.160
  572.6 20.4 %all-gather.14.cloned.1.call-done = bf16[768,2048]{1,0:T(8,128)(2,1)} async-done(((bf16[768,512]{1,0:T(8,128)(2,1)}), bf16[768,2048]{1,0:T(8,128)(2,1)}) %all-gather.14.cloned.1.call-update) | async-done | bytes 3145744 | tf_op jit(solution)/shard_map/all_gather | solution.py:71
  592.9 13.6 multiply_convert_fusion.1
  619.2 183.7 %all-reduce.10.cloned.1.call-done = bf16[1280,2048]{1,0:T(8,128)(2,1)} async-done(((bf16[1280,2048]{1,0:T(8,128)(2,1)}), bf16[1280,2048]{1,0:T(8,128)(2,1)}) %all-reduce.10.cloned.1.call-update) | async-done | bytes 5242896 | tf_op jit(solution)/shard_map/psum | solution.py:198
  832.8 13.0 conditional.28
  901.5 44.9 %reduce-scatter.10.cloned.1.call-done = bf16[1280,256]{0,1:T(8,128)(2,1)} async-done(((bf16[5120,256]{0,1:T(8,128)(2,1)}), bf16[1280,256]{0,1:T(8,128)(2,1)}) %reduce-scatter.10.cloned.1.call-update) | async-done | bytes 655376 | tf_op jit(solution)/shard_map/reduce_scatter | solution.py:243
  983.1 13.4 add_convert_fusion
  1001.0 26.6 %reduce-scatter.24.cloned.1.call-done = bf16[512,768]{1,0:T(8,128)(2,1)} async-done(((bf16[2048,768]{1,0:T(8,128)(2,1)}), bf16[512,768]{1,0:T(8,128)(2,1)}) %reduce-scatter.24.cloned.1.call-update) | async-done | bytes 786448 | tf_op jit(solution)/shard_map/reduce_scatter | solution.py:301
  1030.0 38.0 %reduce-scatter.22.cloned.1.call-done = bf16[512,768]{1,0:T(8,128)(2,1)} async-done(((bf16[2048,768]{1,0:T(8,128)(2,1)}), bf16[512,768]{1,0:T(8,128)(2,1)}) %reduce-scatter.22.cloned.1.call-update) | async-done | bytes 786448 | tf_op jit(solution)/shard_map/reduce_scatter | solution.py:298
  1070.4 22.0 %reduce-scatter.20.cloned.1.call-done = bf16[128,512]{1,0:T(8,128)(2,1)} async-done(((bf16[128,2048]{1,0:T(8,128)(2,1)}), bf16[128,512]{1,0:T(8,128)(2,1)}) %reduce-scatter.20.cloned.1.call-update) | async-done | bytes 131088 | tf_op jit(solution)/shard_map/reduce_scatter | solution.py:292
  1094.0 22.4 %reduce-scatter.18.cloned.1.call-done = bf16[512,128]{1,0:T(8,128)(2,1)} async-done(((bf16[2048,128]{1,0:T(8,128)(2,1)}), bf16[512,128]{1,0:T(8,128)(2,1)}) %reduce-scatter.18.cloned.1.call-update) | async-done | bytes 131088 | tf_op jit(solution)/shard_map/reduce_scatter | solution.py:289
  1118.0 22.7 %reduce-scatter.12.cloned.1.call-done = bf16[512,128]{1,0:T(8,128)(2,1)} async-done(((bf16[2048,128]{1,0:T(8,128)(2,1)}), bf16[512,128]{1,0:T(8,128)(2,1)}) %reduce-scatter.12.cloned.1.call-update) | async-done | bytes 131088 | tf_op jit(solution)/shard_map/reduce_scatter | solution.py:280
  1142.4 20.8 %reduce-scatter.16.cloned.1.call-done = bf16[512,64]{0,1:T(8,128)(2,1)} async-done(((bf16[2048,64]{0,1:T(8,128)(2,1)}), bf16[512,64]{0,1:T(8,128)(2,1)}) %reduce-scatter.16.cloned.1.call-update) | async-done | bytes 65552 | tf_op jit(solution)/shard_map/reduce_scatter | solution.py:286
  1164.7 21.0 %reduce-scatter.14.cloned.1.call-done = bf16[512,64]{0,1:T(8,128)(2,1)} async-done(((bf16[2048,64]{0,1:T(8,128)(2,1)}), bf16[512,64]{0,1:T(8,128)(2,1)}) %reduce-scatter.14.cloned.1.call-update) | async-done | bytes 65552 | tf_op jit(solution)/shard_map/reduce_scatter | solution.py:283
  1187.2 331.0 %all-reduce.12.cloned.1.call-done = (bf16[1280,2048]{1,0:T(8,128)(2,1)}, bf16[1280,2048]{1,0:T(8,128)(2,1)}) async-done(((bf16[1280,2048]{1,0:T(8,128)(2,1)}, bf16[1280,2048]{1,0:T(8,128)(2,1)}), (bf16[1280,2048]{1,0:T(8,128)(2,1)}, bf16[1280,2048]{1,0:T(8,128)(2,1)})) %all-reduce.12.cloned.1.call-update) | async-done | bytes 10485776 | tf_op jit(solution)/shard_map/psum | solution.py:196
  1518.2 10.0 add_convert_fusion.2
  1543.9 19.1 %psum.40 = bf16[512]{0:T(512)(128)(2,1)S(1)} all-reduce(bf16[512]{0:T(512)(128)(2,1)S(1)} %dynamic-slice.3), channel_id=1, replica_groups=mesh['batch'=4,'head'=8] {'head'}, use_global_device_ids=true, to_apply=%region_61.62 | all-reduce | flops 512 | bytes 2048 | tf_op jit(solution)/shard_map/psum | solution.py:267
  1563.6 10.8 fusion.119
  (217 shorter events, 323.9 us)
Async XLA Ops:
  7.2 85.5 %all-gather.8.cloned.1.call-start = ((), (), s32[]{:S(2)}) async-start(), calls=%async_computation.9 | async-start | bytes 3276800 | tf_op jit(solution)/shard_map/all_gather | solution.py:113
  7.2 23.8 %copy-start.2 = (bf16[1280,2048]{1,0:T(8,128)(2,1)S(1)}, bf16[1280,2048]{1,0:T(8,128)(2,1)}, u32[]{:S(2)}) copy-start(bf16[1280,2048]{1,0:T(8,128)(2,1)} %param.45) | copy-start | bytes 15728644
  34.7 27.8 %copy-start.25 = (bf16[512,128]{1,0:T(8,128)(2,1)S(1)}, bf16[512,128]{1,0:T(8,128)(2,1)}, u32[]{:S(2)}) copy-start(bf16[512,128]{1,0:T(8,128)(2,1)} %param.48) | copy-start | bytes 393220
  34.7 38.2 %copy-start.26 = (bf16[512,128]{1,0:T(8,128)(2,1)S(1)}, bf16[512,128]{1,0:T(8,128)(2,1)}, u32[]{:S(2)}) copy-start(bf16[512,128]{1,0:T(8,128)(2,1)} %param.51) | copy-start | bytes 393220
  34.7 46.0 %copy-start.27 = (bf16[128,512]{1,0:T(8,128)(2,1)S(1)}, bf16[128,512]{1,0:T(8,128)(2,1)}, u32[]{:S(2)}) copy-start(bf16[128,512]{1,0:T(8,128)(2,1)} %param.52) | copy-start | bytes 393220
  36.6 10.0 collective-permute-start
  47.7 455.9 %all-reduce.8.cloned.1.call-start = ((), (), s32[]{:S(2)}) async-start(), calls=%async_computation.10 | async-start | bytes 20971520 | tf_op jit(solution)/shard_map/psum | solution.py:178
  122.7 410.1 %all-gather.12.cloned.1.call-start = ((), (), s32[]{:S(2)}) async-start(), calls=%async_computation.12 | async-start | bytes 3932160 | tf_op jit(solution)/shard_map/all_gather | solution.py:70
  123.5 439.4 %all-gather.10.cloned.1.call-start = ((), (), s32[]{:S(2)}) async-start(), calls=%async_computation.11 | async-start | bytes 3932160 | tf_op jit(solution)/shard_map/all_gather | solution.py:69
  124.0 468.9 %all-gather.14.cloned.1.call-start = ((), (), s32[]{:S(2)}) async-start(), calls=%async_computation.13 | async-start | bytes 3932160 | tf_op jit(solution)/shard_map/all_gather | solution.py:71
  124.6 678.3 %all-reduce.10.cloned.1.call-start = ((), (), s32[]{:S(2)}) async-start(), calls=%async_computation.14 | async-start | bytes 10485760 | tf_op jit(solution)/shard_map/psum | solution.py:198
  618.7 327.7 %reduce-scatter.10.cloned.1.call-start = ((), (), s32[]{:S(2)}) async-start(), calls=%async_computation.15 | async-start | bytes 3276800 | tf_op jit(solution)/shard_map/reduce_scatter | solution.py:243
  855.8 142.7 %reduce-scatter.26.cloned.1.call-start = ((), (), s32[]{:S(2)}) async-start(), calls=%async_computation.23 | async-start | bytes 3932160 | tf_op jit(solution)/shard_map/reduce_scatter | solution.py:304
  864.2 163.5 %reduce-scatter.24.cloned.1.call-start = ((), (), s32[]{:S(2)}) async-start(), calls=%async_computation.22 | async-start | bytes 3932160 | tf_op jit(solution)/shard_map/reduce_scatter | solution.py:301
  873.5 194.5 %reduce-scatter.22.cloned.1.call-start = ((), (), s32[]{:S(2)}) async-start(), calls=%async_computation.21 | async-start | bytes 3932160 | tf_op jit(solution)/shard_map/reduce_scatter | solution.py:298
  882.7 209.7 %reduce-scatter.20.cloned.1.call-start = ((), (), s32[]{:S(2)}) async-start(), calls=%async_computation.20 | async-start | bytes 655360 | tf_op jit(solution)/shard_map/reduce_scatter | solution.py:292
  888.5 227.9 %reduce-scatter.18.cloned.1.call-start = ((), (), s32[]{:S(2)}) async-start(), calls=%async_computation.19 | async-start | bytes 655360 | tf_op jit(solution)/shard_map/reduce_scatter | solution.py:289
  893.4 247.3 %reduce-scatter.12.cloned.1.call-start = ((), (), s32[]{:S(2)}) async-start(), calls=%async_computation.16 | async-start | bytes 655360 | tf_op jit(solution)/shard_map/reduce_scatter | solution.py:280
  901.5 51.5 %copy-start.12 = (bf16[2048,128]{1,0:T(8,128)(2,1)S(1)}, bf16[2048,128]{1,0:T(8,128)(2,1)}, u32[]{:S(2)}) copy-start(bf16[2048,128]{1,0:T(8,128)(2,1)} %copy-done.11) | copy-start | bytes 1572868
  946.4 16.7 %collective-permute-start.1 = (bf16[1280,256]{0,1:T(8,128)(2,1)}, bf16[1280,256]{0,1:T(8,128)(2,1)S(1)}, u32[]{:S(2)}, u32[]{:S(2)}) collective-permute-start(bf16[1280,256]{0,1:T(8,128)(2,1)} %reduce-scatter.10.cloned.1.call-done), channel_id=1, source_target_pairs={{0,1},{1,0},{2,3},{3,2},{4,5},{5,4},{6,7},{7,6},{8,9},{9,8},{10,11... | collective-permute-start | bytes 1966088 | tf_op jit(solution)/shard_map/ppermute | solution.py:19
  952.9 210.2 %reduce-scatter.16.cloned.1.call-start = ((), (), s32[]{:S(2)}) async-start(), calls=%async_computation.18 | async-start | bytes 327680 | tf_op jit(solution)/shard_map/reduce_scatter | solution.py:286
  972.9 212.8 %reduce-scatter.14.cloned.1.call-start = ((), (), s32[]{:S(2)}) async-start(), calls=%async_computation.17 | async-start | bytes 327680 | tf_op jit(solution)/shard_map/reduce_scatter | solution.py:283
  982.8 535.4 %all-reduce.12.cloned.1.call-start = ((), (), s32[]{:S(2)}) async-start(), calls=%async_computation.24 | async-start | bytes 20971520 | tf_op jit(solution)/shard_map/psum | solution.py:196
  1528.2 35.3 %copy-start.28 = (f32[1280]{0:T(1024)S(1)}, f32[1280]{0:T(1024)}, u32[]{:S(2)}) copy-start(f32[1280]{0:T(1024)} %get-tuple-element.734) | copy-start | bytes 15364
  (31 other events, 238.7 us)
Sparse Core Ops, SparseCore 0:
  47.8 29.6 all-gather.7
  122.9 380.6 all-reduce.7
  505.2 27.5 all-gather.11
  534.3 28.5 all-gather.9
  564.4 28.5 all-gather.13
  618.9 184.0 all-reduce.9
  855.9 90.4 reduce-scatter.9
  948.9 37.9 reduce-scatter.25
  989.6 37.9 reduce-scatter.23
  1030.0 37.9 reduce-scatter.21
  1070.7 21.6 reduce-scatter.19
  1094.7 21.6 reduce-scatter.17
  1119.1 21.6 reduce-scatter.11
  1143.1 20.0 reduce-scatter.15
  1165.6 20.0 reduce-scatter.13
  1190.2 327.9 all-reduce.11
where the time goes:
time: 1590 us; the launch traced here: 1580 us
  waiting for transfers between devices  1120 us (70%)
  matrix products  175 us (11%)
  blocking collectives  133 us (8%)
  other arithmetic  95.2 us (6%)
  local copies, waits for them, and re-layouts  25 us (2%)
  between operations  23.4 us (1%)
    psum x1, waiting for transfers between devices, per_device(): lax.psum(mlp_part.astype(jnp.bfloat16), 'head').astype(jnp.float32)  331 us
    psum x1, waiting for transfers between devices, per_device(): resid = inputs + lax.psum(attn_part, 'head')  322 us
    psum x1, waiting for transfers between devices, per_device(): lax.psum(dn2_part.astype(jnp.bfloat16), 'head').astype(jnp.float32)  184 us
    dot_general x13, matrix products, cols_inner(): lax.dot_general(left, right, (((1,), (1,)), ((), ())), preferred_element_...  73.1 us
    all_gather x1, blocking collectives, per_device(): lax.all_gather(norm2_gain, 'batch', axis=0, tiled=True)  57.2 us
    dot_general x10, matrix products, rows_inner(): lax.dot_general(left, right, (((0,), (0,)), ((), ())), preferred_element_...  51.8 us
    dot_general x9, matrix products, matmul(): return jnp.dot(left, right, preferred_element_type=jnp.float32)  50.3 us
    reduce_scatter x1, waiting for transfers between devices, per_device(): lax.psum_scatter(d_kv_all.astype(jnp.bfloat16), 'batch', scatter_dimensio...  44.9 us
  transfers between devices with their start and end apart: 18, of which 16 were waited for; matrix products, arithmetic and copies ran while one was open for 9% of the time, Pallas kernels for 0%

commit v1 on v0

v1 whole, which is shorter than its diff:
```python
import math

import jax
import jax.numpy as jnp
from jax import lax
from jax.sharding import PartitionSpec as P

EPSILON = 1e-06
MASKED = -1e30
BF = jnp.bfloat16
F32 = jnp.float32


def from_partner(block, axis):
    count = lax.axis_size(axis)
    route = [(at, at ^ 1) for at in range(count)]
    return lax.ppermute(block, axis, route)


def matmul(left, right):
    return jnp.dot(left, right, preferred_element_type=F32)


def rows_inner(left, right):
    return lax.dot_general(left, right, (((0,), (0,)), ((), ())), preferred_element_type=F32)


def cols_inner(left, right):
    return lax.dot_general(left, right, (((1,), (1,)), ((), ())), preferred_element_type=F32)


def rms_scale(values):
    return lax.rsqrt(jnp.mean(values * values, axis=1, keepdims=True) + EPSILON)


def keep_same(state):
    return state


def order_halves(own, mate, first):
    return jnp.where(first, jnp.concatenate([own, mate], 1), jnp.concatenate([mate, own], 1))


def per_device(
    tokens,
    segment_ids,
    norm1_gain,
    w_query,
    w_key,
    w_value,
    w_gate,
    w_out,
    norm2_gain,
    w_mlp_gate,
    w_mlp_up,
    w_down,
    out_grad,
):
    heads = lax.axis_size("head")
    batches = lax.axis_size("batch")
    row_count, width = tokens.shape
    head_size = w_query.shape[1]
    half = w_key.shape[1]
    chunk = row_count // heads
    me = lax.axis_index("head")
    first = me % 2 == 0
    scale_factor = 1.0 / math.sqrt(head_size)

    kv_shard = jnp.concatenate([w_key, w_value], axis=1)
    kv_mate = from_partner(kv_shard, "head")
    w_in = jnp.concatenate(
        [
            w_query,
            order_halves(w_key, kv_mate[:, :half], first),
            order_halves(w_value, kv_mate[:, half:], first),
            w_gate,
        ],
        axis=1,
    )
    w_in = lax.all_gather(w_in, "batch", axis=0, tiled=True)
    gains = lax.all_gather(jnp.stack([norm1_gain, norm2_gain]), "batch", axis=1, tiled=True)
    gain_one = gains[0].astype(F32)
    gain_two = gains[1].astype(F32)
    out_own = lax.all_gather(w_out, "batch", axis=1, tiled=True)
    out_full = lax.all_gather(out_own, "head", axis=0, tiled=True)
    mgate_full = lax.all_gather(w_mlp_gate, "batch", axis=0, tiled=True)
    mup_full = lax.all_gather(w_mlp_up, "batch", axis=0, tiled=True)
    down_full = lax.all_gather(w_down, "batch", axis=1, tiled=True)

    positions = lax.axis_index("batch") * row_count + jnp.arange(row_count, dtype=jnp.int32)
    inputs = tokens.astype(F32)
    recip_one = rms_scale(inputs)
    normed_one = (inputs * recip_one * gain_one).astype(BF)
    projected = matmul(normed_one, w_in)
    queries = projected[:, :head_size].astype(BF)
    kv_local = projected[:, head_size : 3 * head_size].astype(BF)
    gate_vals = jax.nn.sigmoid(projected[:, 3 * head_size :])
    kv_all = lax.all_gather(kv_local, "batch", axis=0, tiled=True)
    seg_all = lax.all_gather(segment_ids, "batch", axis=0, tiled=True)
    block_rows = row_count
    block_total = batches

    def block_parts(block_index):
        first_row = block_index * block_rows
        key_block = kv_all[first_row : first_row + block_rows, :head_size]
        value_block = kv_all[first_row : first_row + block_rows, head_size:]
        seg_block = seg_all[first_row : first_row + block_rows]
        key_pos = first_row + jnp.arange(block_rows, dtype=jnp.int32)
        allowed = (segment_ids[:, None] == seg_block[None, :]) & (
            key_pos[None, :] <= positions[:, None]
        )
        scores = cols_inner(queries, key_block) * scale_factor
        return (scores, allowed, key_block, value_block)

    def is_live(block_index):
        first_row = block_index * block_rows
        return (first_row <= positions[-1]) & (
            seg_all[first_row + block_rows - 1] >= segment_ids[0]
        )

    run_max = jnp.full((row_count,), MASKED, F32)
    run_sum = jnp.zeros((row_count,), F32)
    for block_index in range(block_total):

        def grow(state, block_index=block_index):
            old_max, old_sum = state
            scores, allowed, key_block, value_block = block_parts(block_index)
            new_max = jnp.maximum(old_max, jnp.max(jnp.where(allowed, scores, MASKED), axis=1))
            weights = jnp.where(allowed, jnp.exp(scores - new_max[:, None]), 0.0)
            return (new_max, old_sum * jnp.exp(old_max - new_max) + jnp.sum(weights, axis=1))

        run_max, run_sum = lax.cond(is_live(block_index), grow, keep_same, (run_max, run_sum))
    log_total = run_max + jnp.log(run_sum)

    def probs_of(block_index):
        scores, allowed, key_block, value_block = block_parts(block_index)
        return (
            jnp.where(allowed, jnp.exp(scores - log_total[:, None]), 0.0),
            key_block,
            value_block,
        )

    attended = jnp.zeros((row_count, head_size), F32)
    for block_index in range(block_total):

        def accumulate(running, block_index=block_index):
            probs, key_block, value_block = probs_of(block_index)
            return running + matmul(probs.astype(BF), value_block)

        attended = lax.cond(is_live(block_index), accumulate, keep_same, attended)

    mixed = (attended * gate_vals).astype(BF)
    mixed_all = lax.all_gather(mixed, "head", axis=1, tiled=True)
    resid = inputs + matmul(mixed_all, out_full)
    recip_two = rms_scale(resid)
    normed_two = (resid * recip_two * gain_two).astype(BF)
    resid_own = lax.dynamic_slice_in_dim(resid, me * chunk, chunk, 0)
    recip_own = lax.dynamic_slice_in_dim(recip_two, me * chunk, chunk, 0)
    mixed_own = lax.dynamic_slice_in_dim(mixed_all, me * chunk, chunk, 0)
    dy_own = lax.dynamic_slice_in_dim(out_grad, me * chunk, chunk, 0).astype(F32)

    gate_pre = matmul(normed_two, mgate_full)
    up_pre = matmul(normed_two, mup_full)
    sig_gate = jax.nn.sigmoid(gate_pre)
    silu_gate = gate_pre * sig_gate
    hidden = (silu_gate * up_pre).astype(BF)
    d_hidden = cols_inner(out_grad, down_full)
    d_gate_pre = (d_hidden * up_pre * sig_gate * (1.0 + gate_pre * (1.0 - sig_gate))).astype(BF)
    d_up_pre = (d_hidden * silu_gate).astype(BF)
    dn2_part = cols_inner(d_gate_pre, mgate_full) + cols_inner(d_up_pre, mup_full)
    dn2 = lax.psum_scatter(dn2_part.astype(BF), "head", scatter_dimension=0, tiled=True).astype(F32)
    mlp_part = matmul(hidden, down_full).astype(BF)
    mlp_own = lax.psum_scatter(mlp_part, "head", scatter_dimension=0, tiled=True).astype(F32)
    output = lax.all_gather((resid_own + mlp_own).astype(BF), "head", axis=0, tiled=True)

    d_gain_two = jnp.sum(dn2 * resid_own * recip_own, axis=0)
    weighted_two = gain_two * dn2
    d_resid = (
        dy_own
        + recip_own * weighted_two
        - resid_own * recip_own**3 * jnp.mean(weighted_two * resid_own, axis=1, keepdims=True)
    )
    d_resid_low = d_resid.astype(BF)
    d_mixed_all = cols_inner(d_resid_low, out_full).astype(BF)
    d_mixed = lax.all_to_all(d_mixed_all, "head", split_axis=1, concat_axis=0, tiled=True).astype(F32)
    d_out_part = rows_inner(mixed_own, d_resid_low).astype(BF)
    d_out_head = lax.psum_scatter(d_out_part, "head", scatter_dimension=0, tiled=True)

    d_attended = (d_mixed * gate_vals).astype(BF)
    d_gate_logit = (d_mixed * attended * gate_vals * (1.0 - gate_vals)).astype(BF)
    delta = jnp.zeros((row_count,), F32)
    for block_index in range(block_total):

        def delta_add(running, block_index=block_index):
            probs, key_block, value_block = probs_of(block_index)
            return running + jnp.sum(probs * cols_inner(d_attended, value_block), axis=1)

        delta = lax.cond(is_live(block_index), delta_add, keep_same, delta)
    d_queries = jnp.zeros((row_count, head_size), F32)
    grad_pieces = []
    for block_index in range(block_total):

        def block_grads(running, block_index=block_index):
            probs, key_block, value_block = probs_of(block_index)
            d_probs = cols_inner(d_attended, value_block)
            d_scores = (probs * (d_probs - delta[:, None]) * scale_factor).astype(BF)
            d_key_block = rows_inner(d_scores, queries)
            d_value_block = rows_inner(probs.astype(BF), d_attended)
            return (
                running + matmul(d_scores, key_block),
                jnp.concatenate([d_key_block, d_value_block], axis=1).astype(BF),
            )

        def block_empty(running):
            return (running, jnp.zeros((block_rows, 2 * head_size), BF))

        d_queries, grad_piece = lax.cond(is_live(block_index), block_grads, block_empty, d_queries)
        grad_pieces.append(grad_piece)
    d_kv_all = jnp.concatenate(grad_pieces, axis=0)
    d_kv_own = lax.psum_scatter(d_kv_all, "batch", scatter_dimension=0, tiled=True)
    d_kv_mate = from_partner(d_kv_own, "head")
    d_kv = (d_kv_own.astype(F32) + d_kv_mate.astype(F32)).astype(BF)
    d_cat = jnp.concatenate(
        [
            d_queries.astype(BF),
            jnp.where(first, d_kv[:, :half], d_kv[:, half:head_size]),
            jnp.where(first, d_kv[:, head_size : head_size + half], d_kv[:, head_size + half :]),
            d_gate_logit,
        ],
        axis=1,
    )
    w_key_own = jnp.where(
        first, w_in[:, head_size : head_size + half], w_in[:, head_size + half : 2 * head_size]
    )
    w_value_own = jnp.where(
        first, w_in[:, 2 * head_size : 2 * head_size + half], w_in[:, 2 * head_size + half : 3 * head_size]
    )
    w_cat = jnp.concatenate(
        [w_in[:, :head_size], w_key_own, w_value_own, w_in[:, 3 * head_size :]], axis=1
    )
    dn1_part = cols_inner(d_cat, w_cat).astype(BF)
    dn1 = lax.psum_scatter(dn1_part, "head", scatter_dimension=0, tiled=True).astype(F32)
    inputs_own = lax.dynamic_slice_in_dim(inputs, me * chunk, chunk, 0)
    recip_in = lax.dynamic_slice_in_dim(recip_one, me * chunk, chunk, 0)
    d_gain_one = jnp.sum(dn1 * inputs_own * recip_in, axis=0)
    weighted_one = gain_one * dn1
    d_tokens = (
        d_resid
        + recip_in * weighted_one
        - inputs_own * recip_in**3 * jnp.mean(weighted_one * inputs_own, axis=1, keepdims=True)
    ).astype(BF)
    d_tokens = lax.all_gather(d_tokens, "head", axis=0, tiled=True)

    d_mlp = jnp.concatenate(
        [rows_inner(normed_two, d_gate_pre).astype(BF), rows_inner(normed_two, d_up_pre).astype(BF)], 1
    )
    d_mlp = lax.psum_scatter(d_mlp, "batch", scatter_dimension=0, tiled=True).astype(F32)
    d_down = rows_inner(hidden, out_grad).astype(BF)
    d_down = lax.psum_scatter(d_down, "batch", scatter_dimension=1, tiled=True).astype(F32)
    d_in = rows_inner(normed_one, d_cat).astype(BF)
    d_in = lax.psum_scatter(d_in, "batch", scatter_dimension=0, tiled=True).astype(F32)
    d_out = lax.psum_scatter(d_out_head, "batch", scatter_dimension=1, tiled=True).astype(F32)
    d_gains = lax.psum(jnp.stack([d_gain_one, d_gain_two]), ("batch", "head"))
    d_gains = lax.dynamic_slice_in_dim(
        d_gains, lax.axis_index("batch") * norm1_gain.shape[0], norm1_gain.shape[0], 1
    )
    hidden_own = w_mlp_gate.shape[1]
    return (
        output,
        d_tokens,
        d_gains[0],
        d_in[:, :head_size],
        d_in[:, head_size : head_size + half],
        d_in[:, head_size + half : 2 * head_size],
        d_in[:, 2 * head_size :],
        d_out,
        d_gains[1],
        d_mlp[:, :hidden_own],
        d_mlp[:, hidden_own:],
        d_down,
    )


def solution(mesh):
    return jax.shard_map(
        per_device,
        mesh=mesh,
        in_specs=(
            P("batch", None),
            P("batch"),
            P("batch"),
            P("batch", "head"),
            P("batch", "head"),
            P("batch", "head"),
            P("batch", "head"),
            P("head", "batch"),
            P("batch"),
            P("batch", "head"),
            P("batch", "head"),
            P("head", "batch"),
            P("batch", None),
        ),
        out_specs=(
            P("batch", None),
            P("batch", None),
            P("batch"),
            P("batch", "head"),
            P("batch", "head"),
            P("batch", "head"),
            P("batch", "head"),
            P("head", "batch"),
            P("batch"),
            P("batch", "head"),
            P("batch", "head"),
            P("head", "batch"),
        ),
        check_vma=False,
    )
```

time: 1590 us -> 1240 us (0.78)
  waiting for transfers between devices: 1120 us -> 879 us
  blocking collectives: 133 us -> 59.1 us
  other arithmetic: 95.2 us -> 52.6 us
  matrix products: 175 us -> 137 us
  local copies, waits for them, and re-layouts: 25 us -> 51.8 us
    psum x3 -> x0, waiting for transfers between devices: 836 us -> none  [the longest x1 331 us: per_device(): lax.psum(mlp_part.astype(jnp.bfloat16), 'head').astype(jnp.float32)]
    reduce_scatter x9, waiting for transfers between devices: 218 us -> 545 us  [the longest x1 103 us: per_device(): lax.psum_scatter(mlp_part, 'head', scatter_dimension=0, tiled=True)]
    all_gather x4 -> x9, waiting for transfers between devices: 51.7 us -> 304 us  [the longest x1 83.3 us: per_device(): lax.all_gather((resid_own + mlp_own).astype(BF), 'head', axis=0, tiled=True)]
    all_gather x8 -> x3, blocking collectives: 107 us -> 18.1 us  [the longest x1 7.65 us: per_device(): out_own = lax.all_gather(w_out, 'batch', axis=1, tiled=True)]
    dot_general x13 -> x10, matrix products: 73.1 us -> 49.5 us  [cols_inner(): lax.dot_general(left, right, (((1,), (1,)), ((), ())), preferred_element_...]
    convert_element_type x18 -> x9, other arithmetic: 46 us -> 23.8 us  [the longest x1 7.94 us: per_device(): inputs = tokens.astype(F32)]
    psum x1, blocking collectives: 19.1 us -> 41 us  [per_device(): d_gains = lax.psum(jnp.stack([d_gain_one, d_gain_two]), ('batch', 'head'))]
    dot_general x10 -> x7, matrix products: 51.8 us -> 36.5 us  [rows_inner(): lax.dot_general(left, right, (((0,), (0,)), ((), ())), preferred_element_...]
  transfers between devices with their start and end apart: 18 -> 21, of which waited for: 16 -> 21; matrix products, arithmetic and copies ran while one was open for 9% -> 12% of each run, Pallas kernels for 0% -> 0%
where the time goes in v1:
time: 1240 us; the launch traced here: 1230 us
  waiting for transfers between devices  879 us (71%)
  matrix products  137 us (11%)
  blocking collectives  59.1 us (5%)
  other arithmetic  52.6 us (4%)
  local copies, waits for them, and re-layouts  51.8 us (4%)
  between operations  22.7 us (2%)
  loops' own time  19 us (2%)
    reduce_scatter x1, waiting for transfers between devices, per_device(): lax.psum_scatter(mlp_part, 'head', scatter_dimension=0, tiled=True)  103 us
    reduce_scatter x1, waiting for transfers between devices, per_device(): lax.psum_scatter(dn2_part.astype(BF), 'head', scatter_dimension=0, tiled=...  94.8 us
    reduce_scatter x1, waiting for transfers between devices, per_device(): lax.psum_scatter(dn1_part, 'head', scatter_dimension=0, tiled=True)  91 us
    all_gather x1, waiting for transfers between devices, per_device(): lax.all_gather((resid_own + mlp_own).astype(BF), 'head', axis=0, tiled=True)  83.3 us
    reduce_scatter x1, waiting for transfers between devices, per_device(): lax.psum_scatter(d_kv_all, 'batch', scatter_dimension=0, tiled=True)  74.5 us
    reduce_scatter x1, waiting for transfers between devices, per_device(): lax.psum_scatter(d_mlp, 'batch', scatter_dimension=0, tiled=True)  58.5 us
    all_gather x1, waiting for transfers between devices, per_device(): mixed_all = lax.all_gather(mixed, 'head', axis=1, tiled=True)  55.6 us
    all_gather x1, waiting for transfers between devices, per_device(): out_full = lax.all_gather(out_own, 'head', axis=0, tiled=True)  52.5 us
  transfers between devices with their start and end apart: 21, of which 21 were waited for; matrix products, arithmetic and copies ran while one was open for 12% of the time, Pallas kernels for 0%

profile of v1, /device:TPU:0, one launch (start us, length us, event | category | flops | bytes accessed | tf_op | source)
XLA Modules:
  0.0 1231.5 jit_solution(9865374111591020541)
XLA Ops:
  28.6 13.7 %all-gather.11.cloned.1.call-done = bf16[2048,512]{1,0:T(8,128)(2,1)} async-done(((bf16[512,512]{1,0:T(8,128)(2,1)}), bf16[2048,512]{1,0:T(8,128)(2,1)}) %all-gather.11.cloned.1.call-update) | async-done | bytes 2097168 | tf_op jit(solution)/shard_map/all_gather | solution.py:80
  99.9 52.5 %all-gather.17.cloned.1.call-done = bf16[1024,2048]{1,0:T(8,128)(2,1)} async-done(((bf16[128,2048]{1,0:T(8,128)(2,1)}), bf16[1024,2048]{1,0:T(8,128)(2,1)}) %all-gather.17.cloned.1.call-update) | async-done | bytes 4194320 | tf_op jit(solution)/shard_map/all_gather | solution.py:85
  152.4 55.6 %all-gather.15.cloned.1.call-done = bf16[1280,1024]{0,1:T(8,128)(2,1)} async-done(((bf16[1280,128]{0,1:T(8,128)(2,1)}), bf16[1280,1024]{0,1:T(8,128)(2,1)}) %all-gather.15.cloned.1.call-update) | async-done | bytes 2621456 | tf_op jit(solution)/shard_map/all_gather | solution.py:153
  208.0 10.3 multiply_reduce_fusion
  225.5 11.0 all-gather.19.cloned.1.call-done
  236.5 9.6 fusion.168
  246.2 20.4 %all-gather.21.cloned.1.call-done = bf16[2048,768]{1,0:T(8,128)(2,1)} async-done(((bf16[512,768]{1,0:T(8,128)(2,1)}), bf16[2048,768]{1,0:T(8,128)(2,1)}) %all-gather.21.cloned.1.call-update) | async-done | bytes 3145744 | tf_op jit(solution)/shard_map/all_gather | solution.py:87
  276.1 20.6 %all-gather.23.cloned.1.call-done = bf16[768,2048]{1,0:T(8,128)(2,1)} async-done(((bf16[768,512]{1,0:T(8,128)(2,1)}), bf16[768,2048]{1,0:T(8,128)(2,1)}) %all-gather.23.cloned.1.call-update) | async-done | bytes 3145744 | tf_op jit(solution)/shard_map/all_gather | solution.py:88
  296.7 13.6 %multiply_convert_fusion.2 = (bf16[1280,768]{1,0:T(8,128)(2,1)}, bf16[1280,768]{1,0:T(8,128)(2,1)}, bf16[1280,768]{1,0:T(8,128)(2,1)S(1)}) fusion(f32[1280,768]{1,0:T(8,128)} %fusion.168, f32[1280,768]{1,0:T(8,128)} %fusion.169, bf16[1280,2048]{1,0:T(8,128)(2,1)} %param.57, bf16[768,2048]{1,0:T(8,128)(2,1)} %all-gather.23.cloned.1.call-done), kind=kOutput, calls=%fused_computation.193 | convolution fusion | flops 4041277440 | bytes 22151168 | tf_op jit(solution)/shard_map/dot_general | solution.py:29
  332.7 94.8 %reduce-scatter.12.cloned.1.call-done = bf16[160,2048]{1,0:T(8,128)(2,1)} async-done(((bf16[1280,2048]{1,0:T(8,128)(2,1)}), bf16[160,2048]{1,0:T(8,128)(2,1)}) %reduce-scatter.12.cloned.1.call-update) | async-done | bytes 655376 | tf_op jit(solution)/shard_map/reduce_scatter | solution.py:171
  429.9 103.4 %reduce-scatter.10.cloned.1.call-done = bf16[160,2048]{1,0:T(8,128)(2,1)} async-done(((bf16[1280,2048]{1,0:T(8,128)(2,1)}), bf16[160,2048]{1,0:T(8,128)(2,1)}) %reduce-scatter.10.cloned.1.call-update) | async-done | bytes 655376 | tf_op jit(solution)/shard_map/reduce_scatter | solution.py:173
  544.6 10.4 all-to-all-done
  568.8 18.2 %conditional.28 = (f32[1280,128]{1,0:T(8,128)}, bf16[1280,256]{0,1:T(8,128)(2,1)}) conditional(s32[]{:T(128)} %bitcast.4, () %tuple.134, (s32[1280]{0:T(1024)S(1)}, s32[5120]{0:T(1024)S(1)}, s32[1280]{0:T(1024)S(1)}, bf16[5120,256]{0,1:T(8,128)(2,1)S(1)}, bf16[1280,128]{0,1:T(8,128)(2,1)S(1)}, /*index=5*/f32[1280]{0:T(1024)S(1)}, ...), branch_computations={%region_41.42_spmd, %region_42.43_spmd} | conditional | flops 2116812800 | bytes 39685136 | solution.py:217
  608.9 74.5 %reduce-scatter.14.cloned.1.call-done = bf16[1280,256]{0,1:T(8,128)(2,1)} async-done(((bf16[5120,256]{0,1:T(8,128)(2,1)}), bf16[1280,256]{0,1:T(8,128)(2,1)}) %reduce-scatter.14.cloned.1.call-update) | async-done | bytes 655376 | tf_op jit(solution)/shard_map/reduce_scatter | solution.py:220
  691.9 12.9 %collective-permute-done.1 = bf16[1280,256]{0,1:T(8,128)(2,1)S(1)} collective-permute-done((bf16[1280,256]{0,1:T(8,128)(2,1)}, bf16[1280,256]{0,1:T(8,128)(2,1)S(1)}, u32[]{:S(2)}, u32[]{:S(2)}) %collective-permute-start.1) | collective-permute-done | bytes 655392 | tf_op jit(solution)/shard_map/ppermute | solution.py:17
  740.8 35.7 %reduce-scatter.20.cloned.1.call-done = bf16[128,2048]{1,0:T(8,128)(2,1)} async-done(((bf16[1024,2048]{1,0:T(8,128)(2,1)}), bf16[128,2048]{1,0:T(8,128)(2,1)}) %reduce-scatter.20.cloned.1.call-update) | async-done | bytes 524304 | tf_op jit(solution)/shard_map/reduce_scatter | solution.py:187
  791.9 91.0 %reduce-scatter.16.cloned.1.call-done = bf16[160,2048]{1,0:T(8,128)(2,1)} async-done(((bf16[1280,2048]{1,0:T(8,128)(2,1)}), bf16[160,2048]{1,0:T(8,128)(2,1)}) %reduce-scatter.16.cloned.1.call-update) | async-done | bytes 655376 | tf_op jit(solution)/shard_map/reduce_scatter | solution.py:242
  887.6 35.6 %reduce-scatter.26.cloned.1.call-done = bf16[768,512]{1,0:T(8,128)(2,1)} async-done(((bf16[768,2048]{1,0:T(8,128)(2,1)}), bf16[768,512]{1,0:T(8,128)(2,1)}) %reduce-scatter.26.cloned.1.call-update) | async-done | bytes 786448 | tf_op jit(solution)/shard_map/reduce_scatter | solution.py:259
  925.6 58.5 %reduce-scatter.24.cloned.1.call-done = bf16[512,1536]{0,1:T(8,128)(2,1)} async-done(((bf16[2048,1536]{0,1:T(8,128)(2,1)}), bf16[512,1536]{0,1:T(8,128)(2,1)}) %reduce-scatter.24.cloned.1.call-update) | async-done | bytes 1572880 | tf_op jit(solution)/shard_map/reduce_scatter | solution.py:257
  989.1 83.3 %all-gather.25.cloned.1.call-done = bf16[1280,2048]{1,0:T(8,128)(2,1)} async-done(((bf16[160,2048]{1,0:T(8,128)(2,1)}), bf16[1280,2048]{1,0:T(8,128)(2,1)}) %all-gather.25.cloned.1.call-update) | async-done | bytes 5242896 | tf_op jit(solution)/shard_map/all_gather | solution.py:174
  1072.4 22.2 %reduce-scatter.22.cloned.1.call-done = bf16[128,512]{1,0:T(8,128)(2,1)} async-done(((bf16[128,2048]{1,0:T(8,128)(2,1)}), bf16[128,512]{1,0:T(8,128)(2,1)}) %reduce-scatter.22.cloned.1.call-update) | async-done | bytes 131088 | tf_op jit(solution)/shard_map/reduce_scatter | solution.py:262
  1096.2 29.7 %reduce-scatter.18.cloned.1.call-done = bf16[512,384]{1,0:T(8,128)(2,1)} async-done(((bf16[2048,384]{1,0:T(8,128)(2,1)}), bf16[512,384]{1,0:T(8,128)(2,1)}) %reduce-scatter.18.cloned.1.call-update) | async-done | bytes 393232 | tf_op jit(solution)/shard_map/reduce_scatter | solution.py:261
  1130.4 41.0 %psum.7 = f32[2,2048]{1,0:T(2,128)S(1)} all-reduce(f32[2,2048]{1,0:T(2,128)S(1)} %pad_maximum_fusion.11), channel_id=1, replica_groups=mesh['batch'=4,'head'=8] {'batch','head'}, use_global_device_ids=true, to_apply=%region_54.55 | all-reduce | flops 4096 | bytes 32768 | tf_op jit(solution)/shard_map/psum | solution.py:263
  1172.1 44.2 %all-gather.27.cloned.1.call-done = bf16[1280,2048]{1,0:T(8,128)(2,1)} async-done(((bf16[160,2048]{1,0:T(8,128)(2,1)}), bf16[1280,2048]{1,0:T(8,128)(2,1)}) %all-gather.27.cloned.1.call-update) | async-done | bytes 5242896 | tf_op jit(solution)/shard_map/all_gather | solution.py:252
  (196 shorter events, 286.1 us)
Async XLA Ops:
  7.2 35.1 %all-gather.11.cloned.1.call-start = ((), (), s32[]{:S(2)}) async-start(), calls=%async_computation.10 | async-start | bytes 2621440 | tf_op jit(solution)/shard_map/all_gather | solution.py:80
  9.3 6.5 collective-permute-start
  18.1 58.8 %all-gather.13.cloned.1.call-start = ((), (), s32[]{:S(2)}) async-start(), calls=%async_computation.11 | async-start | bytes 3276800 | tf_op jit(solution)/shard_map/all_gather | solution.py:98
  51.0 101.4 %all-gather.17.cloned.1.call-start = ((), (), s32[]{:S(2)}) async-start(), calls=%async_computation.13 | async-start | bytes 4718592 | tf_op jit(solution)/shard_map/all_gather | solution.py:85
  58.7 149.3 %all-gather.15.cloned.1.call-start = ((), (), s32[]{:S(2)}) async-start(), calls=%async_computation.12 | async-start | bytes 2949120 | tf_op jit(solution)/shard_map/all_gather | solution.py:153
  95.7 122.7 %copy-start.4 = (f32[1280,128]{0,1:T(8,128)}, f32[1280,128]{0,1:T(8,128)S(1)}, u32[]{:S(2)}) copy-start(f32[1280,128]{0,1:T(8,128)S(1)} %get-tuple-element.854) | copy-start | bytes 1966084
  97.9 138.6 %all-gather.19.cloned.1.call-start = ((), (), s32[]{:S(2)}) async-start(), calls=%async_computation.14 | async-start | bytes 3932160 | tf_op jit(solution)/shard_map/all_gather | solution.py:86
  98.5 168.0 %all-gather.21.cloned.1.call-start = ((), (), s32[]{:S(2)}) async-start(), calls=%async_computation.15 | async-start | bytes 3932160 | tf_op jit(solution)/shard_map/all_gather | solution.py:87
  99.1 197.6 %all-gather.23.cloned.1.call-start = ((), (), s32[]{:S(2)}) async-start(), calls=%async_computation.16 | async-start | bytes 3932160 | tf_op jit(solution)/shard_map/all_gather | solution.py:88
  99.8 327.6 %reduce-scatter.12.cloned.1.call-start = ((), (), s32[]{:S(2)}) async-start(), calls=%async_computation.19 | async-start | bytes 5898240 | tf_op jit(solution)/shard_map/reduce_scatter | solution.py:171
  324.7 208.7 %reduce-scatter.10.cloned.1.call-start = ((), (), s32[]{:S(2)}) async-start(), calls=%async_computation.17 | async-start | bytes 5898240 | tf_op jit(solution)/shard_map/reduce_scatter | solution.py:173
  540.1 15.0 %all-to-all-start = ((bf16[160,8,128]{2,0,1:T(8,128)(2,1)}), bf16[160,8,128]{2,0,1:T(8,128)(2,1)S(1)}, u32[]{:S(2)}, u32[]{:S(2)}) async-start(bf16[160,8,128]{2,0,1:T(8,128)(2,1)} %bitcast.84), calls=%async_computation.2 | async-start | bytes 655360 | tf_op jit(solution)/shard_map/all_to_all | solution.py:185
  544.6 138.8 %reduce-scatter.14.cloned.1.call-start = ((), (), s32[]{:S(2)}) async-start(), calls=%async_computation.20 | async-start | bytes 3276800 | tf_op jit(solution)/shard_map/reduce_scatter | solution.py:220
  604.4 172.1 %reduce-scatter.20.cloned.1.call-start = ((), (), s32[]{:S(2)}) async-start(), calls=%async_computation.24 | async-start | bytes 4718592 | tf_op jit(solution)/shard_map/reduce_scatter | solution.py:187
  608.9 96.1 %copy-start.8 = (bf16[1280,128]{0,1:T(8,128)(2,1)S(1)}, bf16[1280,128]{0,1:T(8,128)(2,1)}, u32[]{:S(2)}) copy-start(bf16[1280,128]{0,1:T(8,128)(2,1)} %get-tuple-element.873) | copy-start | bytes 983044
  608.9 273.9 %reduce-scatter.16.cloned.1.call-start = ((), (), s32[]{:S(2)}) async-start(), calls=%async_computation.21 | async-start | bytes 5898240 | tf_op jit(solution)/shard_map/reduce_scatter | solution.py:242
  683.4 21.4 %collective-permute-start.1 = (bf16[1280,256]{0,1:T(8,128)(2,1)}, bf16[1280,256]{0,1:T(8,128)(2,1)S(1)}, u32[]{:S(2)}, u32[]{:S(2)}) collective-permute-start(bf16[1280,256]{0,1:T(8,128)(2,1)} %reduce-scatter.14.cloned.1.call-done), channel_id=1, source_target_pairs={{0,1},{1,0},{2,3},{3,2},{4,5},{5,4},{6,7},{7,6},{8,9},{9,8},{10,11... | collective-permute-start | bytes 1966088 | tf_op jit(solution)/shard_map/ppermute | solution.py:17
  711.9 211.2 %reduce-scatter.26.cloned.1.call-start = ((), (), s32[]{:S(2)}) async-start(), calls=%async_computation.27 | async-start | bytes 3932160 | tf_op jit(solution)/shard_map/reduce_scatter | solution.py:259
  721.5 262.5 %reduce-scatter.24.cloned.1.call-start = ((), (), s32[]{:S(2)}) async-start(), calls=%async_computation.26 | async-start | bytes 7864320 | tf_op jit(solution)/shard_map/reduce_scatter | solution.py:257
  740.2 332.2 %all-gather.25.cloned.1.call-start = ((), (), s32[]{:S(2)}) async-start(), calls=%async_computation.18 | async-start | bytes 5898240 | tf_op jit(solution)/shard_map/all_gather | solution.py:174
  740.8 353.8 %reduce-scatter.22.cloned.1.call-start = ((), (), s32[]{:S(2)}) async-start(), calls=%async_computation.25 | async-start | bytes 655360 | tf_op jit(solution)/shard_map/reduce_scatter | solution.py:262
  776.5 349.4 %reduce-scatter.18.cloned.1.call-start = ((), (), s32[]{:S(2)}) async-start(), calls=%async_computation.23 | async-start | bytes 1966080 | tf_op jit(solution)/shard_map/reduce_scatter | solution.py:261
  783.8 432.5 %all-gather.27.cloned.1.call-start = ((), (), s32[]{:S(2)}) async-start(), calls=%async_computation.22 | async-start | bytes 5898240 | tf_op jit(solution)/shard_map/all_gather | solution.py:252
  987.5 142.9 %copy-start.14 = (f32[2048]{0:T(1024)S(1)}, f32[2048]{0:T(1024)}, u32[]{:S(2)}) copy-start(f32[2048]{0:T(1024)} %get-tuple-element.857) | copy-start | bytes 24580
  (18 other events, 281.5 us)
Sparse Core Ops, SparseCore 0:
  18.2 24.0 all-gather.10
  51.1 25.6 all-gather.12
  79.0 73.4 all-gather.16
  155.0 52.9 all-gather.14
  209.4 27.0 all-gather.18
  238.0 28.5 all-gather.20
  268.1 28.5 all-gather.22
  324.8 102.5 reduce-scatter.11
  431.0 102.3 reduce-scatter.9
  604.5 78.8 reduce-scatter.13
  687.5 89.0 reduce-scatter.19
  780.5 102.2 reduce-scatter.15
  885.3 37.7 reduce-scatter.25
  925.7 58.3 reduce-scatter.23
  986.1 86.2 all-gather.24
  1074.8 19.7 reduce-scatter.21
  1097.7 28.1 reduce-scatter.17
  1128.6 87.6 all-gather.26

commit v2 on v1

--- a/solution.py
+++ b/solution.py
@@ -1,14 +1,194 @@
+import functools
 import math
 
 import jax
 import jax.numpy as jnp
 from jax import lax
+from jax.experimental import pallas as pl
+from jax.experimental.pallas import tpu as pltpu
 from jax.sharding import PartitionSpec as P
 
 EPSILON = 1e-06
 MASKED = -1e30
 BF = jnp.bfloat16
 F32 = jnp.float32
+
+
+MESH = pl.DeviceIdType.MESH
+VMEM_LIMIT = 60 << 20
+
+
+def ring_place(head, count):
+    high, low = head // 2, head % 2
+    return (1 - low) * high + low * (count - 1 - high)
+
+
+def ring_head(place, count):
+    low = place // (count // 2)
+    high = (1 - low) * place + low * (count - 1 - place)
+    return 2 * high + low
+
+
+def ring_setup(count):
+    batch = lax.axis_index("batch")
+    place = ring_place(lax.axis_index("head"), count)
+    right = (batch, ring_head(lax.rem(place + 1, count), count))
+    left = (batch, ring_head(lax.rem(place + count - 1, count), count))
+    return place, right, left
+
+
+def greet(devices):
+    barrier = pltpu.get_barrier_semaphore()
+    for device in devices:
+        pl.semaphore_signal(barrier, inc=1, device_id=device, device_id_type=MESH)
+    pl.semaphore_wait(barrier, len(devices))
+
+
+def send(source, target, sems, slot, device):
+    copy = pltpu.make_async_remote_copy(
+        src_ref=source,
+        dst_ref=target,
+        send_sem=sems[0].at[slot],
+        recv_sem=sems[1].at[slot],
+        device_id=device,
+        device_id_type=MESH,
+    )
+    copy.start()
+    return copy
+
+
+def sum_kernel(count, part_ref, own_ref, from_left, from_right, send_sem, recv_sem):
+    steps = count // 2
+    rows = part_ref.shape[0] // count
+    width = part_ref.shape[1]
+    side = width // 2
+    place, right, left = ring_setup(count)
+    greet((right, left))
+    sems = (send_sem, recv_sem)
+
+    def part(owner):
+        return part_ref.at[pl.ds(pl.multiple_of(lax.rem(owner + count, count) * rows, rows), rows)]
+
+    far = part(place + steps)
+    copies = [
+        send(far.at[:, pl.ds(0, side)], from_left.at[0, :, pl.ds(0, side)], sems, 0, right),
+        send(far.at[:, pl.ds(side, side)], from_right.at[0, :, pl.ds(side, side)], sems, steps, left),
+    ]
+    for step in range(1, steps):
+        for flow, held, owner, device in (
+            (0, from_left, place + steps - step, right),
+            (1, from_right, place - steps + step, left),
+        ):
+            copies[2 * step - 2 + flow].wait_recv()
+            mine = part(owner)
+            if step == 1:
+                have = pl.ds(flow * side, side)
+                lack = pl.ds((1 - flow) * side, side)
+                held[0, :, have] = (held[0, :, have].astype(F32) + mine[:, have].astype(F32)).astype(BF)
+                held[0, :, lack] = mine[:, lack]
+            else:
+                held[step - 1] = (held[step - 1].astype(F32) + mine[...].astype(F32)).astype(BF)
+            copies.append(
+                send(held.at[step - 1], held.at[step], sems, flow * steps + step, device)
+            )
+    copies[-2].wait_recv()
+    copies[-1].wait_recv()
+    own_ref[...] = (
+        part(place)[...].astype(F32)
+        + from_left[steps - 1].astype(F32)
+        + from_right[steps - 1].astype(F32)
+    )
+    for copy in copies:
+        copy.wait_send()
+
+
+def sum_own(part, collective_id):
+    count = lax.axis_size("head")
+    rows, width = part.shape[0] // count, part.shape[1]
+    vmem = pl.BlockSpec(memory_space=pltpu.VMEM)
+    return pl.pallas_call(
+        functools.partial(sum_kernel, count),
+        out_shape=jax.ShapeDtypeStruct((rows, width), F32),
+        in_specs=[vmem],
+        out_specs=vmem,
+        scratch_shapes=[
+            pltpu.VMEM((count // 2, rows, width), BF),
+            pltpu.VMEM((count // 2, rows, width), BF),
+            pltpu.SemaphoreType.DMA((count,)),
+            pltpu.SemaphoreType.DMA((count,)),
+        ],
+        compiler_params=pltpu.CompilerParams(
+            collective_id=collective_id, has_side_effects=True, vmem_limit_bytes=VMEM_LIMIT
+        ),
+        name=f"sum_own_{collective_id}",
+    )(part)
+
+
+def half_of(extent, flow):
+    if extent[1] % 256:
+        return (pl.ds(flow * (extent[0] // 2), extent[0] // 2), slice(None))
+    return (slice(None), pl.ds(flow * (extent[1] // 2), extent[1] // 2))
+
+
+def spread_kernel(count, arrays, *refs):
+    steps = count // 2
+    own_refs, all_refs = refs[:arrays], refs[arrays : 2 * arrays]
+    send_sem, recv_sem, local_sem = refs[2 * arrays :]
+    place, right, left = ring_setup(count)
+    greet((right, left))
+    sems = (send_sem, recv_sem)
+    local = []
+    for index in range(arrays):
+        copy = pltpu.make_async_copy(own_refs[index], all_refs[index].at[place], local_sem.at[index])
+        copy.start()
+        local.append(copy)
+    waiting = []
+    copies = [None] * (2 * arrays)
+    for step in range(steps):
+        for index in range(arrays):
+            extent = own_refs[index].shape
+            for flow, chunk, device in (
+                (0, place - step, right),
+                (1, place + step, left),
+            ):
+                at = 2 * index + flow
+                if step:
+                    copies[at].wait_recv()
+                chunk = lax.rem(chunk + count, count)
+                target = all_refs[index].at[chunk]
+                source = target if step else own_refs[index]
+                if step == steps - 1:
+                    part = half_of(extent, flow)
+                    source = source.at[part]
+                    target = target.at[part]
+                copies[at] = send(source, target, sems, at * steps + step, device)
+                waiting.append(copies[at])
+    for copy in copies:
+        copy.wait_recv()
+    for copy in waiting:
+        copy.wait_send()
+    for copy in local:
+        copy.wait()
+
+
+def spread(arrays, collective_id, space=pl.ANY):
+    count = lax.axis_size("head")
+    slots = len(arrays) * count
+    return pl.pallas_call(
+        functools.partial(spread_kernel, count, len(arrays)),
+        out_shape=[jax.ShapeDtypeStruct((count, *a.shape), a.dtype) for a in arrays],
+        in_specs=[pl.BlockSpec(memory_space=space)] * len(arrays),
+        out_specs=[pl.BlockSpec(memory_space=space)] * len(arrays),
+        scratch_shapes=[
+            pltpu.SemaphoreType.DMA((slots,)),
+            pltpu.SemaphoreType.DMA((slots,)),
+            pltpu.SemaphoreType.DMA((len(arrays),)),
+        ],
+        compiler_params=pltpu.CompilerParams(
+            collective_id=collective_id, has_side_effects=True, vmem_limit_bytes=VMEM_LIMIT
+        ),
+        name=f"spread_{collective_id}",
+    )(*arrays)
 
 
 def from_partner(block, axis):
@@ -62,8 +242,8 @@
     head_size = w_query.shape[1]
     half = w_key.shape[1]
     chunk = row_count // heads
-    me = lax.axis_index("head")
-    first = me % 2 == 0
+    first = lax.axis_index("head") % 2 == 0
+    me = ring_place(lax.axis_index("head"), heads)
     scale_factor = 1.0 / math.sqrt(head_size)
 
     kv_shard = jnp.concatenate([w_key, w_value], axis=1)
@@ -81,8 +261,8 @@
     gains = lax.all_gather(jnp.stack([norm1_gain, norm2_gain]), "batch", axis=1, tiled=True)
     gain_one = gains[0].astype(F32)
     gain_two = gains[1].astype(F32)
-    out_own = lax.all_gather(w_out, "batch", axis=1, tiled=True)
-    out_full = lax.all_gather(out_own, "head", axis=0, tiled=True)
+    (out_rows,) = spread([w_out], 1)
+    out_full = lax.all_gather(out_rows.reshape(heads * head_size, -1), "batch", axis=1, tiled=True)
     mgate_full = lax.all_gather(w_mlp_gate, "batch", axis=0, tiled=True)
     mup_full = lax.all_gather(w_mlp_up, "batch", axis=0, tiled=True)
     down_full = lax.all_gather(w_down, "batch", axis=1, tiled=True)
@@ -150,7 +330,8 @@
         attended = lax.cond(is_live(block_index), accumulate, keep_same, attended)
 
     mixed = (attended * gate_vals).astype(BF)
-    mixed_all = lax.all_gather(mixed, "head", axis=1, tiled=True)
+    (mixed_all,) = spread([mixed], 2)
+    mixed_all = mixed_all.transpose(1, 0, 2).reshape(row_count, -1)
     resid = inputs + matmul(mixed_all, out_full)
     recip_two = rms_scale(resid)
     normed_two = (resid * recip_two * gain_two).astype(BF)
@@ -168,10 +349,9 @@
     d_gate_pre = (d_hidden * up_pre * sig_gate * (1.0 + gate_pre * (1.0 - sig_gate))).astype(BF)
     d_up_pre = (d_hidden * silu_gate).astype(BF)
     dn2_part = cols_inner(d_gate_pre, mgate_full) + cols_inner(d_up_pre, mup_full)
-    dn2 = lax.psum_scatter(dn2_part.astype(BF), "head", scatter_dimension=0, tiled=True).astype(F32)
+    dn2 = sum_own(dn2_part.astype(BF), 3)
     mlp_part = matmul(hidden, down_full).astype(BF)
-    mlp_own = lax.psum_scatter(mlp_part, "head", scatter_dimension=0, tiled=True).astype(F32)
-    output = lax.all_gather((resid_own + mlp_own).astype(BF), "head", axis=0, tiled=True)
+    output = (resid_own + sum_own(mlp_part, 4)).astype(BF)
 
     d_gain_two = jnp.sum(dn2 * resid_own * recip_own, axis=0)
     weighted_two = gain_two * dn2
@@ -182,9 +362,15 @@
     )
     d_resid_low = d_resid.astype(BF)
     d_mixed_all = cols_inner(d_resid_low, out_full).astype(BF)
-    d_mixed = lax.all_to_all(d_mixed_all, "head", split_axis=1, concat_axis=0, tiled=True).astype(F32)
+    d_mixed_all = d_mixed_all.reshape(chunk, heads, head_size)
+    places = [ring_place(at, heads) for at in range(heads)]
+    d_mixed_all = jnp.stack([d_mixed_all[:, at] for at in places], axis=0)
+    d_mixed = lax.all_to_all(d_mixed_all, "head", split_axis=0, concat_axis=0, tiled=True)
+    d_mixed = jnp.concatenate([d_mixed[ring_head(at, heads)] for at in range(heads)], axis=0)
+    d_mixed = d_mixed.astype(F32)
     d_out_part = rows_inner(mixed_own, d_resid_low).astype(BF)
-    d_out_head = lax.psum_scatter(d_out_part, "head", scatter_dimension=0, tiled=True)
+    d_out_part = lax.psum_scatter(d_out_part, "batch", scatter_dimension=1, tiled=True)
+    d_out = sum_own(d_out_part, 7)
 
     d_attended = (d_mixed * gate_vals).astype(BF)
     d_gate_logit = (d_mixed * attended * gate_vals * (1.0 - gate_vals)).astype(BF)
@@ -239,7 +425,7 @@
         [w_in[:, :head_size], w_key_own, w_value_own, w_in[:, 3 * head_size :]], axis=1
     )
     dn1_part = cols_inner(d_cat, w_cat).astype(BF)
-    dn1 = lax.psum_scatter(dn1_part, "head", scatter_dimension=0, tiled=True).astype(F32)
+    dn1 = sum_own(dn1_part, 5)
     inputs_own = lax.dynamic_slice_in_dim(inputs, me * chunk, chunk, 0)
     recip_in = lax.dynamic_slice_in_dim(recip_one, me * chunk, chunk, 0)
     d_gain_one = jnp.sum(dn1 * inputs_own * recip_in, axis=0)
@@ -249,7 +435,9 @@
         + recip_in * weighted_one
         - inputs_own * recip_in**3 * jnp.mean(weighted_one * inputs_own, axis=1, keepdims=True)
     ).astype(BF)
-    d_tokens = lax.all_gather(d_tokens, "head", axis=0, tiled=True)
+    output, d_tokens = spread([output, d_tokens], 6)
+    output = output.reshape(row_count, width)
+    d_tokens = d_tokens.reshape(row_count, width)
 
     d_mlp = jnp.concatenate(
         [rows_inner(normed_two, d_gate_pre).astype(BF), rows_inner(normed_two, d_up_pre).astype(BF)], 1
@@ -259,7 +447,6 @@
     d_down = lax.psum_scatter(d_down, "batch", scatter_dimension=1, tiled=True).astype(F32)
     d_in = rows_inner(normed_one, d_cat).astype(BF)
     d_in = lax.psum_scatter(d_in, "batch", scatter_dimension=0, tiled=True).astype(F32)
-    d_out = lax.psum_scatter(d_out_head, "batch", scatter_dimension=1, tiled=True).astype(F32)
     d_gains = lax.psum(jnp.stack([d_gain_one, d_gain_two]), ("batch", "head"))
     d_gains = lax.dynamic_slice_in_dim(
         d_gains, lax.axis_index("batch") * norm1_gain.shape[0], norm1_gain.shape[0], 1

time: 1240 us -> 853 us (0.69)
  waiting for transfers between devices: 879 us -> 160 us
  Pallas kernels: 0 us -> 339 us
    reduce_scatter x5 -> x1, waiting for transfers between devices: 347 us -> 0.01 us  [per_device(): lax.psum_scatter(d_out_part, 'batch', scatter_dimension=1, tiled=True)]
    pallas_call x0 -> x7, Pallas kernels: none -> 339 us  [the longest x4 192 us: sum_own(): pl.pallas_call(functools.partial(sum_kernel, count), out_shape=jax.ShapeD...]
    all_gather x4 -> x1, waiting for transfers between devices: 236 us -> 0.01 us  [per_device(): lax.all_gather(out_rows.reshape(heads * head_size, -1), 'batch', axis=1,...]
    reduce_scatter x1, waiting for transfers between devices: 58.5 us -> 0.01 us  [per_device(): lax.psum_scatter(d_mlp, 'batch', scatter_dimension=0, tiled=True)]
    reduce_scatter x1, waiting for transfers between devices: 35.6 us -> 0.01 us  [per_device(): lax.psum_scatter(d_down, 'batch', scatter_dimension=1, tiled=True)]
    reduce_scatter x1, waiting for transfers between devices: 29.7 us -> 0.02 us  [per_device(): lax.psum_scatter(d_in, 'batch', scatter_dimension=0, tiled=True).astype(F32)]
    reduce_scatter x1, waiting for transfers between devices: 74.5 us -> 94.4 us  [per_device(): lax.psum_scatter(d_kv_all, 'batch', scatter_dimension=0, tiled=True)]
    all_gather x1, waiting for transfers between devices: 20.4 us -> 3.48 us  [per_device(): mup_full = lax.all_gather(w_mlp_up, 'batch', axis=0, tiled=True)]
  transfers between devices with their start and end apart: 21 -> 14, of which waited for: 21 -> 7; matrix products, arithmetic and copies ran while one was open for 12% -> 17% of each run, Pallas kernels for 0% -> 27%
where the time goes in v2:
time: 853 us; the launch traced here: 841 us
  Pallas kernels  339 us (40%)
  waiting for transfers between devices  160 us (19%)
  matrix products  141 us (17%)
  local copies, waits for them, and re-layouts  63.4 us (7%)
  other arithmetic  51.1 us (6%)
  blocking collectives  48.5 us (6%)
  between operations  22.5 us (3%)
  starting transfers between devices  9 us (1%)
    pallas_call x4, Pallas kernels, sum_own(): pl.pallas_call(functools.partial(sum_kernel, count), out_shape=jax.ShapeD...  192 us
    pallas_call x3, Pallas kernels, spread(): pl.pallas_call(functools.partial(spread_kernel, count, len(arrays)), out_...  147 us
    reduce_scatter x1, waiting for transfers between devices, per_device(): lax.psum_scatter(d_kv_all, 'batch', scatter_dimension=0, tiled=True)  94.4 us
    dot_general x7, matrix products, matmul(): return jnp.dot(left, right, preferred_element_type=F32)  53.8 us
    dot_general x10, matrix products, cols_inner(): lax.dot_general(left, right, (((1,), (1,)), ((), ())), preferred_element_...  50.9 us
    psum x1, blocking collectives, per_device(): d_gains = lax.psum(jnp.stack([d_gain_one, d_gain_two]), ('batch', 'head'))  38.1 us
    dot_general x7, matrix products, rows_inner(): lax.dot_general(left, right, (((0,), (0,)), ((), ())), preferred_element_...  36.1 us
    unnamed x78, local copies, waits for them, and re-layouts  26.5 us
  transfers between devices with their start and end apart: 14, of which 7 were waited for; matrix products, arithmetic and copies ran while one was open for 17% of the time, Pallas kernels for 27%

profile of v2, /device:TPU:0, one launch (start us, length us, event | category | flops | bytes accessed | tf_op | source)
XLA Modules:
  0.0 841.3 jit_solution(16498615626459024194)
XLA Ops:
  28.6 13.7 %all-gather.8.cloned.1.call-done = bf16[2048,512]{1,0:T(8,128)(2,1)} async-done(((bf16[512,512]{1,0:T(8,128)(2,1)}), bf16[2048,512]{1,0:T(8,128)(2,1)}) %all-gather.8.cloned.1.call-update) | async-done | bytes 2097168 | tf_op jit(solution)/shard_map/all_gather | solution.py:260
  42.3 7.8 fusion.170
  51.1 19.9 %spread_1.1 = bf16[8,128,512]{2,1,0:T(8,128)(2,1)} custom-call(bf16[128,512]{1,0:T(8,128)(2,1)} %refs_0_.1), custom_call_target="tpu_custom_call" | custom-call | tf_op jit(solution)/shard_map/spread_1/pallas_call | solution.py:177
  88.9 11.2 %conditional.16 = (f32[1280]{0:T(1024)}, f32[1280]{0:T(1024)S(1)}) conditional(s32[]{:T(128)} %bitcast.4, () %tuple.125, (s32[1280]{0:T(1024)S(1)}, s32[5120]{0:T(1024)S(1)}, s32[1280]{0:T(1024)S(1)}, bf16[5120,256]{0,1:T(8,128)(2,1)}, bf16[1280,128]{0,1:T(8,128)(2,1)S(1)}) %tuple.327), branch_computations={%region_1.2_spmd, %region_2.5_spmd} | conditional | flops 439095040 | bytes 19087376 | solution.py:312
  110.4 27.1 %spread_2.1 = bf16[8,1280,128]{2,1,0:T(8,128)(2,1)} custom-call(bf16[1280,128]{1,0:T(8,128)(2,1)} %multiply_convert_fusion.7.refs_0_), custom_call_target="tpu_custom_call" | custom-call | tf_op jit(solution)/shard_map/spread_2/pallas_call | solution.py:177
  142.0 10.3 %multiply_reduce_fusion = (f32[1280]{0:T(1024)S(1)}, f32[1280,2048]{1,0:T(8,128)S(1)}) fusion(bf16[1280,1024]{0,1:T(8,128)(2,1)} %bitcast.155, bf16[1024,2048]{1,0:T(8,128)(2,1)} %all-gather.12.cloned.1.call-done, bf16[1280,2048]{1,0:T(8,128)(2,1)} %param.45), kind=kOutput, calls=%fused_computation.186 | convolution fusion | flops 5379193856 | bytes 22549504 | tf_op jit(solution)/shard_map/dot_general | solution.py:201
  159.7 9.7 %fusion.171 = f32[1280,768]{1,0:T(8,128)} fusion(bf16[1280,2048]{1,0:T(8,128)(2,1)} %multiply_convert_fusion, bf16[2048,768]{1,0:T(8,128)(2,1)} %all-gather.14.cloned.1.call-done), kind=kOutput, calls=%fused_computation.299 | convolution fusion | flops 4026531840 | bytes 12320768 | tf_op jit(solution)/shard_map/dot_general | solution.py:201
  172.8 9.6 %fusion.172 = f32[1280,768]{1,0:T(8,128)} fusion(bf16[1280,2048]{1,0:T(8,128)(2,1)} %multiply_convert_fusion, bf16[2048,768]{1,0:T(8,128)(2,1)} %all-gather.16.cloned.1.call-done), kind=kOutput, calls=%fused_computation.300 | convolution fusion | flops 4026531840 | bytes 12320768 | tf_op jit(solution)/shard_map/dot_general | solution.py:201
  182.4 20.4 %all-gather.18.cloned.1.call-done = bf16[768,2048]{1,0:T(8,128)(2,1)} async-done(((bf16[768,512]{1,0:T(8,128)(2,1)}), bf16[768,2048]{1,0:T(8,128)(2,1)}) %all-gather.18.cloned.1.call-update) | async-done | bytes 3145744 | tf_op jit(solution)/shard_map/all_gather | solution.py:268
  202.8 14.2 %multiply_convert_fusion.2 = (bf16[1280,768]{1,0:T(8,128)(2,1)}, bf16[1280,768]{1,0:T(8,128)(2,1)}, bf16[1280,768]{1,0:T(8,128)(2,1)}) fusion(f32[1280,768]{1,0:T(8,128)} %fusion.171, f32[1280,768]{1,0:T(8,128)} %fusion.172, bf16[1280,2048]{1,0:T(8,128)(2,1)} %param.57, bf16[768,2048]{1,0:T(8,128)(2,1)} %all-gather.18.cloned.1.call-done), kind=kOutput, calls=%fused_computation.193 | convolution fusion | flops 4041277440 | bytes 22151168 | tf_op jit(solution)/shard_map/dot_general | solution.py:209
  230.8 60.0 %sum_own_3.1 = f32[160,2048]{1,0:T(8,128)} custom-call(bf16[1280,2048]{1,0:T(8,128)(2,1)} %add_convert_fusion.part_ref), custom_call_target="tpu_custom_call" | custom-call | tf_op jit(solution)/shard_map/sum_own_3/pallas_call | solution.py:109
  293.6 9.1 %convolution_convert_fusion.5.part_ref = bf16[1280,2048]{1,0:T(8,128)(2,1)} fusion(bf16[1280,768]{1,0:T(8,128)(2,1)} %get-tuple-element.878, bf16[768,2048]{1,0:T(8,128)(2,1)} %all-gather.18.cloned.1.call-done), kind=kOutput, calls=%fused_computation.191 | convolution fusion | flops 4029153280 | bytes 10354688 | tf_op jit(solution)/shard_map/dot_general | solution.py:201
  302.7 53.7 %sum_own_4.1 = f32[160,2048]{1,0:T(8,128)} custom-call(bf16[1280,2048]{1,0:T(8,128)(2,1)} %convolution_convert_fusion.5.part_ref), custom_call_target="tpu_custom_call" | custom-call | tf_op jit(solution)/shard_map/sum_own_4/pallas_call | solution.py:109
  370.7 8.6 %all-to-all-done = bf16[8,160,128]{2,1,0:T(8,128)(2,1)S(1)} async-done(((bf16[8,160,128]{2,1,0:T(8,128)(2,1)}), bf16[8,160,128]{2,1,0:T(8,128)(2,1)S(1)}, u32[]{:S(2)}, u32[]{:S(2)}) %all-to-all-start) | async-done | bytes 327712 | tf_op jit(solution)/shard_map/all_to_all | solution.py:368
  381.8 8.0 conditional.24
  390.2 16.8 %conditional.28 = (f32[1280,128]{1,0:T(8,128)}, bf16[1280,256]{1,0:T(8,128)(2,1)}) conditional(s32[]{:T(128)} %bitcast.4, () %tuple.134, (s32[1280]{0:T(1024)S(1)}, s32[5120]{0:T(1024)S(1)}, s32[1280]{0:T(1024)S(1)}, bf16[5120,256]{0,1:T(8,128)(2,1)S(1)}, bf16[1280,128]{0,1:T(8,128)(2,1)S(1)}, /*index=5*/f32[1280]{0:T(1024)S(1)}, ...), branch_computations={%region_39.40_spmd, %region_40.41_spmd} | conditional | flops 2116812800 | bytes 54103084 | solution.py:403
  418.9 8.2 convolution_convert_fusion.7
  433.4 94.4 %reduce-scatter.6.cloned.1.call-done = bf16[1280,256]{1,0:T(8,128)(2,1)} async-done(((bf16[5120,256]{1,0:T(8,128)(2,1)}), bf16[1280,256]{1,0:T(8,128)(2,1)}) %reduce-scatter.6.cloned.1.call-update) | async-done | bytes 655376 | tf_op jit(solution)/shard_map/reduce_scatter | solution.py:406
  530.4 14.1 %collective-permute-done.1 = bf16[1280,256]{1,0:T(8,128)(2,1)S(1)} collective-permute-done((bf16[1280,256]{1,0:T(8,128)(2,1)}, bf16[1280,256]{1,0:T(8,128)(2,1)S(1)}, u32[]{:S(2)}, u32[]{:S(2)}) %collective-permute-start.1) | collective-permute-done | bytes 655392 | tf_op jit(solution)/shard_map/ppermute | solution.py:197
  573.0 8.9 %convert_element_type.172 = f32[1280,2048]{1,0:T(8,128)} convert(bf16[1280,2048]{1,0:T(8,128)(2,1)} %param.45) | non-fusion elementwise | flops 2621440 | bytes 15728640 | tf_op jit(solution)/shard_map/convert_element_type | solution.py:271
  594.2 55.1 %sum_own_5.1 = f32[160,2048]{1,0:T(8,128)} custom-call(bf16[1280,2048]{1,0:T(8,128)(2,1)} %convolution_convert_fusion.4.part_ref), custom_call_target="tpu_custom_call" | custom-call | tf_op jit(solution)/shard_map/sum_own_5/pallas_call | solution.py:109
  654.4 100.0 %spread_6.1 = (bf16[8,160,2048]{2,1,0:T(8,128)(2,1)}, bf16[8,160,2048]{2,1,0:T(8,128)(2,1)}) custom-call(bf16[160,2048]{1,0:T(8,128)(2,1)} %get-tuple-element.875.refs_0_, bf16[160,2048]{1,0:T(8,128)(2,1)} %subtract_convert_fusion.refs_1_), custom_call_target="tpu_custom_call" | custom-call | tf_op jit(solution)/shard_map/spread_6/pallas_call | solution.py:177
  754.4 38.1 %psum.7 = f32[2,2048]{1,0:T(2,128)S(1)} all-reduce(f32[2,2048]{1,0:T(2,128)S(1)} %pad_maximum_fusion.9), channel_id=1, replica_groups=mesh['batch'=4,'head'=8] {'batch','head'}, use_global_device_ids=true, to_apply=%region_51.52 | all-reduce | flops 4096 | bytes 32768 | tf_op jit(solution)/shard_map/psum | solution.py:450
  793.2 22.9 %sum_own_7.1 = f32[128,512]{1,0:T(8,128)} custom-call(bf16[1024,512]{1,0:T(8,128)(2,1)} %reduce-scatter.10.cloned.1.call-done.part_ref), custom_call_target="tpu_custom_call" | custom-call | tf_op jit(solution)/shard_map/sum_own_7/pallas_call | solution.py:109
  (212 shorter events, 223.3 us)
Async XLA Ops:
  7.2 35.1 %all-gather.8.cloned.1.call-start = ((), (), s32[]{:S(2)}) async-start(), calls=%async_computation.6 | async-start | bytes 2621440 | tf_op jit(solution)/shard_map/all_gather | solution.py:260
  9.3 6.5 collective-permute-start
  18.1 70.9 %all-gather.10.cloned.1.call-start = ((), (), s32[]{:S(2)}) async-start(), calls=%async_computation.7 | async-start | bytes 3276800 | tf_op jit(solution)/shard_map/all_gather | solution.py:278
  28.6 21.5 %copy-start.22 = (f32[1280]{0:T(1024)}, f32[1280]{0:T(1024)S(1)}, u32[]{:S(2)}) copy-start(f32[1280]{0:T(1024)S(1)} %add_rsqrt_fusion.1) | copy-start | bytes 15364
  28.6 21.5 %copy-start.19 = (f32[1,2048]{1,0:T(1,128)}, f32[1,2048]{1,0:T(1,128)S(1)}, u32[]{:S(2)}) copy-start(f32[1,2048]{1,0:T(1,128)S(1)} %get-tuple-element.910) | copy-start | bytes 24580
  50.1 22.6 %copy-start.18 = (s32[1280]{0:T(1024)S(1)}, s32[1280]{0:T(1024)}, u32[]{:S(2)}) copy-start(s32[1280]{0:T(1024)} %param.46) | copy-start | bytes 15364
  51.0 91.0 %all-gather.12.cloned.1.call-start = ((), (), s32[]{:S(2)}) async-start(), calls=%async_computation.8 | async-start | bytes 5242880 | tf_op jit(solution)/shard_map/all_gather | solution.py:265
  71.0 88.7 %all-gather.14.cloned.1.call-start = ((), (), s32[]{:S(2)}) async-start(), calls=%async_computation.9 | async-start | bytes 3932160 | tf_op jit(solution)/shard_map/all_gather | solution.py:266
  71.6 101.3 %all-gather.16.cloned.1.call-start = ((), (), s32[]{:S(2)}) async-start(), calls=%async_computation.10 | async-start | bytes 3932160 | tf_op jit(solution)/shard_map/all_gather | solution.py:267
  72.2 130.7 %all-gather.18.cloned.1.call-start = ((), (), s32[]{:S(2)}) async-start(), calls=%async_computation.11 | async-start | bytes 3932160 | tf_op jit(solution)/shard_map/all_gather | solution.py:268
  88.9 20.6 %copy-start.9 = (f32[1280,128]{1,0:T(8,128)}, f32[1280,128]{1,0:T(8,128)S(1)}, u32[]{:S(2)}) copy-start(f32[1280,128]{1,0:T(8,128)S(1)} %copy.208) | copy-start | bytes 1966084
  109.5 32.6 %copy-start.10 = (f32[1280,128]{1,0:T(8,128)}, f32[1280,128]{1,0:T(8,128)S(1)}, u32[]{:S(2)}) copy-start(f32[1280,128]{1,0:T(8,128)S(1)} %get-tuple-element.979) | copy-start | bytes 1966084
  302.7 53.8 %copy-start.8 = (f32[160,2048]{1,0:T(8,128)S(1)}, f32[160,2048]{1,0:T(8,128)}, u32[]{:S(2)}) copy-start(f32[160,2048]{1,0:T(8,128)} %sum_own_3.1) | copy-start | bytes 3932164
  367.0 12.3 %all-to-all-start = ((bf16[8,160,128]{2,1,0:T(8,128)(2,1)}), bf16[8,160,128]{2,1,0:T(8,128)(2,1)S(1)}, u32[]{:S(2)}, u32[]{:S(2)}) async-start(bf16[8,160,128]{2,1,0:T(8,128)(2,1)} %fusion.151), calls=%async_computation | async-start | bytes 655360 | tf_op jit(solution)/shard_map/all_to_all | solution.py:368
  370.7 157.1 %reduce-scatter.6.cloned.1.call-start = ((), (), s32[]{:S(2)}) async-start(), calls=%async_computation.12 | async-start | bytes 3276800 | tf_op jit(solution)/shard_map/reduce_scatter | solution.py:406
  418.9 165.5 %reduce-scatter.14.cloned.1.call-start = ((), (), s32[]{:S(2)}) async-start(), calls=%async_computation.16 | async-start | bytes 3932160 | tf_op jit(solution)/shard_map/reduce_scatter | solution.py:447
  427.1 366.0 %reduce-scatter.10.cloned.1.call-start = ((), (), s32[]{:S(2)}) async-start(), calls=%async_computation.14 | async-start | bytes 5242880 | tf_op jit(solution)/shard_map/reduce_scatter | solution.py:372
  432.9 114.0 %copy-start.14 = (bf16[1280,128]{1,0:T(8,128)(2,1)S(1)}, bf16[1280,128]{1,0:T(8,128)(2,1)}, u32[]{:S(2)}) copy-start(bf16[1280,128]{1,0:T(8,128)(2,1)} %get-tuple-element.886) | copy-start | bytes 983044
  432.9 114.0 %copy-start.20 = (f32[1,2048]{1,0:T(1,128)S(1)}, f32[1,2048]{1,0:T(1,128)}, u32[]{:S(2)}) copy-start(f32[1,2048]{1,0:T(1,128)} %copy-done.19) | copy-start | bytes 24580
  432.9 114.0 %copy-start.23 = (f32[1280]{0:T(1024)S(1)}, f32[1280]{0:T(1024)}, u32[]{:S(2)}) copy-start(f32[1280]{0:T(1024)} %copy-done.22) | copy-start | bytes 15364
  432.9 383.2 %reduce-scatter.8.cloned.1.call-start = ((), (), s32[]{:S(2)}) async-start(), calls=%async_computation.13 | async-start | bytes 1966080 | tf_op jit(solution)/shard_map/reduce_scatter | solution.py:449
  527.8 16.7 %collective-permute-start.1 = (bf16[1280,256]{1,0:T(8,128)(2,1)}, bf16[1280,256]{1,0:T(8,128)(2,1)S(1)}, u32[]{:S(2)}, u32[]{:S(2)}) collective-permute-start(bf16[1280,256]{1,0:T(8,128)(2,1)} %reduce-scatter.6.cloned.1.call-done), channel_id=1, source_target_pairs={{0,1},{1,0},{2,3},{3,2},{4,5},{5,4},{6,7},{7,6},{8,9},{9,8},{10,11... | collective-permute-start | bytes 1966088 | tf_op jit(solution)/shard_map/ppermute | solution.py:197
  554.2 266.3 %reduce-scatter.12.cloned.1.call-start = ((), (), s32[]{:S(2)}) async-start(), calls=%async_computation.15 | async-start | bytes 7864320 | tf_op jit(solution)/shard_map/reduce_scatter | solution.py:445
  649.3 105.0 %copy-start.21 = (f32[2048]{0:T(1024)S(1)}, f32[2048]{0:T(1024)}, u32[]{:S(2)}) copy-start(f32[2048]{0:T(1024)} %get-tuple-element.864) | copy-start | bytes 24580
  (17 other events, 106.5 us)
Sparse Core Ops, SparseCore 0:
  18.2 24.0 all-gather.7
  51.1 25.5 all-gather.9
  78.3 34.5 all-gather.11
  114.3 28.5 all-gather.13
  144.3 28.5 all-gather.15
  174.3 28.5 all-gather.17
  419.0 108.7 reduce-scatter.5
  530.5 37.9 reduce-scatter.13
  571.6 44.5 reduce-scatter.9
  619.3 28.1 reduce-scatter.7
  650.0 58.3 reduce-scatter.11

commit v3 on v2

--- a/solution.py
+++ b/solution.py
@@ -10,6 +10,7 @@
 
 EPSILON = 1e-06
 MASKED = -1e30
+DOCUMENTS = 7
 BF = jnp.bfloat16
 F32 = jnp.float32
 
@@ -191,6 +192,136 @@
     )(*arrays)
 
 
+KEY_BLOCK = 512
+QUERY_BLOCK = 256
+
+
+def key_range(start_ref, base, query_block):
+    first = query_block * QUERY_BLOCK
+    lowest = start_ref[first]
+    highest = start_ref[first + QUERY_BLOCK - 1]
+    begin = lowest // KEY_BLOCK
+    end = (base + first + QUERY_BLOCK - 1) // KEY_BLOCK + 1
+    full_begin = jnp.minimum((highest + KEY_BLOCK - 1) // KEY_BLOCK, end)
+    full_end = jnp.maximum((base + first + 1) // KEY_BLOCK, full_begin)
+    return begin, full_begin, full_end, end
+
+
+def allowed_pairs(key_block, start_row, base_row):
+    shape = (KEY_BLOCK, QUERY_BLOCK)
+    key_pos = key_block * KEY_BLOCK + lax.broadcasted_iota(jnp.int32, shape, 0)
+    query_pos = base_row + lax.broadcasted_iota(jnp.int32, shape, 1)
+    return (key_pos >= start_row) & (key_pos <= query_pos)
+
+
+def attend_kernel(
+    scale, start_sm, base_sm, q_ref, kv_ref, start_ref, logit_ref, o_ref, a_ref, lse_ref
+):
+    base = base_sm[0]
+    size = q_ref.shape[1]
+    factor = scale * math.log2(math.e)
+
+    @pl.loop(0, q_ref.shape[0] // QUERY_BLOCK)
+    def _(block):
+        rows = pl.ds(pl.multiple_of(block * QUERY_BLOCK, QUERY_BLOCK), QUERY_BLOCK)
+        queries = q_ref[rows]
+        start_row = start_ref[:, rows]
+        begin, full_begin, full_end, end = key_range(start_sm, base, block)
+
+        def step(masked, at, state):
+            old_max, old_sum, total = state
+            keys = pl.ds(pl.multiple_of(at * KEY_BLOCK, KEY_BLOCK), KEY_BLOCK)
+            scores = cols_inner(kv_ref[keys, :size], queries)
+            if masked:
+                allowed = allowed_pairs(at, start_row, base + block * QUERY_BLOCK)
+                scores = jnp.where(allowed, scores, MASKED)
+            new_max = jnp.maximum(old_max, jnp.max(scores, axis=0, keepdims=True))
+            keep = jnp.exp2((old_max - new_max) * factor)
+            weights = jnp.exp2(scores * factor - new_max * factor)
+            new_sum = old_sum * keep + jnp.sum(weights, axis=0, keepdims=True)
+            total = total * keep + rows_inner(kv_ref[keys, size:], weights.astype(BF))
+            return new_max, new_sum, total
+
+        state = (
+            jnp.full((1, QUERY_BLOCK), MASKED, F32),
+            jnp.zeros((1, QUERY_BLOCK), F32),
+            jnp.zeros((size, QUERY_BLOCK), F32),
+        )
+        state = lax.fori_loop(begin, full_begin, functools.partial(step, True), state)
+        state = lax.fori_loop(full_begin, full_end, functools.partial(step, False), state)
+        state = lax.fori_loop(full_end, end, functools.partial(step, True), state)
+        run_max, run_sum, total = state
+        lse_ref[:, rows] = run_max * factor + jnp.log2(run_sum)
+        attended = (total / run_sum).T
+        o_ref[rows] = attended
+        a_ref[rows] = (attended * jax.nn.sigmoid(logit_ref[rows])).astype(BF)
+
+
+def attend_back_kernel(
+    scale, start_sm, base_sm, q_ref, kv_ref, start_ref, logit_ref, o_ref, da_ref, lse_ref,
+    dq_ref, dg_ref, dkv_ref, dk_acc, dv_acc,
+):
+    base = base_sm[0]
+    size = q_ref.shape[1]
+    factor = scale * math.log2(math.e)
+    dk_acc[...] = jnp.zeros_like(dk_acc)
+    dv_acc[...] = jnp.zeros_like(dv_acc)
+
+    @pl.loop(0, q_ref.shape[0] // QUERY_BLOCK)
+    def _(block):
+        rows = pl.ds(pl.multiple_of(block * QUERY_BLOCK, QUERY_BLOCK), QUERY_BLOCK)
+        queries = q_ref[rows]
+        start_row = start_ref[:, rows]
+        lse = lse_ref[:, rows]
+        gate = jax.nn.sigmoid(logit_ref[rows])
+        attended = o_ref[rows]
+        d_mixed = da_ref[rows].astype(F32)
+        d_attended = (d_mixed * gate).astype(BF)
+        dg_ref[rows] = (d_mixed * attended * gate * (1.0 - gate)).astype(BF)
+        delta = jnp.sum((d_attended.astype(F32) * attended).T, axis=0, keepdims=True)
+        begin, full_begin, full_end, end = key_range(start_sm, base, block)
+
+        def step(masked, at, d_queries):
+            keys = pl.ds(pl.multiple_of(at * KEY_BLOCK, KEY_BLOCK), KEY_BLOCK)
+            key_block = kv_ref[keys, :size]
+            probs = jnp.exp2(cols_inner(key_block, queries) * factor - lse)
+            if masked:
+                allowed = allowed_pairs(at, start_row, base + block * QUERY_BLOCK)
+                probs = jnp.where(allowed, probs, 0.0)
+            d_probs = cols_inner(kv_ref[keys, size:], d_attended)
+            d_scores = (probs * (d_probs - delta) * scale).astype(BF)
+            dv_acc[keys] += matmul(probs.astype(BF), d_attended)
+            dk_acc[keys] += matmul(d_scores, queries)
+            return d_queries + rows_inner(key_block, d_scores)
+
+        d_queries = jnp.zeros((size, QUERY_BLOCK), F32)
+        d_queries = lax.fori_loop(begin, full_begin, functools.partial(step, True), d_queries)
+        d_queries = lax.fori_loop(full_begin, full_end, functools.partial(step, False), d_queries)
+        d_queries = lax.fori_loop(full_end, end, functools.partial(step, True), d_queries)
+        dq_ref[rows] = d_queries.T.astype(BF)
+
+    @pl.loop(0, kv_ref.shape[0] // KEY_BLOCK)
+    def _(at):
+        keys = pl.ds(pl.multiple_of(at * KEY_BLOCK, KEY_BLOCK), KEY_BLOCK)
+        dkv_ref[keys, :size] = dk_acc[keys].astype(BF)
+        dkv_ref[keys, size:] = dv_acc[keys].astype(BF)
+
+
+def local_call(kernel, scalars, arrays, outs, scratch, flops, name):
+    vmem = pl.BlockSpec(memory_space=pltpu.VMEM)
+    smem = pl.BlockSpec(memory_space=pltpu.SMEM)
+    return pl.pallas_call(
+        kernel,
+        out_shape=outs,
+        in_specs=[smem] * len(scalars) + [vmem] * len(arrays),
+        out_specs=[vmem] * len(outs),
+        scratch_shapes=scratch,
+        compiler_params=pltpu.CompilerParams(vmem_limit_bytes=VMEM_LIMIT),
+        cost_estimate=pl.CostEstimate(flops=flops, bytes_accessed=8 << 20, transcendentals=0),
+        name=name,
+    )(*scalars, *arrays)
+
+
 def from_partner(block, axis):
     count = lax.axis_size(axis)
     route = [(at, at ^ 1) for at in range(count)]
@@ -211,10 +342,6 @@
 
 def rms_scale(values):
     return lax.rsqrt(jnp.mean(values * values, axis=1, keepdims=True) + EPSILON)
-
-
-def keep_same(state):
-    return state
 
 
 def order_halves(own, mate, first):
@@ -267,69 +394,34 @@
     mup_full = lax.all_gather(w_mlp_up, "batch", axis=0, tiled=True)
     down_full = lax.all_gather(w_down, "batch", axis=1, tiled=True)
 
-    positions = lax.axis_index("batch") * row_count + jnp.arange(row_count, dtype=jnp.int32)
     inputs = tokens.astype(F32)
     recip_one = rms_scale(inputs)
     normed_one = (inputs * recip_one * gain_one).astype(BF)
     projected = matmul(normed_one, w_in)
     queries = projected[:, :head_size].astype(BF)
     kv_local = projected[:, head_size : 3 * head_size].astype(BF)
-    gate_vals = jax.nn.sigmoid(projected[:, 3 * head_size :])
+    gate_logit = projected[:, 3 * head_size :]
     kv_all = lax.all_gather(kv_local, "batch", axis=0, tiled=True)
     seg_all = lax.all_gather(segment_ids, "batch", axis=0, tiled=True)
-    block_rows = row_count
-    block_total = batches
-
-    def block_parts(block_index):
-        first_row = block_index * block_rows
-        key_block = kv_all[first_row : first_row + block_rows, :head_size]
-        value_block = kv_all[first_row : first_row + block_rows, head_size:]
-        seg_block = seg_all[first_row : first_row + block_rows]
-        key_pos = first_row + jnp.arange(block_rows, dtype=jnp.int32)
-        allowed = (segment_ids[:, None] == seg_block[None, :]) & (
-            key_pos[None, :] <= positions[:, None]
-        )
-        scores = cols_inner(queries, key_block) * scale_factor
-        return (scores, allowed, key_block, value_block)
-
-    def is_live(block_index):
-        first_row = block_index * block_rows
-        return (first_row <= positions[-1]) & (
-            seg_all[first_row + block_rows - 1] >= segment_ids[0]
-        )
-
-    run_max = jnp.full((row_count,), MASKED, F32)
-    run_sum = jnp.zeros((row_count,), F32)
-    for block_index in range(block_total):
-
-        def grow(state, block_index=block_index):
-            old_max, old_sum = state
-            scores, allowed, key_block, value_block = block_parts(block_index)
-            new_max = jnp.maximum(old_max, jnp.max(jnp.where(allowed, scores, MASKED), axis=1))
-            weights = jnp.where(allowed, jnp.exp(scores - new_max[:, None]), 0.0)
-            return (new_max, old_sum * jnp.exp(old_max - new_max) + jnp.sum(weights, axis=1))
-
-        run_max, run_sum = lax.cond(is_live(block_index), grow, keep_same, (run_max, run_sum))
-    log_total = run_max + jnp.log(run_sum)
-
-    def probs_of(block_index):
-        scores, allowed, key_block, value_block = block_parts(block_index)
-        return (
-            jnp.where(allowed, jnp.exp(scores - log_total[:, None]), 0.0),
-            key_block,
-            value_block,
-        )
-
-    attended = jnp.zeros((row_count, head_size), F32)
-    for block_index in range(block_total):
-
-        def accumulate(running, block_index=block_index):
-            probs, key_block, value_block = probs_of(block_index)
-            return running + matmul(probs.astype(BF), value_block)
-
-        attended = lax.cond(is_live(block_index), accumulate, keep_same, attended)
-
-    mixed = (attended * gate_vals).astype(BF)
+    base = lax.axis_index("batch") * row_count
+    ids = jnp.arange(DOCUMENTS, dtype=jnp.int32)
+    below = jnp.sum((seg_all[None, :] < ids[:, None]).astype(jnp.int32), axis=1)
+    starts = jnp.sum(jnp.where(segment_ids[None, :] == ids[:, None], below[:, None], 0), axis=0)
+    scalars = (starts, base.reshape(1))
+    pair_flops = 4 * row_count * kv_all.shape[0] * head_size
+    attended, mixed, lse = local_call(
+        functools.partial(attend_kernel, scale_factor),
+        scalars,
+        (queries, kv_all, starts[None], gate_logit),
+        [
+            jax.ShapeDtypeStruct((row_count, head_size), F32),
+            jax.ShapeDtypeStruct((row_count, head_size), BF),
+            jax.ShapeDtypeStruct((1, row_count), F32),
+        ],
+        [],
+        pair_flops,
+        "attend",
+    )
     (mixed_all,) = spread([mixed], 2)
     mixed_all = mixed_all.transpose(1, 0, 2).reshape(row_count, -1)
     resid = inputs + matmul(mixed_all, out_full)
@@ -367,48 +459,29 @@
     d_mixed_all = jnp.stack([d_mixed_all[:, at] for at in places], axis=0)
     d_mixed = lax.all_to_all(d_mixed_all, "head", split_axis=0, concat_axis=0, tiled=True)
     d_mixed = jnp.concatenate([d_mixed[ring_head(at, heads)] for at in range(heads)], axis=0)
-    d_mixed = d_mixed.astype(F32)
     d_out_part = rows_inner(mixed_own, d_resid_low).astype(BF)
     d_out_part = lax.psum_scatter(d_out_part, "batch", scatter_dimension=1, tiled=True)
     d_out = sum_own(d_out_part, 7)
 
-    d_attended = (d_mixed * gate_vals).astype(BF)
-    d_gate_logit = (d_mixed * attended * gate_vals * (1.0 - gate_vals)).astype(BF)
-    delta = jnp.zeros((row_count,), F32)
-    for block_index in range(block_total):
-
-        def delta_add(running, block_index=block_index):
-            probs, key_block, value_block = probs_of(block_index)
-            return running + jnp.sum(probs * cols_inner(d_attended, value_block), axis=1)
-
-        delta = lax.cond(is_live(block_index), delta_add, keep_same, delta)
-    d_queries = jnp.zeros((row_count, head_size), F32)
-    grad_pieces = []
-    for block_index in range(block_total):
-
-        def block_grads(running, block_index=block_index):
-            probs, key_block, value_block = probs_of(block_index)
-            d_probs = cols_inner(d_attended, value_block)
-            d_scores = (probs * (d_probs - delta[:, None]) * scale_factor).astype(BF)
-            d_key_block = rows_inner(d_scores, queries)
-            d_value_block = rows_inner(probs.astype(BF), d_attended)
-            return (
-                running + matmul(d_scores, key_block),
-                jnp.concatenate([d_key_block, d_value_block], axis=1).astype(BF),
-            )
-
-        def block_empty(running):
-            return (running, jnp.zeros((block_rows, 2 * head_size), BF))
-
-        d_queries, grad_piece = lax.cond(is_live(block_index), block_grads, block_empty, d_queries)
-        grad_pieces.append(grad_piece)
-    d_kv_all = jnp.concatenate(grad_pieces, axis=0)
+    d_queries, d_gate_logit, d_kv_all = local_call(
+        functools.partial(attend_back_kernel, scale_factor),
+        scalars,
+        (queries, kv_all, starts[None], gate_logit, attended, d_mixed, lse),
+        [
+            jax.ShapeDtypeStruct((row_count, head_size), BF),
+            jax.ShapeDtypeStruct((row_count, head_size), BF),
+            jax.ShapeDtypeStruct(kv_all.shape, BF),
+        ],
+        [pltpu.VMEM((kv_all.shape[0], head_size), F32)] * 2,
+        5 * pair_flops // 2,
+        "attend_back",
+    )
     d_kv_own = lax.psum_scatter(d_kv_all, "batch", scatter_dimension=0, tiled=True)
     d_kv_mate = from_partner(d_kv_own, "head")
     d_kv = (d_kv_own.astype(F32) + d_kv_mate.astype(F32)).astype(BF)
     d_cat = jnp.concatenate(
         [
-            d_queries.astype(BF),
+            d_queries,
             jnp.where(first, d_kv[:, :half], d_kv[:, half:head_size]),
             jnp.where(first, d_kv[:, head_size : head_size + half], d_kv[:, head_size + half :]),
             d_gate_logit,
@@ -447,10 +520,11 @@
     d_down = lax.psum_scatter(d_down, "batch", scatter_dimension=1, tiled=True).astype(F32)
     d_in = rows_inner(normed_one, d_cat).astype(BF)
     d_in = lax.psum_scatter(d_in, "batch", scatter_dimension=0, tiled=True).astype(F32)
-    d_gains = lax.psum(jnp.stack([d_gain_one, d_gain_two]), ("batch", "head"))
-    d_gains = lax.dynamic_slice_in_dim(
-        d_gains, lax.axis_index("batch") * norm1_gain.shape[0], norm1_gain.shape[0], 1
-    )
+    d_gains = jnp.concatenate([d_gain_one, d_gain_two])
+    d_gains = lax.all_gather(d_gains, "head", axis=0)
+    d_gains = jnp.sum(d_gains, axis=0).reshape(2, batches, -1)
+    d_gains = lax.all_to_all(d_gains, "batch", split_axis=1, concat_axis=1, tiled=True)
+    d_gains = jnp.sum(d_gains, axis=1)
     hidden_own = w_mlp_gate.shape[1]
     return (
         output,

time: 853 us -> 743 us (0.87)
  waiting for transfers between devices: 160 us -> 107 us
  local copies, waits for them, and re-layouts: 63.4 us -> 35.6 us
  matrix products: 141 us -> 114 us
  Pallas kernels: 339 us -> 364 us
  other arithmetic: 51.1 us -> 36.7 us
    reduce_scatter x1, waiting for transfers between devices: 94.4 us -> 31 us  [per_device(): lax.psum_scatter(d_kv_all, 'batch', scatter_dimension=0, tiled=True)]
    psum x1 -> x0, blocking collectives: 38.1 us -> none  [per_device(): d_gains = lax.psum(jnp.stack([d_gain_one, d_gain_two]), ('batch', 'head'))]
    all_gather x0 -> x1, blocking collectives: none -> 30.5 us  [per_device(): d_gains = lax.all_gather(d_gains, 'head', axis=0)]
    pallas_call x0 -> x2, Pallas kernels: none -> 19.8 us  [local_call(): pl.pallas_call(kernel, out_shape=outs, in_specs=[smem] * len(scalars) + [...]
    dot_general x10 -> x5, matrix products: 50.9 us -> 33.6 us  [cols_inner(): lax.dot_general(left, right, (((1,), (1,)), ((), ())), preferred_element_...]
    all_gather x1, waiting for transfers between devices: 3.48 us -> 20.3 us  [per_device(): mup_full = lax.all_gather(w_mlp_up, 'batch', axis=0, tiled=True)]
    another operation x9 -> x2, local copies, waits for them, and re-layouts: 16.9 us -> 0.16 us
    all_to_all x0 -> x1, blocking collectives: none -> 12.4 us  [per_device(): lax.all_to_all(d_mixed_all, 'head', split_axis=0, concat_axis=0, tiled=True)]
  transfers between devices with their start and end apart: 14 -> 14, of which waited for: 7 -> 6; matrix products, arithmetic and copies ran while one was open for 17% -> 15% of each run, Pallas kernels for 27% -> 33%
where the time goes in v3:
time: 743 us; the launch traced here: 735 us
  Pallas kernels  364 us (49%)
  matrix products  114 us (15%)
  waiting for transfers between devices  107 us (14%)
  blocking collectives  53.3 us (7%)
  other arithmetic  36.7 us (5%)
  local copies, waits for them, and re-layouts  35.6 us (5%)
  between operations  14.9 us (2%)
  starting transfers between devices  8.65 us (1%)
    pallas_call x4, Pallas kernels, sum_own(): pl.pallas_call(functools.partial(sum_kernel, count), out_shape=jax.ShapeD...  190 us
    pallas_call x3, Pallas kernels, spread(): pl.pallas_call(functools.partial(spread_kernel, count, len(arrays)), out_...  154 us
    dot_general x5, matrix products, matmul(): return jnp.dot(left, right, preferred_element_type=F32)  44.4 us
    dot_general x5, matrix products, rows_inner(): lax.dot_general(left, right, (((0,), (0,)), ((), ())), preferred_element_...  35.5 us
    dot_general x5, matrix products, cols_inner(): lax.dot_general(left, right, (((1,), (1,)), ((), ())), preferred_element_...  33.6 us
    reduce_scatter x1, waiting for transfers between devices, per_device(): lax.psum_scatter(d_kv_all, 'batch', scatter_dimension=0, tiled=True)  31 us
    all_gather x1, blocking collectives, per_device(): d_gains = lax.all_gather(d_gains, 'head', axis=0)  30.5 us
    unnamed x71, local copies, waits for them, and re-layouts  21.5 us
  transfers between devices with their start and end apart: 14, of which 6 were waited for; matrix products, arithmetic and copies ran while one was open for 15% of the time, Pallas kernels for 33%

profile of v3, /device:TPU:0, one launch (start us, length us, event | category | flops | bytes accessed | tf_op | source)
XLA Modules:
  0.0 734.7 jit_solution(12113693223348818073)
XLA Ops:
  27.0 15.3 %all-gather.9.cloned.1.call-done = bf16[2048,512]{1,0:T(8,128)(2,1)} async-done(((bf16[512,512]{1,0:T(8,128)(2,1)}), bf16[2048,512]{1,0:T(8,128)(2,1)}) %all-gather.9.cloned.1.call-update) | async-done | bytes 2097168 | tf_op jit(solution)/shard_map/all_gather | solution.py:387
  50.8 19.9 %spread_1.1 = bf16[8,128,512]{2,1,0:T(8,128)(2,1)} custom-call(bf16[128,512]{1,0:T(8,128)(2,1)} %refs_0_.1), custom_call_target="tpu_custom_call" | custom-call | tf_op jit(solution)/shard_map/spread_1/pallas_call | solution.py:178
  81.4 8.8 %attend.1 = (f32[1280,128]{1,0:T(8,128)}, bf16[1280,128]{1,0:T(8,128)(2,1)}, f32[1,1280]{1,0:T(1,128)}) custom-call(s32[1280]{0:T(1024)} %copy-done.10, s32[1]{0:T(128)} %bitcast.1.base_sm, bf16[1280,128]{1,0:T(8,128)(2,1)} %slice.169.q_ref, bf16[5120,256]{1,0:T(8,128)(2,1)} %all-gather.11.cloned.1.call-done.kv_ref, s32[1,1280]{1,0:T(1,128)} %broadcast_in_dim.16.start_ref, ...), custom_call_target="tpu_custom_call" | custom-call | flops 3355443200 | bytes 8388608 | tf_op jit(solution)/shard_map/attend/pallas_call | solution.py:313
  90.2 32.2 %spread_2.1 = bf16[8,1280,128]{2,1,0:T(8,128)(2,1)} custom-call(bf16[1280,128]{1,0:T(8,128)(2,1)} %get-tuple-element.20.refs_0_), custom_call_target="tpu_custom_call" | custom-call | tf_op jit(solution)/shard_map/spread_2/pallas_call | solution.py:178
  125.4 10.0 %multiply_reduce_fusion = (f32[1280]{0:T(1024)S(1)}, f32[1280,2048]{1,0:T(8,128)S(1)}) fusion(bf16[1280,1024]{0,1:T(8,128)(2,1)S(1)} %bitcast.110, bf16[1024,2048]{1,0:T(8,128)(2,1)} %all-gather.13.cloned.1.call-done, bf16[1280,2048]{1,0:T(8,128)(2,1)} %param.13), kind=kOutput, calls=%fused_computation.2 | convolution fusion | flops 5379193856 | bytes 22549504 | tf_op jit(solution)/shard_map/dot_general | solution.py:332
  142.7 9.6 %fusion.40 = f32[1280,768]{1,0:T(8,128)} fusion(bf16[1280,2048]{1,0:T(8,128)(2,1)} %multiply_convert_fusion, bf16[2048,768]{1,0:T(8,128)(2,1)} %all-gather.15.cloned.1.call-done), kind=kOutput, calls=%fused_computation.106 | convolution fusion | flops 4026531840 | bytes 12320768 | tf_op jit(solution)/shard_map/dot_general | solution.py:332
  152.4 20.3 %all-gather.17.cloned.1.call-done = bf16[2048,768]{1,0:T(8,128)(2,1)} async-done(((bf16[512,768]{1,0:T(8,128)(2,1)}), bf16[2048,768]{1,0:T(8,128)(2,1)}) %all-gather.17.cloned.1.call-update) | async-done | bytes 3145744 | tf_op jit(solution)/shard_map/all_gather | solution.py:394
  172.7 9.6 %fusion.41 = f32[1280,768]{1,0:T(8,128)} fusion(bf16[1280,2048]{1,0:T(8,128)(2,1)} %multiply_convert_fusion, bf16[2048,768]{1,0:T(8,128)(2,1)} %all-gather.17.cloned.1.call-done), kind=kOutput, calls=%fused_computation.107 | convolution fusion | flops 4026531840 | bytes 12320768 | tf_op jit(solution)/shard_map/dot_general | solution.py:332
  182.2 20.4 %all-gather.19.cloned.1.call-done = bf16[768,2048]{1,0:T(8,128)(2,1)} async-done(((bf16[768,512]{1,0:T(8,128)(2,1)}), bf16[768,2048]{1,0:T(8,128)(2,1)}) %all-gather.19.cloned.1.call-update) | async-done | bytes 3145744 | tf_op jit(solution)/shard_map/all_gather | solution.py:395
  202.6 13.9 %multiply_convert_fusion.2 = (bf16[1280,768]{1,0:T(8,128)(2,1)}, bf16[1280,768]{1,0:T(8,128)(2,1)S(1)}, bf16[1280,768]{1,0:T(8,128)(2,1)}) fusion(f32[1280,768]{1,0:T(8,128)} %fusion.40, f32[1280,768]{1,0:T(8,128)} %fusion.41, bf16[1280,2048]{1,0:T(8,128)(2,1)} %param.25, bf16[768,2048]{1,0:T(8,128)(2,1)} %all-gather.19.cloned.1.call-done), kind=kOutput, calls=%fused_computation.9 | convolution fusion | flops 4041277440 | bytes 22151168 | tf_op jit(solution)/shard_map/dot_general | solution.py:340
  220.8 7.7 %add_convert_fusion.part_ref = bf16[1280,2048]{1,0:T(8,128)(2,1)} fusion(f32[1280,2048]{1,0:T(8,128)S(1)} %fusion.42, bf16[1280,768]{1,0:T(8,128)(2,1)} %get-tuple-element.94, bf16[2048,768]{1,0:T(8,128)(2,1)S(1)} %copy-done.16), kind=kOutput, calls=%fused_computation | convolution fusion | flops 4031774720 | bytes 20840448 | tf_op jit(solution)/shard_map/dot_general | solution.py:340
  228.6 60.2 %sum_own_3.1 = f32[160,2048]{1,0:T(8,128)} custom-call(bf16[1280,2048]{1,0:T(8,128)(2,1)} %add_convert_fusion.part_ref), custom_call_target="tpu_custom_call" | custom-call | tf_op jit(solution)/shard_map/sum_own_3/pallas_call | solution.py:110
  290.9 7.7 %convolution_convert_fusion.1.part_ref = bf16[1280,2048]{1,0:T(8,128)(2,1)} fusion(bf16[1280,768]{1,0:T(8,128)(2,1)} %get-tuple-element.96, bf16[768,2048]{1,0:T(8,128)(2,1)S(1)} %copy-done.15), kind=kOutput, calls=%fused_computation.7 | convolution fusion | flops 4029153280 | bytes 10354688 | tf_op jit(solution)/shard_map/dot_general | solution.py:332
  298.6 53.8 %sum_own_4.1 = f32[160,2048]{1,0:T(8,128)} custom-call(bf16[1280,2048]{1,0:T(8,128)(2,1)} %convolution_convert_fusion.1.part_ref), custom_call_target="tpu_custom_call" | custom-call | tf_op jit(solution)/shard_map/sum_own_4/pallas_call | solution.py:110
  358.1 12.4 %all_to_all.10 = bf16[8,160,128]{2,1,0:T(8,128)(2,1)S(1)} all-to-all(bf16[8,160,128]{2,1,0:T(8,128)(2,1)S(1)} %fusion.21), channel_id=1, replica_groups=mesh['batch'=4,'head'=8] {'head'}, dimensions={0} | all-to-all | bytes 655360 | tf_op jit(solution)/shard_map/all_to_all | solution.py:460
  371.4 11.0 %attend_back.1 = (bf16[1280,128]{1,0:T(8,128)(2,1)}, bf16[1280,128]{1,0:T(8,128)(2,1)}, bf16[5120,256]{1,0:T(8,128)(2,1)}) custom-call(s32[1280]{0:T(1024)} %copy-done.10, s32[1]{0:T(128)} %bitcast.1.base_sm, bf16[1280,128]{1,0:T(8,128)(2,1)} %slice.169.q_ref, bf16[5120,256]{1,0:T(8,128)(2,1)} %all-gather.11.cloned.1.call-done.kv_ref, ...), custom_call_target="tpu_custom_call" | custom-call | flops 8388608000 | bytes 8388608 | tf_op jit(solution)/shard_map/attend_back/pallas_call | solution.py:313
  382.5 9.0 %convolution_convert_fusion.3 = bf16[768,2048]{1,0:T(8,128)(2,1)} fusion(bf16[1280,768]{1,0:T(8,128)(2,1)} %get-tuple-element.96, bf16[1280,2048]{1,0:T(8,128)(2,1)} %param.25), kind=kOutput, calls=%fused_computation.15 | convolution fusion | flops 4028104704 | bytes 10354688 | tf_op jit(solution)/shard_map/dot_general | solution.py:336
  396.2 31.0 %reduce-scatter.6.cloned.1.call-done = bf16[1280,256]{1,0:T(8,128)(2,1)} async-done(((bf16[5120,256]{1,0:T(8,128)(2,1)}), bf16[1280,256]{1,0:T(8,128)(2,1)}) %reduce-scatter.6.cloned.1.call-update) | async-done | bytes 655376 | tf_op jit(solution)/shard_map/reduce_scatter | solution.py:479
  428.6 15.2 %collective-permute-done.1 = bf16[1280,256]{1,0:T(8,128)(2,1)S(1)} collective-permute-done((bf16[1280,256]{1,0:T(8,128)(2,1)}, bf16[1280,256]{1,0:T(8,128)(2,1)S(1)}, u32[]{:S(2)}, u32[]{:S(2)}) %collective-permute-start.1) | collective-permute-done | bytes 655392 | tf_op jit(solution)/shard_map/ppermute | solution.py:328
  472.4 8.9 %convert_element_type.84 = f32[1280,2048]{1,0:T(8,128)} convert(bf16[1280,2048]{1,0:T(8,128)(2,1)} %param.13) | non-fusion elementwise | flops 2621440 | bytes 15728640 | tf_op jit(solution)/shard_map/convert_element_type | solution.py:397
  490.5 56.8 %sum_own_5.1 = f32[160,2048]{1,0:T(8,128)} custom-call(bf16[1280,2048]{1,0:T(8,128)(2,1)} %convolution_convert_fusion.part_ref), custom_call_target="tpu_custom_call" | custom-call | tf_op jit(solution)/shard_map/sum_own_5/pallas_call | solution.py:110
  549.4 30.5 %all-gather = f32[32768]{0:T(1024)S(1)} all-gather(f32[4096]{0:T(1024)S(1)} %pad_maximum_fusion.4), channel_id=2, replica_groups=mesh['batch'=4,'head'=8] {'head'}, dimensions={0}, use_global_device_ids=true | all-gather | bytes 147456 | tf_op jit(solution)/shard_map/all_gather | solution.py:524
  586.8 102.1 %spread_6.1 = (bf16[8,160,2048]{2,1,0:T(8,128)(2,1)}, bf16[8,160,2048]{2,1,0:T(8,128)(2,1)}) custom-call(bf16[160,2048]{1,0:T(8,128)(2,1)} %get-tuple-element.93.refs_0_, bf16[160,2048]{1,0:T(8,128)(2,1)} %subtract_convert_fusion.refs_1_), custom_call_target="tpu_custom_call" | custom-call | tf_op jit(solution)/shard_map/spread_6/pallas_call | solution.py:178
  689.4 19.8 %sum_own_7.1 = f32[128,512]{1,0:T(8,128)} custom-call(bf16[1024,512]{1,0:T(8,128)(2,1)} %reduce-scatter.10.cloned.1.call-done.part_ref), custom_call_target="tpu_custom_call" | custom-call | tf_op jit(solution)/shard_map/sum_own_7/pallas_call | solution.py:110
  (164 shorter events, 133.8 us)
Async XLA Ops:
  7.2 11.0 %copy-start.12 = (bf16[512]{0:T(512)(128)(2,1)S(1)}, bf16[512]{0:T(512)(128)(2,1)}, u32[]{:S(2)}) copy-start(bf16[512]{0:T(512)(128)(2,1)} %param.15) | copy-start | bytes 3076
  7.2 11.0 %copy-start.13 = (bf16[512]{0:T(512)(128)(2,1)S(1)}, bf16[512]{0:T(512)(128)(2,1)}, u32[]{:S(2)}) copy-start(bf16[512]{0:T(512)(128)(2,1)} %param.21) | copy-start | bytes 3076
  7.2 35.1 %all-gather.9.cloned.1.call-start = ((), (), s32[]{:S(2)}) async-start(), calls=%async_computation.7 | async-start | bytes 2621440 | tf_op jit(solution)/shard_map/all_gather | solution.py:387
  9.3 6.5 collective-permute-start
  18.1 63.3 %all-gather.11.cloned.1.call-start = ((), (), s32[]{:S(2)}) async-start(), calls=%async_computation.8 | async-start | bytes 3276800 | tf_op jit(solution)/shard_map/all_gather | solution.py:404
  49.9 22.7 %copy-start.9 = (s32[1280]{0:T(1024)S(1)}, s32[1280]{0:T(1024)}, u32[]{:S(2)}) copy-start(s32[1280]{0:T(1024)} %param.14) | copy-start | bytes 15364
  50.8 74.6 %all-gather.13.cloned.1.call-start = ((), (), s32[]{:S(2)}) async-start(), calls=%async_computation.9 | async-start | bytes 5242880 | tf_op jit(solution)/shard_map/all_gather | solution.py:392
  70.8 72.0 %all-gather.15.cloned.1.call-start = ((), (), s32[]{:S(2)}) async-start(), calls=%async_computation.10 | async-start | bytes 3932160 | tf_op jit(solution)/shard_map/all_gather | solution.py:393
  71.3 101.3 %all-gather.17.cloned.1.call-start = ((), (), s32[]{:S(2)}) async-start(), calls=%async_computation.11 | async-start | bytes 3932160 | tf_op jit(solution)/shard_map/all_gather | solution.py:394
  71.9 130.7 %all-gather.19.cloned.1.call-start = ((), (), s32[]{:S(2)}) async-start(), calls=%async_computation.12 | async-start | bytes 3932160 | tf_op jit(solution)/shard_map/all_gather | solution.py:395
  72.5 354.7 %reduce-scatter.6.cloned.1.call-start = ((), (), s32[]{:S(2)}) async-start(), calls=%async_computation.13 | async-start | bytes 3276800 | tf_op jit(solution)/shard_map/reduce_scatter | solution.py:479
  125.4 10.0 %copy-start.5 = (bf16[1280,8,128]{0,2,1:T(8,128)(2,1)}, bf16[1280,8,128]{0,2,1:T(8,128)(2,1)S(1)}, u32[]{:S(2)}) copy-start(bf16[1280,8,128]{0,2,1:T(8,128)(2,1)S(1)} %copy.99) | copy-start | bytes 7864324
  202.6 13.9 %copy-start.14 = (bf16[2048,768]{1,0:T(8,128)(2,1)S(1)}, bf16[2048,768]{1,0:T(8,128)(2,1)}, u32[]{:S(2)}) copy-start(bf16[2048,768]{1,0:T(8,128)(2,1)} %all-gather.15.cloned.1.call-done) | copy-start | bytes 9437188
  228.6 62.3 %copy-start.15 = (bf16[768,2048]{1,0:T(8,128)(2,1)S(1)}, bf16[768,2048]{1,0:T(8,128)(2,1)}, u32[]{:S(2)}) copy-start(bf16[768,2048]{1,0:T(8,128)(2,1)} %all-gather.19.cloned.1.call-done) | copy-start | bytes 9437188
  298.6 53.8 %copy-start.2 = (f32[160,2048]{1,0:T(8,128)S(1)}, f32[160,2048]{1,0:T(8,128)}, u32[]{:S(2)}) copy-start(f32[160,2048]{1,0:T(8,128)} %sum_own_3.1) | copy-start | bytes 3932164
  382.5 99.3 %reduce-scatter.14.cloned.1.call-start = ((), (), s32[]{:S(2)}) async-start(), calls=%async_computation.17 | async-start | bytes 3932160 | tf_op jit(solution)/shard_map/reduce_scatter | solution.py:520
  391.6 297.9 %reduce-scatter.10.cloned.1.call-start = ((), (), s32[]{:S(2)}) async-start(), calls=%async_computation.15 | async-start | bytes 5242880 | tf_op jit(solution)/shard_map/reduce_scatter | solution.py:463
  396.1 50.1 %copy-start.19 = (bf16[1280,128]{1,0:T(8,128)(2,1)S(1)}, bf16[1280,128]{1,0:T(8,128)(2,1)}, u32[]{:S(2)}) copy-start(bf16[1280,128]{1,0:T(8,128)(2,1)} %get-tuple-element.23) | copy-start | bytes 983044
  396.1 50.1 %copy-start.20 = (bf16[1280,128]{1,0:T(8,128)(2,1)S(1)}, bf16[1280,128]{1,0:T(8,128)(2,1)}, u32[]{:S(2)}) copy-start(bf16[1280,128]{1,0:T(8,128)(2,1)} %get-tuple-element.25) | copy-start | bytes 983044
  396.1 313.2 %reduce-scatter.8.cloned.1.call-start = ((), (), s32[]{:S(2)}) async-start(), calls=%async_computation.14 | async-start | bytes 1966080 | tf_op jit(solution)/shard_map/reduce_scatter | solution.py:522
  427.2 16.7 %collective-permute-start.1 = (bf16[1280,256]{1,0:T(8,128)(2,1)}, bf16[1280,256]{1,0:T(8,128)(2,1)S(1)}, u32[]{:S(2)}, u32[]{:S(2)}) collective-permute-start(bf16[1280,256]{1,0:T(8,128)(2,1)} %reduce-scatter.6.cloned.1.call-done), channel_id=1, source_target_pairs={{0,1},{1,0},{2,3},{3,2},{4,5},{5,4},{6,7},{7,6},{8,9},{9,8},{10,11... | collective-permute-start | bytes 1966088 | tf_op jit(solution)/shard_map/ppermute | solution.py:328
  453.6 260.1 %reduce-scatter.12.cloned.1.call-start = ((), (), s32[]{:S(2)}) async-start(), calls=%async_computation.16 | async-start | bytes 7864320 | tf_op jit(solution)/shard_map/reduce_scatter | solution.py:518
  547.2 37.0 %copy-start.1 = (f32[160,2048]{1,0:T(8,128)S(1)}, f32[160,2048]{1,0:T(8,128)}, u32[]{:S(2)}) copy-start(f32[160,2048]{1,0:T(8,128)} %sum_own_5.1) | copy-start | bytes 3932164
  580.7 108.2 %all-to-all-start.1 = ((f32[2,4,512]{2,0,1:T(2,128)}), f32[2,4,512]{2,0,1:T(2,128)S(1)}, u32[]{:S(2)}, u32[]{:S(2)}) async-start(f32[2,4,512]{2,0,1:T(2,128)} %copy.108), calls=%async_computation.2 | async-start | bytes 32768 | tf_op jit(solution)/shard_map/all_to_all | solution.py:526
  (13 other events, 52.2 us)
Sparse Core Ops, SparseCore 0:
  18.2 24.0 all-gather.8
  50.9 25.5 all-gather.10
  78.1 34.5 all-gather.12
  114.1 28.5 all-gather.14
  144.1 28.5 all-gather.16
  174.1 28.5 all-gather.18
  382.6 44.5 reduce-scatter.5
  429.9 37.9 reduce-scatter.13
  470.9 44.5 reduce-scatter.9
  518.6 28.1 reduce-scatter.7
  549.4 58.5 reduce-scatter.11

commit v4 on v3

--- a/solution.py
+++ b/solution.py
@@ -322,6 +322,91 @@
     )(*scalars, *arrays)
 
 
+def ring_routes(count):
+    spots = [ring_head(at, count) for at in range(count)]
+    right = [(spots[at], spots[(at + 1) % count]) for at in range(count)]
+    left = [(spots[at], spots[at - 1]) for at in range(count)]
+    return right, left
+
+
+def add_low(one, other):
+    return (one.astype(F32) + other.astype(F32)).astype(BF)
+
+
+def flow_sum(part):
+    count = lax.axis_size("head")
+    place = ring_place(lax.axis_index("head"), count)
+    right, left = ring_routes(count)
+    rows, side = part.shape[0] // count, part.shape[1] // 2
+    steps = count // 2
+
+    def mine(owner):
+        return lax.dynamic_slice_in_dim(part, lax.rem(owner + count, count) * rows, rows, 0)
+
+    far = mine(place + steps)
+    for step in range(steps):
+        if step == 0:
+            going, coming = far[:, :side], far[:, side:]
+        from_left = lax.ppermute(going, "head", right)
+        from_right = lax.ppermute(coming, "head", left)
+        if step == steps - 1:
+            break
+        one, two = mine(place + steps - 1 - step), mine(place - steps + 1 + step)
+        if step == 0:
+            going = jnp.concatenate([add_low(from_left, one[:, :side]), one[:, side:]], 1)
+            coming = jnp.concatenate([two[:, :side], add_low(from_right, two[:, side:])], 1)
+        else:
+            going, coming = add_low(from_left, one), add_low(from_right, two)
+    return mine(place).astype(F32) + from_left.astype(F32) + from_right.astype(F32)
+
+
+def flow_spread(own):
+    count = lax.axis_size("head")
+    place = ring_place(lax.axis_index("head"), count)
+    right, left = ring_routes(count)
+    side = own.shape[1] // 2
+    going = coming = own
+    pieces = [(0, own)]
+    for step in range(1, count // 2):
+        going = lax.ppermute(going, "head", right)
+        coming = lax.ppermute(coming, "head", left)
+        pieces += [(-step, going), (step, coming)]
+    one = lax.ppermute(going[:, :side], "head", right)
+    two = lax.ppermute(coming[:, side:], "head", left)
+    pieces.append((count // 2, jnp.concatenate([one, two], 1)))
+    whole = jnp.zeros((count * own.shape[0], own.shape[1]), own.dtype)
+    for shift, piece in pieces:
+        at = lax.rem(place + shift + count, count) * own.shape[0]
+        whole = lax.dynamic_update_slice_in_dim(whole, piece, at, 0)
+    return whole
+
+
+def swap(block, axis, stride):
+    return lax.ppermute(block, axis, [(at, at ^ stride) for at in range(lax.axis_size(axis))])
+
+
+def halve_batch(block, rows):
+    me = lax.axis_index("batch")
+    stride = 1
+    while stride < lax.axis_size("batch"):
+        block = block.reshape(-1, 2, rows, block.shape[-1])
+        bit = (me // stride) % 2
+        keep = lax.dynamic_index_in_dim(block, bit, 1, keepdims=False)
+        give = lax.dynamic_index_in_dim(block, 1 - bit, 1, keepdims=False)
+        got = swap(give, "batch", stride)
+        block = (keep.astype(F32) + got.astype(F32)).astype(block.dtype)
+        stride *= 2
+    return block.reshape(rows, -1)
+
+
+def sum_heads(block):
+    stride = 1
+    while stride < lax.axis_size("head"):
+        block = block + swap(block, "head", stride)
+        stride *= 2
+    return block
+
+
 def from_partner(block, axis):
     count = lax.axis_size(axis)
     route = [(at, at ^ 1) for at in range(count)]
@@ -442,8 +527,9 @@
     d_up_pre = (d_hidden * silu_gate).astype(BF)
     dn2_part = cols_inner(d_gate_pre, mgate_full) + cols_inner(d_up_pre, mup_full)
     dn2 = sum_own(dn2_part.astype(BF), 3)
-    mlp_part = matmul(hidden, down_full).astype(BF)
-    output = (resid_own + sum_own(mlp_part, 4)).astype(BF)
+    hidden_late, dn2 = lax.optimization_barrier((hidden, dn2))
+    mlp_part = matmul(hidden_late, down_full).astype(BF)
+    output = flow_spread((resid_own + flow_sum(mlp_part)).astype(BF))
 
     d_gain_two = jnp.sum(dn2 * resid_own * recip_own, axis=0)
     weighted_two = gain_two * dn2
@@ -461,7 +547,7 @@
     d_mixed = jnp.concatenate([d_mixed[ring_head(at, heads)] for at in range(heads)], axis=0)
     d_out_part = rows_inner(mixed_own, d_resid_low).astype(BF)
     d_out_part = lax.psum_scatter(d_out_part, "batch", scatter_dimension=1, tiled=True)
-    d_out = sum_own(d_out_part, 7)
+    d_out = flow_sum(d_out_part)
 
     d_queries, d_gate_logit, d_kv_all = local_call(
         functools.partial(attend_back_kernel, scale_factor),
@@ -476,7 +562,7 @@
         5 * pair_flops // 2,
         "attend_back",
     )
-    d_kv_own = lax.psum_scatter(d_kv_all, "batch", scatter_dimension=0, tiled=True)
+    d_kv_own = halve_batch(d_kv_all, row_count)
     d_kv_mate = from_partner(d_kv_own, "head")
     d_kv = (d_kv_own.astype(F32) + d_kv_mate.astype(F32)).astype(BF)
     d_cat = jnp.concatenate(
@@ -498,7 +584,7 @@
         [w_in[:, :head_size], w_key_own, w_value_own, w_in[:, 3 * head_size :]], axis=1
     )
     dn1_part = cols_inner(d_cat, w_cat).astype(BF)
-    dn1 = sum_own(dn1_part, 5)
+    dn1 = flow_sum(dn1_part)
     inputs_own = lax.dynamic_slice_in_dim(inputs, me * chunk, chunk, 0)
     recip_in = lax.dynamic_slice_in_dim(recip_one, me * chunk, chunk, 0)
     d_gain_one = jnp.sum(dn1 * inputs_own * recip_in, axis=0)
@@ -508,9 +594,7 @@
         + recip_in * weighted_one
         - inputs_own * recip_in**3 * jnp.mean(weighted_one * inputs_own, axis=1, keepdims=True)
     ).astype(BF)
-    output, d_tokens = spread([output, d_tokens], 6)
-    output = output.reshape(row_count, width)
-    d_tokens = d_tokens.reshape(row_count, width)
+    d_tokens = flow_spread(d_tokens)
 
     d_mlp = jnp.concatenate(
         [rows_inner(normed_two, d_gate_pre).astype(BF), rows_inner(normed_two, d_up_pre).astype(BF)], 1
@@ -520,11 +604,8 @@
     d_down = lax.psum_scatter(d_down, "batch", scatter_dimension=1, tiled=True).astype(F32)
     d_in = rows_inner(normed_one, d_cat).astype(BF)
     d_in = lax.psum_scatter(d_in, "batch", scatter_dimension=0, tiled=True).astype(F32)
-    d_gains = jnp.concatenate([d_gain_one, d_gain_two])
-    d_gains = lax.all_gather(d_gains, "head", axis=0)
-    d_gains = jnp.sum(d_gains, axis=0).reshape(2, batches, -1)
-    d_gains = lax.all_to_all(d_gains, "batch", split_axis=1, concat_axis=1, tiled=True)
-    d_gains = jnp.sum(d_gains, axis=1)
+    d_gains = jnp.stack([d_gain_one, d_gain_two]).reshape(2, batches, -1).transpose(1, 0, 2)
+    d_gains = sum_heads(halve_batch(d_gains.reshape(2 * batches, -1), 2))
     hidden_own = w_mlp_gate.shape[1]
     return (
         output,

time: 743 us -> 670 us (0.902)
  Pallas kernels: 364 us -> 132 us
  waiting for transfers between devices: 107 us -> 218 us
  starting transfers between devices: 8.65 us -> 67.4 us
  blocking collectives: 53.3 us -> 10.4 us
  local copies, waits for them, and re-layouts: 35.6 us -> 61.7 us
  other arithmetic: 36.7 us -> 50.4 us
  matrix products: 114 us -> 105 us
    ppermute x0 -> x47, waiting for transfers between devices: none -> 144 us  [the longest x12 39.3 us: flow_sum(): from_left = lax.ppermute(going, 'head', right)]
    pallas_call x4 -> x1, Pallas kernels: 190 us -> 59.9 us  [sum_own(): pl.pallas_call(functools.partial(sum_kernel, count), out_shape=jax.ShapeD...]
    pallas_call x3 -> x2, Pallas kernels: 154 us -> 52.1 us  [spread(): pl.pallas_call(functools.partial(spread_kernel, count, len(arrays)), out_...]
    ppermute x0 -> x47, starting transfers between devices: none -> 58.3 us  [the longest x12 17 us: flow_sum(): from_left = lax.ppermute(going, 'head', right)]
    reduce_scatter x1 -> x0, waiting for transfers between devices: 31 us -> none  [per_device(): lax.psum_scatter(d_kv_all, 'batch', scatter_dimension=0, tiled=True)]
    all_gather x1 -> x0, blocking collectives: 30.5 us -> none  [per_device(): d_gains = lax.all_gather(d_gains, 'head', axis=0)]
    dynamic_update_slice x0 -> x12, local copies, waits for them, and re-layouts: none -> 13.9 us  [flow_spread(): whole = lax.dynamic_update_slice_in_dim(whole, piece, at, 0)]
    all_to_all x1 -> x0, blocking collectives: 12.4 us -> none  [per_device(): lax.all_to_all(d_mixed_all, 'head', split_axis=0, concat_axis=0, tiled=True)]
  transfers between devices with their start and end apart: 14 -> 60, of which waited for: 6 -> 33; matrix products, arithmetic and copies ran while one was open for 15% -> 23% of each run, Pallas kernels for 33% -> 11%
where the time goes in v4:
time: 670 us; the launch traced here: 661 us
  waiting for transfers between devices  218 us (33%)
  Pallas kernels  132 us (20%)
  matrix products  105 us (16%)
  starting transfers between devices  67.4 us (10%)
  local copies, waits for them, and re-layouts  61.7 us (9%)
  other arithmetic  50.4 us (8%)
  between operations  15.6 us (2%)
  blocking collectives  10.4 us (2%)
    pallas_call x1, Pallas kernels, sum_own(): pl.pallas_call(functools.partial(sum_kernel, count), out_shape=jax.ShapeD...  59.9 us
    pallas_call x2, Pallas kernels, spread(): pl.pallas_call(functools.partial(spread_kernel, count, len(arrays)), out_...  52.1 us
    dot_general x5, matrix products, matmul(): return jnp.dot(left, right, preferred_element_type=F32)  44 us
    ppermute x12, waiting for transfers between devices, flow_sum(): from_left = lax.ppermute(going, 'head', right)  39.3 us
    ppermute x7, waiting for transfers between devices, swap(): lax.ppermute(block, axis, [(at, at ^ stride) for at in range(lax.axis_siz...  39.1 us
    ppermute x12, waiting for transfers between devices, flow_sum(): from_right = lax.ppermute(coming, 'head', left)  35.1 us
    dot_general x5, matrix products, cols_inner(): lax.dot_general(left, right, (((1,), (1,)), ((), ())), preferred_element_...  30.9 us
    dot_general x5, matrix products, rows_inner(): lax.dot_general(left, right, (((0,), (0,)), ((), ())), preferred_element_...  30.5 us
  transfers between devices with their start and end apart: 60, of which 33 were waited for; matrix products, arithmetic and copies ran while one was open for 23% of the time, Pallas kernels for 11%

profile of v4, /device:TPU:0, one launch (start us, length us, event | category | flops | bytes accessed | tf_op | source)
XLA Modules:
  0.0 660.8 jit_solution(16977052386456607091)
XLA Ops:
  27.0 15.3 %all-gather.8.cloned.1.call-done = bf16[2048,512]{1,0:T(8,128)(2,1)} async-done(((bf16[512,512]{1,0:T(8,128)(2,1)}), bf16[2048,512]{1,0:T(8,128)(2,1)}) %all-gather.8.cloned.1.call-update) | async-done | bytes 2097168 | tf_op jit(solution)/shard_map/all_gather | solution.py:472
  42.3 7.6 %fusion.43 = (bf16[1280,512]{1,0:T(8,128)(2,1)S(1)}, f32[1280,512]{1,0:T(8,128)}) fusion(bf16[2048,512]{1,0:T(8,128)(2,1)} %all-gather.8.cloned.1.call-done, bf16[1280,2048]{1,0:T(8,128)(2,1)} %param.13, f32[2048]{0:T(1024)S(1)} %bitcast.139, f32[1280]{0:T(1024)S(1)} %add_rsqrt_fusion.1), kind=kOutput, calls=%fused_computation.168 | convolution fusion | flops 2695495680 | bytes 11285504 | tf_op jit(solution)/shard_map/dot_general | solution.py:417
  50.8 19.9 %spread_1.1 = bf16[8,128,512]{2,1,0:T(8,128)(2,1)} custom-call(bf16[128,512]{1,0:T(8,128)(2,1)} %refs_0_.1), custom_call_target="tpu_custom_call" | custom-call | tf_op jit(solution)/shard_map/spread_1/pallas_call | solution.py:178
  81.3 8.8 %attend.1 = (f32[1280,128]{1,0:T(8,128)}, bf16[1280,128]{1,0:T(8,128)(2,1)}, f32[1,1280]{1,0:T(1,128)}) custom-call(s32[1280]{0:T(1024)} %copy-done.16, s32[1]{0:T(128)} %bitcast.1.base_sm, bf16[1280,128]{1,0:T(8,128)(2,1)} %slice.257.q_ref, bf16[5120,256]{1,0:T(8,128)(2,1)} %all-gather.10.cloned.1.call-done.kv_ref, s32[1,1280]{1,0:T(1,128)} %broadcast_in_dim.16.start_ref, ...), custom_call_target="tpu_custom_call" | custom-call | flops 3355443200 | bytes 8388608 | tf_op jit(solution)/shard_map/attend/pallas_call | solution.py:313
  90.1 32.2 %spread_2.1 = bf16[8,1280,128]{2,1,0:T(8,128)(2,1)} custom-call(bf16[1280,128]{1,0:T(8,128)(2,1)} %get-tuple-element.20.refs_0_), custom_call_target="tpu_custom_call" | custom-call | tf_op jit(solution)/shard_map/spread_2/pallas_call | solution.py:178
  126.8 10.2 %multiply_reduce_fusion = (f32[1280]{0:T(1024)S(1)}, f32[1280,2048]{1,0:T(8,128)S(1)}) fusion(bf16[1280,1024]{0,1:T(8,128)(2,1)} %bitcast.130, bf16[1024,2048]{1,0:T(8,128)(2,1)} %all-gather.12.cloned.1.call-done, bf16[1280,2048]{1,0:T(8,128)(2,1)} %param.13), kind=kOutput, calls=%fused_computation.2 | convolution fusion | flops 5379193856 | bytes 22549504 | tf_op jit(solution)/shard_map/dot_general | solution.py:417
  144.3 9.6 %fusion.44 = f32[1280,768]{1,0:T(8,128)} fusion(bf16[1280,2048]{1,0:T(8,128)(2,1)} %multiply_convert_fusion, bf16[2048,768]{1,0:T(8,128)(2,1)} %all-gather.14.cloned.1.call-done), kind=kOutput, calls=%fused_computation.169 | convolution fusion | flops 4026531840 | bytes 12320768 | tf_op jit(solution)/shard_map/dot_general | solution.py:417
  153.9 18.7 %all-gather.16.cloned.1.call-done = bf16[2048,768]{1,0:T(8,128)(2,1)} async-done(((bf16[512,768]{1,0:T(8,128)(2,1)}), bf16[2048,768]{1,0:T(8,128)(2,1)}) %all-gather.16.cloned.1.call-update) | async-done | bytes 3145744 | tf_op jit(solution)/shard_map/all_gather | solution.py:479
  172.6 9.6 %fusion.45 = f32[1280,768]{1,0:T(8,128)} fusion(bf16[1280,2048]{1,0:T(8,128)(2,1)} %multiply_convert_fusion, bf16[2048,768]{1,0:T(8,128)(2,1)} %all-gather.16.cloned.1.call-done), kind=kOutput, calls=%fused_computation.170 | convolution fusion | flops 4026531840 | bytes 12320768 | tf_op jit(solution)/shard_map/dot_general | solution.py:417
  182.2 20.4 %all-gather.18.cloned.1.call-done = bf16[768,2048]{1,0:T(8,128)(2,1)} async-done(((bf16[768,512]{1,0:T(8,128)(2,1)}), bf16[768,2048]{1,0:T(8,128)(2,1)}) %all-gather.18.cloned.1.call-update) | async-done | bytes 3145744 | tf_op jit(solution)/shard_map/all_gather | solution.py:480
  202.6 13.8 %multiply_convert_fusion.2 = (bf16[1280,768]{1,0:T(8,128)(2,1)}, bf16[1280,768]{1,0:T(8,128)(2,1)S(1)}, bf16[1280,768]{1,0:T(8,128)(2,1)}) fusion(f32[1280,768]{1,0:T(8,128)} %fusion.44, f32[1280,768]{1,0:T(8,128)} %fusion.45, bf16[1280,2048]{1,0:T(8,128)(2,1)} %param.25, bf16[768,2048]{1,0:T(8,128)(2,1)} %all-gather.18.cloned.1.call-done), kind=kOutput, calls=%fused_computation.9 | convolution fusion | flops 4041277440 | bytes 22151168 | tf_op jit(solution)/shard_map/dot_general | solution.py:425
  220.8 7.7 %add_convert_fusion.part_ref = bf16[1280,2048]{1,0:T(8,128)(2,1)} fusion(f32[1280,2048]{1,0:T(8,128)S(1)} %fusion.46, bf16[1280,768]{1,0:T(8,128)(2,1)} %get-tuple-element.84, bf16[2048,768]{1,0:T(8,128)(2,1)S(1)} %copy-done.21), kind=kOutput, calls=%fused_computation | convolution fusion | flops 4031774720 | bytes 20840448 | tf_op jit(solution)/shard_map/dot_general | solution.py:425
  228.6 59.9 %sum_own_3.1 = f32[160,2048]{1,0:T(8,128)} custom-call(bf16[1280,2048]{1,0:T(8,128)(2,1)} %add_convert_fusion.part_ref), custom_call_target="tpu_custom_call" | custom-call | tf_op jit(solution)/shard_map/sum_own_3/pallas_call | solution.py:110
  304.1 9.0 %convolution_convert_fusion.3 = bf16[768,2048]{1,0:T(8,128)(2,1)} fusion(bf16[1280,768]{1,0:T(8,128)(2,1)} %get-tuple-element.21, bf16[1280,2048]{1,0:T(8,128)(2,1)} %param.25), kind=kOutput, calls=%fused_computation.15 | convolution fusion | flops 4028104704 | bytes 10354688 | tf_op jit(solution)/shard_map/dot_general | solution.py:421
  314.0 10.9 %attend_back.1 = (bf16[1280,128]{1,0:T(8,128)(2,1)}, bf16[1280,128]{1,0:T(8,128)(2,1)}, bf16[5120,256]{1,0:T(8,128)(2,1)}) custom-call(s32[1280]{0:T(1024)} %copy-done.16, s32[1]{0:T(128)} %bitcast.1.base_sm, bf16[1280,128]{1,0:T(8,128)(2,1)} %slice.257.q_ref, bf16[5120,256]{1,0:T(8,128)(2,1)} %all-gather.10.cloned.1.call-done.kv_ref, ...), custom_call_target="tpu_custom_call" | custom-call | flops 8388608000 | bytes 8388608 | tf_op jit(solution)/shard_map/attend_back/pallas_call | solution.py:313
  335.8 10.0 %collective-permute-start.18 = (bf16[1,1280,256]{2,1,0:T(8,128)(2,1)}, bf16[1,1280,256]{2,1,0:T(8,128)(2,1)S(1)}, u32[]{:S(2)}, u32[]{:S(2)}) collective-permute-start(bf16[1,1280,256]{2,1,0:T(8,128)(2,1)} %constant_dynamic-slice_fusion.9), channel_id=1, source_target_pairs={{0,16},{8,24},{16,0},{24,8},{1,17},{9,25},{17,1},{25,9},{2,18},{10... | collective-permute-start | bytes 1966088 | tf_op jit(solution)/shard_map/ppermute | solution.py:385
  345.8 18.7 %collective-permute-done.18 = bf16[1,1280,256]{2,1,0:T(8,128)(2,1)S(1)} collective-permute-done((bf16[1,1280,256]{2,1,0:T(8,128)(2,1)}, bf16[1,1280,256]{2,1,0:T(8,128)(2,1)S(1)}, u32[]{:S(2)}, u32[]{:S(2)}) %collective-permute-start.18) | collective-permute-done | bytes 655392 | tf_op jit(solution)/shard_map/ppermute | solution.py:385
  366.2 15.1 %collective-permute-done.19 = bf16[1280,256]{1,0:T(8,128)(2,1)S(1)} collective-permute-done((bf16[1280,256]{1,0:T(8,128)(2,1)S(1)}, bf16[1280,256]{1,0:T(8,128)(2,1)S(1)}, u32[]{:S(2)}, u32[]{:S(2)}) %collective-permute-start.19) | collective-permute-done | bytes 655392 | tf_op jit(solution)/shard_map/ppermute | solution.py:413
  453.5 8.1 %collective-permute-done.4 = bf16[160,2048]{1,0:T(8,128)(2,1)S(1)} collective-permute-done((bf16[160,2048]{1,0:T(8,128)(2,1)S(1)}, bf16[160,2048]{1,0:T(8,128)(2,1)S(1)}, u32[]{:S(2)}, u32[]{:S(2)}) %collective-permute-start.4) | collective-permute-done | bytes 655392 | tf_op jit(solution)/shard_map/ppermute | solution.py:350
  473.3 13.1 %collective-permute-done.9 = bf16[160,2048]{1,0:T(8,128)(2,1)S(1)} collective-permute-done((bf16[160,2048]{1,0:T(8,128)(2,1)S(1)}, bf16[160,2048]{1,0:T(8,128)(2,1)S(1)}, u32[]{:S(2)}, u32[]{:S(2)}) %collective-permute-start.9) | collective-permute-done | bytes 655392 | tf_op jit(solution)/shard_map/ppermute | solution.py:371
  488.5 13.5 %collective-permute-done.25 = bf16[160,2048]{1,0:T(8,128)(2,1)S(1)} collective-permute-done((bf16[160,2048]{1,0:T(8,128)(2,1)S(1)}, bf16[160,2048]{1,0:T(8,128)(2,1)S(1)}, u32[]{:S(2)}, u32[]{:S(2)}) %collective-permute-start.25) | collective-permute-done | bytes 655392 | tf_op jit(solution)/shard_map/ppermute | solution.py:351
  505.7 7.9 %convert_element_type.296 = f32[1280,2048]{1,0:T(8,128)} convert(bf16[1280,2048]{1,0:T(8,128)(2,1)} %param.13) | non-fusion elementwise | flops 2621440 | bytes 15728640 | tf_op jit(solution)/shard_map/convert_element_type | solution.py:482
  516.7 12.0 %collective-permute-done.22 = bf16[160,2048]{1,0:T(8,128)(2,1)} collective-permute-done((bf16[160,2048]{1,0:T(8,128)(2,1)}, bf16[160,2048]{1,0:T(8,128)(2,1)}, u32[]{:S(2)}, u32[]{:S(2)}) %collective-permute-start.22) | collective-permute-done | bytes 655392 | tf_op jit(solution)/shard_map/ppermute | solution.py:350
  572.7 12.8 %collective-permute-done.39 = f32[2,512]{1,0:T(2,128)S(1)} collective-permute-done((f32[2,512]{1,0:T(2,128)S(1)}, f32[2,512]{1,0:T(2,128)S(1)}, u32[]{:S(2)}, u32[]{:S(2)}) %collective-permute-start.39) | collective-permute-done | bytes 4128 | tf_op jit(solution)/shard_map/ppermute | solution.py:385
  (313 shorter events, 280.3 us)
Async XLA Ops:
  7.2 35.1 %all-gather.8.cloned.1.call-start = ((), (), s32[]{:S(2)}) async-start(), calls=%async_computation.5 | async-start | bytes 2621440 | tf_op jit(solution)/shard_map/all_gather | solution.py:472
  18.1 63.2 %all-gather.10.cloned.1.call-start = ((), (), s32[]{:S(2)}) async-start(), calls=%async_computation.6 | async-start | bytes 3276800 | tf_op jit(solution)/shard_map/all_gather | solution.py:489
  50.8 76.1 %all-gather.12.cloned.1.call-start = ((), (), s32[]{:S(2)}) async-start(), calls=%async_computation.7 | async-start | bytes 5242880 | tf_op jit(solution)/shard_map/all_gather | solution.py:477
  70.7 73.5 %all-gather.14.cloned.1.call-start = ((), (), s32[]{:S(2)}) async-start(), calls=%async_computation.8 | async-start | bytes 3932160 | tf_op jit(solution)/shard_map/all_gather | solution.py:478
  71.3 101.3 %all-gather.16.cloned.1.call-start = ((), (), s32[]{:S(2)}) async-start(), calls=%async_computation.9 | async-start | bytes 3932160 | tf_op jit(solution)/shard_map/all_gather | solution.py:479
  71.9 130.7 %all-gather.18.cloned.1.call-start = ((), (), s32[]{:S(2)}) async-start(), calls=%async_computation.10 | async-start | bytes 3932160 | tf_op jit(solution)/shard_map/all_gather | solution.py:480
  303.9 290.6 %reduce-scatter.11.cloned.1.call-start = ((), (), s32[]{:S(2)}) async-start(), calls=%async_computation.14 | async-start | bytes 3932160 | tf_op jit(solution)/shard_map/reduce_scatter | solution.py:604
  313.1 283.8 %reduce-scatter.5.cloned.1.call-start = ((), (), s32[]{:S(2)}) async-start(), calls=%async_computation.11 | async-start | bytes 1966080 | tf_op jit(solution)/shard_map/reduce_scatter | solution.py:606
  335.8 28.7 %collective-permute-start.18 = (bf16[1,1280,256]{2,1,0:T(8,128)(2,1)}, bf16[1,1280,256]{2,1,0:T(8,128)(2,1)S(1)}, u32[]{:S(2)}, u32[]{:S(2)}) collective-permute-start(bf16[1,1280,256]{2,1,0:T(8,128)(2,1)} %constant_dynamic-slice_fusion.9), channel_id=1, source_target_pairs={{0,16},{8,24},{16,0},{24,8},{1,17},{9,25},{17,1},{25,9},{2,18},{10... | collective-permute-start | bytes 1966088 | tf_op jit(solution)/shard_map/ppermute | solution.py:385
  389.4 222.3 %reduce-scatter.7.cloned.1.call-start = ((), (), s32[]{:S(2)}) async-start(), calls=%async_computation.12 | async-start | bytes 5242880 | tf_op jit(solution)/shard_map/reduce_scatter | solution.py:549
  393.8 252.1 %reduce-scatter.9.cloned.1.call-start = ((), (), s32[]{:S(2)}) async-start(), calls=%async_computation.13 | async-start | bytes 7864320 | tf_op jit(solution)/shard_map/reduce_scatter | solution.py:602
  471.2 30.9 %collective-permute-start.25 = (bf16[160,2048]{1,0:T(8,128)(2,1)S(1)}, bf16[160,2048]{1,0:T(8,128)(2,1)S(1)}, u32[]{:S(2)}, u32[]{:S(2)}) collective-permute-start(bf16[160,2048]{1,0:T(8,128)(2,1)S(1)} %pad_maximum_fusion.5), channel_id=1, source_target_pairs={{0,1},{2,0},{4,2},{6,4},{7,6},{5,7},{3,5},{1,3},{8,9},{10,8},{12,1... | collective-permute-start | bytes 1966088 | tf_op jit(solution)/shard_map/ppermute | solution.py:351
  471.7 30.3 %collective-permute-start.21 = (bf16[160,2048]{1,0:T(8,128)(2,1)S(1)}, bf16[160,2048]{1,0:T(8,128)(2,1)S(1)}, u32[]{:S(2)}, u32[]{:S(2)}) collective-permute-start(bf16[160,2048]{1,0:T(8,128)(2,1)S(1)} %pad_maximum_fusion.4), channel_id=1, source_target_pairs={{0,2},{2,4},{4,6},{6,7},{7,5},{5,3},{3,1},{1,0},{8,10},{10,12},{12... | collective-permute-start | bytes 1966088 | tf_op jit(solution)/shard_map/ppermute | solution.py:350
  486.5 28.2 %collective-permute-start.11 = (bf16[160,2048]{1,0:T(8,128)(2,1)S(1)}, bf16[160,2048]{1,0:T(8,128)(2,1)}, u32[]{:S(2)}, u32[]{:S(2)}) collective-permute-start(bf16[160,2048]{1,0:T(8,128)(2,1)S(1)} %collective-permute-done.9), channel_id=1, source_target_pairs={{0,2},{2,4},{4,6},{6,7},{7,5},{5,3},{3,1},{1,0},{8,10},{10,12},{12... | collective-permute-start | bytes 1966088 | tf_op jit(solution)/shard_map/ppermute | solution.py:371
  488.0 28.2 %collective-permute-start.12 = (bf16[160,2048]{1,0:T(8,128)(2,1)S(1)}, bf16[160,2048]{1,0:T(8,128)(2,1)}, u32[]{:S(2)}, u32[]{:S(2)}) collective-permute-start(bf16[160,2048]{1,0:T(8,128)(2,1)S(1)} %collective-permute-done.10), channel_id=1, source_target_pairs={{0,1},{2,0},{4,2},{6,4},{7,6},{5,7},{3,5},{1,3},{8,9},{10,8},{12,1... | collective-permute-start | bytes 1966088 | tf_op jit(solution)/shard_map/ppermute | solution.py:372
  503.6 25.2 %collective-permute-start.22 = (bf16[160,2048]{1,0:T(8,128)(2,1)}, bf16[160,2048]{1,0:T(8,128)(2,1)}, u32[]{:S(2)}, u32[]{:S(2)}) collective-permute-start(bf16[160,2048]{1,0:T(8,128)(2,1)} %get-tuple-element.89), channel_id=1, source_target_pairs={{0,2},{2,4},{4,6},{6,7},{7,5},{5,3},{3,1},{1,0},{8,10},{10,12},{12... | collective-permute-start | bytes 1966088 | tf_op jit(solution)/shard_map/ppermute | solution.py:350
  505.0 25.2 %collective-permute-start.26 = (bf16[160,2048]{1,0:T(8,128)(2,1)}, bf16[160,2048]{1,0:T(8,128)(2,1)}, u32[]{:S(2)}, u32[]{:S(2)}) collective-permute-start(bf16[160,2048]{1,0:T(8,128)(2,1)} %get-tuple-element.90), channel_id=1, source_target_pairs={{0,1},{2,0},{4,2},{6,4},{7,6},{5,7},{3,5},{1,3},{8,9},{10,8},{12,1... | collective-permute-start | bytes 1966088 | tf_op jit(solution)/shard_map/ppermute | solution.py:351
  514.7 28.0 %collective-permute-start.13 = (bf16[160,2048]{1,0:T(8,128)(2,1)}, bf16[160,2048]{1,0:T(8,128)(2,1)S(1)}, u32[]{:S(2)}, u32[]{:S(2)}) collective-permute-start(bf16[160,2048]{1,0:T(8,128)(2,1)} %collective-permute-done.11), channel_id=1, source_target_pairs={{0,2},{2,4},{4,6},{6,7},{7,5},{5,3},{3,1},{1,0},{8,10},{10,12},{12... | collective-permute-start | bytes 1966088 | tf_op jit(solution)/shard_map/ppermute | solution.py:371
  516.2 28.8 %collective-permute-start.14 = (bf16[160,2048]{1,0:T(8,128)(2,1)}, bf16[160,2048]{1,0:T(8,128)(2,1)S(1)}, u32[]{:S(2)}, u32[]{:S(2)}) collective-permute-start(bf16[160,2048]{1,0:T(8,128)(2,1)} %collective-permute-done.12), channel_id=1, source_target_pairs={{0,1},{2,0},{4,2},{6,4},{7,6},{5,7},{3,5},{1,3},{8,9},{10,8},{12,1... | collective-permute-start | bytes 1966088 | tf_op jit(solution)/shard_map/ppermute | solution.py:372
  533.9 20.4 %collective-permute-start.27 = (bf16[160,2048]{1,0:T(8,128)(2,1)S(1)}, bf16[160,2048]{1,0:T(8,128)(2,1)S(1)}, u32[]{:S(2)}, u32[]{:S(2)}) collective-permute-start(bf16[160,2048]{1,0:T(8,128)(2,1)S(1)} %get-tuple-element.88), channel_id=1, source_target_pairs={{0,1},{2,0},{4,2},{6,4},{7,6},{5,7},{3,5},{1,3},{8,9},{10,8},{12,1... | collective-permute-start | bytes 1966088 | tf_op jit(solution)/shard_map/ppermute | solution.py:351
  543.5 43.3 %collective-permute-start.15 = (bf16[160,1024]{1,0:T(8,128)(2,1)}, bf16[160,1024]{1,0:T(8,128)(2,1)}, u32[]{:S(2)}, u32[]{:S(2)}) collective-permute-start(bf16[160,1024]{1,0:T(8,128)(2,1)} %slice.261), channel_id=1, source_target_pairs={{0,2},{2,4},{4,6},{6,7},{7,5},{5,3},{3,1},{1,0},{8,10},{10,12},{12... | collective-permute-start | bytes 983048 | tf_op jit(solution)/shard_map/ppermute | solution.py:374
  545.8 41.0 %collective-permute-start.16 = (bf16[160,1024]{1,0:T(8,128)(2,1)}, bf16[160,1024]{1,0:T(8,128)(2,1)}, u32[]{:S(2)}, u32[]{:S(2)}) collective-permute-start(bf16[160,1024]{1,0:T(8,128)(2,1)} %slice.262), channel_id=1, source_target_pairs={{0,1},{2,0},{4,2},{6,4},{7,6},{5,7},{3,5},{1,3},{8,9},{10,8},{12,1... | collective-permute-start | bytes 983048 | tf_op jit(solution)/shard_map/ppermute | solution.py:375
  568.7 22.0 %collective-permute-start.28 = (bf16[160,2048]{1,0:T(8,128)(2,1)S(1)}, bf16[160,2048]{1,0:T(8,128)(2,1)S(1)}, u32[]{:S(2)}, u32[]{:S(2)}) collective-permute-start(bf16[160,2048]{1,0:T(8,128)(2,1)S(1)} %get-tuple-element.81), channel_id=1, source_target_pairs={{0,2},{2,4},{4,6},{6,7},{7,5},{5,3},{3,1},{1,0},{8,10},{10,12},{12... | collective-permute-start | bytes 1966088 | tf_op jit(solution)/shard_map/ppermute | solution.py:371
  569.7 21.2 %collective-permute-start.29 = (bf16[160,2048]{1,0:T(8,128)(2,1)S(1)}, bf16[160,2048]{1,0:T(8,128)(2,1)S(1)}, u32[]{:S(2)}, u32[]{:S(2)}) collective-permute-start(bf16[160,2048]{1,0:T(8,128)(2,1)S(1)} %get-tuple-element.81), channel_id=1, source_target_pairs={{0,1},{2,0},{4,2},{6,4},{7,6},{5,7},{3,5},{1,3},{8,9},{10,8},{12,1... | collective-permute-start | bytes 1966088 | tf_op jit(solution)/shard_map/ppermute | solution.py:372
  (67 other events, 828.8 us)
Sparse Core Ops, SparseCore 0:
  18.2 24.0 all-gather.7
  50.9 25.5 all-gather.9
  78.1 34.5 all-gather.11
  114.1 28.5 all-gather.13
  144.1 28.5 all-gather.15
  174.1 28.5 all-gather.17
  313.2 41.8 reduce-scatter.10
  389.5 28.1 reduce-scatter.4
  420.2 44.4 reduce-scatter.6
  467.3 58.3 reduce-scatter.8

commit v5 on v4

--- a/solution.py
+++ b/solution.py
@@ -58,77 +58,17 @@
     return copy
 
 
-def sum_kernel(count, part_ref, own_ref, from_left, from_right, send_sem, recv_sem):
-    steps = count // 2
-    rows = part_ref.shape[0] // count
-    width = part_ref.shape[1]
-    side = width // 2
-    place, right, left = ring_setup(count)
-    greet((right, left))
-    sems = (send_sem, recv_sem)
-
-    def part(owner):
-        return part_ref.at[pl.ds(pl.multiple_of(lax.rem(owner + count, count) * rows, rows), rows)]
-
-    far = part(place + steps)
-    copies = [
-        send(far.at[:, pl.ds(0, side)], from_left.at[0, :, pl.ds(0, side)], sems, 0, right),
-        send(far.at[:, pl.ds(side, side)], from_right.at[0, :, pl.ds(side, side)], sems, steps, left),
-    ]
-    for step in range(1, steps):
-        for flow, held, owner, device in (
-            (0, from_left, place + steps - step, right),
-            (1, from_right, place - steps + step, left),
-        ):
-            copies[2 * step - 2 + flow].wait_recv()
-            mine = part(owner)
-            if step == 1:
-                have = pl.ds(flow * side, side)
-                lack = pl.ds((1 - flow) * side, side)
-                held[0, :, have] = (held[0, :, have].astype(F32) + mine[:, have].astype(F32)).astype(BF)
-                held[0, :, lack] = mine[:, lack]
-            else:
-                held[step - 1] = (held[step - 1].astype(F32) + mine[...].astype(F32)).astype(BF)
-            copies.append(
-                send(held.at[step - 1], held.at[step], sems, flow * steps + step, device)
-            )
-    copies[-2].wait_recv()
-    copies[-1].wait_recv()
-    own_ref[...] = (
-        part(place)[...].astype(F32)
-        + from_left[steps - 1].astype(F32)
-        + from_right[steps - 1].astype(F32)
-    )
-    for copy in copies:
-        copy.wait_send()
-
-
-def sum_own(part, collective_id):
-    count = lax.axis_size("head")
-    rows, width = part.shape[0] // count, part.shape[1]
-    vmem = pl.BlockSpec(memory_space=pltpu.VMEM)
-    return pl.pallas_call(
-        functools.partial(sum_kernel, count),
-        out_shape=jax.ShapeDtypeStruct((rows, width), F32),
-        in_specs=[vmem],
-        out_specs=vmem,
-        scratch_shapes=[
-            pltpu.VMEM((count // 2, rows, width), BF),
-            pltpu.VMEM((count // 2, rows, width), BF),
-            pltpu.SemaphoreType.DMA((count,)),
-            pltpu.SemaphoreType.DMA((count,)),
-        ],
-        compiler_params=pltpu.CompilerParams(
-            collective_id=collective_id, has_side_effects=True, vmem_limit_bytes=VMEM_LIMIT
-        ),
-        name=f"sum_own_{collective_id}",
-    )(part)
-
-
 def half_of(extent, flow):
     if extent[1] % 256:
         return (pl.ds(flow * (extent[0] // 2), extent[0] // 2), slice(None))
     return (slice(None), pl.ds(flow * (extent[1] // 2), extent[1] // 2))
+
+
+def place_of(whole, own, chunk):
+    if len(whole.shape) == 3:
+        return whole.at[chunk]
+    wide = own.shape[1]
+    return whole.at[:, pl.ds(pl.multiple_of(chunk * wide, wide), wide)]
 
 
 def spread_kernel(count, arrays, *refs):
@@ -140,7 +80,9 @@
     sems = (send_sem, recv_sem)
     local = []
     for index in range(arrays):
-        copy = pltpu.make_async_copy(own_refs[index], all_refs[index].at[place], local_sem.at[index])
+        copy = pltpu.make_async_copy(
+            own_refs[index], place_of(all_refs[index], own_refs[index], place), local_sem.at[index]
+        )
         copy.start()
         local.append(copy)
     waiting = []
@@ -156,7 +98,7 @@
                 if step:
                     copies[at].wait_recv()
                 chunk = lax.rem(chunk + count, count)
-                target = all_refs[index].at[chunk]
+                target = place_of(all_refs[index], own_refs[index], chunk)
                 source = target if step else own_refs[index]
                 if step == steps - 1:
                     part = half_of(extent, flow)
@@ -172,12 +114,13 @@
         copy.wait()
 
 
-def spread(arrays, collective_id, space=pl.ANY):
+def spread(arrays, collective_id, columns=False, space=pl.ANY):
     count = lax.axis_size("head")
+    shapes = [(a.shape[0], count * a.shape[1]) if columns else (count, *a.shape) for a in arrays]
     slots = len(arrays) * count
     return pl.pallas_call(
         functools.partial(spread_kernel, count, len(arrays)),
-        out_shape=[jax.ShapeDtypeStruct((count, *a.shape), a.dtype) for a in arrays],
+        out_shape=[jax.ShapeDtypeStruct(shape, a.dtype) for shape, a in zip(shapes, arrays)],
         in_specs=[pl.BlockSpec(memory_space=space)] * len(arrays),
         out_specs=[pl.BlockSpec(memory_space=space)] * len(arrays),
         scratch_shapes=[
@@ -190,6 +133,231 @@
         ),
         name=f"spread_{collective_id}",
     )(*arrays)
+
+
+def mlp_kernel(
+    count, x_hbm, a_hbm, dy_hbm, gain_ref, out_w, gate_w, up_w, down_w,
+    n2_hbm, hid_hbm, grad_hbm, mlp_hbm, dn2_ref, h1_ref,
+    x_s, a_s, dy_s, n2_s, hid_s, grad_s, mlp_s, h1_s,
+    right_part, left_part, right_got, left_got,
+    in_sem, out_sem, send_sem, recv_sem,
+):
+    steps = count // 2
+    rows = x_hbm.shape[0] // count
+    width = x_hbm.shape[1]
+    hidden = gate_w.shape[1]
+    side = width // 2
+    tile = 256
+    inner = 256 if hidden % 256 == 0 else 128
+    place, right, left = ring_setup(count)
+    greet((right, left))
+
+    def owners(group):
+        first = jnp.where(group == 0, 1, 0)
+        one = lax.rem(place + steps - group, count)
+        two = lax.rem(place - steps + group + first * steps + count, count)
+        return one, two
+
+    def span(owner):
+        return pl.ds(pl.multiple_of(owner * rows, rows), rows)
+
+    def loads(group, slot):
+        return [
+            pltpu.make_async_copy(
+                source.at[span(owner)],
+                target.at[slot, pl.ds(at * rows, rows)],
+                in_sem.at[slot, 2 * index + at],
+            )
+            for index, (source, target) in enumerate(((x_hbm, x_s), (a_hbm, a_s), (dy_hbm, dy_s)))
+            for at, owner in enumerate(owners(group))
+        ]
+
+    def stores(group, slot):
+        return [
+            pltpu.make_async_copy(
+                source.at[slot, pl.ds(at * rows, rows)],
+                target.at[span(owner)],
+                out_sem.at[slot, 2 * index + at],
+            )
+            for index, (source, target) in enumerate(
+                ((n2_s, n2_hbm), (hid_s, hid_hbm), (grad_s, grad_hbm), (mlp_s, mlp_hbm))
+            )
+            for at, owner in enumerate(owners(group))
+        ]
+
+    def passing(source, target, flow, step, device):
+        return pltpu.make_async_remote_copy(
+            src_ref=source,
+            dst_ref=target,
+            send_sem=send_sem.at[flow * steps + step],
+            recv_sem=recv_sem.at[flow * steps + step],
+            device_id=device,
+            device_id_type=MESH,
+        )
+
+    def first_copies():
+        ahead, behind = pl.ds(0, side), pl.ds(side, side)
+        return (
+            passing(right_part.at[0, :, ahead], right_got.at[0, :, ahead], 0, 0, right),
+            passing(right_part.at[0, :, behind], left_got.at[0, :, behind], 1, 0, left),
+        )
+
+    def later_copies(step):
+        return (
+            passing(right_part.at[step], right_got.at[step], 0, step, right),
+            passing(left_part.at[step], left_got.at[step], 1, step, left),
+        )
+
+    for copy in loads(0, 0):
+        copy.start()
+
+    @pl.loop(0, steps)
+    def _(group):
+        slot = lax.rem(group, 2)
+        for copy in loads(group, slot):
+            copy.wait()
+
+        @pl.when(group + 1 < steps)
+        def _():
+            for copy in loads(group + 1, 1 - slot):
+                copy.start()
+
+        @pl.when(group >= 2)
+        def _():
+            for copy in stores(group - 2, slot):
+                copy.wait()
+
+        mixed = a_s[slot]
+
+        def residual(at, total):
+            cols = pl.ds(pl.multiple_of(at * tile, tile), tile)
+            values = x_s[slot, :, cols].astype(F32) + matmul(mixed, out_w[:, cols])
+            h1_s[:, cols] = values
+            return total + jnp.sum(values * values, axis=1, keepdims=True)
+
+        total = lax.fori_loop(0, width // tile, residual, jnp.zeros((2 * rows, 1), F32))
+        scale = lax.rsqrt(total / width + EPSILON)
+
+        @pl.when(group == 0)
+        def _():
+            h1_ref[...] = h1_s[pl.ds(rows, rows)]
+
+        @pl.loop(0, width // tile)
+        def _(at):
+            cols = pl.ds(pl.multiple_of(at * tile, tile), tile)
+            n2_s[slot, :, cols] = (h1_s[:, cols] * scale * gain_ref[:, cols]).astype(BF)
+
+        normed = n2_s[slot]
+        dy = dy_s[slot]
+
+        @pl.loop(0, hidden // inner)
+        def _(at):
+            cols = pl.ds(pl.multiple_of(at * inner, inner), inner)
+            cols_up = pl.ds(pl.multiple_of(hidden + at * inner, inner), inner)
+            gate = matmul(normed, gate_w[:, cols])
+            up = matmul(normed, up_w[:, cols])
+            d_hidden = cols_inner(dy, down_w[cols])
+            sig = jax.nn.sigmoid(gate)
+            silu = gate * sig
+            hid_s[slot, :, cols] = (silu * up).astype(BF)
+            grad_s[slot, :, cols] = (d_hidden * up * sig * (1.0 + gate * (1.0 - sig))).astype(BF)
+            grad_s[slot, :, cols_up] = (d_hidden * silu).astype(BF)
+
+        hid = hid_s[slot]
+        d_gate = grad_s[slot, :, :hidden]
+        d_up = grad_s[slot, :, hidden:]
+
+        @pl.loop(0, width // tile)
+        def _(at):
+            cols = pl.ds(pl.multiple_of(at * tile, tile), tile)
+            part = (cols_inner(d_gate, gate_w[cols]) + cols_inner(d_up, up_w[cols])).astype(BF)
+            right_part[group, :, cols] = part[:rows]
+            left_part[group, :, cols] = part[rows:]
+            mlp_s[slot, :, cols] = matmul(hid, down_w[:, cols]).astype(BF)
+
+        for copy in stores(group, slot):
+            copy.start()
+
+        @pl.when(group == 0)
+        def _():
+            for copy in first_copies():
+                copy.start()
+
+        @pl.when(group == 1)
+        def _():
+            one, two = first_copies()
+            one.wait_recv()
+            two.wait_recv()
+            ahead, behind = pl.ds(0, side), pl.ds(side, side)
+            right_part[1, :, ahead] = add_low(right_part[1, :, ahead], right_got[0, :, ahead])
+            left_part[1, :, behind] = add_low(left_part[1, :, behind], left_got[0, :, behind])
+
+        @pl.when(group >= 2)
+        def _():
+            one, two = later_copies(group - 1)
+            one.wait_recv()
+            right_part[group] = add_low(right_part[group], right_got[group - 1])
+            two.wait_recv()
+            left_part[group] = add_low(left_part[group], left_got[group - 1])
+
+        @pl.when(group >= 1)
+        def _():
+            for copy in later_copies(group):
+                copy.start()
+
+    for copy in later_copies(steps - 1):
+        copy.wait_recv()
+    dn2_ref[...] = (
+        left_part[0].astype(F32) + right_got[steps - 1].astype(F32) + left_got[steps - 1].astype(F32)
+    )
+    for copy in first_copies():
+        copy.wait_send()
+    for step in range(1, steps):
+        for copy in later_copies(step):
+            copy.wait_send()
+    for group in range(max(steps - 2, 0), steps):
+        for copy in stores(group, group % 2):
+            copy.wait()
+
+
+def mlp_back(tokens, mixed, dy, gain, out_w, gate_w, up_w, down_w, collective_id):
+    count = lax.axis_size("head")
+    total, width = tokens.shape
+    hidden = gate_w.shape[1]
+    rows, steps = total // count, count // 2
+    vmem = pl.BlockSpec(memory_space=pltpu.VMEM)
+    hbm = pl.BlockSpec(memory_space=pl.ANY)
+
+    def slots(wide, dtype=BF):
+        return pltpu.VMEM((2, 2 * rows, wide), dtype)
+
+    part = pltpu.VMEM((steps, rows, width), BF)
+    flops = 2 * total * width * (mixed.shape[1] + 6 * hidden)
+    return pl.pallas_call(
+        functools.partial(mlp_kernel, count),
+        out_shape=[
+            jax.ShapeDtypeStruct((total, width), BF),
+            jax.ShapeDtypeStruct((total, hidden), BF),
+            jax.ShapeDtypeStruct((total, 2 * hidden), BF),
+            jax.ShapeDtypeStruct((total, width), BF),
+            jax.ShapeDtypeStruct((rows, width), F32),
+            jax.ShapeDtypeStruct((rows, width), F32),
+        ],
+        in_specs=[hbm] * 3 + [vmem] * 5,
+        out_specs=[hbm] * 4 + [vmem] * 2,
+        scratch_shapes=[
+            slots(width), slots(mixed.shape[1]), slots(width), slots(width), slots(hidden),
+            slots(2 * hidden), slots(width), pltpu.VMEM((2 * rows, width), F32),
+            part, part, part, part,
+            pltpu.SemaphoreType.DMA((2, 6)), pltpu.SemaphoreType.DMA((2, 8)),
+            pltpu.SemaphoreType.DMA((count,)), pltpu.SemaphoreType.DMA((count,)),
+        ],
+        compiler_params=pltpu.CompilerParams(
+            collective_id=collective_id, has_side_effects=True, vmem_limit_bytes=VMEM_LIMIT
+        ),
+        cost_estimate=pl.CostEstimate(flops=flops, bytes_accessed=40 << 20, transcendentals=0),
+        name="mlp_back",
+    )(tokens, mixed, dy, gain, out_w, gate_w, up_w, down_w)
 
 
 KEY_BLOCK = 512
@@ -507,28 +675,13 @@
         pair_flops,
         "attend",
     )
-    (mixed_all,) = spread([mixed], 2)
-    mixed_all = mixed_all.transpose(1, 0, 2).reshape(row_count, -1)
-    resid = inputs + matmul(mixed_all, out_full)
-    recip_two = rms_scale(resid)
-    normed_two = (resid * recip_two * gain_two).astype(BF)
-    resid_own = lax.dynamic_slice_in_dim(resid, me * chunk, chunk, 0)
-    recip_own = lax.dynamic_slice_in_dim(recip_two, me * chunk, chunk, 0)
+    (mixed_all,) = spread([mixed], 2, columns=True)
+    normed_two, hidden, d_pre, mlp_part, dn2, resid_own = mlp_back(
+        tokens, mixed_all, out_grad, gain_two[None], out_full, mgate_full, mup_full, down_full, 3
+    )
+    recip_own = rms_scale(resid_own)
     mixed_own = lax.dynamic_slice_in_dim(mixed_all, me * chunk, chunk, 0)
     dy_own = lax.dynamic_slice_in_dim(out_grad, me * chunk, chunk, 0).astype(F32)
-
-    gate_pre = matmul(normed_two, mgate_full)
-    up_pre = matmul(normed_two, mup_full)
-    sig_gate = jax.nn.sigmoid(gate_pre)
-    silu_gate = gate_pre * sig_gate
-    hidden = (silu_gate * up_pre).astype(BF)
-    d_hidden = cols_inner(out_grad, down_full)
-    d_gate_pre = (d_hidden * up_pre * sig_gate * (1.0 + gate_pre * (1.0 - sig_gate))).astype(BF)
-    d_up_pre = (d_hidden * silu_gate).astype(BF)
-    dn2_part = cols_inner(d_gate_pre, mgate_full) + cols_inner(d_up_pre, mup_full)
-    dn2 = sum_own(dn2_part.astype(BF), 3)
-    hidden_late, dn2 = lax.optimization_barrier((hidden, dn2))
-    mlp_part = matmul(hidden_late, down_full).astype(BF)
     output = flow_spread((resid_own + flow_sum(mlp_part)).astype(BF))
 
     d_gain_two = jnp.sum(dn2 * resid_own * recip_own, axis=0)
@@ -596,9 +749,7 @@
     ).astype(BF)
     d_tokens = flow_spread(d_tokens)
 
-    d_mlp = jnp.concatenate(
-        [rows_inner(normed_two, d_gate_pre).astype(BF), rows_inner(normed_two, d_up_pre).astype(BF)], 1
-    )
+    d_mlp = rows_inner(normed_two, d_pre).astype(BF)
     d_mlp = lax.psum_scatter(d_mlp, "batch", scatter_dimension=0, tiled=True).astype(F32)
     d_down = rows_inner(hidden, out_grad).astype(BF)
     d_down = lax.psum_scatter(d_down, "batch", scatter_dimension=1, tiled=True).astype(F32)

time: 670 us -> 662 us (0.988)
  matrix products: 105 us -> 46.2 us
  waiting for transfers between devices: 218 us -> 258 us
  Pallas kernels: 132 us -> 156 us
  local copies, waits for them, and re-layouts: 61.7 us -> 51.7 us
    dot_general x5 -> x1, matrix products: 44 us -> 7.58 us  [matmul(): return jnp.dot(left, right, preferred_element_type=F32)]
    all_gather x1, waiting for transfers between devices: 0.01 us -> 35.9 us  [per_device(): lax.all_gather(out_rows.reshape(heads * head_size, -1), 'batch', axis=1,...]
    dot_general x5 -> x2, matrix products: 30.9 us -> 4.99 us  [cols_inner(): lax.dot_general(left, right, (((1,), (1,)), ((), ())), preferred_element_...]
    pallas_call x1, Pallas kernels: 59.9 us -> 83.8 us  [mlp_back(): pl.pallas_call(functools.partial(mlp_kernel, count), out_shape=[jax.Shape...]
    all_gather x1, waiting for transfers between devices: 20.4 us -> 30 us  [per_device(): down_full = lax.all_gather(w_down, 'batch', axis=1, tiled=True)]
    unnamed x86 -> x76, local copies, waits for them, and re-layouts: 19.7 us -> 11.5 us
    dot_general x5 -> x4, matrix products: 30.5 us -> 33.7 us  [rows_inner(): lax.dot_general(left, right, (((0,), (0,)), ((), ())), preferred_element_...]
  transfers between devices with their start and end apart: 60 -> 60, of which waited for: 33 -> 32; matrix products, arithmetic and copies ran while one was open for 23% -> 18% of each run, Pallas kernels for 11% -> 11%
where the time goes in v5:
time: 662 us; the launch traced here: 656 us
  waiting for transfers between devices  258 us (39%)
  Pallas kernels  156 us (24%)
  starting transfers between devices  69.1 us (10%)
  local copies, waits for them, and re-layouts  51.7 us (8%)
  other arithmetic  49.5 us (7%)
  matrix products  46.2 us (7%)
  between operations  15.2 us (2%)
  blocking collectives  10.5 us (2%)
    pallas_call x1, Pallas kernels, mlp_back(): pl.pallas_call(functools.partial(mlp_kernel, count), out_shape=[jax.Shape...  83.8 us
    pallas_call x2, Pallas kernels, spread(): pl.pallas_call(functools.partial(spread_kernel, count, len(arrays)), out_...  52.1 us
    ppermute x12, waiting for transfers between devices, flow_sum(): from_left = lax.ppermute(going, 'head', right)  40 us
    ppermute x12, waiting for transfers between devices, flow_sum(): from_right = lax.ppermute(coming, 'head', left)  37.9 us
    all_gather x1, waiting for transfers between devices, per_device(): lax.all_gather(out_rows.reshape(heads * head_size, -1), 'batch', axis=1,...  35.9 us
    ppermute x7, waiting for transfers between devices, swap(): lax.ppermute(block, axis, [(at, at ^ stride) for at in range(lax.axis_siz...  35.5 us
    dot_general x4, matrix products, rows_inner(): lax.dot_general(left, right, (((0,), (0,)), ((), ())), preferred_element_...  33.7 us
    ppermute x6, waiting for transfers between devices, flow_spread(): going = lax.ppermute(going, 'head', right)  30 us
  transfers between devices with their start and end apart: 60, of which 32 were waited for; matrix products, arithmetic and copies ran while one was open for 18% of the time, Pallas kernels for 11%

profile of v5, /device:TPU:0, one launch (start us, length us, event | category | flops | bytes accessed | tf_op | source)
XLA Modules:
  0.0 656.2 jit_solution(15601100384027862993)
XLA Ops:
  26.8 14.7 %all-gather.8.cloned.1.call-done = bf16[2048,512]{1,0:T(8,128)(2,1)} async-done(((bf16[512,512]{1,0:T(8,128)(2,1)}), bf16[2048,512]{1,0:T(8,128)(2,1)}) %all-gather.8.cloned.1.call-update) | async-done | bytes 2097168 | tf_op jit(solution)/shard_map/all_gather | solution.py:640
  41.4 7.6 %fusion.42 = (bf16[1280,512]{1,0:T(8,128)(2,1)S(1)}, f32[1280,512]{1,0:T(8,128)}) fusion(bf16[2048,512]{1,0:T(8,128)(2,1)} %all-gather.8.cloned.1.call-done, f32[2048]{0:T(1024)S(1)} %bitcast.111, f32[1280]{0:T(1024)S(1)} %add_rsqrt_fusion, bf16[1280,2048]{1,0:T(8,128)(2,1)} %x_hbm.1), kind=kOutput, calls=%fused_computation.157 | convolution fusion | flops 2695495680 | bytes 11285504 | tf_op jit(solution)/shard_map/dot_general | solution.py:585
  51.9 19.9 %spread_1.1 = bf16[8,128,512]{2,1,0:T(8,128)(2,1)} custom-call(bf16[128,512]{1,0:T(8,128)(2,1)} %refs_0_.1), custom_call_target="tpu_custom_call" | custom-call | tf_op jit(solution)/shard_map/spread_1/pallas_call | solution.py:121
  80.8 8.8 %attend.1 = (f32[1280,128]{1,0:T(8,128)}, bf16[1280,128]{1,0:T(8,128)(2,1)}, f32[1,1280]{1,0:T(1,128)}) custom-call(s32[1280]{0:T(1024)} %copy-done.18, s32[1]{0:T(128)} %bitcast.1.base_sm, bf16[1280,128]{1,0:T(8,128)(2,1)} %slice.257.q_ref, bf16[5120,256]{1,0:T(8,128)(2,1)} %all-gather.10.cloned.1.call-done.kv_ref, s32[1,1280]{1,0:T(1,128)} %broadcast_in_dim.16.start_ref, ...), custom_call_target="tpu_custom_call" | custom-call | flops 3355443200 | bytes 8388608 | tf_op jit(solution)/shard_map/attend/pallas_call | solution.py:481
  89.6 32.3 %spread_2.1.a_hbm = bf16[1280,1024]{1,0:T(8,128)(2,1)} custom-call(bf16[1280,128]{1,0:T(8,128)(2,1)} %get-tuple-element.24.refs_0_), custom_call_target="tpu_custom_call" | custom-call | tf_op jit(solution)/shard_map/spread_2/pallas_call | solution.py:121
  121.9 13.9 %all-gather.16.cloned.1.call-done.up_w = bf16[2048,768]{1,0:T(8,128)(2,1)} async-done(((bf16[512,768]{1,0:T(8,128)(2,1)}), bf16[2048,768]{1,0:T(8,128)(2,1)}) %all-gather.16.cloned.1.call-update) | async-done | bytes 3145744 | tf_op jit(solution)/shard_map/all_gather | solution.py:647
  135.8 30.0 %all-gather.18.cloned.1.call-done.down_w = bf16[768,2048]{1,0:T(8,128)(2,1)} async-done(((bf16[768,512]{1,0:T(8,128)(2,1)}), bf16[768,2048]{1,0:T(8,128)(2,1)}) %all-gather.18.cloned.1.call-update) | async-done | bytes 3145744 | tf_op jit(solution)/shard_map/all_gather | solution.py:648
  165.8 35.9 %all-gather.12.cloned.1.call-done.out_w = bf16[1024,2048]{1,0:T(8,128)(2,1)} async-done(((bf16[1024,512]{1,0:T(8,128)(2,1)}), bf16[1024,2048]{1,0:T(8,128)(2,1)}) %all-gather.12.cloned.1.call-update) | async-done | bytes 4194320 | tf_op jit(solution)/shard_map/all_gather | solution.py:645
  201.7 83.8 %mlp_back.1 = (bf16[1280,2048]{1,0:T(8,128)(2,1)}, bf16[1280,768]{1,0:T(8,128)(2,1)}, bf16[1280,1536]{1,0:T(8,128)(2,1)}, bf16[1280,2048]{1,0:T(8,128)(2,1)}, f32[160,2048]{1,0:T(8,128)}, /*index=5*/f32[160,2048]{1,0:T(8,128)}) custom-call(bf16[1280,2048]{1,0:T(8,128)(2,1)} %x_hbm.1, bf16[1280,1024]{1,0:T(8,128)(2,1)} %spread_2.1.a_hbm, ...), custom_call_target="tpu_custom_call" | custom-call | flops 29527900160 | bytes 41943040 | tf_op jit(solution)/shard_map/mlp_back/pallas_call | solution.py:336
  302.2 9.1 %convolution_convert_fusion.3 = bf16[768,2048]{1,0:T(8,128)(2,1)} fusion(bf16[1280,768]{1,0:T(8,128)(2,1)} %get-tuple-element.35, bf16[1280,2048]{1,0:T(8,128)(2,1)} %dy_hbm.1), kind=kOutput, calls=%fused_computation.5 | convolution fusion | flops 4028104704 | bytes 10354688 | tf_op jit(solution)/shard_map/dot_general | solution.py:589
  312.4 10.9 %attend_back.1 = (bf16[1280,128]{1,0:T(8,128)(2,1)}, bf16[1280,128]{1,0:T(8,128)(2,1)}, bf16[5120,256]{1,0:T(8,128)(2,1)}) custom-call(s32[1280]{0:T(1024)} %copy-done.18, s32[1]{0:T(128)} %bitcast.1.base_sm, bf16[1280,128]{1,0:T(8,128)(2,1)} %slice.257.q_ref, bf16[5120,256]{1,0:T(8,128)(2,1)} %all-gather.10.cloned.1.call-done.kv_ref, ...), custom_call_target="tpu_custom_call" | custom-call | flops 8388608000 | bytes 8388608 | tf_op jit(solution)/shard_map/attend_back/pallas_call | solution.py:481
  336.9 9.5 %collective-permute-start.18 = (bf16[1,1280,256]{2,1,0:T(8,128)(2,1)}, bf16[1,1280,256]{2,1,0:T(8,128)(2,1)S(1)}, u32[]{:S(2)}, u32[]{:S(2)}) collective-permute-start(bf16[1,1280,256]{2,1,0:T(8,128)(2,1)} %constant_dynamic-slice_fusion.9), channel_id=1, source_target_pairs={{0,16},{8,24},{16,0},{24,8},{1,17},{9,25},{17,1},{25,9},{2,18},{10... | collective-permute-start | bytes 1966088 | tf_op jit(solution)/shard_map/ppermute | solution.py:553
  346.4 16.3 %collective-permute-done.18 = bf16[1,1280,256]{2,1,0:T(8,128)(2,1)S(1)} collective-permute-done((bf16[1,1280,256]{2,1,0:T(8,128)(2,1)}, bf16[1,1280,256]{2,1,0:T(8,128)(2,1)S(1)}, u32[]{:S(2)}, u32[]{:S(2)}) %collective-permute-start.18) | collective-permute-done | bytes 655392 | tf_op jit(solution)/shard_map/ppermute | solution.py:553
  365.5 15.1 %collective-permute-done.19 = bf16[1280,256]{1,0:T(8,128)(2,1)S(1)} collective-permute-done((bf16[1280,256]{1,0:T(8,128)(2,1)S(1)}, bf16[1280,256]{1,0:T(8,128)(2,1)S(1)}, u32[]{:S(2)}, u32[]{:S(2)}) %collective-permute-start.19) | collective-permute-done | bytes 655392 | tf_op jit(solution)/shard_map/ppermute | solution.py:581
  408.9 11.6 %collective-permute-done.6 = bf16[160,2048]{1,0:T(8,128)(2,1)} collective-permute-done((bf16[160,2048]{1,0:T(8,128)(2,1)S(1)}, bf16[160,2048]{1,0:T(8,128)(2,1)}, u32[]{:S(2)}, u32[]{:S(2)}) %collective-permute-start.6) | collective-permute-done | bytes 655392 | tf_op jit(solution)/shard_map/ppermute | solution.py:519
  427.6 13.4 %convolution_convert_fusion = bf16[2048,1536]{1,0:T(8,128)(2,1)} fusion(bf16[1280,2048]{1,0:T(8,128)(2,1)} %get-tuple-element.33, bf16[1280,1536]{1,0:T(8,128)(2,1)S(1)} %copy-done.26), kind=kOutput, calls=%fused_computation.2 | convolution fusion | flops 8056209408 | bytes 15466496 | tf_op jit(solution)/shard_map/dot_general | solution.py:589
  452.9 8.6 %collective-permute-done.4 = bf16[160,2048]{1,0:T(8,128)(2,1)S(1)} collective-permute-done((bf16[160,2048]{1,0:T(8,128)(2,1)S(1)}, bf16[160,2048]{1,0:T(8,128)(2,1)S(1)}, u32[]{:S(2)}, u32[]{:S(2)}) %collective-permute-start.4) | collective-permute-done | bytes 655392 | tf_op jit(solution)/shard_map/ppermute | solution.py:518
  472.4 13.2 %collective-permute-done.9 = bf16[160,2048]{1,0:T(8,128)(2,1)S(1)} collective-permute-done((bf16[160,2048]{1,0:T(8,128)(2,1)S(1)}, bf16[160,2048]{1,0:T(8,128)(2,1)S(1)}, u32[]{:S(2)}, u32[]{:S(2)}) %collective-permute-start.9) | collective-permute-done | bytes 655392 | tf_op jit(solution)/shard_map/ppermute | solution.py:539
  487.5 13.6 %collective-permute-done.25 = bf16[160,2048]{1,0:T(8,128)(2,1)S(1)} collective-permute-done((bf16[160,2048]{1,0:T(8,128)(2,1)S(1)}, bf16[160,2048]{1,0:T(8,128)(2,1)S(1)}, u32[]{:S(2)}, u32[]{:S(2)}) %collective-permute-start.25) | collective-permute-done | bytes 655392 | tf_op jit(solution)/shard_map/ppermute | solution.py:519
  504.8 7.9 %convert_element_type.278 = f32[1280,2048]{1,0:T(8,128)} convert(bf16[1280,2048]{1,0:T(8,128)(2,1)} %x_hbm.1) | non-fusion elementwise | flops 2621440 | bytes 15728640 | tf_op jit(solution)/shard_map/convert_element_type | solution.py:650
  515.7 12.0 %collective-permute-done.22 = bf16[160,2048]{1,0:T(8,128)(2,1)} collective-permute-done((bf16[160,2048]{1,0:T(8,128)(2,1)}, bf16[160,2048]{1,0:T(8,128)(2,1)}, u32[]{:S(2)}, u32[]{:S(2)}) %collective-permute-start.22) | collective-permute-done | bytes 655392 | tf_op jit(solution)/shard_map/ppermute | solution.py:518
  545.5 7.3 %collective-permute-done.23 = bf16[160,2048]{1,0:T(8,128)(2,1)S(1)} collective-permute-done((bf16[160,2048]{1,0:T(8,128)(2,1)S(1)}, bf16[160,2048]{1,0:T(8,128)(2,1)S(1)}, u32[]{:S(2)}, u32[]{:S(2)}) %collective-permute-start.23) | collective-permute-done | bytes 655392 | tf_op jit(solution)/shard_map/ppermute | solution.py:518
  572.8 12.5 %collective-permute-done.39 = f32[2,512]{1,0:T(2,128)S(1)} collective-permute-done((f32[2,512]{1,0:T(2,128)S(1)}, f32[2,512]{1,0:T(2,128)S(1)}, u32[]{:S(2)}, u32[]{:S(2)}) %collective-permute-start.39) | collective-permute-done | bytes 4128 | tf_op jit(solution)/shard_map/ppermute | solution.py:553
  597.9 7.5 %collective-permute-done.30 = bf16[160,2048]{1,0:T(8,128)(2,1)S(1)} collective-permute-done((bf16[160,2048]{1,0:T(8,128)(2,1)S(1)}, bf16[160,2048]{1,0:T(8,128)(2,1)S(1)}, u32[]{:S(2)}, u32[]{:S(2)}) %collective-permute-start.30) | collective-permute-done | bytes 655392 | tf_op jit(solution)/shard_map/ppermute | solution.py:539
  (290 shorter events, 225.7 us)
Async XLA Ops:
  7.2 34.2 %all-gather.8.cloned.1.call-start = ((), (), s32[]{:S(2)}) async-start(), calls=%async_computation.5 | async-start | bytes 2621440 | tf_op jit(solution)/shard_map/all_gather | solution.py:640
  17.2 63.6 %all-gather.10.cloned.1.call-start = ((), (), s32[]{:S(2)}) async-start(), calls=%async_computation.6 | async-start | bytes 3276800 | tf_op jit(solution)/shard_map/all_gather | solution.py:657
  49.9 72.0 %all-gather.14.cloned.1.call-start = ((), (), s32[]{:S(2)}) async-start(), calls=%async_computation.8 | async-start | bytes 3932160 | tf_op jit(solution)/shard_map/all_gather | solution.py:646
  50.7 85.1 %all-gather.16.cloned.1.call-start = ((), (), s32[]{:S(2)}) async-start(), calls=%async_computation.9 | async-start | bytes 3932160 | tf_op jit(solution)/shard_map/all_gather | solution.py:647
  51.2 114.5 %all-gather.18.cloned.1.call-start = ((), (), s32[]{:S(2)}) async-start(), calls=%async_computation.10 | async-start | bytes 3932160 | tf_op jit(solution)/shard_map/all_gather | solution.py:648
  51.8 149.9 %all-gather.12.cloned.1.call-start = ((), (), s32[]{:S(2)}) async-start(), calls=%async_computation.7 | async-start | bytes 5242880 | tf_op jit(solution)/shard_map/all_gather | solution.py:645
  302.1 292.2 %reduce-scatter.11.cloned.1.call-start = ((), (), s32[]{:S(2)}) async-start(), calls=%async_computation.14 | async-start | bytes 3932160 | tf_op jit(solution)/shard_map/reduce_scatter | solution.py:755
  311.3 285.5 %reduce-scatter.5.cloned.1.call-start = ((), (), s32[]{:S(2)}) async-start(), calls=%async_computation.11 | async-start | bytes 1966080 | tf_op jit(solution)/shard_map/reduce_scatter | solution.py:757
  336.9 25.7 %collective-permute-start.18 = (bf16[1,1280,256]{2,1,0:T(8,128)(2,1)}, bf16[1,1280,256]{2,1,0:T(8,128)(2,1)S(1)}, u32[]{:S(2)}, u32[]{:S(2)}) collective-permute-start(bf16[1,1280,256]{2,1,0:T(8,128)(2,1)} %constant_dynamic-slice_fusion.9), channel_id=1, source_target_pairs={{0,16},{8,24},{16,0},{24,8},{1,17},{9,25},{17,1},{25,9},{2,18},{10... | collective-permute-start | bytes 1966088 | tf_op jit(solution)/shard_map/ppermute | solution.py:553
  388.7 222.9 %reduce-scatter.7.cloned.1.call-start = ((), (), s32[]{:S(2)}) async-start(), calls=%async_computation.12 | async-start | bytes 5242880 | tf_op jit(solution)/shard_map/reduce_scatter | solution.py:702
  393.1 252.8 %reduce-scatter.9.cloned.1.call-start = ((), (), s32[]{:S(2)}) async-start(), calls=%async_computation.13 | async-start | bytes 7864320 | tf_op jit(solution)/shard_map/reduce_scatter | solution.py:753
  470.2 31.0 %collective-permute-start.25 = (bf16[160,2048]{1,0:T(8,128)(2,1)S(1)}, bf16[160,2048]{1,0:T(8,128)(2,1)S(1)}, u32[]{:S(2)}, u32[]{:S(2)}) collective-permute-start(bf16[160,2048]{1,0:T(8,128)(2,1)S(1)} %pad_maximum_fusion.4), channel_id=1, source_target_pairs={{0,1},{2,0},{4,2},{6,4},{7,6},{5,7},{3,5},{1,3},{8,9},{10,8},{12,1... | collective-permute-start | bytes 1966088 | tf_op jit(solution)/shard_map/ppermute | solution.py:519
  471.0 30.1 %collective-permute-start.21 = (bf16[160,2048]{1,0:T(8,128)(2,1)S(1)}, bf16[160,2048]{1,0:T(8,128)(2,1)S(1)}, u32[]{:S(2)}, u32[]{:S(2)}) collective-permute-start(bf16[160,2048]{1,0:T(8,128)(2,1)S(1)} %pad_maximum_fusion.3), channel_id=1, source_target_pairs={{0,2},{2,4},{4,6},{6,7},{7,5},{5,3},{3,1},{1,0},{8,10},{10,12},{12... | collective-permute-start | bytes 1966088 | tf_op jit(solution)/shard_map/ppermute | solution.py:518
  485.5 28.2 %collective-permute-start.11 = (bf16[160,2048]{1,0:T(8,128)(2,1)S(1)}, bf16[160,2048]{1,0:T(8,128)(2,1)}, u32[]{:S(2)}, u32[]{:S(2)}) collective-permute-start(bf16[160,2048]{1,0:T(8,128)(2,1)S(1)} %collective-permute-done.9), channel_id=1, source_target_pairs={{0,2},{2,4},{4,6},{6,7},{7,5},{5,3},{3,1},{1,0},{8,10},{10,12},{12... | collective-permute-start | bytes 1966088 | tf_op jit(solution)/shard_map/ppermute | solution.py:539
  487.1 28.2 %collective-permute-start.12 = (bf16[160,2048]{1,0:T(8,128)(2,1)S(1)}, bf16[160,2048]{1,0:T(8,128)(2,1)}, u32[]{:S(2)}, u32[]{:S(2)}) collective-permute-start(bf16[160,2048]{1,0:T(8,128)(2,1)S(1)} %collective-permute-done.10), channel_id=1, source_target_pairs={{0,1},{2,0},{4,2},{6,4},{7,6},{5,7},{3,5},{1,3},{8,9},{10,8},{12,1... | collective-permute-start | bytes 1966088 | tf_op jit(solution)/shard_map/ppermute | solution.py:540
  502.7 25.1 %collective-permute-start.22 = (bf16[160,2048]{1,0:T(8,128)(2,1)}, bf16[160,2048]{1,0:T(8,128)(2,1)}, u32[]{:S(2)}, u32[]{:S(2)}) collective-permute-start(bf16[160,2048]{1,0:T(8,128)(2,1)} %get-tuple-element.94), channel_id=1, source_target_pairs={{0,2},{2,4},{4,6},{6,7},{7,5},{5,3},{3,1},{1,0},{8,10},{10,12},{12... | collective-permute-start | bytes 1966088 | tf_op jit(solution)/shard_map/ppermute | solution.py:518
  504.2 25.2 %collective-permute-start.26 = (bf16[160,2048]{1,0:T(8,128)(2,1)}, bf16[160,2048]{1,0:T(8,128)(2,1)}, u32[]{:S(2)}, u32[]{:S(2)}) collective-permute-start(bf16[160,2048]{1,0:T(8,128)(2,1)} %get-tuple-element.95), channel_id=1, source_target_pairs={{0,1},{2,0},{4,2},{6,4},{7,6},{5,7},{3,5},{1,3},{8,9},{10,8},{12,1... | collective-permute-start | bytes 1966088 | tf_op jit(solution)/shard_map/ppermute | solution.py:519
  513.7 28.0 %collective-permute-start.13 = (bf16[160,2048]{1,0:T(8,128)(2,1)}, bf16[160,2048]{1,0:T(8,128)(2,1)S(1)}, u32[]{:S(2)}, u32[]{:S(2)}) collective-permute-start(bf16[160,2048]{1,0:T(8,128)(2,1)} %collective-permute-done.11), channel_id=1, source_target_pairs={{0,2},{2,4},{4,6},{6,7},{7,5},{5,3},{3,1},{1,0},{8,10},{10,12},{12... | collective-permute-start | bytes 1966088 | tf_op jit(solution)/shard_map/ppermute | solution.py:539
  515.3 28.8 %collective-permute-start.14 = (bf16[160,2048]{1,0:T(8,128)(2,1)}, bf16[160,2048]{1,0:T(8,128)(2,1)S(1)}, u32[]{:S(2)}, u32[]{:S(2)}) collective-permute-start(bf16[160,2048]{1,0:T(8,128)(2,1)} %collective-permute-done.12), channel_id=1, source_target_pairs={{0,1},{2,0},{4,2},{6,4},{7,6},{5,7},{3,5},{1,3},{8,9},{10,8},{12,1... | collective-permute-start | bytes 1966088 | tf_op jit(solution)/shard_map/ppermute | solution.py:540
  531.5 21.3 %collective-permute-start.23 = (bf16[160,2048]{1,0:T(8,128)(2,1)S(1)}, bf16[160,2048]{1,0:T(8,128)(2,1)S(1)}, u32[]{:S(2)}, u32[]{:S(2)}) collective-permute-start(bf16[160,2048]{1,0:T(8,128)(2,1)S(1)} %get-tuple-element.92), channel_id=1, source_target_pairs={{0,2},{2,4},{4,6},{6,7},{7,5},{5,3},{3,1},{1,0},{8,10},{10,12},{12... | collective-permute-start | bytes 1966088 | tf_op jit(solution)/shard_map/ppermute | solution.py:518
  542.5 45.3 %collective-permute-start.15 = (bf16[160,1024]{1,0:T(8,128)(2,1)}, bf16[160,1024]{1,0:T(8,128)(2,1)}, u32[]{:S(2)}, u32[]{:S(2)}) collective-permute-start(bf16[160,1024]{1,0:T(8,128)(2,1)} %slice.261), channel_id=1, source_target_pairs={{0,2},{2,4},{4,6},{6,7},{7,5},{5,3},{3,1},{1,0},{8,10},{10,12},{12... | collective-permute-start | bytes 983048 | tf_op jit(solution)/shard_map/ppermute | solution.py:542
  544.9 42.9 %collective-permute-start.16 = (bf16[160,1024]{1,0:T(8,128)(2,1)}, bf16[160,1024]{1,0:T(8,128)(2,1)}, u32[]{:S(2)}, u32[]{:S(2)}) collective-permute-start(bf16[160,1024]{1,0:T(8,128)(2,1)} %slice.262), channel_id=1, source_target_pairs={{0,1},{2,0},{4,2},{6,4},{7,6},{5,7},{3,5},{1,3},{8,9},{10,8},{12,1... | collective-permute-start | bytes 983048 | tf_op jit(solution)/shard_map/ppermute | solution.py:543
  568.4 22.1 %collective-permute-start.28 = (bf16[160,2048]{1,0:T(8,128)(2,1)S(1)}, bf16[160,2048]{1,0:T(8,128)(2,1)S(1)}, u32[]{:S(2)}, u32[]{:S(2)}) collective-permute-start(bf16[160,2048]{1,0:T(8,128)(2,1)S(1)} %get-tuple-element.89), channel_id=1, source_target_pairs={{0,2},{2,4},{4,6},{6,7},{7,5},{5,3},{3,1},{1,0},{8,10},{10,12},{12... | collective-permute-start | bytes 1966088 | tf_op jit(solution)/shard_map/ppermute | solution.py:539
  569.9 20.9 %collective-permute-start.29 = (bf16[160,2048]{1,0:T(8,128)(2,1)S(1)}, bf16[160,2048]{1,0:T(8,128)(2,1)S(1)}, u32[]{:S(2)}, u32[]{:S(2)}) collective-permute-start(bf16[160,2048]{1,0:T(8,128)(2,1)S(1)} %get-tuple-element.89), channel_id=1, source_target_pairs={{0,1},{2,0},{4,2},{6,4},{7,6},{5,7},{3,5},{1,3},{8,9},{10,8},{12,1... | collective-permute-start | bytes 1966088 | tf_op jit(solution)/shard_map/ppermute | solution.py:540
  (63 other events, 781.9 us)
Sparse Core Ops, SparseCore 0:
  17.3 24.0 all-gather.7
  50.0 25.5 all-gather.9
  77.2 28.5 all-gather.13
  107.2 28.5 all-gather.15
  137.2 28.5 all-gather.17
  167.2 34.4 all-gather.11
  311.4 39.4 reduce-scatter.10
  388.8 28.1 reduce-scatter.4
  419.5 44.4 reduce-scatter.6
  466.6 58.3 reduce-scatter.8

commit v6 on v5

--- a/solution.py
+++ b/solution.py
@@ -64,49 +64,81 @@
     return (slice(None), pl.ds(flow * (extent[1] // 2), extent[1] // 2))
 
 
-def place_of(whole, own, chunk):
-    if len(whole.shape) == 3:
+def place_of(whole, own, chunk, form):
+    rows, wide = own.shape[-2:]
+    if form == "lead":
         return whole.at[chunk]
-    wide = own.shape[1]
+    if form == "rows":
+        return whole.at[pl.ds(pl.multiple_of(chunk * rows, rows), rows)]
     return whole.at[:, pl.ds(pl.multiple_of(chunk * wide, wide), wide)]
 
 
-def spread_kernel(count, arrays, *refs):
+def spread_kernel(count, batches, plans, *refs):
     steps = count // 2
+    arrays = len(plans)
     own_refs, all_refs = refs[:arrays], refs[arrays : 2 * arrays]
     send_sem, recv_sem, local_sem = refs[2 * arrays :]
     place, right, left = ring_setup(count)
-    greet((right, left))
+    head = lax.axis_index("head")
+    batch = lax.axis_index("batch")
+    across, core = batch // 2, lax.rem(batch, 2)
+    others = batches // 2
+    twin = (across * 2 + 1 - core, head)
+    peers = [(lax.rem(across + hop, others) * 2 + core, head) for hop in range(1, others)]
+    ring = any(axis == "head" for axis, _ in plans)
+    grid = any(axis == "batch" for axis, _ in plans)
+    greet((right, left) * ring + (twin, *peers) * grid)
     sems = (send_sem, recv_sem)
-    local = []
-    for index in range(arrays):
-        copy = pltpu.make_async_copy(
-            own_refs[index], place_of(all_refs[index], own_refs[index], place), local_sem.at[index]
-        )
+    slot = 0
+    waiting, arriving, local = [], [], []
+
+    def go(source, target, device):
+        nonlocal slot
+        copy = send(source, target, sems, slot, device)
+        slot += 1
+        waiting.append(copy)
+        return copy
+
+    onward = []
+    for index, (axis, form) in enumerate(plans):
+        own, whole = own_refs[index], all_refs[index]
+        spot = place if axis == "head" else batch
+        mine = place_of(whole, own, spot, form)
+        copy = pltpu.make_async_copy(own, mine, local_sem.at[index])
         copy.start()
         local.append(copy)
-    waiting = []
+        if axis == "batch":
+            for hop, peer in enumerate(peers, 1):
+                source = lax.rem(across + others - hop, others) * 2 + core
+                onward.append((go(own, mine, peer), place_of(whole, own, source, form)))
+            arriving.append(go(own, mine, twin))
     copies = [None] * (2 * arrays)
     for step in range(steps):
-        for index in range(arrays):
-            extent = own_refs[index].shape
-            for flow, chunk, device in (
-                (0, place - step, right),
-                (1, place + step, left),
-            ):
+        for index, (axis, form) in enumerate(plans):
+            if axis != "head":
+                continue
+            own = own_refs[index]
+            for flow, chunk, device in ((0, place - step, right), (1, place + step, left)):
                 at = 2 * index + flow
                 if step:
                     copies[at].wait_recv()
                 chunk = lax.rem(chunk + count, count)
-                target = place_of(all_refs[index], own_refs[index], chunk)
-                source = target if step else own_refs[index]
+                target = place_of(all_refs[index], own, chunk, form)
+                source = target if step else own
                 if step == steps - 1:
-                    part = half_of(extent, flow)
+                    part = half_of(own.shape, flow)
                     source = source.at[part]
                     target = target.at[part]
-                copies[at] = send(source, target, sems, at * steps + step, device)
-                waiting.append(copies[at])
+                copies[at] = go(source, target, device)
+        if step == 0 or not ring:
+            for copy, block in onward:
+                copy.wait_recv()
+                arriving.append(go(block, block, twin))
+            onward = []
     for copy in copies:
+        if copy is not None:
+            arriving.append(copy)
+    for copy in arriving:
         copy.wait_recv()
     for copy in waiting:
         copy.wait_send()
@@ -114,15 +146,26 @@
         copy.wait()
 
 
-def spread(arrays, collective_id, columns=False, space=pl.ANY):
+def spread(arrays, plans, collective_id):
     count = lax.axis_size("head")
-    shapes = [(a.shape[0], count * a.shape[1]) if columns else (count, *a.shape) for a in arrays]
-    slots = len(arrays) * count
+    batches = lax.axis_size("batch")
+    shapes = []
+    slots = 0
+    for array, (axis, form) in zip(arrays, plans):
+        many = count if axis == "head" else batches
+        slots += count if axis == "head" else batches - 1
+        if form == "lead":
+            shapes.append((many, *array.shape))
+        elif form == "rows":
+            shapes.append((many * array.shape[0], array.shape[1]))
+        else:
+            shapes.append((array.shape[0], many * array.shape[1]))
+    hbm = pl.BlockSpec(memory_space=pl.ANY)
     return pl.pallas_call(
-        functools.partial(spread_kernel, count, len(arrays)),
+        functools.partial(spread_kernel, count, batches, plans),
         out_shape=[jax.ShapeDtypeStruct(shape, a.dtype) for shape, a in zip(shapes, arrays)],
-        in_specs=[pl.BlockSpec(memory_space=space)] * len(arrays),
-        out_specs=[pl.BlockSpec(memory_space=space)] * len(arrays),
+        in_specs=[hbm] * len(arrays),
+        out_specs=[hbm] * len(arrays),
         scratch_shapes=[
             pltpu.SemaphoreType.DMA((slots,)),
             pltpu.SemaphoreType.DMA((slots,)),
@@ -501,7 +544,7 @@
     return (one.astype(F32) + other.astype(F32)).astype(BF)
 
 
-def flow_sum(part):
+def flow_steps(part):
     count = lax.axis_size("head")
     place = ring_place(lax.axis_index("head"), count)
     right, left = ring_routes(count)
@@ -512,20 +555,33 @@
         return lax.dynamic_slice_in_dim(part, lax.rem(owner + count, count) * rows, rows, 0)
 
     far = mine(place + steps)
-    for step in range(steps):
-        if step == 0:
-            going, coming = far[:, :side], far[:, side:]
+    going, coming = far[:, :side], far[:, side:]
+    for step in range(steps - 1):
         from_left = lax.ppermute(going, "head", right)
         from_right = lax.ppermute(coming, "head", left)
-        if step == steps - 1:
-            break
         one, two = mine(place + steps - 1 - step), mine(place - steps + 1 + step)
         if step == 0:
             going = jnp.concatenate([add_low(from_left, one[:, :side]), one[:, side:]], 1)
             coming = jnp.concatenate([two[:, :side], add_low(from_right, two[:, side:])], 1)
         else:
             going, coming = add_low(from_left, one), add_low(from_right, two)
-    return mine(place).astype(F32) + from_left.astype(F32) + from_right.astype(F32)
+        going, coming = yield going, coming
+    from_left = lax.ppermute(going, "head", right)
+    from_right = lax.ppermute(coming, "head", left)
+    yield mine(place).astype(F32) + from_left.astype(F32) + from_right.astype(F32)
+
+
+def flow_sum(part):
+    flow = flow_steps(part)
+    state = next(flow)
+    while isinstance(state, tuple):
+        state = flow.send(state)
+    return state
+
+
+def after(flow, state, array):
+    array, going, coming = lax.optimization_barrier((array, *state))
+    return array, flow.send((going, coming))
 
 
 def flow_spread(own):
@@ -641,8 +697,6 @@
     gains = lax.all_gather(jnp.stack([norm1_gain, norm2_gain]), "batch", axis=1, tiled=True)
     gain_one = gains[0].astype(F32)
     gain_two = gains[1].astype(F32)
-    (out_rows,) = spread([w_out], 1)
-    out_full = lax.all_gather(out_rows.reshape(heads * head_size, -1), "batch", axis=1, tiled=True)
     mgate_full = lax.all_gather(w_mlp_gate, "batch", axis=0, tiled=True)
     mup_full = lax.all_gather(w_mlp_up, "batch", axis=0, tiled=True)
     down_full = lax.all_gather(w_down, "batch", axis=1, tiled=True)
@@ -654,8 +708,12 @@
     queries = projected[:, :head_size].astype(BF)
     kv_local = projected[:, head_size : 3 * head_size].astype(BF)
     gate_logit = projected[:, 3 * head_size :]
-    kv_all = lax.all_gather(kv_local, "batch", axis=0, tiled=True)
-    seg_all = lax.all_gather(segment_ids, "batch", axis=0, tiled=True)
+    out_rows, kv_all, seg_all = spread(
+        [w_out, kv_local, segment_ids.reshape(-1, 128)],
+        (("head", "rows"), ("batch", "rows"), ("batch", "lead")),
+        1,
+    )
+    seg_all = seg_all.reshape(-1)
     base = lax.axis_index("batch") * row_count
     ids = jnp.arange(DOCUMENTS, dtype=jnp.int32)
     below = jnp.sum((seg_all[None, :] < ids[:, None]).astype(jnp.int32), axis=1)
@@ -675,14 +733,15 @@
         pair_flops,
         "attend",
     )
-    (mixed_all,) = spread([mixed], 2, columns=True)
+    mixed_all, out_full = spread([mixed, out_rows], (("head", "cols"), ("batch", "cols")), 2)
     normed_two, hidden, d_pre, mlp_part, dn2, resid_own = mlp_back(
         tokens, mixed_all, out_grad, gain_two[None], out_full, mgate_full, mup_full, down_full, 3
     )
     recip_own = rms_scale(resid_own)
     mixed_own = lax.dynamic_slice_in_dim(mixed_all, me * chunk, chunk, 0)
     dy_own = lax.dynamic_slice_in_dim(out_grad, me * chunk, chunk, 0).astype(F32)
-    output = flow_spread((resid_own + flow_sum(mlp_part)).astype(BF))
+    out_flow = flow_steps(mlp_part)
+    out_state = next(out_flow)
 
     d_gain_two = jnp.sum(dn2 * resid_own * recip_own, axis=0)
     weighted_two = gain_two * dn2
@@ -702,6 +761,7 @@
     d_out_part = lax.psum_scatter(d_out_part, "batch", scatter_dimension=1, tiled=True)
     d_out = flow_sum(d_out_part)
 
+    d_mixed, out_state = after(out_flow, out_state, d_mixed)
     d_queries, d_gate_logit, d_kv_all = local_call(
         functools.partial(attend_back_kernel, scale_factor),
         scalars,
@@ -715,7 +775,12 @@
         5 * pair_flops // 2,
         "attend_back",
     )
+    d_kv_all, out_state = after(out_flow, out_state, d_kv_all)
     d_kv_own = halve_batch(d_kv_all, row_count)
+    d_kv_own, out_state = after(out_flow, out_state, d_kv_own)
+    while isinstance(out_state, tuple):
+        out_state = out_flow.send(out_state)
+    output = flow_spread((resid_own + out_state).astype(BF))
     d_kv_mate = from_partner(d_kv_own, "head")
     d_kv = (d_kv_own.astype(F32) + d_kv_mate.astype(F32)).astype(BF)
     d_cat = jnp.concatenate(

time: 662 us -> 615 us (0.929)
  waiting for transfers between devices: 258 us -> 155 us
  Pallas kernels: 156 us -> 219 us
  starting transfers between devices: 69.1 us -> 60.1 us
    pallas_call x2, Pallas kernels: 52.1 us -> 124 us  [spread(): pl.pallas_call(functools.partial(spread_kernel, count, batches, plans), o...]
    all_gather x2 -> x0, waiting for transfers between devices: 35.9 us -> none  [the longest x1 35.9 us: per_device(): lax.all_gather(out_rows.reshape(heads * head_size, -1), 'batch', axis=1,...]
    all_gather x1, waiting for transfers between devices: 30 us -> 0.02 us  [per_device(): down_full = lax.all_gather(w_down, 'batch', axis=1, tiled=True)]
    ppermute x7, waiting for transfers between devices: 35.5 us -> 21.5 us  [swap(): lax.ppermute(block, axis, [(at, at ^ stride) for at in range(lax.axis_siz...]
    all_gather x1, waiting for transfers between devices: 13.9 us -> 0.02 us  [per_device(): mup_full = lax.all_gather(w_mlp_up, 'batch', axis=0, tiled=True)]
    ppermute x24, waiting for transfers between devices: 77.9 us -> 68.3 us  [the longest x12 34.9 us: flow_steps(): from_left = lax.ppermute(going, 'head', right)]
    ppermute x7, starting transfers between devices: 18.5 us -> 9.23 us  [swap(): lax.ppermute(block, axis, [(at, at ^ stride) for at in range(lax.axis_siz...]
    unnamed x76 -> x81, local copies, waits for them, and re-layouts: 11.5 us -> 18.6 us
  transfers between devices with their start and end apart: 60 -> 58, of which waited for: 32 -> 27; matrix products, arithmetic and copies ran while one was open for 18% -> 22% of each run, Pallas kernels for 11% -> 23%
where the time goes in v6:
time: 615 us; the launch traced here: 608 us
  Pallas kernels  219 us (36%)
  waiting for transfers between devices  155 us (25%)
  starting transfers between devices  60.1 us (10%)
  local copies, waits for them, and re-layouts  56.2 us (9%)
  other arithmetic  52.4 us (9%)
  matrix products  44.3 us (7%)
  between operations  15.4 us (3%)
    pallas_call x2, Pallas kernels, spread(): pl.pallas_call(functools.partial(spread_kernel, count, batches, plans), o...  124 us
    pallas_call x1, Pallas kernels, mlp_back(): pl.pallas_call(functools.partial(mlp_kernel, count), out_shape=[jax.Shape...  77.6 us
    ppermute x12, waiting for transfers between devices, flow_steps(): from_left = lax.ppermute(going, 'head', right)  34.9 us
    dot_general x4, matrix products, rows_inner(): lax.dot_general(left, right, (((0,), (0,)), ((), ())), preferred_element_...  33.6 us
    ppermute x12, waiting for transfers between devices, flow_steps(): from_right = lax.ppermute(coming, 'head', left)  33.4 us
    ppermute x6, waiting for transfers between devices, flow_spread(): going = lax.ppermute(going, 'head', right)  33.2 us
    ppermute x7, waiting for transfers between devices, swap(): lax.ppermute(block, axis, [(at, at ^ stride) for at in range(lax.axis_siz...  21.5 us
    unnamed x81, local copies, waits for them, and re-layouts  18.6 us
  transfers between devices with their start and end apart: 58, of which 27 were waited for; matrix products, arithmetic and copies ran while one was open for 22% of the time, Pallas kernels for 23%

profile of v6, /device:TPU:0, one launch (start us, length us, event | category | flops | bytes accessed | tf_op | source)
XLA Modules:
  0.0 607.5 jit_solution(15576851884083469353)
XLA Ops:
  19.5 5.2 all_gather.15
  29.4 12.1 %all-gather.5.cloned.1.call-done = bf16[2048,512]{1,0:T(8,128)(2,1)} async-done(((bf16[512,512]{1,0:T(8,128)(2,1)}), bf16[2048,512]{1,0:T(8,128)(2,1)}) %all-gather.5.cloned.1.call-update) | async-done | bytes 2097168 | tf_op jit(solution)/shard_map/all_gather | solution.py:696
  41.4 5.7 fusion.42
  48.9 45.5 %spread_1.1 = (bf16[1024,512]{1,0:T(8,128)(2,1)}, bf16[5120,256]{1,0:T(8,128)(2,1)}, s32[4,10,128]{2,1,0:T(8,128)}) custom-call(bf16[128,512]{1,0:T(8,128)(2,1)} %refs_0_.1, bf16[1280,256]{1,0:T(8,128)(2,1)} %slice.257.refs_1_, s32[10,128]{1,0:T(8,128)} %bitcast.114), custom_call_target="tpu_custom_call" | custom-call | tf_op jit(solution)/shard_map/spread_1/pallas_call | solution.py:164
  96.9 7.6 %attend.1 = (f32[1280,128]{1,0:T(8,128)}, bf16[1280,128]{1,0:T(8,128)(2,1)}, f32[1,1280]{1,0:T(1,128)}) custom-call(s32[1280]{0:T(1024)} %copy-done.22, s32[1]{0:T(128)} %bitcast.2.base_sm, bf16[1280,128]{1,0:T(8,128)(2,1)} %slice.258.q_ref, bf16[5120,256]{1,0:T(8,128)(2,1)} %get-tuple-element.39.kv_ref, s32[1,1280]{1,0:T(1,128)} %broadcast_in_dim.16.start_ref, ...), custom_call_target="tpu_custom_call" | custom-call | flops 3355443200 | bytes 8388608 | tf_op jit(solution)/shard_map/attend/pallas_call | solution.py:524
  104.5 78.1 %spread_2.1 = (bf16[1280,1024]{1,0:T(8,128)(2,1)}, bf16[1024,2048]{1,0:T(8,128)(2,1)}) custom-call(bf16[1280,128]{1,0:T(8,128)(2,1)} %get-tuple-element.40.refs_0_, bf16[1024,512]{1,0:T(8,128)(2,1)} %get-tuple-element.41.refs_1_), custom_call_target="tpu_custom_call" | custom-call | tf_op jit(solution)/shard_map/spread_2/pallas_call | solution.py:164
  182.7 77.6 %mlp_back.1 = (bf16[1280,2048]{1,0:T(8,128)(2,1)}, bf16[1280,768]{1,0:T(8,128)(2,1)}, bf16[1280,1536]{1,0:T(8,128)(2,1)}, bf16[1280,2048]{1,0:T(8,128)(2,1)}, f32[160,2048]{1,0:T(8,128)}, /*index=5*/f32[160,2048]{1,0:T(8,128)}) custom-call(bf16[1280,2048]{1,0:T(8,128)(2,1)} %x_hbm.1, bf16[1280,1024]{1,0:T(8,128)(2,1)} %get-tuple-element.42.a_hbm, ...), custom_call_target="tpu_custom_call" | custom-call | flops 29527900160 | bytes 41943040 | tf_op jit(solution)/shard_map/mlp_back/pallas_call | solution.py:379
  281.9 9.0 %convolution_convert_fusion.3 = bf16[768,2048]{1,0:T(8,128)(2,1)} fusion(bf16[1280,768]{1,0:T(8,128)(2,1)} %get-tuple-element.63, bf16[1280,2048]{1,0:T(8,128)(2,1)} %dy_hbm.1), kind=kOutput, calls=%fused_computation.5 | convolution fusion | flops 4028104704 | bytes 10354688 | tf_op jit(solution)/shard_map/dot_general | solution.py:645
  302.7 9.9 %attend_back.1 = (bf16[1280,128]{1,0:T(8,128)(2,1)}, bf16[1280,128]{1,0:T(8,128)(2,1)}, bf16[5120,256]{1,0:T(8,128)(2,1)}) custom-call(s32[1280]{0:T(1024)} %copy-done.22, s32[1]{0:T(128)} %bitcast.2.base_sm, bf16[1280,128]{1,0:T(8,128)(2,1)} %slice.258.q_ref, bf16[5120,256]{1,0:T(8,128)(2,1)} %get-tuple-element.39.kv_ref, ...), custom_call_target="tpu_custom_call" | custom-call | flops 8388608000 | bytes 8388608 | tf_op jit(solution)/shard_map/attend_back/pallas_call | solution.py:524
  330.9 6.6 %collective-permute-done.7 = bf16[160,2048]{1,0:T(8,128)(2,1)} collective-permute-done((bf16[160,2048]{1,0:T(8,128)(2,1)}, bf16[160,2048]{1,0:T(8,128)(2,1)}, u32[]{:S(2)}, u32[]{:S(2)}) %collective-permute-start.7) | collective-permute-done | bytes 655392 | tf_op jit(solution)/shard_map/ppermute | solution.py:560
  348.1 14.6 %collective-permute-done.19 = bf16[1280,256]{1,0:T(8,128)(2,1)S(1)} collective-permute-done((bf16[1280,256]{1,0:T(8,128)(2,1)S(1)}, bf16[1280,256]{1,0:T(8,128)(2,1)S(1)}, u32[]{:S(2)}, u32[]{:S(2)}) %collective-permute-start.19) | collective-permute-done | bytes 655392 | tf_op jit(solution)/shard_map/ppermute | solution.py:637
  363.9 6.8 %convolution_convert_fusion.4 = bf16[2048,384]{1,0:T(8,128)(2,1)} fusion(f32[2048]{0:T(1024)S(1)} %bitcast.109, f32[1280]{0:T(1024)S(1)} %add_rsqrt_fusion, bf16[1280,2048]{1,0:T(8,128)(2,1)} %x_hbm.1, bf16[1280,128]{1,0:T(8,128)(2,1)S(1)} %copy-done.28, bf16[1280,64]{1,0:T(8,128)(2,1)S(1)} %get-tuple-element.145, ...), kind=kOutput, calls=%fused_computation.6 | convolution fusion | flops 2028470272 | bytes 7812096 | tf_op jit(solution)/shard_map/dot_general | solution.py:645
  370.8 4.3 convolution_convert_fusion.2
  375.2 13.4 %convolution_convert_fusion = bf16[2048,1536]{1,0:T(8,128)(2,1)} fusion(bf16[1280,2048]{1,0:T(8,128)(2,1)} %get-tuple-element.61, bf16[1280,1536]{1,0:T(8,128)(2,1)} %get-tuple-element.62), kind=kOutput, calls=%fused_computation.2 | convolution fusion | flops 8056209408 | bytes 15466496 | tf_op jit(solution)/shard_map/dot_general | solution.py:645
  398.9 9.8 %collective-permute-done.10 = bf16[160,2048]{1,0:T(8,128)(2,1)S(1)} collective-permute-done((bf16[160,2048]{1,0:T(8,128)(2,1)}, bf16[160,2048]{1,0:T(8,128)(2,1)S(1)}, u32[]{:S(2)}, u32[]{:S(2)}) %collective-permute-start.10) | collective-permute-done | bytes 655392 | tf_op jit(solution)/shard_map/ppermute | solution.py:570
  420.3 13.1 %collective-permute-done.11 = bf16[160,2048]{1,0:T(8,128)(2,1)S(1)} collective-permute-done((bf16[160,2048]{1,0:T(8,128)(2,1)S(1)}, bf16[160,2048]{1,0:T(8,128)(2,1)S(1)}, u32[]{:S(2)}, u32[]{:S(2)}) %collective-permute-start.11) | collective-permute-done | bytes 655392 | tf_op jit(solution)/shard_map/ppermute | solution.py:595
  435.5 12.9 %collective-permute-done.25 = bf16[160,2048]{1,0:T(8,128)(2,1)S(1)} collective-permute-done((bf16[160,2048]{1,0:T(8,128)(2,1)S(1)}, bf16[160,2048]{1,0:T(8,128)(2,1)S(1)}, u32[]{:S(2)}, u32[]{:S(2)}) %collective-permute-start.25) | collective-permute-done | bytes 655392 | tf_op jit(solution)/shard_map/ppermute | solution.py:561
  452.1 9.2 %convert_element_type.277 = f32[1280,2048]{1,0:T(8,128)} convert(bf16[1280,2048]{1,0:T(8,128)(2,1)} %x_hbm.1) | non-fusion elementwise | flops 2621440 | bytes 15728640 | tf_op jit(solution)/shard_map/convert_element_type | solution.py:704
  464.2 11.5 %collective-permute-done.22 = bf16[160,2048]{1,0:T(8,128)(2,1)} collective-permute-done((bf16[160,2048]{1,0:T(8,128)(2,1)}, bf16[160,2048]{1,0:T(8,128)(2,1)}, u32[]{:S(2)}, u32[]{:S(2)}) %collective-permute-start.22) | collective-permute-done | bytes 655392 | tf_op jit(solution)/shard_map/ppermute | solution.py:560
  493.2 9.2 %collective-permute-done.23 = bf16[160,2048]{1,0:T(8,128)(2,1)S(1)} collective-permute-done((bf16[160,2048]{1,0:T(8,128)(2,1)S(1)}, bf16[160,2048]{1,0:T(8,128)(2,1)S(1)}, u32[]{:S(2)}, u32[]{:S(2)}) %collective-permute-start.23) | collective-permute-done | bytes 655392 | tf_op jit(solution)/shard_map/ppermute | solution.py:569
  522.2 12.7 %collective-permute-done.39 = f32[2,512]{1,0:T(2,128)S(1)} collective-permute-done((f32[2,512]{1,0:T(2,128)S(1)}, f32[2,512]{1,0:T(2,128)S(1)}, u32[]{:S(2)}, u32[]{:S(2)}) %collective-permute-start.39) | collective-permute-done | bytes 4128 | tf_op jit(solution)/shard_map/ppermute | solution.py:609
  547.4 10.0 %collective-permute-done.30 = bf16[160,2048]{1,0:T(8,128)(2,1)S(1)} collective-permute-done((bf16[160,2048]{1,0:T(8,128)(2,1)S(1)}, bf16[160,2048]{1,0:T(8,128)(2,1)S(1)}, u32[]{:S(2)}, u32[]{:S(2)}) %collective-permute-start.30) | collective-permute-done | bytes 655392 | tf_op jit(solution)/shard_map/ppermute | solution.py:595
  567.7 6.0 collective-permute-done.32
  578.9 5.0 collective-permute-done.46
  (289 shorter events, 196.2 us)
Async XLA Ops:
  7.2 34.2 %all-gather.5.cloned.1.call-start = ((), (), s32[]{:S(2)}) async-start(), calls=%async_computation.5 | async-start | bytes 2621440 | tf_op jit(solution)/shard_map/all_gather | solution.py:696
  17.2 165.4 %all-gather.11.cloned.1.call-start = ((), (), s32[]{:S(2)}) async-start(), calls=%async_computation.8 | async-start | bytes 3932160 | tf_op jit(solution)/shard_map/all_gather | solution.py:702
  18.0 164.7 %all-gather.7.cloned.1.call-start = ((), (), s32[]{:S(2)}) async-start(), calls=%async_computation.6 | async-start | bytes 3932160 | tf_op jit(solution)/shard_map/all_gather | solution.py:700
  18.7 164.0 %all-gather.9.cloned.1.call-start = ((), (), s32[]{:S(2)}) async-start(), calls=%async_computation.7 | async-start | bytes 3932160 | tf_op jit(solution)/shard_map/all_gather | solution.py:701
  266.0 25.0 %collective-permute-start.1 = (bf16[160,1024]{1,0:T(8,128)(2,1)}, bf16[160,1024]{1,0:T(8,128)(2,1)}, u32[]{:S(2)}, u32[]{:S(2)}) collective-permute-start(bf16[160,1024]{1,0:T(8,128)(2,1)} %get-tuple-element.123), channel_id=1, source_target_pairs={{0,2},{2,4},{4,6},{6,7},{7,5},{5,3},{3,1},{1,0},{8,10},{10,12},{12... | collective-permute-start | bytes 983048 | tf_op jit(solution)/shard_map/ppermute | solution.py:560
  266.8 24.2 %collective-permute-start.2 = (bf16[160,1024]{1,0:T(8,128)(2,1)}, bf16[160,1024]{1,0:T(8,128)(2,1)}, u32[]{:S(2)}, u32[]{:S(2)}) collective-permute-start(bf16[160,1024]{1,0:T(8,128)(2,1)} %get-tuple-element.125), channel_id=1, source_target_pairs={{0,1},{2,0},{4,2},{6,4},{7,6},{5,7},{3,5},{1,3},{8,9},{10,8},{12,1... | collective-permute-start | bytes 983048 | tf_op jit(solution)/shard_map/ppermute | solution.py:561
  281.8 258.2 %reduce-scatter.11.cloned.1.call-start = ((), (), s32[]{:S(2)}) async-start(), calls=%async_computation.12 | async-start | bytes 3932160 | tf_op jit(solution)/shard_map/reduce_scatter | solution.py:820
  290.9 255.4 %reduce-scatter.5.cloned.1.call-start = ((), (), s32[]{:S(2)}) async-start(), calls=%async_computation.9 | async-start | bytes 1966080 | tf_op jit(solution)/shard_map/reduce_scatter | solution.py:822
  370.8 192.9 %reduce-scatter.7.cloned.1.call-start = ((), (), s32[]{:S(2)}) async-start(), calls=%async_computation.10 | async-start | bytes 5242880 | tf_op jit(solution)/shard_map/reduce_scatter | solution.py:761
  375.1 221.8 %reduce-scatter.9.cloned.1.call-start = ((), (), s32[]{:S(2)}) async-start(), calls=%async_computation.11 | async-start | bytes 7864320 | tf_op jit(solution)/shard_map/reduce_scatter | solution.py:818
  418.1 30.2 %collective-permute-start.25 = (bf16[160,2048]{1,0:T(8,128)(2,1)S(1)}, bf16[160,2048]{1,0:T(8,128)(2,1)S(1)}, u32[]{:S(2)}, u32[]{:S(2)}) collective-permute-start(bf16[160,2048]{1,0:T(8,128)(2,1)S(1)} %pad_maximum_fusion.4), channel_id=1, source_target_pairs={{0,1},{2,0},{4,2},{6,4},{7,6},{5,7},{3,5},{1,3},{8,9},{10,8},{12,1... | collective-permute-start | bytes 1966088 | tf_op jit(solution)/shard_map/ppermute | solution.py:561
  419.7 28.6 %collective-permute-start.21 = (bf16[160,2048]{1,0:T(8,128)(2,1)S(1)}, bf16[160,2048]{1,0:T(8,128)(2,1)S(1)}, u32[]{:S(2)}, u32[]{:S(2)}) collective-permute-start(bf16[160,2048]{1,0:T(8,128)(2,1)S(1)} %pad_maximum_fusion.3), channel_id=1, source_target_pairs={{0,2},{2,4},{4,6},{6,7},{7,5},{5,3},{3,1},{1,0},{8,10},{10,12},{12... | collective-permute-start | bytes 1966088 | tf_op jit(solution)/shard_map/ppermute | solution.py:560
  433.4 28.7 %collective-permute-start.13 = (bf16[160,2048]{1,0:T(8,128)(2,1)S(1)}, bf16[160,2048]{1,0:T(8,128)(2,1)}, u32[]{:S(2)}, u32[]{:S(2)}) collective-permute-start(bf16[160,2048]{1,0:T(8,128)(2,1)S(1)} %collective-permute-done.11), channel_id=1, source_target_pairs={{0,2},{2,4},{4,6},{6,7},{7,5},{5,3},{3,1},{1,0},{8,10},{10,12},{12... | collective-permute-start | bytes 1966088 | tf_op jit(solution)/shard_map/ppermute | solution.py:595
  434.3 29.4 %collective-permute-start.14 = (bf16[160,2048]{1,0:T(8,128)(2,1)S(1)}, bf16[160,2048]{1,0:T(8,128)(2,1)}, u32[]{:S(2)}, u32[]{:S(2)}) collective-permute-start(bf16[160,2048]{1,0:T(8,128)(2,1)S(1)} %collective-permute-done.12), channel_id=1, source_target_pairs={{0,1},{2,0},{4,2},{6,4},{7,6},{5,7},{3,5},{1,3},{8,9},{10,8},{12,1... | collective-permute-start | bytes 1966088 | tf_op jit(solution)/shard_map/ppermute | solution.py:596
  450.0 25.7 %collective-permute-start.22 = (bf16[160,2048]{1,0:T(8,128)(2,1)}, bf16[160,2048]{1,0:T(8,128)(2,1)}, u32[]{:S(2)}, u32[]{:S(2)}) collective-permute-start(bf16[160,2048]{1,0:T(8,128)(2,1)} %get-tuple-element.110), channel_id=1, source_target_pairs={{0,2},{2,4},{4,6},{6,7},{7,5},{5,3},{3,1},{1,0},{8,10},{10,12},{12... | collective-permute-start | bytes 1966088 | tf_op jit(solution)/shard_map/ppermute | solution.py:560
  451.5 25.1 %collective-permute-start.26 = (bf16[160,2048]{1,0:T(8,128)(2,1)}, bf16[160,2048]{1,0:T(8,128)(2,1)}, u32[]{:S(2)}, u32[]{:S(2)}) collective-permute-start(bf16[160,2048]{1,0:T(8,128)(2,1)} %get-tuple-element.111), channel_id=1, source_target_pairs={{0,1},{2,0},{4,2},{6,4},{7,6},{5,7},{3,5},{1,3},{8,9},{10,8},{12,1... | collective-permute-start | bytes 1966088 | tf_op jit(solution)/shard_map/ppermute | solution.py:561
  462.1 27.5 %collective-permute-start.15 = (bf16[160,2048]{1,0:T(8,128)(2,1)}, bf16[160,2048]{1,0:T(8,128)(2,1)S(1)}, u32[]{:S(2)}, u32[]{:S(2)}) collective-permute-start(bf16[160,2048]{1,0:T(8,128)(2,1)} %collective-permute-done.13), channel_id=1, source_target_pairs={{0,2},{2,4},{4,6},{6,7},{7,5},{5,3},{3,1},{1,0},{8,10},{10,12},{12... | collective-permute-start | bytes 1966088 | tf_op jit(solution)/shard_map/ppermute | solution.py:595
  463.7 27.6 %collective-permute-start.16 = (bf16[160,2048]{1,0:T(8,128)(2,1)}, bf16[160,2048]{1,0:T(8,128)(2,1)S(1)}, u32[]{:S(2)}, u32[]{:S(2)}) collective-permute-start(bf16[160,2048]{1,0:T(8,128)(2,1)} %collective-permute-done.14), channel_id=1, source_target_pairs={{0,1},{2,0},{4,2},{6,4},{7,6},{5,7},{3,5},{1,3},{8,9},{10,8},{12,1... | collective-permute-start | bytes 1966088 | tf_op jit(solution)/shard_map/ppermute | solution.py:596
  478.7 23.7 %collective-permute-start.23 = (bf16[160,2048]{1,0:T(8,128)(2,1)S(1)}, bf16[160,2048]{1,0:T(8,128)(2,1)S(1)}, u32[]{:S(2)}, u32[]{:S(2)}) collective-permute-start(bf16[160,2048]{1,0:T(8,128)(2,1)S(1)} %get-tuple-element.108), channel_id=1, source_target_pairs={{0,2},{2,4},{4,6},{6,7},{7,5},{5,3},{3,1},{1,0},{8,10},{10,12},{12... | collective-permute-start | bytes 1966088 | tf_op jit(solution)/shard_map/ppermute | solution.py:569
  480.3 22.1 %collective-permute-start.27 = (bf16[160,2048]{1,0:T(8,128)(2,1)S(1)}, bf16[160,2048]{1,0:T(8,128)(2,1)S(1)}, u32[]{:S(2)}, u32[]{:S(2)}) collective-permute-start(bf16[160,2048]{1,0:T(8,128)(2,1)S(1)} %get-tuple-element.109), channel_id=1, source_target_pairs={{0,1},{2,0},{4,2},{6,4},{7,6},{5,7},{3,5},{1,3},{8,9},{10,8},{12,1... | collective-permute-start | bytes 1966088 | tf_op jit(solution)/shard_map/ppermute | solution.py:570
  490.4 46.0 %collective-permute-start.17 = (bf16[160,1024]{1,0:T(8,128)(2,1)}, bf16[160,1024]{1,0:T(8,128)(2,1)}, u32[]{:S(2)}, u32[]{:S(2)}) collective-permute-start(bf16[160,1024]{1,0:T(8,128)(2,1)} %slice.277), channel_id=1, source_target_pairs={{0,2},{2,4},{4,6},{6,7},{7,5},{5,3},{3,1},{1,0},{8,10},{10,12},{12... | collective-permute-start | bytes 983048 | tf_op jit(solution)/shard_map/ppermute | solution.py:598
  492.0 44.4 %collective-permute-start.18 = (bf16[160,1024]{1,0:T(8,128)(2,1)}, bf16[160,1024]{1,0:T(8,128)(2,1)}, u32[]{:S(2)}, u32[]{:S(2)}) collective-permute-start(bf16[160,1024]{1,0:T(8,128)(2,1)} %slice.278), channel_id=1, source_target_pairs={{0,1},{2,0},{4,2},{6,4},{7,6},{5,7},{3,5},{1,3},{8,9},{10,8},{12,1... | collective-permute-start | bytes 983048 | tf_op jit(solution)/shard_map/ppermute | solution.py:599
  517.7 24.8 %collective-permute-start.28 = (bf16[160,2048]{1,0:T(8,128)(2,1)}, bf16[160,2048]{1,0:T(8,128)(2,1)S(1)}, u32[]{:S(2)}, u32[]{:S(2)}) collective-permute-start(bf16[160,2048]{1,0:T(8,128)(2,1)} %get-tuple-element.105), channel_id=1, source_target_pairs={{0,2},{2,4},{4,6},{6,7},{7,5},{5,3},{3,1},{1,0},{8,10},{10,12},{12... | collective-permute-start | bytes 1966088 | tf_op jit(solution)/shard_map/ppermute | solution.py:595
  519.2 23.6 %collective-permute-start.29 = (bf16[160,2048]{1,0:T(8,128)(2,1)}, bf16[160,2048]{1,0:T(8,128)(2,1)S(1)}, u32[]{:S(2)}, u32[]{:S(2)}) collective-permute-start(bf16[160,2048]{1,0:T(8,128)(2,1)} %get-tuple-element.105), channel_id=1, source_target_pairs={{0,1},{2,0},{4,2},{6,4},{7,6},{5,7},{3,5},{1,3},{8,9},{10,8},{12,1... | collective-permute-start | bytes 1966088 | tf_op jit(solution)/shard_map/ppermute | solution.py:596
  (64 other events, 792.3 us)
Sparse Core Ops, SparseCore 0:
  17.3 24.0 all-gather.4
  43.0 41.4 all-gather.10
  86.1 28.5 all-gather.6
  116.0 45.5 all-gather.8
  291.1 38.2 reduce-scatter.10
  370.9 29.1 reduce-scatter.4
  402.6 44.4 reduce-scatter.6
  449.8 58.3 reduce-scatter.8

commit v7 on v6

--- a/solution.py
+++ b/solution.py
@@ -180,10 +180,10 @@
 
 def mlp_kernel(
     count, x_hbm, a_hbm, dy_hbm, gain_ref, out_w, gate_w, up_w, down_w,
-    n2_hbm, hid_hbm, grad_hbm, mlp_hbm, dn2_ref, h1_ref,
-    x_s, a_s, dy_s, n2_s, hid_s, grad_s, mlp_s, h1_s,
+    n2_hbm, hid_hbm, grad_hbm, mlp_hbm, h1_ref, dh1_ref, low_ref, dgain_ref, da_ref,
+    x_s, a_s, dy_s, n2_s, hid_s, grad_s, mlp_s, h1_s, dy_own, da_part,
     right_part, left_part, right_got, left_got,
-    in_sem, out_sem, send_sem, recv_sem,
+    in_sem, out_sem, send_sem, recv_sem, da_send, da_recv,
 ):
     steps = count // 2
     rows = x_hbm.shape[0] // count
@@ -192,8 +192,14 @@
     side = width // 2
     tile = 256
     inner = 256 if hidden % 256 == 0 else 128
+    size = da_ref.shape[1]
     place, right, left = ring_setup(count)
-    greet((right, left))
+
+    def member(hop):
+        spot = lax.rem(place + hop, count)
+        return spot, (lax.axis_index("batch"), ring_head(spot, count))
+
+    greet([member(hop)[1] for hop in range(1, count)])
 
     def owners(group):
         first = jnp.where(group == 0, 1, 0)
@@ -284,6 +290,7 @@
         @pl.when(group == 0)
         def _():
             h1_ref[...] = h1_s[pl.ds(rows, rows)]
+            dy_own[...] = dy_s[slot, pl.ds(rows, rows)]
 
         @pl.loop(0, width // tile)
         def _(at):
@@ -350,9 +357,64 @@
 
     for copy in later_copies(steps - 1):
         copy.wait_recv()
-    dn2_ref[...] = (
-        left_part[0].astype(F32) + right_got[steps - 1].astype(F32) + left_got[steps - 1].astype(F32)
-    )
+
+    def tile_of(at):
+        return pl.ds(pl.multiple_of(at * tile, tile), tile)
+
+    def collect(at, state):
+        squares, mean = state
+        cols = tile_of(at)
+        dn2 = (
+            left_part[0, :, cols].astype(F32)
+            + right_got[steps - 1, :, cols].astype(F32)
+            + left_got[steps - 1, :, cols].astype(F32)
+        )
+        dh1_ref[:, cols] = dn2
+        h1 = h1_ref[:, cols]
+        squares = squares + jnp.sum(h1 * h1, axis=1, keepdims=True)
+        return squares, mean + jnp.sum(gain_ref[:, cols] * dn2 * h1, axis=1, keepdims=True)
+
+    zero = jnp.zeros((rows, 1), F32)
+    squares, mean = lax.fori_loop(0, width // tile, collect, (zero, zero))
+    scale_own = lax.rsqrt(squares / width + EPSILON)
+    pull = scale_own * scale_own * scale_own * (mean / width)
+
+    @pl.loop(0, width // tile)
+    def _(at):
+        cols = tile_of(at)
+        dn2, h1 = dh1_ref[:, cols], h1_ref[:, cols]
+        dgain_ref[:, cols] = jnp.sum(dn2 * h1 * scale_own, axis=0, keepdims=True)
+        d_resid = dy_own[:, cols].astype(F32) + scale_own * (gain_ref[:, cols] * dn2) - h1 * pull
+        dh1_ref[:, cols] = d_resid
+        low_ref[:, cols] = d_resid.astype(BF)
+
+    def da_copy(hop):
+        return pltpu.make_async_remote_copy(
+            src_ref=da_part.at[hop],
+            dst_ref=da_ref.at[span(place)],
+            send_sem=da_send.at[hop],
+            recv_sem=da_recv.at[hop],
+            device_id=member(hop)[1],
+            device_id_type=MESH,
+        )
+
+    low = low_ref[...]
+
+    @pl.loop(1, count)
+    def _(hop):
+        spot = member(hop)[0]
+        part = cols_inner(low, out_w[pl.ds(pl.multiple_of(spot * size, size), size)])
+        da_part[hop] = part.astype(BF)
+        da_copy(hop).start()
+
+    own_w = out_w[pl.ds(pl.multiple_of(place * size, size), size)]
+    da_ref[span(place)] = cols_inner(low, own_w).astype(BF)
+
+    @pl.loop(1, count)
+    def _(hop):
+        da_copy(hop).wait_recv()
+        da_copy(hop).wait_send()
+
     for copy in first_copies():
         copy.wait_send()
     for step in range(1, steps):
@@ -368,6 +430,7 @@
     total, width = tokens.shape
     hidden = gate_w.shape[1]
     rows, steps = total // count, count // 2
+    size = mixed.shape[1] // count
     vmem = pl.BlockSpec(memory_space=pltpu.VMEM)
     hbm = pl.BlockSpec(memory_space=pl.ANY)
 
@@ -385,14 +448,19 @@
             jax.ShapeDtypeStruct((total, width), BF),
             jax.ShapeDtypeStruct((rows, width), F32),
             jax.ShapeDtypeStruct((rows, width), F32),
+            jax.ShapeDtypeStruct((rows, width), BF),
+            jax.ShapeDtypeStruct((1, width), F32),
+            jax.ShapeDtypeStruct((total, size), BF),
         ],
         in_specs=[hbm] * 3 + [vmem] * 5,
-        out_specs=[hbm] * 4 + [vmem] * 2,
+        out_specs=[hbm] * 4 + [vmem] * 5,
         scratch_shapes=[
             slots(width), slots(mixed.shape[1]), slots(width), slots(width), slots(hidden),
             slots(2 * hidden), slots(width), pltpu.VMEM((2 * rows, width), F32),
+            pltpu.VMEM((rows, width), BF), pltpu.VMEM((count, rows, size), BF),
             part, part, part, part,
             pltpu.SemaphoreType.DMA((2, 6)), pltpu.SemaphoreType.DMA((2, 8)),
+            pltpu.SemaphoreType.DMA((count,)), pltpu.SemaphoreType.DMA((count,)),
             pltpu.SemaphoreType.DMA((count,)), pltpu.SemaphoreType.DMA((count,)),
         ],
         compiler_params=pltpu.CompilerParams(
@@ -514,8 +582,104 @@
     @pl.loop(0, kv_ref.shape[0] // KEY_BLOCK)
     def _(at):
         keys = pl.ds(pl.multiple_of(at * KEY_BLOCK, KEY_BLOCK), KEY_BLOCK)
-        dkv_ref[keys, :size] = dk_acc[keys].astype(BF)
-        dkv_ref[keys, size:] = dv_acc[keys].astype(BF)
+        dk, dv = dk_acc[keys].astype(BF), dv_acc[keys].astype(BF)
+        half = size // 2
+        dkv_ref[keys, :size] = jnp.concatenate([dk[:, :half], dv[:, :half]], axis=1)
+        dkv_ref[keys, size:] = jnp.concatenate([dk[:, half:], dv[:, half:]], axis=1)
+
+
+def fold_kernel(
+    batches, part_ref, own_ref, core_got, x_first, x_second, y_first, y_second, held, send_sem, recv_sem
+):
+    rows, size = own_ref.shape
+    half = rows // 2
+    others = batches // 2
+    head = lax.axis_index("head")
+    batch = lax.axis_index("batch")
+    across, core, low = batch // 2, lax.rem(batch, 2), lax.rem(head, 2)
+    twin = (across * 2 + 1 - core, head)
+    mate = (batch, head + 1 - 2 * low)
+    spots = [lax.rem(across + hop, others) for hop in range(others)]
+    peers = [(spot * 2 + core, head) for spot in spots]
+    greet((twin, mate, *peers[1:]))
+    sems = (send_sem, recv_sem)
+    slot = 0
+    copies = []
+    mine = pl.ds(pl.multiple_of(low * size, size), size)
+    given = pl.ds(pl.multiple_of((1 - low) * size, size), size)
+    top, bottom = pl.ds(0, half), pl.ds(half, half)
+
+    def block(at, side):
+        return pl.ds(pl.multiple_of((2 * at + side) * rows, rows), rows)
+
+    def go(source, target, device):
+        nonlocal slot
+        copy = send(source, target, sems, slot, device)
+        slot += 1
+        copies.append(copy)
+        return copy
+
+    order = list(range(1, others)) + [0]
+    first = [go(part_ref.at[block(spots[hop], 1 - core)], core_got.at[spots[hop]], twin) for hop in order]
+    tops, bottoms = [], []
+    for copy, hop in zip(first, order):
+        copy.wait_recv()
+        spot = spots[hop]
+        core_got[spot] = add_low(core_got[spot], part_ref[block(spot, core)])
+        bottoms.append(go(core_got.at[spot, bottom, given], y_first.at[spot], mate))
+        if hop:
+            tops.append(go(core_got.at[spot, top], x_first.at[hop - 1], peers[hop]))
+    total = core_got[across, top].astype(F32)
+    for hop in range(1, others):
+        tops[hop - 1].wait_recv()
+        total = total + x_first[hop - 1].astype(F32)
+    held[...] = total.astype(BF)
+    last = go(held.at[:, given], y_second, mate)
+    ends = []
+    for copy, hop in zip(bottoms, order):
+        copy.wait_recv()
+        spot = spots[hop]
+        y_first[spot] = add_low(y_first[spot], core_got[spot, bottom, mine])
+        if hop:
+            ends.append(go(y_first.at[spot], x_second.at[hop - 1], peers[hop]))
+    last.wait_recv()
+    own_ref[top] = add_low(held[:, mine], y_second[...])
+    total = y_first[across].astype(F32)
+    for hop in range(1, others):
+        ends[hop - 1].wait_recv()
+        total = total + x_second[hop - 1].astype(F32)
+    own_ref[bottom] = total.astype(BF)
+    for copy in copies:
+        copy.wait_send()
+
+
+def fold(part, rows, collective_id):
+    batches = lax.axis_size("batch")
+    others = batches // 2
+    size = part.shape[1] // 2
+    half = rows // 2
+    vmem = pl.BlockSpec(memory_space=pltpu.VMEM)
+    sems = pltpu.SemaphoreType.DMA((4 * others,))
+    return pl.pallas_call(
+        functools.partial(fold_kernel, batches),
+        out_shape=jax.ShapeDtypeStruct((rows, size), BF),
+        in_specs=[vmem],
+        out_specs=vmem,
+        scratch_shapes=[
+            pltpu.VMEM((others, rows, 2 * size), BF),
+            pltpu.VMEM((others - 1, half, 2 * size), BF),
+            pltpu.VMEM((others - 1, half, size), BF),
+            pltpu.VMEM((others, half, size), BF),
+            pltpu.VMEM((half, size), BF),
+            pltpu.VMEM((half, 2 * size), BF),
+            sems,
+            sems,
+        ],
+        compiler_params=pltpu.CompilerParams(
+            collective_id=collective_id, has_side_effects=True, vmem_limit_bytes=VMEM_LIMIT
+        ),
+        name="fold",
+    )(part)
 
 
 def local_call(kernel, scalars, arrays, outs, scratch, flops, name):
@@ -734,32 +898,20 @@
         "attend",
     )
     mixed_all, out_full = spread([mixed, out_rows], (("head", "cols"), ("batch", "cols")), 2)
-    normed_two, hidden, d_pre, mlp_part, dn2, resid_own = mlp_back(
+    normed_two, hidden, d_pre, mlp_part, resid_own, d_resid, d_resid_low, d_gain_two, d_mixed = mlp_back(
         tokens, mixed_all, out_grad, gain_two[None], out_full, mgate_full, mup_full, down_full, 3
     )
-    recip_own = rms_scale(resid_own)
     mixed_own = lax.dynamic_slice_in_dim(mixed_all, me * chunk, chunk, 0)
-    dy_own = lax.dynamic_slice_in_dim(out_grad, me * chunk, chunk, 0).astype(F32)
     out_flow = flow_steps(mlp_part)
     out_state = next(out_flow)
-
-    d_gain_two = jnp.sum(dn2 * resid_own * recip_own, axis=0)
-    weighted_two = gain_two * dn2
-    d_resid = (
-        dy_own
-        + recip_own * weighted_two
-        - resid_own * recip_own**3 * jnp.mean(weighted_two * resid_own, axis=1, keepdims=True)
-    )
-    d_resid_low = d_resid.astype(BF)
-    d_mixed_all = cols_inner(d_resid_low, out_full).astype(BF)
-    d_mixed_all = d_mixed_all.reshape(chunk, heads, head_size)
-    places = [ring_place(at, heads) for at in range(heads)]
-    d_mixed_all = jnp.stack([d_mixed_all[:, at] for at in places], axis=0)
-    d_mixed = lax.all_to_all(d_mixed_all, "head", split_axis=0, concat_axis=0, tiled=True)
-    d_mixed = jnp.concatenate([d_mixed[ring_head(at, heads)] for at in range(heads)], axis=0)
-    d_out_part = rows_inner(mixed_own, d_resid_low).astype(BF)
-    d_out_part = lax.psum_scatter(d_out_part, "batch", scatter_dimension=1, tiled=True)
-    d_out = flow_sum(d_out_part)
+    d_down = rows_inner(hidden, out_grad).astype(BF)
+    normed_late, d_down, *out_state = lax.optimization_barrier((normed_two, d_down, *out_state))
+    out_state = out_flow.send(tuple(out_state))
+    d_mlp = rows_inner(normed_late, d_pre).astype(BF)
+    d_mixed, d_mlp, *out_state = lax.optimization_barrier((d_mixed, d_mlp, *out_state))
+    out_state = tuple(out_state)
+    d_down = lax.psum_scatter(d_down, "batch", scatter_dimension=1, tiled=True).astype(F32)
+    d_mlp = lax.psum_scatter(d_mlp, "batch", scatter_dimension=0, tiled=True).astype(F32)
 
     d_mixed, out_state = after(out_flow, out_state, d_mixed)
     d_queries, d_gate_logit, d_kv_all = local_call(
@@ -776,22 +928,16 @@
         "attend_back",
     )
     d_kv_all, out_state = after(out_flow, out_state, d_kv_all)
-    d_kv_own = halve_batch(d_kv_all, row_count)
-    d_kv_own, out_state = after(out_flow, out_state, d_kv_own)
+    d_kv = fold(d_kv_all, row_count, 4)
     while isinstance(out_state, tuple):
         out_state = out_flow.send(out_state)
-    output = flow_spread((resid_own + out_state).astype(BF))
-    d_kv_mate = from_partner(d_kv_own, "head")
-    d_kv = (d_kv_own.astype(F32) + d_kv_mate.astype(F32)).astype(BF)
-    d_cat = jnp.concatenate(
-        [
-            d_queries,
-            jnp.where(first, d_kv[:, :half], d_kv[:, half:head_size]),
-            jnp.where(first, d_kv[:, head_size : head_size + half], d_kv[:, head_size + half :]),
-            d_gate_logit,
-        ],
-        axis=1,
-    )
+    out_total = out_state
+    d_kv, out_total = lax.optimization_barrier((d_kv, out_total))
+    output = flow_spread((resid_own + out_total).astype(BF))
+    d_cat = jnp.concatenate([d_queries, d_kv, d_gate_logit], axis=1)
+    d_out_part = rows_inner(mixed_own, d_resid_low).astype(BF)
+    d_out_part = lax.psum_scatter(d_out_part, "batch", scatter_dimension=1, tiled=True)
+    d_out = flow_sum(d_out_part)
     w_key_own = jnp.where(
         first, w_in[:, head_size : head_size + half], w_in[:, head_size + half : 2 * head_size]
     )
@@ -814,13 +960,9 @@
     ).astype(BF)
     d_tokens = flow_spread(d_tokens)
 
-    d_mlp = rows_inner(normed_two, d_pre).astype(BF)
-    d_mlp = lax.psum_scatter(d_mlp, "batch", scatter_dimension=0, tiled=True).astype(F32)
-    d_down = rows_inner(hidden, out_grad).astype(BF)
-    d_down = lax.psum_scatter(d_down, "batch", scatter_dimension=1, tiled=True).astype(F32)
     d_in = rows_inner(normed_one, d_cat).astype(BF)
     d_in = lax.psum_scatter(d_in, "batch", scatter_dimension=0, tiled=True).astype(F32)
-    d_gains = jnp.stack([d_gain_one, d_gain_two]).reshape(2, batches, -1).transpose(1, 0, 2)
+    d_gains = jnp.stack([d_gain_one, d_gain_two[0]]).reshape(2, batches, -1).transpose(1, 0, 2)
     d_gains = sum_heads(halve_batch(d_gains.reshape(2 * batches, -1), 2))
     hidden_own = w_mlp_gate.shape[1]
     return (

time: 615 us -> 576 us (0.937)
  Pallas kernels: 219 us -> 262 us
  waiting for transfers between devices: 155 us -> 115 us
  local copies, waits for them, and re-layouts: 56.2 us -> 41.3 us
  other arithmetic: 52.4 us -> 39.9 us
  starting transfers between devices: 60.1 us -> 49.9 us
    pallas_call x0 -> x1, Pallas kernels: none -> 27.2 us  [fold(): pl.pallas_call(functools.partial(fold_kernel, batches), out_shape=jax.Sha...]
    ppermute x2 -> x1, waiting for transfers between devices: 18.1 us -> 3.5 us  [from_partner(): return lax.ppermute(block, axis, route)]
    unnamed x81 -> x44, local copies, waits for them, and re-layouts: 18.6 us -> 7.02 us
    pallas_call x1, Pallas kernels: 77.6 us -> 89 us  [mlp_back(): pl.pallas_call(functools.partial(mlp_kernel, count), out_shape=[jax.Shape...]
    ppermute x12, waiting for transfers between devices: 34.9 us -> 24.8 us  [flow_steps(): from_left = lax.ppermute(going, 'head', right)]
    ppermute x6, waiting for transfers between devices: 33.2 us -> 26.7 us  [flow_spread(): going = lax.ppermute(going, 'head', right)]
    ppermute x7 -> x5, waiting for transfers between devices: 21.5 us -> 17 us  [swap(): lax.ppermute(block, axis, [(at, at ^ stride) for at in range(lax.axis_siz...]
  transfers between devices with their start and end apart: 58 -> 54, of which waited for: 27 -> 21; matrix products, arithmetic and copies ran while one was open for 22% -> 17% of each run, Pallas kernels for 23% -> 30%
where the time goes in v7:
time: 576 us; the launch traced here: 570 us
  Pallas kernels  262 us (45%)
  waiting for transfers between devices  115 us (20%)
  starting transfers between devices  49.9 us (9%)
  matrix products  42 us (7%)
  local copies, waits for them, and re-layouts  41.3 us (7%)
  other arithmetic  39.9 us (7%)
  between operations  15.4 us (3%)
    pallas_call x2, Pallas kernels, spread(): pl.pallas_call(functools.partial(spread_kernel, count, batches, plans), o...  125 us
    pallas_call x1, Pallas kernels, mlp_back(): pl.pallas_call(functools.partial(mlp_kernel, count), out_shape=[jax.Shape...  89 us
    dot_general x4, matrix products, rows_inner(): lax.dot_general(left, right, (((0,), (0,)), ((), ())), preferred_element_...  32.9 us
    ppermute x12, waiting for transfers between devices, flow_steps(): from_right = lax.ppermute(coming, 'head', left)  27.6 us
    pallas_call x1, Pallas kernels, fold(): pl.pallas_call(functools.partial(fold_kernel, batches), out_shape=jax.Sha...  27.2 us
    ppermute x6, waiting for transfers between devices, flow_spread(): going = lax.ppermute(going, 'head', right)  26.7 us
    ppermute x12, waiting for transfers between devices, flow_steps(): from_left = lax.ppermute(going, 'head', right)  24.8 us
    pallas_call x2, Pallas kernels, local_call(): pl.pallas_call(kernel, out_shape=outs, in_specs=[smem] * len(scalars) + [...  20.6 us
  transfers between devices with their start and end apart: 54, of which 21 were waited for; matrix products, arithmetic and copies ran while one was open for 17% of the time, Pallas kernels for 30%

profile of v7, /device:TPU:0, one launch (start us, length us, event | category | flops | bytes accessed | tf_op | source)
XLA Modules:
  0.0 570.5 jit_solution(14093665543604750836)
XLA Ops:
  12.3 3.5 collective-permute-done
  20.4 5.2 all_gather.15
  25.6 4.1 multiply_reduce_fusion
  30.3 12.0 %all-gather.5.cloned.1.call-done = bf16[2048,512]{1,0:T(8,128)(2,1)} async-done(((bf16[512,512]{1,0:T(8,128)(2,1)}), bf16[2048,512]{1,0:T(8,128)(2,1)}) %all-gather.5.cloned.1.call-update) | async-done | bytes 2097168 | tf_op jit(solution)/shard_map/all_gather | solution.py:860
  42.3 5.7 %fusion.19 = (bf16[1280,512]{1,0:T(8,128)(2,1)S(1)}, f32[1280,512]{1,0:T(8,128)S(1)}) fusion(bf16[2048,512]{1,0:T(8,128)(2,1)} %all-gather.5.cloned.1.call-done, f32[2048]{0:T(1024)S(1)} %bitcast.29, f32[1280]{0:T(1024)S(1)} %add_rsqrt_fusion, bf16[1280,2048]{1,0:T(8,128)(2,1)} %x_hbm.1), kind=kOutput, calls=%fused_computation.106 | convolution fusion | flops 2695495680 | bytes 11285504 | tf_op jit(solution)/shard_map/dot_general | solution.py:805
  49.7 45.4 %spread_1.1 = (bf16[1024,512]{1,0:T(8,128)(2,1)}, bf16[5120,256]{1,0:T(8,128)(2,1)}, s32[4,10,128]{2,1,0:T(8,128)}) custom-call(bf16[128,512]{1,0:T(8,128)(2,1)} %refs_0_.1, bf16[1280,256]{1,0:T(8,128)(2,1)} %slice.177.refs_1_, s32[10,128]{1,0:T(8,128)} %bitcast.33), custom_call_target="tpu_custom_call" | custom-call | tf_op jit(solution)/shard_map/spread_1/pallas_call | solution.py:164
  97.7 8.8 %attend.1 = (f32[1280,128]{1,0:T(8,128)}, bf16[1280,128]{1,0:T(8,128)(2,1)}, f32[1,1280]{1,0:T(1,128)}) custom-call(s32[1280]{0:T(1024)} %copy-done.13, s32[1]{0:T(128)} %bitcast.2.base_sm, bf16[1280,128]{1,0:T(8,128)(2,1)} %slice.178.q_ref, bf16[5120,256]{1,0:T(8,128)(2,1)} %get-tuple-element.49.kv_ref, s32[1,1280]{1,0:T(1,128)} %broadcast_in_dim.16.start_ref, ...), custom_call_target="tpu_custom_call" | custom-call | flops 3355443200 | bytes 8388608 | tf_op jit(solution)/shard_map/attend/pallas_call | solution.py:688
  106.5 79.5 %spread_2.1 = (bf16[1280,1024]{1,0:T(8,128)(2,1)}, bf16[1024,2048]{1,0:T(8,128)(2,1)}) custom-call(bf16[1280,128]{1,0:T(8,128)(2,1)} %get-tuple-element.50.refs_0_, bf16[1024,512]{1,0:T(8,128)(2,1)} %get-tuple-element.51.refs_1_), custom_call_target="tpu_custom_call" | custom-call | tf_op jit(solution)/shard_map/spread_2/pallas_call | solution.py:164
  186.1 89.0 %mlp_back.1 = (bf16[1280,2048]{1,0:T(8,128)(2,1)}, bf16[1280,768]{1,0:T(8,128)(2,1)}, bf16[1280,1536]{1,0:T(8,128)(2,1)}, bf16[1280,2048]{1,0:T(8,128)(2,1)}, f3...) custom-call(bf16[1280,2048]{1,0:T(8,128)(2,1)} %x_hbm.1, ...), custom_call_target="tpu_custom_call" | custom-call | flops 29527900160 | bytes 41943040 | tf_op jit(solution)/shard_map/mlp_back/pallas_call | solution.py:442
  278.7 9.1 %convolution_convert_fusion.3 = bf16[768,2048]{1,0:T(8,128)(2,1)} fusion(bf16[1280,768]{1,0:T(8,128)(2,1)} %get-tuple-element.58, bf16[1280,2048]{1,0:T(8,128)(2,1)} %dy_hbm.1), kind=kOutput, calls=%fused_computation.5 | convolution fusion | flops 4028104704 | bytes 10354688 | tf_op jit(solution)/shard_map/dot_general | solution.py:809
  291.6 12.6 %convolution_convert_fusion.1 = bf16[2048,1536]{1,0:T(8,128)(2,1)} fusion(bf16[1280,2048]{1,0:T(8,128)(2,1)} %get-tuple-element.60, bf16[1280,1536]{1,0:T(8,128)(2,1)S(1)} %copy-done.17), kind=kOutput, calls=%fused_computation.3 | convolution fusion | flops 8056209408 | bytes 15466496 | tf_op jit(solution)/shard_map/dot_general | solution.py:809
  308.0 11.8 %attend_back.1 = (bf16[1280,128]{1,0:T(8,128)(2,1)}, bf16[1280,128]{1,0:T(8,128)(2,1)}, bf16[5120,256]{1,0:T(8,128)(2,1)}) custom-call(s32[1280]{0:T(1024)} %copy-done.13, s32[1]{0:T(128)} %bitcast.2.base_sm, bf16[1280,128]{1,0:T(8,128)(2,1)} %slice.178.q_ref, bf16[5120,256]{1,0:T(8,128)(2,1)} %get-tuple-element.49.kv_ref, ...), custom_call_target="tpu_custom_call" | custom-call | flops 8388608000 | bytes 8388608 | tf_op jit(solution)/shard_map/attend_back/pallas_call | solution.py:688
  324.7 27.2 %fold.1 = bf16[1280,128]{1,0:T(8,128)(2,1)} custom-call(bf16[5120,256]{1,0:T(8,128)(2,1)} %get-tuple-element.72.part_ref), custom_call_target="tpu_custom_call" | custom-call | tf_op jit(solution)/shard_map/fold/pallas_call | solution.py:663
  354.6 6.8 %convolution_convert_fusion.4 = bf16[2048,384]{1,0:T(8,128)(2,1)} fusion(bf16[1280,384]{1,0:T(8,128)(2,1)S(1)} %constant_dynamic-update-slice_fusion.14, f32[2048]{0:T(1024)S(1)} %bitcast.30, f32[1280]{0:T(1024)S(1)} %add_rsqrt_fusion, bf16[1280,2048]{1,0:T(8,128)(2,1)} %x_hbm.1), kind=kOutput, calls=%fused_computation.6 | convolution fusion | flops 2024538112 | bytes 7812096 | tf_op jit(solution)/shard_map/dot_general | solution.py:809
  361.6 4.3 convolution_convert_fusion.2
  388.0 9.4 %collective-permute-done.9 = bf16[160,2048]{1,0:T(8,128)(2,1)S(1)} collective-permute-done((bf16[160,2048]{1,0:T(8,128)(2,1)S(1)}, bf16[160,2048]{1,0:T(8,128)(2,1)S(1)}, u32[]{:S(2)}, u32[]{:S(2)}) %collective-permute-start.9) | collective-permute-done | bytes 655392 | tf_op jit(solution)/shard_map/ppermute | solution.py:759
  399.9 13.8 %collective-permute-done.22 = bf16[160,2048]{1,0:T(8,128)(2,1)S(1)} collective-permute-done((bf16[160,2048]{1,0:T(8,128)(2,1)S(1)}, bf16[160,2048]{1,0:T(8,128)(2,1)S(1)}, u32[]{:S(2)}, u32[]{:S(2)}) %collective-permute-start.22) | collective-permute-done | bytes 655392 | tf_op jit(solution)/shard_map/ppermute | solution.py:725
  417.3 7.9 %convert_element_type.236 = f32[1280,2048]{1,0:T(8,128)} convert(bf16[1280,2048]{1,0:T(8,128)(2,1)} %x_hbm.1) | non-fusion elementwise | flops 2621440 | bytes 15728640 | tf_op jit(solution)/shard_map/convert_element_type | solution.py:868
  429.3 10.3 %collective-permute-done.19 = bf16[160,2048]{1,0:T(8,128)(2,1)S(1)} collective-permute-done((bf16[160,2048]{1,0:T(8,128)(2,1)}, bf16[160,2048]{1,0:T(8,128)(2,1)S(1)}, u32[]{:S(2)}, u32[]{:S(2)}) %collective-permute-start.19) | collective-permute-done | bytes 655392 | tf_op jit(solution)/shard_map/ppermute | solution.py:724
  456.2 11.4 %collective-permute-done.20 = bf16[160,2048]{1,0:T(8,128)(2,1)S(1)} collective-permute-done((bf16[160,2048]{1,0:T(8,128)(2,1)S(1)}, bf16[160,2048]{1,0:T(8,128)(2,1)S(1)}, u32[]{:S(2)}, u32[]{:S(2)}) %collective-permute-start.20) | collective-permute-done | bytes 655392 | tf_op jit(solution)/shard_map/ppermute | solution.py:733
  487.3 12.7 %collective-permute-done.36 = f32[2,512]{1,0:T(2,128)S(1)} collective-permute-done((f32[2,512]{1,0:T(2,128)S(1)}, f32[2,512]{1,0:T(2,128)S(1)}, u32[]{:S(2)}, u32[]{:S(2)}) %collective-permute-start.36) | collective-permute-done | bytes 4128 | tf_op jit(solution)/shard_map/ppermute | solution.py:773
  509.9 9.8 %collective-permute-done.27 = bf16[160,2048]{1,0:T(8,128)(2,1)} collective-permute-done((bf16[160,2048]{1,0:T(8,128)(2,1)S(1)}, bf16[160,2048]{1,0:T(8,128)(2,1)}, u32[]{:S(2)}, u32[]{:S(2)}) %collective-permute-start.27) | collective-permute-done | bytes 655392 | tf_op jit(solution)/shard_map/ppermute | solution.py:759
  531.1 5.0 collective-permute-done.29
  541.4 5.0 collective-permute-done.43
  (234 shorter events, 144.6 us)
Async XLA Ops:
  7.2 35.1 %all-gather.5.cloned.1.call-start = ((), (), s32[]{:S(2)}) async-start(), calls=%async_computation.4 | async-start | bytes 2621440 | tf_op jit(solution)/shard_map/all_gather | solution.py:860
  18.1 167.9 %all-gather.11.cloned.1.call-start = ((), (), s32[]{:S(2)}) async-start(), calls=%async_computation.7 | async-start | bytes 3932160 | tf_op jit(solution)/shard_map/all_gather | solution.py:866
  18.8 167.2 %all-gather.7.cloned.1.call-start = ((), (), s32[]{:S(2)}) async-start(), calls=%async_computation.5 | async-start | bytes 3932160 | tf_op jit(solution)/shard_map/all_gather | solution.py:864
  19.6 166.5 %all-gather.9.cloned.1.call-start = ((), (), s32[]{:S(2)}) async-start(), calls=%async_computation.6 | async-start | bytes 3932160 | tf_op jit(solution)/shard_map/all_gather | solution.py:865
  20.2 488.7 %reduce-scatter.5.cloned.1.call-start = ((), (), s32[]{:S(2)}) async-start(), calls=%async_computation.8 | async-start | bytes 1966080 | tf_op jit(solution)/shard_map/reduce_scatter | solution.py:964
  321.7 30.3 %collective-permute-start.7 = (bf16[160,2048]{1,0:T(8,128)(2,1)S(1)}, bf16[160,2048]{1,0:T(8,128)(2,1)S(1)}, u32[]{:S(2)}, u32[]{:S(2)}) collective-permute-start(bf16[160,2048]{1,0:T(8,128)(2,1)S(1)} %get-tuple-element.73), channel_id=1, source_target_pairs={{0,2},{2,4},{4,6},{6,7},{7,5},{5,3},{3,1},{1,0},{8,10},{10,12},{12... | collective-permute-start | bytes 1966088 | tf_op jit(solution)/shard_map/ppermute | solution.py:733
  322.7 29.3 %collective-permute-start.8 = (bf16[160,2048]{1,0:T(8,128)(2,1)S(1)}, bf16[160,2048]{1,0:T(8,128)(2,1)S(1)}, u32[]{:S(2)}, u32[]{:S(2)}) collective-permute-start(bf16[160,2048]{1,0:T(8,128)(2,1)S(1)} %get-tuple-element.74), channel_id=1, source_target_pairs={{0,1},{2,0},{4,2},{6,4},{7,6},{5,7},{3,5},{1,3},{8,9},{10,8},{12,1... | collective-permute-start | bytes 1966088 | tf_op jit(solution)/shard_map/ppermute | solution.py:734
  361.5 165.6 %reduce-scatter.7.cloned.1.call-start = ((), (), s32[]{:S(2)}) async-start(), calls=%async_computation.9 | async-start | bytes 5242880 | tf_op jit(solution)/shard_map/reduce_scatter | solution.py:939
  365.9 183.5 %reduce-scatter.11.cloned.1.call-start = ((), (), s32[]{:S(2)}) async-start(), calls=%async_computation.11 | async-start | bytes 3932160 | tf_op jit(solution)/shard_map/reduce_scatter | solution.py:913
  366.7 193.2 %reduce-scatter.9.cloned.1.call-start = ((), (), s32[]{:S(2)}) async-start(), calls=%async_computation.10 | async-start | bytes 7864320 | tf_op jit(solution)/shard_map/reduce_scatter | solution.py:914
  385.8 27.8 %collective-permute-start.22 = (bf16[160,2048]{1,0:T(8,128)(2,1)S(1)}, bf16[160,2048]{1,0:T(8,128)(2,1)S(1)}, u32[]{:S(2)}, u32[]{:S(2)}) collective-permute-start(bf16[160,2048]{1,0:T(8,128)(2,1)S(1)} %pad_maximum_fusion.3), channel_id=1, source_target_pairs={{0,1},{2,0},{4,2},{6,4},{7,6},{5,7},{3,5},{1,3},{8,9},{10,8},{12,1... | collective-permute-start | bytes 1966088 | tf_op jit(solution)/shard_map/ppermute | solution.py:725
  386.2 27.4 %collective-permute-start.18 = (bf16[160,2048]{1,0:T(8,128)(2,1)S(1)}, bf16[160,2048]{1,0:T(8,128)(2,1)S(1)}, u32[]{:S(2)}, u32[]{:S(2)}) collective-permute-start(bf16[160,2048]{1,0:T(8,128)(2,1)S(1)} %pad_maximum_fusion.2), channel_id=1, source_target_pairs={{0,2},{2,4},{4,6},{6,7},{7,5},{5,3},{3,1},{1,0},{8,10},{10,12},{12... | collective-permute-start | bytes 1966088 | tf_op jit(solution)/shard_map/ppermute | solution.py:724
  397.4 29.9 %collective-permute-start.11 = (bf16[160,2048]{1,0:T(8,128)(2,1)S(1)}, bf16[160,2048]{1,0:T(8,128)(2,1)}, u32[]{:S(2)}, u32[]{:S(2)}) collective-permute-start(bf16[160,2048]{1,0:T(8,128)(2,1)S(1)} %collective-permute-done.9), channel_id=1, source_target_pairs={{0,2},{2,4},{4,6},{6,7},{7,5},{5,3},{3,1},{1,0},{8,10},{10,12},{12... | collective-permute-start | bytes 1966088 | tf_op jit(solution)/shard_map/ppermute | solution.py:759
  399.9 28.2 %collective-permute-start.12 = (bf16[160,2048]{1,0:T(8,128)(2,1)S(1)}, bf16[160,2048]{1,0:T(8,128)(2,1)}, u32[]{:S(2)}, u32[]{:S(2)}) collective-permute-start(bf16[160,2048]{1,0:T(8,128)(2,1)S(1)} %collective-permute-done.10), channel_id=1, source_target_pairs={{0,1},{2,0},{4,2},{6,4},{7,6},{5,7},{3,5},{1,3},{8,9},{10,8},{12,1... | collective-permute-start | bytes 1966088 | tf_op jit(solution)/shard_map/ppermute | solution.py:760
  415.2 24.4 %collective-permute-start.19 = (bf16[160,2048]{1,0:T(8,128)(2,1)}, bf16[160,2048]{1,0:T(8,128)(2,1)S(1)}, u32[]{:S(2)}, u32[]{:S(2)}) collective-permute-start(bf16[160,2048]{1,0:T(8,128)(2,1)} %get-tuple-element.128), channel_id=1, source_target_pairs={{0,2},{2,4},{4,6},{6,7},{7,5},{5,3},{3,1},{1,0},{8,10},{10,12},{12... | collective-permute-start | bytes 1966088 | tf_op jit(solution)/shard_map/ppermute | solution.py:724
  415.6 26.2 %collective-permute-start.23 = (bf16[160,2048]{1,0:T(8,128)(2,1)}, bf16[160,2048]{1,0:T(8,128)(2,1)}, u32[]{:S(2)}, u32[]{:S(2)}) collective-permute-start(bf16[160,2048]{1,0:T(8,128)(2,1)} %get-tuple-element.129), channel_id=1, source_target_pairs={{0,1},{2,0},{4,2},{6,4},{7,6},{5,7},{3,5},{1,3},{8,9},{10,8},{12,1... | collective-permute-start | bytes 1966088 | tf_op jit(solution)/shard_map/ppermute | solution.py:725
  427.2 26.4 %collective-permute-start.13 = (bf16[160,2048]{1,0:T(8,128)(2,1)}, bf16[160,2048]{1,0:T(8,128)(2,1)S(1)}, u32[]{:S(2)}, u32[]{:S(2)}) collective-permute-start(bf16[160,2048]{1,0:T(8,128)(2,1)} %collective-permute-done.11), channel_id=1, source_target_pairs={{0,2},{2,4},{4,6},{6,7},{7,5},{5,3},{3,1},{1,0},{8,10},{10,12},{12... | collective-permute-start | bytes 1966088 | tf_op jit(solution)/shard_map/ppermute | solution.py:759
  428.0 28.1 %collective-permute-start.14 = (bf16[160,2048]{1,0:T(8,128)(2,1)}, bf16[160,2048]{1,0:T(8,128)(2,1)S(1)}, u32[]{:S(2)}, u32[]{:S(2)}) collective-permute-start(bf16[160,2048]{1,0:T(8,128)(2,1)} %collective-permute-done.12), channel_id=1, source_target_pairs={{0,1},{2,0},{4,2},{6,4},{7,6},{5,7},{3,5},{1,3},{8,9},{10,8},{12,1... | collective-permute-start | bytes 1966088 | tf_op jit(solution)/shard_map/ppermute | solution.py:760
  443.7 23.8 %collective-permute-start.20 = (bf16[160,2048]{1,0:T(8,128)(2,1)S(1)}, bf16[160,2048]{1,0:T(8,128)(2,1)S(1)}, u32[]{:S(2)}, u32[]{:S(2)}) collective-permute-start(bf16[160,2048]{1,0:T(8,128)(2,1)S(1)} %get-tuple-element.126), channel_id=1, source_target_pairs={{0,2},{2,4},{4,6},{6,7},{7,5},{5,3},{3,1},{1,0},{8,10},{10,12},{12... | collective-permute-start | bytes 1966088 | tf_op jit(solution)/shard_map/ppermute | solution.py:733
  444.2 25.5 %collective-permute-start.24 = (bf16[160,2048]{1,0:T(8,128)(2,1)S(1)}, bf16[160,2048]{1,0:T(8,128)(2,1)S(1)}, u32[]{:S(2)}, u32[]{:S(2)}) collective-permute-start(bf16[160,2048]{1,0:T(8,128)(2,1)S(1)} %get-tuple-element.127), channel_id=1, source_target_pairs={{0,1},{2,0},{4,2},{6,4},{7,6},{5,7},{3,5},{1,3},{8,9},{10,8},{12,1... | collective-permute-start | bytes 1966088 | tf_op jit(solution)/shard_map/ppermute | solution.py:734
  453.7 47.5 %collective-permute-start.15 = (bf16[160,1024]{1,0:T(8,128)(2,1)S(1)}, bf16[160,1024]{1,0:T(8,128)(2,1)}, u32[]{:S(2)}, u32[]{:S(2)}) collective-permute-start(bf16[160,1024]{1,0:T(8,128)(2,1)S(1)} %slice.181), channel_id=1, source_target_pairs={{0,2},{2,4},{4,6},{6,7},{7,5},{5,3},{3,1},{1,0},{8,10},{10,12},{12... | collective-permute-start | bytes 983048 | tf_op jit(solution)/shard_map/ppermute | solution.py:762
  456.1 45.0 %collective-permute-start.16 = (bf16[160,1024]{1,0:T(8,128)(2,1)S(1)}, bf16[160,1024]{1,0:T(8,128)(2,1)}, u32[]{:S(2)}, u32[]{:S(2)}) collective-permute-start(bf16[160,1024]{1,0:T(8,128)(2,1)S(1)} %slice.182), channel_id=1, source_target_pairs={{0,1},{2,0},{4,2},{6,4},{7,6},{5,7},{3,5},{1,3},{8,9},{10,8},{12,1... | collective-permute-start | bytes 983048 | tf_op jit(solution)/shard_map/ppermute | solution.py:763
  483.1 21.9 %collective-permute-start.25 = (bf16[160,2048]{1,0:T(8,128)(2,1)S(1)}, bf16[160,2048]{1,0:T(8,128)(2,1)S(1)}, u32[]{:S(2)}, u32[]{:S(2)}) collective-permute-start(bf16[160,2048]{1,0:T(8,128)(2,1)S(1)} %get-tuple-element.123), channel_id=1, source_target_pairs={{0,2},{2,4},{4,6},{6,7},{7,5},{5,3},{3,1},{1,0},{8,10},{10,12},{12... | collective-permute-start | bytes 1966088 | tf_op jit(solution)/shard_map/ppermute | solution.py:759
  484.3 21.0 %collective-permute-start.26 = (bf16[160,2048]{1,0:T(8,128)(2,1)S(1)}, bf16[160,2048]{1,0:T(8,128)(2,1)S(1)}, u32[]{:S(2)}, u32[]{:S(2)}) collective-permute-start(bf16[160,2048]{1,0:T(8,128)(2,1)S(1)} %get-tuple-element.123), channel_id=1, source_target_pairs={{0,1},{2,0},{4,2},{6,4},{7,6},{5,7},{3,5},{1,3},{8,9},{10,8},{12,1... | collective-permute-start | bytes 1966088 | tf_op jit(solution)/shard_map/ppermute | solution.py:760
  (48 other events, 534.1 us)
Sparse Core Ops, SparseCore 0:
  18.2 24.0 all-gather.4
  43.9 41.4 all-gather.10
  86.9 28.5 all-gather.6
  116.9 46.1 all-gather.8
  361.6 27.4 reduce-scatter.4
  391.7 44.5 reduce-scatter.6
  438.7 37.9 reduce-scatter.10
  479.4 58.4 reduce-scatter.8

commit v8 on v7

--- a/solution.py
+++ b/solution.py
@@ -471,6 +471,214 @@
     )(tokens, mixed, dy, gain, out_w, gate_w, up_w, down_w)
 
 
+def entry_kernel(
+    count, batches, x_ref, w_ref, out_ref, gain_ref, seg_ref,
+    n1_ref, q_ref, logit_ref, kv_ref, w_all, out_all, gain_all, seg_all,
+    send_sem, recv_sem, local_sem,
+):
+    steps = count // 2
+    others = batches // 2
+    rows, width = x_ref.shape
+    depth = w_ref.shape[0]
+    size, wide = out_ref.shape
+    block = 256
+    place, right, left = ring_setup(count)
+    head = lax.axis_index("head")
+    batch = lax.axis_index("batch")
+    across, core, low = batch // 2, lax.rem(batch, 2), lax.rem(head, 2)
+    twin = (across * 2 + 1 - core, head)
+    mate = (batch, head + 1 - 2 * low)
+    spots = [lax.rem(across + hop, others) for hop in range(others)]
+    backs = [lax.rem(across + others - hop, others) for hop in range(others)]
+    peers = [(spot * 2 + core, head) for spot in spots]
+    far_peers = [(spot * 2 + 1 - core, head) for spot in spots]
+    greet((twin, mate, right, left, *peers[1:], *far_peers[1:]))
+    sems = (send_sem, recv_sem)
+    slot = 0
+    copies = []
+
+    def go(source, target, device):
+        nonlocal slot
+        copy = send(source, target, sems, slot, device)
+        slot += 1
+        copies.append(copy)
+        return copy
+
+    def part(at, extent):
+        return pl.ds(pl.multiple_of(at * extent, extent), extent)
+
+    def both(view, own):
+        out = [go(own, view(batch), peers[hop]) for hop in range(1, others)]
+        return out, [go(own, view(batch), twin)]
+
+    def pass_on(view, arrived):
+        out = []
+        for hop in range(1, others):
+            arrived[hop - 1].wait_recv()
+            there = view(backs[hop] * 2 + core)
+            out.append(go(there, there, twin))
+        return out
+
+    local = []
+
+    def stay(source, target):
+        copy = pltpu.make_async_copy(source, target, local_sem.at[len(local)])
+        copy.start()
+        local.append(copy)
+
+    def main_view(at):
+        return w_all.at[part(at, depth), pl.ds(0, 3 * size)]
+
+    def mate_view(at):
+        return w_all.at[part(at, depth), pl.ds(3 * size, size)]
+
+    def out_view(chunk, at):
+        return out_all.at[part(chunk, size), part(at, wide)]
+
+    small = []
+    for own, whole in ((gain_ref, gain_all), (seg_ref, seg_all)):
+        for device in (twin, *peers[1:], *far_peers[1:]):
+            small.append(go(own, whole.at[batch], device))
+        stay(own, whole.at[batch])
+    from_mate = go(w_ref.at[:, pl.ds(2 * size, size)], mate_view(batch), mate)
+    main_out, main_twin = both(main_view, w_ref)
+    stay(w_ref, main_view(batch))
+    out_peers = [go(out_ref, out_view(place, batch), peers[hop]) for hop in range(1, others)]
+    stay(out_ref, out_view(place, batch))
+    flows = [[None, None] for _ in range(others)]
+
+    def ring(step):
+        for hop in range(others):
+            lane = spots[0] if hop == 0 else backs[hop]
+            at = lane * 2 + core
+            if step == 0 and hop:
+                out_peers[hop - 1].wait_recv()
+            for flow, chunk, device in ((0, place - step, right), (1, place + step, left)):
+                if step:
+                    flows[hop][flow].wait_recv()
+                target = out_view(lax.rem(chunk + count, count), at)
+                source = out_ref if step == 0 and hop == 0 else target
+                if step == steps - 1:
+                    cut = (pl.ds(flow * (size // 2), size // 2), slice(None))
+                    source, target = source.at[cut], target.at[cut]
+                flows[hop][flow] = go(source, target, device)
+
+    for copy in small:
+        copy.wait_recv()
+    for copy in local[:2]:
+        copy.wait()
+
+    def normalize(at):
+        here = part(at, block)
+
+        def squares(tile, total):
+            values = x_ref[here, part(tile, 256)].astype(F32)
+            return total + jnp.sum(values * values, axis=1, keepdims=True)
+
+        total = lax.fori_loop(0, width // 256, squares, jnp.zeros((block, 1), F32))
+        scale = lax.rsqrt(total / width + EPSILON)
+
+        @pl.loop(0, batches)
+        def _(owner):
+            for tile in range(depth // 128):
+                cols = pl.ds(pl.multiple_of(owner * depth + tile * 128, 128), 128)
+                values = x_ref[here, cols].astype(F32) * scale
+                n1_ref[here, cols] = (values * gain_all[owner, pl.ds(tile, 1)]).astype(BF)
+
+    blocks = rows // block
+    middle = blocks // 2
+
+    @pl.loop(0, middle)
+    def _(at):
+        normalize(at)
+
+    from_mate.wait_recv()
+    mate_out, mate_twin = both(mate_view, mate_view(batch))
+    ring(0)
+
+    @pl.loop(middle, blocks)
+    def _(at):
+        normalize(at)
+
+    main_passed = pass_on(main_view, main_out)
+    mate_passed = pass_on(mate_view, mate_out)
+    for copy in (*main_twin, *mate_twin, *main_passed, *mate_passed):
+        copy.wait_recv()
+    for copy in local[2:]:
+        copy.wait()
+
+    def kv_view(at):
+        return kv_ref.at[part(at, rows)]
+
+    @pl.loop(0, blocks)
+    def _(at):
+        here = part(at, block)
+        values = matmul(n1_ref[here], w_all[:, pl.ds(2 * size, 2 * size)])
+        one, two = values[:, :size], values[:, size:]
+        first = jnp.where(low == 0, one, two).astype(BF)
+        second = jnp.where(low == 0, two, one).astype(BF)
+        half = size // 2
+        there = pl.ds(pl.multiple_of(batch * rows + at * block, block), block)
+        kv_ref[there, pl.ds(0, size)] = jnp.concatenate([first[:, :half], second[:, :half]], 1)
+        kv_ref[there, pl.ds(size, size)] = jnp.concatenate([first[:, half:], second[:, half:]], 1)
+
+    kv_out, kv_twin = both(kv_view, kv_view(batch))
+    ring(1)
+
+    @pl.loop(0, blocks)
+    def _(at):
+        here = part(at, block)
+        values = matmul(n1_ref[here], w_all[:, pl.ds(0, 2 * size)])
+        q_ref[here] = values[:, :size].astype(BF)
+        logit_ref[here] = values[:, size:]
+
+    for step in range(2, steps):
+        ring(step)
+    kv_passed = pass_on(kv_view, kv_out)
+    for pair in flows:
+        for copy in pair:
+            copy.wait_recv()
+    swaps = []
+    for hop in range(others):
+        there = out_all.at[:, part(spots[hop] * 2 + core, wide)]
+        swaps.append(go(there, there, twin))
+    for copy in (*kv_twin, *kv_passed, *swaps):
+        copy.wait_recv()
+    for copy in copies:
+        copy.wait_send()
+
+
+def entry(tokens, w_shard, w_out, gains, segments, collective_id):
+    count = lax.axis_size("head")
+    batches = lax.axis_size("batch")
+    others = batches // 2
+    rows, width = tokens.shape
+    size, wide = w_out.shape
+    vmem = pl.BlockSpec(memory_space=pltpu.VMEM)
+    slots = 4 * (batches - 1) + 2 * (batches - 1) + others * (count + 3)
+    sems = pltpu.SemaphoreType.DMA((slots,))
+    return pl.pallas_call(
+        functools.partial(entry_kernel, count, batches),
+        out_shape=[
+            jax.ShapeDtypeStruct((rows, width), BF),
+            jax.ShapeDtypeStruct((rows, size), BF),
+            jax.ShapeDtypeStruct((rows, size), F32),
+            jax.ShapeDtypeStruct((batches * rows, 2 * size), BF),
+            jax.ShapeDtypeStruct((width, 4 * size), BF),
+            jax.ShapeDtypeStruct((count * size, batches * wide), BF),
+            jax.ShapeDtypeStruct((batches, *gains.shape), F32),
+            jax.ShapeDtypeStruct((batches, *segments.shape), jnp.int32),
+        ],
+        in_specs=[vmem] * 5,
+        out_specs=[vmem] * 8,
+        scratch_shapes=[sems, sems, pltpu.SemaphoreType.DMA((4,))],
+        compiler_params=pltpu.CompilerParams(
+            collective_id=collective_id, has_side_effects=True, vmem_limit_bytes=VMEM_LIMIT
+        ),
+        name="entry",
+    )(tokens, w_shard, w_out, gains, segments)
+
+
 KEY_BLOCK = 512
 QUERY_BLOCK = 256
 
@@ -795,12 +1003,6 @@
     return block
 
 
-def from_partner(block, axis):
-    count = lax.axis_size(axis)
-    route = [(at, at ^ 1) for at in range(count)]
-    return lax.ppermute(block, axis, route)
-
-
 def matmul(left, right):
     return jnp.dot(left, right, preferred_element_type=F32)
 
@@ -815,10 +1017,6 @@
 
 def rms_scale(values):
     return lax.rsqrt(jnp.mean(values * values, axis=1, keepdims=True) + EPSILON)
-
-
-def order_halves(own, mate, first):
-    return jnp.where(first, jnp.concatenate([own, mate], 1), jnp.concatenate([mate, own], 1))
 
 
 def per_device(
@@ -842,42 +1040,20 @@
     head_size = w_query.shape[1]
     half = w_key.shape[1]
     chunk = row_count // heads
-    first = lax.axis_index("head") % 2 == 0
     me = ring_place(lax.axis_index("head"), heads)
     scale_factor = 1.0 / math.sqrt(head_size)
 
-    kv_shard = jnp.concatenate([w_key, w_value], axis=1)
-    kv_mate = from_partner(kv_shard, "head")
-    w_in = jnp.concatenate(
-        [
-            w_query,
-            order_halves(w_key, kv_mate[:, :half], first),
-            order_halves(w_value, kv_mate[:, half:], first),
-            w_gate,
-        ],
-        axis=1,
+    w_shard = jnp.concatenate([w_query, w_gate, w_key, w_value], axis=1)
+    gains = jnp.concatenate([norm1_gain, norm2_gain]).reshape(-1, 128).astype(F32)
+    normed_one, queries, gate_logit, kv_all, w_in, out_full, gains, seg_all = entry(
+        tokens, w_shard, w_out, gains, segment_ids.reshape(-1, 128), 1
     )
-    w_in = lax.all_gather(w_in, "batch", axis=0, tiled=True)
-    gains = lax.all_gather(jnp.stack([norm1_gain, norm2_gain]), "batch", axis=1, tiled=True)
-    gain_one = gains[0].astype(F32)
-    gain_two = gains[1].astype(F32)
+    seg_all = seg_all.reshape(-1)
+    gains = gains.reshape(batches, 2, -1).transpose(1, 0, 2).reshape(2, width)
+    gain_one, gain_two = gains[0], gains[1]
     mgate_full = lax.all_gather(w_mlp_gate, "batch", axis=0, tiled=True)
     mup_full = lax.all_gather(w_mlp_up, "batch", axis=0, tiled=True)
-    down_full = lax.all_gather(w_down, "batch", axis=1, tiled=True)
-
-    inputs = tokens.astype(F32)
-    recip_one = rms_scale(inputs)
-    normed_one = (inputs * recip_one * gain_one).astype(BF)
-    projected = matmul(normed_one, w_in)
-    queries = projected[:, :head_size].astype(BF)
-    kv_local = projected[:, head_size : 3 * head_size].astype(BF)
-    gate_logit = projected[:, 3 * head_size :]
-    out_rows, kv_all, seg_all = spread(
-        [w_out, kv_local, segment_ids.reshape(-1, 128)],
-        (("head", "rows"), ("batch", "rows"), ("batch", "lead")),
-        1,
-    )
-    seg_all = seg_all.reshape(-1)
+
     base = lax.axis_index("batch") * row_count
     ids = jnp.arange(DOCUMENTS, dtype=jnp.int32)
     below = jnp.sum((seg_all[None, :] < ids[:, None]).astype(jnp.int32), axis=1)
@@ -897,7 +1073,7 @@
         pair_flops,
         "attend",
     )
-    mixed_all, out_full = spread([mixed, out_rows], (("head", "cols"), ("batch", "cols")), 2)
+    mixed_all, down_full = spread([mixed, w_down], (("head", "cols"), ("batch", "cols")), 2)
     normed_two, hidden, d_pre, mlp_part, resid_own, d_resid, d_resid_low, d_gain_two, d_mixed = mlp_back(
         tokens, mixed_all, out_grad, gain_two[None], out_full, mgate_full, mup_full, down_full, 3
     )
@@ -934,23 +1110,15 @@
     out_total = out_state
     d_kv, out_total = lax.optimization_barrier((d_kv, out_total))
     output = flow_spread((resid_own + out_total).astype(BF))
-    d_cat = jnp.concatenate([d_queries, d_kv, d_gate_logit], axis=1)
+    d_cat = jnp.concatenate([d_queries, d_gate_logit, d_kv], axis=1)
     d_out_part = rows_inner(mixed_own, d_resid_low).astype(BF)
     d_out_part = lax.psum_scatter(d_out_part, "batch", scatter_dimension=1, tiled=True)
     d_out = flow_sum(d_out_part)
-    w_key_own = jnp.where(
-        first, w_in[:, head_size : head_size + half], w_in[:, head_size + half : 2 * head_size]
-    )
-    w_value_own = jnp.where(
-        first, w_in[:, 2 * head_size : 2 * head_size + half], w_in[:, 2 * head_size + half : 3 * head_size]
-    )
-    w_cat = jnp.concatenate(
-        [w_in[:, :head_size], w_key_own, w_value_own, w_in[:, 3 * head_size :]], axis=1
-    )
+    w_cat = w_in[:, : 3 * head_size]
     dn1_part = cols_inner(d_cat, w_cat).astype(BF)
     dn1 = flow_sum(dn1_part)
-    inputs_own = lax.dynamic_slice_in_dim(inputs, me * chunk, chunk, 0)
-    recip_in = lax.dynamic_slice_in_dim(recip_one, me * chunk, chunk, 0)
+    inputs_own = lax.dynamic_slice_in_dim(tokens, me * chunk, chunk, 0).astype(F32)
+    recip_in = rms_scale(inputs_own)
     d_gain_one = jnp.sum(dn1 * inputs_own * recip_in, axis=0)
     weighted_one = gain_one * dn1
     d_tokens = (
@@ -970,9 +1138,9 @@
         d_tokens,
         d_gains[0],
         d_in[:, :head_size],
-        d_in[:, head_size : head_size + half],
-        d_in[:, head_size + half : 2 * head_size],
-        d_in[:, 2 * head_size :],
+        d_in[:, 2 * head_size : 2 * head_size + half],
+        d_in[:, 2 * head_size + half :],
+        d_in[:, head_size : 2 * head_size],
         d_out,
         d_gains[1],
         d_mlp[:, :hidden_own],

time: 576 us -> 536 us (0.931)
  other arithmetic: 39.9 us -> 28.9 us
  waiting for transfers between devices: 115 us -> 104 us
    pallas_call x0 -> x1, Pallas kernels: none -> 70.4 us  [entry(): pl.pallas_call(functools.partial(entry_kernel, count, batches), out_shape...]
    pallas_call x2 -> x1, Pallas kernels: 125 us -> 58.3 us  [spread(): pl.pallas_call(functools.partial(spread_kernel, count, batches, plans), o...]
    all_gather x2 -> x0, waiting for transfers between devices: 12 us -> none  [the longest x1 12 us: per_device(): w_in = lax.all_gather(w_in, 'batch', axis=0, tiled=True)]
    ppermute x6, waiting for transfers between devices: 26.7 us -> 36 us  [flow_spread(): going = lax.ppermute(going, 'head', right)]
    convert_element_type x2 -> x1, other arithmetic: 8.49 us -> 1.3 us  [per_device(): jnp.concatenate([norm1_gain, norm2_gain]).reshape(-1, 128).astype(F32)]
  transfers between devices with their start and end apart: 54 -> 51, of which waited for: 21 -> 20; matrix products, arithmetic and copies ran while one was open for 17% -> 16% of each run, Pallas kernels for 30% -> 33%
where the time goes in v8:
time: 536 us; the launch traced here: 535 us
  Pallas kernels  264 us (49%)
  waiting for transfers between devices  104 us (19%)
  starting transfers between devices  47.1 us (9%)
  local copies, waits for them, and re-layouts  38.6 us (7%)
  matrix products  36.8 us (7%)
  other arithmetic  28.9 us (5%)
  between operations  14.7 us (3%)
    pallas_call x1, Pallas kernels, mlp_back(): pl.pallas_call(functools.partial(mlp_kernel, count), out_shape=[jax.Shape...  86.8 us
    pallas_call x1, Pallas kernels, entry(): pl.pallas_call(functools.partial(entry_kernel, count, batches), out_shape...  70.4 us
    pallas_call x1, Pallas kernels, spread(): pl.pallas_call(functools.partial(spread_kernel, count, batches, plans), o...  58.3 us
    ppermute x6, waiting for transfers between devices, flow_spread(): going = lax.ppermute(going, 'head', right)  36 us
    dot_general x4, matrix products, rows_inner(): lax.dot_general(left, right, (((0,), (0,)), ((), ())), preferred_element_...  32 us
    pallas_call x1, Pallas kernels, fold(): pl.pallas_call(functools.partial(fold_kernel, batches), out_shape=jax.Sha...  28.2 us
    ppermute x12, waiting for transfers between devices, flow_steps(): from_left = lax.ppermute(going, 'head', right)  27.3 us
    ppermute x12, waiting for transfers between devices, flow_steps(): from_right = lax.ppermute(coming, 'head', left)  22.5 us
  transfers between devices with their start and end apart: 51, of which 20 were waited for; matrix products, arithmetic and copies ran while one was open for 16% of the time, Pallas kernels for 33%

profile of v8, /device:TPU:0, one launch (start us, length us, event | category | flops | bytes accessed | tf_op | source)
XLA Modules:
  0.0 534.9 jit_solution(11445134527958338035)
XLA Ops:
  13.9 70.4 %entry.1 = (bf16[1280,2048]{1,0:T(8,128)(2,1)}, bf16[1280,128]{1,0:T(8,128)(2,1)}, f32[1280,128]{1,0:T(8,128)}, bf16[5120,256]{1,0:T(8,128)(2,1)}, bf16[2048,512...) custom-call(bf16[1280,2048]{1,0:T(8,128)(2,1)} %x_hbm.1, ...), custom_call_target="tpu_custom_call" | custom-call | tf_op jit(solution)/shard_map/entry/pallas_call | solution.py:660
  87.3 8.8 %attend.1 = (f32[1280,128]{1,0:T(8,128)}, bf16[1280,128]{1,0:T(8,128)(2,1)}, f32[1,1280]{1,0:T(1,128)}) custom-call(s32[1280]{0:T(1024)} %copy-done.9, s32[1]{0:T(128)} %bitcast.3.base_sm, bf16[1280,128]{1,0:T(8,128)(2,1)} %get-tuple-element.54.q_ref, bf16[5120,256]{1,0:T(8,128)(2,1)} %get-tuple-element.55.kv_ref, s32[1,1280]{1,0:T(1,128)} %broadcast_in_dim.24.start_ref, ...), custom_call_target="tpu_custom_call" | custom-call | flops 3355443200 | bytes 8388608 | tf_op jit(solution)/shard_map/attend/pallas_call | solution.py:896
  96.0 58.3 %spread_2.1 = (bf16[1280,1024]{1,0:T(8,128)(2,1)}, bf16[768,2048]{1,0:T(8,128)(2,1)}) custom-call(bf16[1280,128]{1,0:T(8,128)(2,1)} %get-tuple-element.57.refs_0_, bf16[768,512]{1,0:T(8,128)(2,1)} %refs_1_.1), custom_call_target="tpu_custom_call" | custom-call | tf_op jit(solution)/shard_map/spread_2/pallas_call | solution.py:164
  154.4 86.8 %mlp_back.1 = (bf16[1280,2048]{1,0:T(8,128)(2,1)}, bf16[1280,768]{1,0:T(8,128)(2,1)}, bf16[1280,1536]{1,0:T(8,128)(2,1)}, bf16[1280,2048]{1,0:T(8,128)(2,1)}, f3...) custom-call(bf16[1280,2048]{1,0:T(8,128)(2,1)} %x_hbm.1, ...), custom_call_target="tpu_custom_call" | custom-call | flops 29527900160 | bytes 41943040 | tf_op jit(solution)/shard_map/mlp_back/pallas_call | solution.py:442
  244.8 8.1 %convolution_convert_fusion.3 = bf16[768,2048]{1,0:T(8,128)(2,1)} fusion(bf16[1280,768]{1,0:T(8,128)(2,1)S(1)} %copy-done.11, bf16[1280,2048]{1,0:T(8,128)(2,1)} %dy_hbm.1), kind=kOutput, calls=%fused_computation.3 | convolution fusion | flops 4028104704 | bytes 10354688 | tf_op jit(solution)/shard_map/dot_general | solution.py:1011
  256.6 12.7 %convolution_convert_fusion.1 = bf16[2048,1536]{1,0:T(8,128)(2,1)} fusion(bf16[1280,2048]{1,0:T(8,128)(2,1)} %get-tuple-element.68, bf16[1280,1536]{1,0:T(8,128)(2,1)S(1)} %copy-done.12), kind=kOutput, calls=%fused_computation.1 | convolution fusion | flops 8056209408 | bytes 15466496 | tf_op jit(solution)/shard_map/dot_general | solution.py:1011
  273.1 11.8 %attend_back.1 = (bf16[1280,128]{1,0:T(8,128)(2,1)}, bf16[1280,128]{1,0:T(8,128)(2,1)}, bf16[5120,256]{1,0:T(8,128)(2,1)}) custom-call(s32[1280]{0:T(1024)} %copy-done.9, s32[1]{0:T(128)} %bitcast.3.base_sm, bf16[1280,128]{1,0:T(8,128)(2,1)} %get-tuple-element.54.q_ref, bf16[5120,256]{1,0:T(8,128)(2,1)} %get-tuple-element.55.kv_ref, ...), custom_call_target="tpu_custom_call" | custom-call | flops 8388608000 | bytes 8388608 | tf_op jit(solution)/shard_map/attend_back/pallas_call | solution.py:896
  290.4 28.2 %fold.1 = bf16[1280,128]{1,0:T(8,128)(2,1)} custom-call(bf16[5120,256]{1,0:T(8,128)(2,1)} %get-tuple-element.80.part_ref), custom_call_target="tpu_custom_call" | custom-call | tf_op jit(solution)/shard_map/fold/pallas_call | solution.py:871
  320.8 6.9 %convolution_convert_fusion.4 = bf16[2048,384]{1,0:T(8,128)(2,1)} fusion(bf16[1280,2048]{1,0:T(8,128)(2,1)} %get-tuple-element.90, bf16[1280,384]{1,0:T(8,128)(2,1)} %constant_dynamic-update-slice_fusion.14), kind=kOutput, calls=%fused_computation.4 | convolution fusion | flops 2014052352 | bytes 7798784 | tf_op jit(solution)/shard_map/dot_general | solution.py:1011
  327.8 4.3 convolution_convert_fusion.2
  333.3 4.8 convolution_convert_fusion
  340.4 3.0 broadcast.51.clone
  352.1 10.8 %collective-permute-done.8 = bf16[160,2048]{1,0:T(8,128)(2,1)S(1)} collective-permute-done((bf16[160,2048]{1,0:T(8,128)(2,1)S(1)}, bf16[160,2048]{1,0:T(8,128)(2,1)S(1)}, u32[]{:S(2)}, u32[]{:S(2)}) %collective-permute-start.8) | collective-permute-done | bytes 655392 | tf_op jit(solution)/shard_map/ppermute | solution.py:967
  365.0 12.7 %collective-permute-done.21 = bf16[160,2048]{1,0:T(8,128)(2,1)S(1)} collective-permute-done((bf16[160,2048]{1,0:T(8,128)(2,1)S(1)}, bf16[160,2048]{1,0:T(8,128)(2,1)S(1)}, u32[]{:S(2)}, u32[]{:S(2)}) %collective-permute-start.21) | collective-permute-done | bytes 655392 | tf_op jit(solution)/shard_map/ppermute | solution.py:933
  384.7 6.5 %collective-permute-done.10 = bf16[160,2048]{1,0:T(8,128)(2,1)} collective-permute-done((bf16[160,2048]{1,0:T(8,128)(2,1)S(1)}, bf16[160,2048]{1,0:T(8,128)(2,1)}, u32[]{:S(2)}, u32[]{:S(2)}) %collective-permute-start.10) | collective-permute-done | bytes 655392 | tf_op jit(solution)/shard_map/ppermute | solution.py:967
  393.2 11.9 %collective-permute-done.18 = bf16[160,2048]{1,0:T(8,128)(2,1)S(1)} collective-permute-done((bf16[160,2048]{1,0:T(8,128)(2,1)}, bf16[160,2048]{1,0:T(8,128)(2,1)S(1)}, u32[]{:S(2)}, u32[]{:S(2)}) %collective-permute-start.18) | collective-permute-done | bytes 655392 | tf_op jit(solution)/shard_map/ppermute | solution.py:932
  414.9 4.2 collective-permute-done.12
  421.3 11.9 %collective-permute-done.19 = bf16[160,2048]{1,0:T(8,128)(2,1)S(1)} collective-permute-done((bf16[160,2048]{1,0:T(8,128)(2,1)S(1)}, bf16[160,2048]{1,0:T(8,128)(2,1)S(1)}, u32[]{:S(2)}, u32[]{:S(2)}) %collective-permute-start.19) | collective-permute-done | bytes 655392 | tf_op jit(solution)/shard_map/ppermute | solution.py:941
  442.4 3.0 broadcast.51.clone.1
  452.0 12.7 %collective-permute-done.35 = f32[2,512]{1,0:T(2,128)S(1)} collective-permute-done((f32[2,512]{1,0:T(2,128)S(1)}, f32[2,512]{1,0:T(2,128)S(1)}, u32[]{:S(2)}, u32[]{:S(2)}) %collective-permute-start.35) | collective-permute-done | bytes 4128 | tf_op jit(solution)/shard_map/ppermute | solution.py:981
  474.7 9.5 %collective-permute-done.26 = bf16[160,2048]{1,0:T(8,128)(2,1)} collective-permute-done((bf16[160,2048]{1,0:T(8,128)(2,1)S(1)}, bf16[160,2048]{1,0:T(8,128)(2,1)}, u32[]{:S(2)}, u32[]{:S(2)}) %collective-permute-start.26) | collective-permute-done | bytes 655392 | tf_op jit(solution)/shard_map/ppermute | solution.py:967
  495.5 4.9 collective-permute-done.28
  505.8 5.4 %collective-permute-done.42 = bf16[128,512]{1,0:T(8,128)(2,1)S(1)} collective-permute-done((bf16[128,512]{1,0:T(8,128)(2,1)S(1)}, bf16[128,512]{1,0:T(8,128)(2,1)S(1)}, u32[]{:S(2)}, u32[]{:S(2)}) %collective-permute-start.42) | collective-permute-done | bytes 131104 | tf_op jit(solution)/shard_map/ppermute | solution.py:933
  524.7 3.3 fusion.13
  (204 shorter events, 119.4 us)
Async XLA Ops:
  7.2 147.2 %all-gather.3.cloned.1.call-start = ((), (), s32[]{:S(2)}) async-start(), calls=%async_computation.4 | async-start | bytes 3932160 | tf_op jit(solution)/shard_map/all_gather | solution.py:1054
  7.9 146.5 %all-gather.5.cloned.1.call-start = ((), (), s32[]{:S(2)}) async-start(), calls=%async_computation.5 | async-start | bytes 3932160 | tf_op jit(solution)/shard_map/all_gather | solution.py:1055
  8.7 464.9 %reduce-scatter.5.cloned.1.call-start = ((), (), s32[]{:S(2)}) async-start(), calls=%async_computation.6 | async-start | bytes 1966080 | tf_op jit(solution)/shard_map/reduce_scatter | solution.py:1132
  286.8 31.8 %collective-permute-start.6 = (bf16[160,2048]{1,0:T(8,128)(2,1)S(1)}, bf16[160,2048]{1,0:T(8,128)(2,1)S(1)}, u32[]{:S(2)}, u32[]{:S(2)}) collective-permute-start(bf16[160,2048]{1,0:T(8,128)(2,1)S(1)} %get-tuple-element.81), channel_id=1, source_target_pairs={{0,2},{2,4},{4,6},{6,7},{7,5},{5,3},{3,1},{1,0},{8,10},{10,12},{12... | collective-permute-start | bytes 1966088 | tf_op jit(solution)/shard_map/ppermute | solution.py:941
  287.8 30.8 %collective-permute-start.7 = (bf16[160,2048]{1,0:T(8,128)(2,1)S(1)}, bf16[160,2048]{1,0:T(8,128)(2,1)S(1)}, u32[]{:S(2)}, u32[]{:S(2)}) collective-permute-start(bf16[160,2048]{1,0:T(8,128)(2,1)S(1)} %get-tuple-element.82), channel_id=1, source_target_pairs={{0,1},{2,0},{4,2},{6,4},{7,6},{5,7},{3,5},{1,3},{8,9},{10,8},{12,1... | collective-permute-start | bytes 1966088 | tf_op jit(solution)/shard_map/ppermute | solution.py:942
  327.7 163.8 %reduce-scatter.7.cloned.1.call-start = ((), (), s32[]{:S(2)}) async-start(), calls=%async_computation.7 | async-start | bytes 5242880 | tf_op jit(solution)/shard_map/reduce_scatter | solution.py:1115
  332.1 182.1 %reduce-scatter.11.cloned.1.call-start = ((), (), s32[]{:S(2)}) async-start(), calls=%async_computation.9 | async-start | bytes 3932160 | tf_op jit(solution)/shard_map/reduce_scatter | solution.py:1089
  332.7 192.0 %reduce-scatter.9.cloned.1.call-start = ((), (), s32[]{:S(2)}) async-start(), calls=%async_computation.8 | async-start | bytes 7864320 | tf_op jit(solution)/shard_map/reduce_scatter | solution.py:1090
  349.9 27.8 %collective-permute-start.21 = (bf16[160,2048]{1,0:T(8,128)(2,1)S(1)}, bf16[160,2048]{1,0:T(8,128)(2,1)S(1)}, u32[]{:S(2)}, u32[]{:S(2)}) collective-permute-start(bf16[160,2048]{1,0:T(8,128)(2,1)S(1)} %pad_maximum_fusion.3), channel_id=1, source_target_pairs={{0,1},{2,0},{4,2},{6,4},{7,6},{5,7},{3,5},{1,3},{8,9},{10,8},{12,1... | collective-permute-start | bytes 1966088 | tf_op jit(solution)/shard_map/ppermute | solution.py:933
  351.4 26.3 %collective-permute-start.17 = (bf16[160,2048]{1,0:T(8,128)(2,1)S(1)}, bf16[160,2048]{1,0:T(8,128)(2,1)S(1)}, u32[]{:S(2)}, u32[]{:S(2)}) collective-permute-start(bf16[160,2048]{1,0:T(8,128)(2,1)S(1)} %pad_maximum_fusion.2), channel_id=1, source_target_pairs={{0,2},{2,4},{4,6},{6,7},{7,5},{5,3},{3,1},{1,0},{8,10},{10,12},{12... | collective-permute-start | bytes 1966088 | tf_op jit(solution)/shard_map/ppermute | solution.py:932
  363.0 28.2 %collective-permute-start.10 = (bf16[160,2048]{1,0:T(8,128)(2,1)S(1)}, bf16[160,2048]{1,0:T(8,128)(2,1)}, u32[]{:S(2)}, u32[]{:S(2)}) collective-permute-start(bf16[160,2048]{1,0:T(8,128)(2,1)S(1)} %collective-permute-done.8), channel_id=1, source_target_pairs={{0,2},{2,4},{4,6},{6,7},{7,5},{5,3},{3,1},{1,0},{8,10},{10,12},{12... | collective-permute-start | bytes 1966088 | tf_op jit(solution)/shard_map/ppermute | solution.py:967
  363.9 28.2 %collective-permute-start.11 = (bf16[160,2048]{1,0:T(8,128)(2,1)S(1)}, bf16[160,2048]{1,0:T(8,128)(2,1)}, u32[]{:S(2)}, u32[]{:S(2)}) collective-permute-start(bf16[160,2048]{1,0:T(8,128)(2,1)S(1)} %collective-permute-done.9), channel_id=1, source_target_pairs={{0,1},{2,0},{4,2},{6,4},{7,6},{5,7},{3,5},{1,3},{8,9},{10,8},{12,1... | collective-permute-start | bytes 1966088 | tf_op jit(solution)/shard_map/ppermute | solution.py:968
  379.3 25.8 %collective-permute-start.18 = (bf16[160,2048]{1,0:T(8,128)(2,1)}, bf16[160,2048]{1,0:T(8,128)(2,1)S(1)}, u32[]{:S(2)}, u32[]{:S(2)}) collective-permute-start(bf16[160,2048]{1,0:T(8,128)(2,1)} %get-tuple-element.138), channel_id=1, source_target_pairs={{0,2},{2,4},{4,6},{6,7},{7,5},{5,3},{3,1},{1,0},{8,10},{10,12},{12... | collective-permute-start | bytes 1966088 | tf_op jit(solution)/shard_map/ppermute | solution.py:932
  380.5 25.4 %collective-permute-start.22 = (bf16[160,2048]{1,0:T(8,128)(2,1)}, bf16[160,2048]{1,0:T(8,128)(2,1)}, u32[]{:S(2)}, u32[]{:S(2)}) collective-permute-start(bf16[160,2048]{1,0:T(8,128)(2,1)} %get-tuple-element.139), channel_id=1, source_target_pairs={{0,1},{2,0},{4,2},{6,4},{7,6},{5,7},{3,5},{1,3},{8,9},{10,8},{12,1... | collective-permute-start | bytes 1966088 | tf_op jit(solution)/shard_map/ppermute | solution.py:933
  391.2 28.0 %collective-permute-start.12 = (bf16[160,2048]{1,0:T(8,128)(2,1)}, bf16[160,2048]{1,0:T(8,128)(2,1)S(1)}, u32[]{:S(2)}, u32[]{:S(2)}) collective-permute-start(bf16[160,2048]{1,0:T(8,128)(2,1)} %collective-permute-done.10), channel_id=1, source_target_pairs={{0,2},{2,4},{4,6},{6,7},{7,5},{5,3},{3,1},{1,0},{8,10},{10,12},{12... | collective-permute-start | bytes 1966088 | tf_op jit(solution)/shard_map/ppermute | solution.py:967
  392.1 28.1 %collective-permute-start.13 = (bf16[160,2048]{1,0:T(8,128)(2,1)}, bf16[160,2048]{1,0:T(8,128)(2,1)S(1)}, u32[]{:S(2)}, u32[]{:S(2)}) collective-permute-start(bf16[160,2048]{1,0:T(8,128)(2,1)} %collective-permute-done.11), channel_id=1, source_target_pairs={{0,1},{2,0},{4,2},{6,4},{7,6},{5,7},{3,5},{1,3},{8,9},{10,8},{12,1... | collective-permute-start | bytes 1966088 | tf_op jit(solution)/shard_map/ppermute | solution.py:968
  407.9 25.3 %collective-permute-start.19 = (bf16[160,2048]{1,0:T(8,128)(2,1)S(1)}, bf16[160,2048]{1,0:T(8,128)(2,1)S(1)}, u32[]{:S(2)}, u32[]{:S(2)}) collective-permute-start(bf16[160,2048]{1,0:T(8,128)(2,1)S(1)} %get-tuple-element.136), channel_id=1, source_target_pairs={{0,2},{2,4},{4,6},{6,7},{7,5},{5,3},{3,1},{1,0},{8,10},{10,12},{12... | collective-permute-start | bytes 1966088 | tf_op jit(solution)/shard_map/ppermute | solution.py:941
  409.1 24.8 %collective-permute-start.23 = (bf16[160,2048]{1,0:T(8,128)(2,1)S(1)}, bf16[160,2048]{1,0:T(8,128)(2,1)S(1)}, u32[]{:S(2)}, u32[]{:S(2)}) collective-permute-start(bf16[160,2048]{1,0:T(8,128)(2,1)S(1)} %get-tuple-element.137), channel_id=1, source_target_pairs={{0,1},{2,0},{4,2},{6,4},{7,6},{5,7},{3,5},{1,3},{8,9},{10,8},{12,1... | collective-permute-start | bytes 1966088 | tf_op jit(solution)/shard_map/ppermute | solution.py:942
  419.2 46.9 %collective-permute-start.14 = (bf16[160,1024]{1,0:T(8,128)(2,1)S(1)}, bf16[160,1024]{1,0:T(8,128)(2,1)}, u32[]{:S(2)}, u32[]{:S(2)}) collective-permute-start(bf16[160,1024]{1,0:T(8,128)(2,1)S(1)} %slice.138), channel_id=1, source_target_pairs={{0,2},{2,4},{4,6},{6,7},{7,5},{5,3},{3,1},{1,0},{8,10},{10,12},{12... | collective-permute-start | bytes 983048 | tf_op jit(solution)/shard_map/ppermute | solution.py:970
  420.1 46.0 %collective-permute-start.15 = (bf16[160,1024]{1,0:T(8,128)(2,1)S(1)}, bf16[160,1024]{1,0:T(8,128)(2,1)}, u32[]{:S(2)}, u32[]{:S(2)}) collective-permute-start(bf16[160,1024]{1,0:T(8,128)(2,1)S(1)} %slice.139), channel_id=1, source_target_pairs={{0,1},{2,0},{4,2},{6,4},{7,6},{5,7},{3,5},{1,3},{8,9},{10,8},{12,1... | collective-permute-start | bytes 983048 | tf_op jit(solution)/shard_map/ppermute | solution.py:971
  448.1 21.7 %collective-permute-start.24 = (bf16[160,2048]{1,0:T(8,128)(2,1)S(1)}, bf16[160,2048]{1,0:T(8,128)(2,1)S(1)}, u32[]{:S(2)}, u32[]{:S(2)}) collective-permute-start(bf16[160,2048]{1,0:T(8,128)(2,1)S(1)} %get-tuple-element.133), channel_id=1, source_target_pairs={{0,2},{2,4},{4,6},{6,7},{7,5},{5,3},{3,1},{1,0},{8,10},{10,12},{12... | collective-permute-start | bytes 1966088 | tf_op jit(solution)/shard_map/ppermute | solution.py:967
  449.0 21.0 %collective-permute-start.25 = (bf16[160,2048]{1,0:T(8,128)(2,1)S(1)}, bf16[160,2048]{1,0:T(8,128)(2,1)S(1)}, u32[]{:S(2)}, u32[]{:S(2)}) collective-permute-start(bf16[160,2048]{1,0:T(8,128)(2,1)S(1)} %get-tuple-element.133), channel_id=1, source_target_pairs={{0,1},{2,0},{4,2},{6,4},{7,6},{5,7},{3,5},{1,3},{8,9},{10,8},{12,1... | collective-permute-start | bytes 1966088 | tf_op jit(solution)/shard_map/ppermute | solution.py:968
  500.5 19.6 %collective-permute-start.30 = (bf16[160,1024]{1,0:T(8,128)(2,1)S(1)}, bf16[160,1024]{1,0:T(8,128)(2,1)}, u32[]{:S(2)}, u32[]{:S(2)}) collective-permute-start(bf16[160,1024]{1,0:T(8,128)(2,1)S(1)} %slice.141), channel_id=1, source_target_pairs={{0,2},{2,4},{4,6},{6,7},{7,5},{5,3},{3,1},{1,0},{8,10},{10,12},{12... | collective-permute-start | bytes 983048 | tf_op jit(solution)/shard_map/ppermute | solution.py:970
  501.2 18.9 %collective-permute-start.31 = (bf16[160,1024]{1,0:T(8,128)(2,1)S(1)}, bf16[160,1024]{1,0:T(8,128)(2,1)S(1)}, u32[]{:S(2)}, u32[]{:S(2)}) collective-permute-start(bf16[160,1024]{1,0:T(8,128)(2,1)S(1)} %slice.142), channel_id=1, source_target_pairs={{0,1},{2,0},{4,2},{6,4},{7,6},{5,7},{3,5},{1,3},{8,9},{10,8},{12,1... | collective-permute-start | bytes 983048 | tf_op jit(solution)/shard_map/ppermute | solution.py:971
  (40 other events, 469.8 us)
Sparse Core Ops, SparseCore 0:
  9.6 45.4 all-gather.2
  56.6 31.6 all-gather.4
  327.8 27.5 reduce-scatter.4
  358.0 44.4 reduce-scatter.6
  404.9 38.0 reduce-scatter.10
  445.5 58.3 reduce-scatter.8

commit v9 on v8

--- a/solution.py
+++ b/solution.py
@@ -472,8 +472,8 @@
 
 
 def entry_kernel(
-    count, batches, x_ref, w_ref, out_ref, gain_ref, seg_ref,
-    n1_ref, q_ref, logit_ref, kv_ref, w_all, out_all, gain_all, seg_all,
+    count, batches, x_ref, w_ref, out_ref, gain_ref, seg_ref, down_ref,
+    n1_ref, q_ref, logit_ref, kv_ref, w_all, out_all, gain_all, seg_all, down_all,
     send_sem, recv_sem, local_sem,
 ):
     steps = count // 2
@@ -610,6 +610,12 @@
     def kv_view(at):
         return kv_ref.at[part(at, rows)]
 
+    def down_view(at):
+        return down_all.at[:, part(at, down_ref.shape[1])]
+
+    down_out, down_twin = both(down_view, down_ref)
+    stay(down_ref, down_view(batch))
+
     @pl.loop(0, blocks)
     def _(at):
         here = part(at, block)
@@ -635,6 +641,8 @@
     for step in range(2, steps):
         ring(step)
     kv_passed = pass_on(kv_view, kv_out)
+    down_passed = pass_on(down_view, down_out)
+    local[-1].wait()
     for pair in flows:
         for copy in pair:
             copy.wait_recv()
@@ -642,20 +650,21 @@
     for hop in range(others):
         there = out_all.at[:, part(spots[hop] * 2 + core, wide)]
         swaps.append(go(there, there, twin))
-    for copy in (*kv_twin, *kv_passed, *swaps):
+    for copy in (*kv_twin, *kv_passed, *swaps, *down_twin, *down_passed):
         copy.wait_recv()
     for copy in copies:
         copy.wait_send()
 
 
-def entry(tokens, w_shard, w_out, gains, segments, collective_id):
+def entry(tokens, w_shard, w_out, gains, segments, w_down, collective_id):
     count = lax.axis_size("head")
     batches = lax.axis_size("batch")
     others = batches // 2
     rows, width = tokens.shape
     size, wide = w_out.shape
     vmem = pl.BlockSpec(memory_space=pltpu.VMEM)
-    slots = 4 * (batches - 1) + 2 * (batches - 1) + others * (count + 3)
+    hbm = pl.BlockSpec(memory_space=pl.ANY)
+    slots = 6 * batches + others * (count + 3)
     sems = pltpu.SemaphoreType.DMA((slots,))
     return pl.pallas_call(
         functools.partial(entry_kernel, count, batches),
@@ -668,15 +677,16 @@
             jax.ShapeDtypeStruct((count * size, batches * wide), BF),
             jax.ShapeDtypeStruct((batches, *gains.shape), F32),
             jax.ShapeDtypeStruct((batches, *segments.shape), jnp.int32),
+            jax.ShapeDtypeStruct((w_down.shape[0], batches * w_down.shape[1]), BF),
         ],
-        in_specs=[vmem] * 5,
-        out_specs=[vmem] * 8,
-        scratch_shapes=[sems, sems, pltpu.SemaphoreType.DMA((4,))],
+        in_specs=[vmem] * 5 + [hbm],
+        out_specs=[vmem] * 8 + [hbm],
+        scratch_shapes=[sems, sems, pltpu.SemaphoreType.DMA((5,))],
         compiler_params=pltpu.CompilerParams(
             collective_id=collective_id, has_side_effects=True, vmem_limit_bytes=VMEM_LIMIT
         ),
         name="entry",
-    )(tokens, w_shard, w_out, gains, segments)
+    )(tokens, w_shard, w_out, gains, segments, w_down)
 
 
 KEY_BLOCK = 512
@@ -1045,9 +1055,10 @@
 
     w_shard = jnp.concatenate([w_query, w_gate, w_key, w_value], axis=1)
     gains = jnp.concatenate([norm1_gain, norm2_gain]).reshape(-1, 128).astype(F32)
-    normed_one, queries, gate_logit, kv_all, w_in, out_full, gains, seg_all = entry(
-        tokens, w_shard, w_out, gains, segment_ids.reshape(-1, 128), 1
+    normed_one, queries, gate_logit, kv_all, w_in, out_full, gains, seg_all, down_full = entry(
+        tokens, w_shard, w_out, gains, segment_ids.reshape(-1, 128), w_down, 1
     )
+    gains, w_mlp_gate, w_mlp_up = lax.optimization_barrier((gains, w_mlp_gate, w_mlp_up))
     seg_all = seg_all.reshape(-1)
     gains = gains.reshape(batches, 2, -1).transpose(1, 0, 2).reshape(2, width)
     gain_one, gain_two = gains[0], gains[1]
@@ -1073,7 +1084,7 @@
         pair_flops,
         "attend",
     )
-    mixed_all, down_full = spread([mixed, w_down], (("head", "cols"), ("batch", "cols")), 2)
+    (mixed_all,) = spread([mixed], (("head", "cols"),), 2)
     normed_two, hidden, d_pre, mlp_part, resid_own, d_resid, d_resid_low, d_gain_two, d_mixed = mlp_back(
         tokens, mixed_all, out_grad, gain_two[None], out_full, mgate_full, mup_full, down_full, 3
     )

time: 536 us -> 534 us (level)
  waiting for transfers between devices: 104 us -> 123 us
  Pallas kernels: 264 us -> 246 us
    pallas_call x1, Pallas kernels: 58.3 us -> 30.6 us  [spread(): pl.pallas_call(functools.partial(spread_kernel, count, batches, plans), o...]
    all_gather x1, waiting for transfers between devices: 0.02 us -> 17.8 us  [per_device(): mup_full = lax.all_gather(w_mlp_up, 'batch', axis=0, tiled=True)]
    pallas_call x1, Pallas kernels: 86.8 us -> 95.4 us  [mlp_back(): pl.pallas_call(functools.partial(mlp_kernel, count), out_shape=[jax.Shape...]
  transfers between devices with their start and end apart: 51 -> 51, of which waited for: 20 -> 22; matrix products, arithmetic and copies ran while one was open for 16% -> 15% of each run, Pallas kernels for 33% -> 15%
where the time goes in v9:
time: 534 us; the launch traced here: 535 us
  Pallas kernels  246 us (46%)
  waiting for transfers between devices  123 us (23%)
  starting transfers between devices  47.8 us (9%)
  local copies, waits for them, and re-layouts  37.8 us (7%)
  matrix products  36.8 us (7%)
  other arithmetic  28.8 us (5%)
  between operations  14.7 us (3%)
    pallas_call x1, Pallas kernels, mlp_back(): pl.pallas_call(functools.partial(mlp_kernel, count), out_shape=[jax.Shape...  95.4 us
    pallas_call x1, Pallas kernels, entry(): pl.pallas_call(functools.partial(entry_kernel, count, batches), out_shape...  69.4 us
    ppermute x6, waiting for transfers between devices, flow_spread(): going = lax.ppermute(going, 'head', right)  38.1 us
    dot_general x4, matrix products, rows_inner(): lax.dot_general(left, right, (((0,), (0,)), ((), ())), preferred_element_...  32 us
    pallas_call x1, Pallas kernels, fold(): pl.pallas_call(functools.partial(fold_kernel, batches), out_shape=jax.Sha...  31.9 us
    pallas_call x1, Pallas kernels, spread(): pl.pallas_call(functools.partial(spread_kernel, count, batches, plans), o...  30.6 us
    ppermute x12, waiting for transfers between devices, flow_steps(): from_left = lax.ppermute(going, 'head', right)  28.6 us
    ppermute x12, waiting for transfers between devices, flow_steps(): from_right = lax.ppermute(coming, 'head', left)  19.5 us
  transfers between devices with their start and end apart: 51, of which 22 were waited for; matrix products, arithmetic and copies ran while one was open for 15% of the time, Pallas kernels for 15%

profile of v9, /device:TPU:0, one launch (start us, length us, event | category | flops | bytes accessed | tf_op | source)
XLA Modules:
  0.0 535.0 jit_solution(2540111023116130962)
XLA Ops:
  12.3 69.4 %entry.1 = (bf16[1280,2048]{1,0:T(8,128)(2,1)}, bf16[1280,128]{1,0:T(8,128)(2,1)}, f32[1280,128]{1,0:T(8,128)}, bf16[5120,256]{1,0:T(8,128)(2,1)}, bf16[2048,512...) custom-call(bf16[1280,2048]{1,0:T(8,128)(2,1)} %x_hbm.1, ...), custom_call_target="tpu_custom_call" | custom-call | tf_op jit(solution)/shard_map/entry/pallas_call | solution.py:669
  84.2 7.6 %attend.1 = (f32[1280,128]{1,0:T(8,128)}, bf16[1280,128]{1,0:T(8,128)(2,1)}, f32[1,1280]{1,0:T(1,128)}) custom-call(s32[1280]{0:T(1024)} %copy-done.9, s32[1]{0:T(128)} %bitcast.3.base_sm, bf16[1280,128]{1,0:T(8,128)(2,1)} %get-tuple-element.56.q_ref, bf16[5120,256]{1,0:T(8,128)(2,1)} %get-tuple-element.57.kv_ref, s32[1,1280]{1,0:T(1,128)} %broadcast_in_dim.24.start_ref, ...), custom_call_target="tpu_custom_call" | custom-call | flops 3355443200 | bytes 8388608 | tf_op jit(solution)/shard_map/attend/pallas_call | solution.py:906
  91.9 30.6 %spread_2.1.a_hbm = bf16[1280,1024]{1,0:T(8,128)(2,1)} custom-call(bf16[1280,128]{1,0:T(8,128)(2,1)} %get-tuple-element.59.refs_0_), custom_call_target="tpu_custom_call" | custom-call | tf_op jit(solution)/shard_map/spread_2/pallas_call | solution.py:164
  123.2 17.8 %all-gather.5.cloned.1.call-done.up_w = bf16[2048,768]{1,0:T(8,128)(2,1)} async-done(((bf16[512,768]{1,0:T(8,128)(2,1)}), bf16[2048,768]{1,0:T(8,128)(2,1)}) %all-gather.5.cloned.1.call-update) | async-done | bytes 3145744 | tf_op jit(solution)/shard_map/all_gather | solution.py:1066
  141.0 95.4 %mlp_back.1 = (bf16[1280,2048]{1,0:T(8,128)(2,1)}, bf16[1280,768]{1,0:T(8,128)(2,1)}, bf16[1280,1536]{1,0:T(8,128)(2,1)}, bf16[1280,2048]{1,0:T(8,128)(2,1)}, f3...) custom-call(bf16[1280,2048]{1,0:T(8,128)(2,1)} %x_hbm.1, ...), custom_call_target="tpu_custom_call" | custom-call | flops 29527900160 | bytes 41943040 | tf_op jit(solution)/shard_map/mlp_back/pallas_call | solution.py:442
  239.9 8.2 %convolution_convert_fusion.3 = bf16[768,2048]{1,0:T(8,128)(2,1)} fusion(bf16[1280,768]{1,0:T(8,128)(2,1)S(1)} %copy-done.12, bf16[1280,2048]{1,0:T(8,128)(2,1)} %dy_hbm.1), kind=kOutput, calls=%fused_computation.3 | convolution fusion | flops 4028104704 | bytes 10354688 | tf_op jit(solution)/shard_map/dot_general | solution.py:1021
  251.8 12.6 %convolution_convert_fusion.1 = bf16[2048,1536]{1,0:T(8,128)(2,1)} fusion(bf16[1280,2048]{1,0:T(8,128)(2,1)} %get-tuple-element.72, bf16[1280,1536]{1,0:T(8,128)(2,1)S(1)} %copy-done.13), kind=kOutput, calls=%fused_computation.1 | convolution fusion | flops 8056209408 | bytes 15466496 | tf_op jit(solution)/shard_map/dot_general | solution.py:1021
  269.7 10.8 %attend_back.1 = (bf16[1280,128]{1,0:T(8,128)(2,1)}, bf16[1280,128]{1,0:T(8,128)(2,1)}, bf16[5120,256]{1,0:T(8,128)(2,1)}) custom-call(s32[1280]{0:T(1024)} %copy-done.9, s32[1]{0:T(128)} %bitcast.3.base_sm, bf16[1280,128]{1,0:T(8,128)(2,1)} %get-tuple-element.56.q_ref, bf16[5120,256]{1,0:T(8,128)(2,1)} %get-tuple-element.57.kv_ref, ...), custom_call_target="tpu_custom_call" | custom-call | flops 8388608000 | bytes 8388608 | tf_op jit(solution)/shard_map/attend_back/pallas_call | solution.py:906
  287.7 31.9 %fold.1 = bf16[1280,128]{1,0:T(8,128)(2,1)} custom-call(bf16[5120,256]{1,0:T(8,128)(2,1)} %get-tuple-element.84.part_ref), custom_call_target="tpu_custom_call" | custom-call | tf_op jit(solution)/shard_map/fold/pallas_call | solution.py:881
  321.9 6.9 %convolution_convert_fusion.4 = bf16[2048,384]{1,0:T(8,128)(2,1)} fusion(bf16[1280,2048]{1,0:T(8,128)(2,1)} %get-tuple-element.94, bf16[1280,384]{1,0:T(8,128)(2,1)} %constant_dynamic-update-slice_fusion.14), kind=kOutput, calls=%fused_computation.4 | convolution fusion | flops 2014052352 | bytes 7798784 | tf_op jit(solution)/shard_map/dot_general | solution.py:1021
  328.9 4.2 convolution_convert_fusion.2
  334.3 4.9 convolution_convert_fusion
  352.6 11.4 %collective-permute-done.8 = bf16[160,2048]{1,0:T(8,128)(2,1)S(1)} collective-permute-done((bf16[160,2048]{1,0:T(8,128)(2,1)S(1)}, bf16[160,2048]{1,0:T(8,128)(2,1)S(1)}, u32[]{:S(2)}, u32[]{:S(2)}) %collective-permute-start.8) | collective-permute-done | bytes 655392 | tf_op jit(solution)/shard_map/ppermute | solution.py:977
  366.1 11.7 %collective-permute-done.21 = bf16[160,2048]{1,0:T(8,128)(2,1)S(1)} collective-permute-done((bf16[160,2048]{1,0:T(8,128)(2,1)S(1)}, bf16[160,2048]{1,0:T(8,128)(2,1)S(1)}, u32[]{:S(2)}, u32[]{:S(2)}) %collective-permute-start.21) | collective-permute-done | bytes 655392 | tf_op jit(solution)/shard_map/ppermute | solution.py:943
  385.1 7.1 %collective-permute-done.10 = bf16[160,2048]{1,0:T(8,128)(2,1)} collective-permute-done((bf16[160,2048]{1,0:T(8,128)(2,1)S(1)}, bf16[160,2048]{1,0:T(8,128)(2,1)}, u32[]{:S(2)}, u32[]{:S(2)}) %collective-permute-start.10) | collective-permute-done | bytes 655392 | tf_op jit(solution)/shard_map/ppermute | solution.py:977
  394.3 11.8 %collective-permute-done.18 = bf16[160,2048]{1,0:T(8,128)(2,1)S(1)} collective-permute-done((bf16[160,2048]{1,0:T(8,128)(2,1)}, bf16[160,2048]{1,0:T(8,128)(2,1)S(1)}, u32[]{:S(2)}, u32[]{:S(2)}) %collective-permute-start.18) | collective-permute-done | bytes 655392 | tf_op jit(solution)/shard_map/ppermute | solution.py:942
  415.4 4.8 collective-permute-done.12
  422.4 11.8 %collective-permute-done.19 = bf16[160,2048]{1,0:T(8,128)(2,1)S(1)} collective-permute-done((bf16[160,2048]{1,0:T(8,128)(2,1)S(1)}, bf16[160,2048]{1,0:T(8,128)(2,1)S(1)}, u32[]{:S(2)}, u32[]{:S(2)}) %collective-permute-start.19) | collective-permute-done | bytes 655392 | tf_op jit(solution)/shard_map/ppermute | solution.py:951
  443.2 3.0 broadcast.51.clone.1
  453.6 12.7 %collective-permute-done.35 = f32[2,512]{1,0:T(2,128)S(1)} collective-permute-done((f32[2,512]{1,0:T(2,128)S(1)}, f32[2,512]{1,0:T(2,128)S(1)}, u32[]{:S(2)}, u32[]{:S(2)}) %collective-permute-start.35) | collective-permute-done | bytes 4128 | tf_op jit(solution)/shard_map/ppermute | solution.py:991
  476.2 9.8 %collective-permute-done.26 = bf16[160,2048]{1,0:T(8,128)(2,1)} collective-permute-done((bf16[160,2048]{1,0:T(8,128)(2,1)S(1)}, bf16[160,2048]{1,0:T(8,128)(2,1)}, u32[]{:S(2)}, u32[]{:S(2)}) %collective-permute-start.26) | collective-permute-done | bytes 655392 | tf_op jit(solution)/shard_map/ppermute | solution.py:977
  497.4 5.0 collective-permute-done.28
  507.6 5.0 collective-permute-done.42
  524.9 3.3 fusion.13
  (206 shorter events, 122.6 us)
Async XLA Ops:
  7.2 116.0 %all-gather.3.cloned.1.call-start = ((), (), s32[]{:S(2)}) async-start(), calls=%async_computation.4 | async-start | bytes 3932160 | tf_op jit(solution)/shard_map/all_gather | solution.py:1065
  81.7 59.3 %all-gather.5.cloned.1.call-start = ((), (), s32[]{:S(2)}) async-start(), calls=%async_computation.5 | async-start | bytes 3932160 | tf_op jit(solution)/shard_map/all_gather | solution.py:1066
  82.4 392.7 %reduce-scatter.5.cloned.1.call-start = ((), (), s32[]{:S(2)}) async-start(), calls=%async_computation.6 | async-start | bytes 1966080 | tf_op jit(solution)/shard_map/reduce_scatter | solution.py:1143
  284.2 35.5 %collective-permute-start.6 = (bf16[160,2048]{1,0:T(8,128)(2,1)S(1)}, bf16[160,2048]{1,0:T(8,128)(2,1)S(1)}, u32[]{:S(2)}, u32[]{:S(2)}) collective-permute-start(bf16[160,2048]{1,0:T(8,128)(2,1)S(1)} %get-tuple-element.85), channel_id=1, source_target_pairs={{0,2},{2,4},{4,6},{6,7},{7,5},{5,3},{3,1},{1,0},{8,10},{10,12},{12... | collective-permute-start | bytes 1966088 | tf_op jit(solution)/shard_map/ppermute | solution.py:951
  284.6 35.1 %collective-permute-start.7 = (bf16[160,2048]{1,0:T(8,128)(2,1)S(1)}, bf16[160,2048]{1,0:T(8,128)(2,1)S(1)}, u32[]{:S(2)}, u32[]{:S(2)}) collective-permute-start(bf16[160,2048]{1,0:T(8,128)(2,1)S(1)} %get-tuple-element.86), channel_id=1, source_target_pairs={{0,1},{2,0},{4,2},{6,4},{7,6},{5,7},{3,5},{1,3},{8,9},{10,8},{12,1... | collective-permute-start | bytes 1966088 | tf_op jit(solution)/shard_map/ppermute | solution.py:952
  328.8 164.5 %reduce-scatter.7.cloned.1.call-start = ((), (), s32[]{:S(2)}) async-start(), calls=%async_computation.7 | async-start | bytes 5242880 | tf_op jit(solution)/shard_map/reduce_scatter | solution.py:1126
  333.1 182.6 %reduce-scatter.11.cloned.1.call-start = ((), (), s32[]{:S(2)}) async-start(), calls=%async_computation.9 | async-start | bytes 3932160 | tf_op jit(solution)/shard_map/reduce_scatter | solution.py:1100
  333.7 191.2 %reduce-scatter.9.cloned.1.call-start = ((), (), s32[]{:S(2)}) async-start(), calls=%async_computation.8 | async-start | bytes 7864320 | tf_op jit(solution)/shard_map/reduce_scatter | solution.py:1101
  345.6 18.4 %collective-permute-start.8 = (bf16[160,2048]{1,0:T(8,128)(2,1)S(1)}, bf16[160,2048]{1,0:T(8,128)(2,1)S(1)}, u32[]{:S(2)}, u32[]{:S(2)}) collective-permute-start(bf16[160,2048]{1,0:T(8,128)(2,1)S(1)} %get-tuple-element.139), channel_id=1, source_target_pairs={{0,2},{2,4},{4,6},{6,7},{7,5},{5,3},{3,1},{1,0},{8,10},{10,12},{12... | collective-permute-start | bytes 1966088 | tf_op jit(solution)/shard_map/ppermute | solution.py:977
  345.6 18.4 %collective-permute-start.9 = (bf16[160,2048]{1,0:T(8,128)(2,1)S(1)}, bf16[160,2048]{1,0:T(8,128)(2,1)S(1)}, u32[]{:S(2)}, u32[]{:S(2)}) collective-permute-start(bf16[160,2048]{1,0:T(8,128)(2,1)S(1)} %get-tuple-element.139), channel_id=1, source_target_pairs={{0,1},{2,0},{4,2},{6,4},{7,6},{5,7},{3,5},{1,3},{8,9},{10,8},{12,1... | collective-permute-start | bytes 1966088 | tf_op jit(solution)/shard_map/ppermute | solution.py:978
  350.2 27.6 %collective-permute-start.21 = (bf16[160,2048]{1,0:T(8,128)(2,1)S(1)}, bf16[160,2048]{1,0:T(8,128)(2,1)S(1)}, u32[]{:S(2)}, u32[]{:S(2)}) collective-permute-start(bf16[160,2048]{1,0:T(8,128)(2,1)S(1)} %pad_maximum_fusion.3), channel_id=1, source_target_pairs={{0,1},{2,0},{4,2},{6,4},{7,6},{5,7},{3,5},{1,3},{8,9},{10,8},{12,1... | collective-permute-start | bytes 1966088 | tf_op jit(solution)/shard_map/ppermute | solution.py:943
  352.5 25.5 %collective-permute-start.17 = (bf16[160,2048]{1,0:T(8,128)(2,1)S(1)}, bf16[160,2048]{1,0:T(8,128)(2,1)S(1)}, u32[]{:S(2)}, u32[]{:S(2)}) collective-permute-start(bf16[160,2048]{1,0:T(8,128)(2,1)S(1)} %pad_maximum_fusion.2), channel_id=1, source_target_pairs={{0,2},{2,4},{4,6},{6,7},{7,5},{5,3},{3,1},{1,0},{8,10},{10,12},{12... | collective-permute-start | bytes 1966088 | tf_op jit(solution)/shard_map/ppermute | solution.py:942
  364.0 28.2 %collective-permute-start.10 = (bf16[160,2048]{1,0:T(8,128)(2,1)S(1)}, bf16[160,2048]{1,0:T(8,128)(2,1)}, u32[]{:S(2)}, u32[]{:S(2)}) collective-permute-start(bf16[160,2048]{1,0:T(8,128)(2,1)S(1)} %collective-permute-done.8), channel_id=1, source_target_pairs={{0,2},{2,4},{4,6},{6,7},{7,5},{5,3},{3,1},{1,0},{8,10},{10,12},{12... | collective-permute-start | bytes 1966088 | tf_op jit(solution)/shard_map/ppermute | solution.py:977
  364.0 28.2 %collective-permute-start.11 = (bf16[160,2048]{1,0:T(8,128)(2,1)S(1)}, bf16[160,2048]{1,0:T(8,128)(2,1)}, u32[]{:S(2)}, u32[]{:S(2)}) collective-permute-start(bf16[160,2048]{1,0:T(8,128)(2,1)S(1)} %collective-permute-done.9), channel_id=1, source_target_pairs={{0,1},{2,0},{4,2},{6,4},{7,6},{5,7},{3,5},{1,3},{8,9},{10,8},{12,1... | collective-permute-start | bytes 1966088 | tf_op jit(solution)/shard_map/ppermute | solution.py:978
  379.6 26.6 %collective-permute-start.18 = (bf16[160,2048]{1,0:T(8,128)(2,1)}, bf16[160,2048]{1,0:T(8,128)(2,1)S(1)}, u32[]{:S(2)}, u32[]{:S(2)}) collective-permute-start(bf16[160,2048]{1,0:T(8,128)(2,1)} %get-tuple-element.142), channel_id=1, source_target_pairs={{0,2},{2,4},{4,6},{6,7},{7,5},{5,3},{3,1},{1,0},{8,10},{10,12},{12... | collective-permute-start | bytes 1966088 | tf_op jit(solution)/shard_map/ppermute | solution.py:942
  380.7 25.4 %collective-permute-start.22 = (bf16[160,2048]{1,0:T(8,128)(2,1)}, bf16[160,2048]{1,0:T(8,128)(2,1)}, u32[]{:S(2)}, u32[]{:S(2)}) collective-permute-start(bf16[160,2048]{1,0:T(8,128)(2,1)} %get-tuple-element.143), channel_id=1, source_target_pairs={{0,1},{2,0},{4,2},{6,4},{7,6},{5,7},{3,5},{1,3},{8,9},{10,8},{12,1... | collective-permute-start | bytes 1966088 | tf_op jit(solution)/shard_map/ppermute | solution.py:943
  392.2 28.0 %collective-permute-start.12 = (bf16[160,2048]{1,0:T(8,128)(2,1)}, bf16[160,2048]{1,0:T(8,128)(2,1)S(1)}, u32[]{:S(2)}, u32[]{:S(2)}) collective-permute-start(bf16[160,2048]{1,0:T(8,128)(2,1)} %collective-permute-done.10), channel_id=1, source_target_pairs={{0,2},{2,4},{4,6},{6,7},{7,5},{5,3},{3,1},{1,0},{8,10},{10,12},{12... | collective-permute-start | bytes 1966088 | tf_op jit(solution)/shard_map/ppermute | solution.py:977
  392.2 28.1 %collective-permute-start.13 = (bf16[160,2048]{1,0:T(8,128)(2,1)}, bf16[160,2048]{1,0:T(8,128)(2,1)S(1)}, u32[]{:S(2)}, u32[]{:S(2)}) collective-permute-start(bf16[160,2048]{1,0:T(8,128)(2,1)} %collective-permute-done.11), channel_id=1, source_target_pairs={{0,1},{2,0},{4,2},{6,4},{7,6},{5,7},{3,5},{1,3},{8,9},{10,8},{12,1... | collective-permute-start | bytes 1966088 | tf_op jit(solution)/shard_map/ppermute | solution.py:978
  408.1 26.1 %collective-permute-start.19 = (bf16[160,2048]{1,0:T(8,128)(2,1)S(1)}, bf16[160,2048]{1,0:T(8,128)(2,1)S(1)}, u32[]{:S(2)}, u32[]{:S(2)}) collective-permute-start(bf16[160,2048]{1,0:T(8,128)(2,1)S(1)} %get-tuple-element.140), channel_id=1, source_target_pairs={{0,2},{2,4},{4,6},{6,7},{7,5},{5,3},{3,1},{1,0},{8,10},{10,12},{12... | collective-permute-start | bytes 1966088 | tf_op jit(solution)/shard_map/ppermute | solution.py:951
  409.3 24.9 %collective-permute-start.23 = (bf16[160,2048]{1,0:T(8,128)(2,1)S(1)}, bf16[160,2048]{1,0:T(8,128)(2,1)S(1)}, u32[]{:S(2)}, u32[]{:S(2)}) collective-permute-start(bf16[160,2048]{1,0:T(8,128)(2,1)S(1)} %get-tuple-element.141), channel_id=1, source_target_pairs={{0,1},{2,0},{4,2},{6,4},{7,6},{5,7},{3,5},{1,3},{8,9},{10,8},{12,1... | collective-permute-start | bytes 1966088 | tf_op jit(solution)/shard_map/ppermute | solution.py:952
  420.2 46.0 %collective-permute-start.14 = (bf16[160,1024]{1,0:T(8,128)(2,1)S(1)}, bf16[160,1024]{1,0:T(8,128)(2,1)}, u32[]{:S(2)}, u32[]{:S(2)}) collective-permute-start(bf16[160,1024]{1,0:T(8,128)(2,1)S(1)} %slice.138), channel_id=1, source_target_pairs={{0,2},{2,4},{4,6},{6,7},{7,5},{5,3},{3,1},{1,0},{8,10},{10,12},{12... | collective-permute-start | bytes 983048 | tf_op jit(solution)/shard_map/ppermute | solution.py:980
  420.3 45.9 %collective-permute-start.15 = (bf16[160,1024]{1,0:T(8,128)(2,1)S(1)}, bf16[160,1024]{1,0:T(8,128)(2,1)}, u32[]{:S(2)}, u32[]{:S(2)}) collective-permute-start(bf16[160,1024]{1,0:T(8,128)(2,1)S(1)} %slice.139), channel_id=1, source_target_pairs={{0,1},{2,0},{4,2},{6,4},{7,6},{5,7},{3,5},{1,3},{8,9},{10,8},{12,1... | collective-permute-start | bytes 983048 | tf_op jit(solution)/shard_map/ppermute | solution.py:981
  448.9 22.4 %collective-permute-start.24 = (bf16[160,2048]{1,0:T(8,128)(2,1)S(1)}, bf16[160,2048]{1,0:T(8,128)(2,1)S(1)}, u32[]{:S(2)}, u32[]{:S(2)}) collective-permute-start(bf16[160,2048]{1,0:T(8,128)(2,1)S(1)} %get-tuple-element.137), channel_id=1, source_target_pairs={{0,2},{2,4},{4,6},{6,7},{7,5},{5,3},{3,1},{1,0},{8,10},{10,12},{12... | collective-permute-start | bytes 1966088 | tf_op jit(solution)/shard_map/ppermute | solution.py:977
  450.6 21.0 %collective-permute-start.25 = (bf16[160,2048]{1,0:T(8,128)(2,1)S(1)}, bf16[160,2048]{1,0:T(8,128)(2,1)S(1)}, u32[]{:S(2)}, u32[]{:S(2)}) collective-permute-start(bf16[160,2048]{1,0:T(8,128)(2,1)S(1)} %get-tuple-element.137), channel_id=1, source_target_pairs={{0,1},{2,0},{4,2},{6,4},{7,6},{5,7},{3,5},{1,3},{8,9},{10,8},{12,1... | collective-permute-start | bytes 1966088 | tf_op jit(solution)/shard_map/ppermute | solution.py:978
  (41 other events, 505.1 us)
Sparse Core Ops, SparseCore 0:
  81.8 28.9 all-gather.2
  112.4 28.5 all-gather.4
  329.0 27.3 reduce-scatter.4
  358.8 44.4 reduce-scatter.6
  405.8 38.0 reduce-scatter.10
  446.4 58.3 reduce-scatter.8

commit v10 on v9

--- a/solution.py
+++ b/solution.py
@@ -180,10 +180,10 @@
 
 def mlp_kernel(
     count, x_hbm, a_hbm, dy_hbm, gain_ref, out_w, gate_w, up_w, down_w,
-    n2_hbm, hid_hbm, grad_hbm, mlp_hbm, h1_ref, dh1_ref, low_ref, dgain_ref, da_ref,
-    x_s, a_s, dy_s, n2_s, hid_s, grad_s, mlp_s, h1_s, dy_own, da_part,
+    n2_hbm, hid_hbm, grad_hbm, mlp_hbm, h1_ref, dh1_ref, low_ref, dgain_ref, da_ref, ahead_ref, behind_ref,
+    x_s, a_s, dy_s, n2_s, hid_s, grad_s, mlp_s, h1_s, dy_own, da_part, mlp_far, mlp_got,
     right_part, left_part, right_got, left_got,
-    in_sem, out_sem, send_sem, recv_sem, da_send, da_recv,
+    in_sem, out_sem, send_sem, recv_sem, da_send, da_recv, far_send, far_recv,
 ):
     steps = count // 2
     rows = x_hbm.shape[0] // count
@@ -330,6 +330,15 @@
 
         @pl.when(group == 0)
         def _():
+            mlp_far[...] = mlp_s[slot, pl.ds(0, rows)]
+
+        @pl.when(group == 1)
+        def _():
+            ahead_ref[...] = mlp_s[slot, pl.ds(0, rows)]
+            behind_ref[...] = mlp_s[slot, pl.ds(rows, rows)]
+
+        @pl.when(group == 0)
+        def _():
             for copy in first_copies():
                 copy.start()
 
@@ -357,6 +366,19 @@
 
     for copy in later_copies(steps - 1):
         copy.wait_recv()
+    far_copies = [
+        pltpu.make_async_remote_copy(
+            src_ref=mlp_far.at[:, pl.ds(flow * side, side)],
+            dst_ref=mlp_got.at[flow],
+            send_sem=far_send.at[flow],
+            recv_sem=far_recv.at[flow],
+            device_id=device,
+            device_id_type=MESH,
+        )
+        for flow, device in ((0, right), (1, left))
+    ]
+    for copy in far_copies:
+        copy.start()
 
     def tile_of(at):
         return pl.ds(pl.multiple_of(at * tile, tile), tile)
@@ -414,6 +436,12 @@
     def _(hop):
         da_copy(hop).wait_recv()
         da_copy(hop).wait_send()
+
+    for flow, held in ((0, ahead_ref), (1, behind_ref)):
+        far_copies[flow].wait_recv()
+        cols = pl.ds(flow * side, side)
+        held[:, cols] = add_low(held[:, cols], mlp_got[flow])
+        far_copies[flow].wait_send()
 
     for copy in first_copies():
         copy.wait_send()
@@ -451,17 +479,21 @@
             jax.ShapeDtypeStruct((rows, width), BF),
             jax.ShapeDtypeStruct((1, width), F32),
             jax.ShapeDtypeStruct((total, size), BF),
+            jax.ShapeDtypeStruct((rows, width), BF),
+            jax.ShapeDtypeStruct((rows, width), BF),
         ],
         in_specs=[hbm] * 3 + [vmem] * 5,
-        out_specs=[hbm] * 4 + [vmem] * 5,
+        out_specs=[hbm] * 4 + [vmem] * 7,
         scratch_shapes=[
             slots(width), slots(mixed.shape[1]), slots(width), slots(width), slots(hidden),
             slots(2 * hidden), slots(width), pltpu.VMEM((2 * rows, width), F32),
             pltpu.VMEM((rows, width), BF), pltpu.VMEM((count, rows, size), BF),
+            pltpu.VMEM((rows, width), BF), pltpu.VMEM((2, rows, width // 2), BF),
             part, part, part, part,
             pltpu.SemaphoreType.DMA((2, 6)), pltpu.SemaphoreType.DMA((2, 8)),
             pltpu.SemaphoreType.DMA((count,)), pltpu.SemaphoreType.DMA((count,)),
             pltpu.SemaphoreType.DMA((count,)), pltpu.SemaphoreType.DMA((count,)),
+            pltpu.SemaphoreType.DMA((2,)), pltpu.SemaphoreType.DMA((2,)),
         ],
         compiler_params=pltpu.CompilerParams(
             collective_id=collective_id, has_side_effects=True, vmem_limit_bytes=VMEM_LIMIT
@@ -663,7 +695,6 @@
     rows, width = tokens.shape
     size, wide = w_out.shape
     vmem = pl.BlockSpec(memory_space=pltpu.VMEM)
-    hbm = pl.BlockSpec(memory_space=pl.ANY)
     slots = 6 * batches + others * (count + 3)
     sems = pltpu.SemaphoreType.DMA((slots,))
     return pl.pallas_call(
@@ -679,8 +710,8 @@
             jax.ShapeDtypeStruct((batches, *segments.shape), jnp.int32),
             jax.ShapeDtypeStruct((w_down.shape[0], batches * w_down.shape[1]), BF),
         ],
-        in_specs=[vmem] * 5 + [hbm],
-        out_specs=[vmem] * 8 + [hbm],
+        in_specs=[vmem] * 6,
+        out_specs=[vmem] * 9,
         scratch_shapes=[sems, sems, pltpu.SemaphoreType.DMA((5,))],
         compiler_params=pltpu.CompilerParams(
             collective_id=collective_id, has_side_effects=True, vmem_limit_bytes=VMEM_LIMIT
@@ -900,6 +931,214 @@
     )(part)
 
 
+def tail_kernel(
+    count, batches, cat_ref, w_ref, x_ref, gain_ref, dh1_ref, out_ref, wout_ref, second_ref,
+    out_all, tok_all, gains_ref, wout_own,
+    part_ref, tok_ref, got, wout_got, gain_own, gain_got, gain_mid, gain_heads,
+    send_sem, recv_sem, local_sem,
+):
+    steps = count // 2
+    rows, width = x_ref.shape
+    depth = cat_ref.shape[1]
+    tile = 256
+    place, right, left = ring_setup(count)
+    batch, head = lax.axis_index("batch"), lax.axis_index("head")
+    others = [lax.rem(batch + hop, batches) for hop in range(1, batches)]
+    members = [(batch, ring_head(lax.rem(place + hop, count), count)) for hop in range(1, count)]
+    greet((*members, *[(other, head) for other in others]))
+    sems = (send_sem, recv_sem)
+    slot = 0
+    copies = []
+
+    def go(source, target, device):
+        nonlocal slot
+        copy = send(source, target, sems, slot, device)
+        slot += 1
+        copies.append(copy)
+        return copy
+
+    def span(owner, extent):
+        return pl.ds(pl.multiple_of(lax.rem(owner + count, count) * extent, extent), extent)
+
+    def compute(owner):
+        here = span(owner, rows)
+        values = cat_ref[here]
+
+        @pl.loop(0, width // tile)
+        def _(at):
+            cols = pl.ds(pl.multiple_of(at * tile, tile), tile)
+            part_ref[here, cols] = cols_inner(values, w_ref[cols, pl.ds(0, depth)]).astype(BF)
+
+    def gather(own, whole, step, last):
+        out = []
+        for flow, chunk, device in ((0, place - step, right), (1, place + step, left)):
+            if step:
+                last[flow].wait_recv()
+            target = whole.at[lax.rem(chunk + count, count)]
+            source = target if step else own
+            if step == steps - 1:
+                cut = (slice(None), pl.ds(flow * (width // 2), width // 2))
+                source, target = source.at[cut], target.at[cut]
+            out.append(go(source, target, device))
+        return out
+
+    def reduce(parts, held, step, last):
+        extent, side = held.shape[2], held.shape[3] // 2
+        out = []
+        for flow, owner, device in (
+            (0, place + steps - step, right),
+            (1, place - steps + step, left),
+        ):
+            have = pl.ds(flow * side, side)
+            lack = pl.ds((1 - flow) * side, side)
+            mine = parts.at[span(owner, extent)]
+            if step == 0:
+                out.append(go(mine.at[:, have], held.at[flow, 0, :, have], device))
+                continue
+            last[flow].wait_recv()
+            if step == 1:
+                held[flow, 0, :, have] = add_low(held[flow, 0, :, have], mine[:, have])
+                held[flow, 0, :, lack] = mine[:, lack]
+            else:
+                held[flow, step - 1] = add_low(held[flow, step - 1], mine[...])
+            out.append(go(held.at[flow, step - 1], held.at[flow, step], device))
+        return out
+
+    keep_out = pltpu.make_async_copy(out_ref, out_all.at[place], local_sem.at[0])
+    keep_out.start()
+    compute(place + steps)
+    sums = reduce(part_ref, got, 0, None)
+    outs = gather(out_ref, out_all, 0, None)
+    wsums = reduce(wout_ref, wout_got, 0, None)
+
+    @pl.loop(1, count)
+    def _(hop):
+        compute(place + steps + hop)
+
+    for step in range(1, steps):
+        sums = reduce(part_ref, got, step, sums)
+        wsums = reduce(wout_ref, wout_got, step, wsums)
+        outs = gather(out_ref, out_all, step, outs)
+    for copy in sums:
+        copy.wait_recv()
+
+    def tile_of(at):
+        return pl.ds(pl.multiple_of(at * tile, tile), tile)
+
+    def total(cols):
+        return (
+            part_ref[span(place, rows), cols].astype(F32)
+            + got[0, steps - 1, :, cols].astype(F32)
+            + got[1, steps - 1, :, cols].astype(F32)
+        )
+
+    def collect(at, state):
+        squares, mean = state
+        cols = tile_of(at)
+        x = x_ref[:, cols].astype(F32)
+        squares = squares + jnp.sum(x * x, axis=1, keepdims=True)
+        return squares, mean + jnp.sum(gain_ref[:, cols] * total(cols) * x, axis=1, keepdims=True)
+
+    zero = jnp.zeros((rows, 1), F32)
+    squares, mean = lax.fori_loop(0, width // tile, collect, (zero, zero))
+    scale = lax.rsqrt(squares / width + EPSILON)
+    pull = scale * scale * scale * (mean / width)
+
+    @pl.loop(0, width // tile)
+    def _(at):
+        cols = tile_of(at)
+        x, dn1 = x_ref[:, cols].astype(F32), total(cols)
+        gain_own[pl.ds(0, 1), cols] = jnp.sum(dn1 * x * scale, axis=0, keepdims=True)
+        gain_own[pl.ds(1, 1), cols] = second_ref[:, cols]
+        tok_ref[:, cols] = (dh1_ref[:, cols] + scale * (gain_ref[:, cols] * dn1) - x * pull).astype(BF)
+
+    keep_tok = pltpu.make_async_copy(tok_ref, tok_all.at[place], local_sem.at[1])
+    keep_tok.start()
+    toks = gather(tok_ref, tok_all, 0, None)
+    wide = width // batches
+
+    def slice_of(at):
+        return pl.ds(pl.multiple_of(at * wide, wide), wide)
+
+    gains = [
+        go(gain_own.at[:, slice_of(other)], gain_got.at[hop], (other, head))
+        for hop, other in enumerate(others)
+    ]
+    toks = gather(tok_ref, tok_all, 1, toks)
+    middle = gain_own[:, slice_of(batch)]
+    for hop, copy in enumerate(gains):
+        copy.wait_recv()
+        middle = middle + gain_got[hop]
+    gain_mid[...] = middle
+    gain_heads[place] = middle
+    gains = [go(gain_mid, gain_heads.at[place], member) for member in members]
+    for step in range(2, steps):
+        toks = gather(tok_ref, tok_all, step, toks)
+    for copy in gains:
+        copy.wait_recv()
+    middle = gain_heads[0]
+    for at in range(1, count):
+        middle = middle + gain_heads[at]
+    gains_ref[...] = middle
+    for copy in (*wsums, *outs):
+        copy.wait_recv()
+    wout_own[...] = (
+        wout_ref[span(place, wout_own.shape[0])].astype(F32)
+        + wout_got[0, steps - 1].astype(F32)
+        + wout_got[1, steps - 1].astype(F32)
+    )
+    for copy in toks:
+        copy.wait_recv()
+    for copy in copies:
+        copy.wait_send()
+    keep_out.wait()
+    keep_tok.wait()
+
+
+def tail(d_cat, w_in, x_own, gain, d_resid, out_own, wout_part, second, collective_id):
+    count = lax.axis_size("head")
+    batches = lax.axis_size("batch")
+    steps = count // 2
+    rows, width = x_own.shape
+    size, wide = wout_part.shape[0] // count, wout_part.shape[1]
+    vmem = pl.BlockSpec(memory_space=pltpu.VMEM)
+    hbm = pl.BlockSpec(memory_space=pl.ANY)
+    whole = jax.ShapeDtypeStruct((count, rows, width), BF)
+    sems = pltpu.SemaphoreType.DMA((5 * count + batches,))
+    gains = (2, width // batches)
+    return pl.pallas_call(
+        functools.partial(tail_kernel, count, batches),
+        out_shape=[
+            whole,
+            whole,
+            jax.ShapeDtypeStruct(gains, F32),
+            jax.ShapeDtypeStruct((size, wide), F32),
+        ],
+        in_specs=[vmem] * 8,
+        out_specs=[hbm, hbm, vmem, vmem],
+        scratch_shapes=[
+            pltpu.VMEM((count * rows, width), BF),
+            pltpu.VMEM((rows, width), BF),
+            pltpu.VMEM((2, steps, rows, width), BF),
+            pltpu.VMEM((2, steps, size, wide), BF),
+            pltpu.VMEM((2, width), F32),
+            pltpu.VMEM((batches - 1, *gains), F32),
+            pltpu.VMEM(gains, F32),
+            pltpu.VMEM((count, *gains), F32),
+            sems,
+            sems,
+            pltpu.SemaphoreType.DMA((2,)),
+        ],
+        compiler_params=pltpu.CompilerParams(
+            collective_id=collective_id, has_side_effects=True, vmem_limit_bytes=VMEM_LIMIT
+        ),
+        cost_estimate=pl.CostEstimate(
+            flops=2 * count * rows * width * d_cat.shape[1], bytes_accessed=400 << 20, transcendentals=0
+        ),
+        name="tail",
+    )(d_cat, w_in, x_own, gain, d_resid, out_own, wout_part, second)
+
+
 def local_call(kernel, scalars, arrays, outs, scratch, flops, name):
     vmem = pl.BlockSpec(memory_space=pltpu.VMEM)
     smem = pl.BlockSpec(memory_space=pltpu.SMEM)
@@ -926,91 +1165,25 @@
     return (one.astype(F32) + other.astype(F32)).astype(BF)
 
 
-def flow_steps(part):
+def flow_steps(part, going, coming):
     count = lax.axis_size("head")
     place = ring_place(lax.axis_index("head"), count)
     right, left = ring_routes(count)
-    rows, side = part.shape[0] // count, part.shape[1] // 2
+    rows = part.shape[0] // count
     steps = count // 2
 
     def mine(owner):
         return lax.dynamic_slice_in_dim(part, lax.rem(owner + count, count) * rows, rows, 0)
 
-    far = mine(place + steps)
-    going, coming = far[:, :side], far[:, side:]
-    for step in range(steps - 1):
+    for step in range(1, steps - 1):
         from_left = lax.ppermute(going, "head", right)
         from_right = lax.ppermute(coming, "head", left)
-        one, two = mine(place + steps - 1 - step), mine(place - steps + 1 + step)
-        if step == 0:
-            going = jnp.concatenate([add_low(from_left, one[:, :side]), one[:, side:]], 1)
-            coming = jnp.concatenate([two[:, :side], add_low(from_right, two[:, side:])], 1)
-        else:
-            going, coming = add_low(from_left, one), add_low(from_right, two)
+        going = add_low(from_left, mine(place + steps - 1 - step))
+        coming = add_low(from_right, mine(place - steps + 1 + step))
         going, coming = yield going, coming
     from_left = lax.ppermute(going, "head", right)
     from_right = lax.ppermute(coming, "head", left)
     yield mine(place).astype(F32) + from_left.astype(F32) + from_right.astype(F32)
-
-
-def flow_sum(part):
-    flow = flow_steps(part)
-    state = next(flow)
-    while isinstance(state, tuple):
-        state = flow.send(state)
-    return state
-
-
-def after(flow, state, array):
-    array, going, coming = lax.optimization_barrier((array, *state))
-    return array, flow.send((going, coming))
-
-
-def flow_spread(own):
-    count = lax.axis_size("head")
-    place = ring_place(lax.axis_index("head"), count)
-    right, left = ring_routes(count)
-    side = own.shape[1] // 2
-    going = coming = own
-    pieces = [(0, own)]
-    for step in range(1, count // 2):
-        going = lax.ppermute(going, "head", right)
-        coming = lax.ppermute(coming, "head", left)
-        pieces += [(-step, going), (step, coming)]
-    one = lax.ppermute(going[:, :side], "head", right)
-    two = lax.ppermute(coming[:, side:], "head", left)
-    pieces.append((count // 2, jnp.concatenate([one, two], 1)))
-    whole = jnp.zeros((count * own.shape[0], own.shape[1]), own.dtype)
-    for shift, piece in pieces:
-        at = lax.rem(place + shift + count, count) * own.shape[0]
-        whole = lax.dynamic_update_slice_in_dim(whole, piece, at, 0)
-    return whole
-
-
-def swap(block, axis, stride):
-    return lax.ppermute(block, axis, [(at, at ^ stride) for at in range(lax.axis_size(axis))])
-
-
-def halve_batch(block, rows):
-    me = lax.axis_index("batch")
-    stride = 1
-    while stride < lax.axis_size("batch"):
-        block = block.reshape(-1, 2, rows, block.shape[-1])
-        bit = (me // stride) % 2
-        keep = lax.dynamic_index_in_dim(block, bit, 1, keepdims=False)
-        give = lax.dynamic_index_in_dim(block, 1 - bit, 1, keepdims=False)
-        got = swap(give, "batch", stride)
-        block = (keep.astype(F32) + got.astype(F32)).astype(block.dtype)
-        stride *= 2
-    return block.reshape(rows, -1)
-
-
-def sum_heads(block):
-    stride = 1
-    while stride < lax.axis_size("head"):
-        block = block + swap(block, "head", stride)
-        stride *= 2
-    return block
 
 
 def matmul(left, right):
@@ -1085,22 +1258,29 @@
         "attend",
     )
     (mixed_all,) = spread([mixed], (("head", "cols"),), 2)
-    normed_two, hidden, d_pre, mlp_part, resid_own, d_resid, d_resid_low, d_gain_two, d_mixed = mlp_back(
+    (
+        normed_two, hidden, d_pre, mlp_part, resid_own, d_resid, d_resid_low, d_gain_two, d_mixed,
+        going, coming,
+    ) = mlp_back(
         tokens, mixed_all, out_grad, gain_two[None], out_full, mgate_full, mup_full, down_full, 3
     )
+    hold = lax.optimization_barrier
     mixed_own = lax.dynamic_slice_in_dim(mixed_all, me * chunk, chunk, 0)
-    out_flow = flow_steps(mlp_part)
-    out_state = next(out_flow)
+    flow = flow_steps(mlp_part, going, coming)
+    state = next(flow)
+    d_out_part = rows_inner(mixed_own, d_resid_low).astype(BF)
+    hidden, d_out_part = hold((hidden, d_out_part))
+    d_out_part = lax.psum_scatter(d_out_part, "batch", scatter_dimension=1, tiled=True)
     d_down = rows_inner(hidden, out_grad).astype(BF)
-    normed_late, d_down, *out_state = lax.optimization_barrier((normed_two, d_down, *out_state))
-    out_state = out_flow.send(tuple(out_state))
-    d_mlp = rows_inner(normed_late, d_pre).astype(BF)
-    d_mixed, d_mlp, *out_state = lax.optimization_barrier((d_mixed, d_mlp, *out_state))
-    out_state = tuple(out_state)
+    normed_two, d_down, state = hold((normed_two, d_down, state))
     d_down = lax.psum_scatter(d_down, "batch", scatter_dimension=1, tiled=True).astype(F32)
+    state = flow.send(state)
+    d_mlp = rows_inner(normed_two, d_pre).astype(BF)
+    d_mixed, d_mlp, state = hold((d_mixed, d_mlp, state))
     d_mlp = lax.psum_scatter(d_mlp, "batch", scatter_dimension=0, tiled=True).astype(F32)
-
-    d_mixed, out_state = after(out_flow, out_state, d_mixed)
+    while isinstance(state, tuple):
+        state = flow.send(state)
+
     d_queries, d_gate_logit, d_kv_all = local_call(
         functools.partial(attend_back_kernel, scale_factor),
         scalars,
@@ -1114,35 +1294,20 @@
         5 * pair_flops // 2,
         "attend_back",
     )
-    d_kv_all, out_state = after(out_flow, out_state, d_kv_all)
+    d_kv_all, state, d_out_part = hold((d_kv_all, state, d_out_part))
+    out_own = (resid_own + state).astype(BF)
     d_kv = fold(d_kv_all, row_count, 4)
-    while isinstance(out_state, tuple):
-        out_state = out_flow.send(out_state)
-    out_total = out_state
-    d_kv, out_total = lax.optimization_barrier((d_kv, out_total))
-    output = flow_spread((resid_own + out_total).astype(BF))
     d_cat = jnp.concatenate([d_queries, d_gate_logit, d_kv], axis=1)
-    d_out_part = rows_inner(mixed_own, d_resid_low).astype(BF)
-    d_out_part = lax.psum_scatter(d_out_part, "batch", scatter_dimension=1, tiled=True)
-    d_out = flow_sum(d_out_part)
-    w_cat = w_in[:, : 3 * head_size]
-    dn1_part = cols_inner(d_cat, w_cat).astype(BF)
-    dn1 = flow_sum(dn1_part)
-    inputs_own = lax.dynamic_slice_in_dim(tokens, me * chunk, chunk, 0).astype(F32)
-    recip_in = rms_scale(inputs_own)
-    d_gain_one = jnp.sum(dn1 * inputs_own * recip_in, axis=0)
-    weighted_one = gain_one * dn1
-    d_tokens = (
-        d_resid
-        + recip_in * weighted_one
-        - inputs_own * recip_in**3 * jnp.mean(weighted_one * inputs_own, axis=1, keepdims=True)
-    ).astype(BF)
-    d_tokens = flow_spread(d_tokens)
-
+    d_cat, d_down = hold((d_cat, d_down))
     d_in = rows_inner(normed_one, d_cat).astype(BF)
+    d_cat, d_in = hold((d_cat, d_in))
     d_in = lax.psum_scatter(d_in, "batch", scatter_dimension=0, tiled=True).astype(F32)
-    d_gains = jnp.stack([d_gain_one, d_gain_two[0]]).reshape(2, batches, -1).transpose(1, 0, 2)
-    d_gains = sum_heads(halve_batch(d_gains.reshape(2 * batches, -1), 2))
+    inputs_own = lax.dynamic_slice_in_dim(tokens, me * chunk, chunk, 0)
+    output, d_tokens, d_gains, d_out = tail(
+        d_cat, w_in, inputs_own, gain_one[None], d_resid, out_own, d_out_part, d_gain_two, 5
+    )
+    output = output.reshape(row_count, width)
+    d_tokens = d_tokens.reshape(row_count, width)
     hidden_own = w_mlp_gate.shape[1]
     return (
         output,

time: 534 us -> 576 us (1.079)
  Pallas kernels: 246 us -> 419 us
  waiting for transfers between devices: 123 us -> 63.2 us
  starting transfers between devices: 47.8 us -> 6.42 us
  other arithmetic: 28.8 us -> 12.9 us
  local copies, waits for them, and re-layouts: 37.8 us -> 25.5 us
    pallas_call x0 -> x1, Pallas kernels: none -> 172 us  [tail(): pl.pallas_call(functools.partial(tail_kernel, count, batches), out_shape=...]
    ppermute x21 -> x0, waiting for transfers between devices: 55.8 us -> none  [the longest x6 38.1 us: flow_spread(): going = lax.ppermute(going, 'head', right)]
    reduce_scatter x1, waiting for transfers between devices: 0.01 us -> 45.2 us  [per_device(): lax.psum_scatter(d_out_part, 'batch', scatter_dimension=1, tiled=True)]
    ppermute x12 -> x3, waiting for transfers between devices: 28.6 us -> 0.91 us  [flow_steps(): from_left = lax.ppermute(going, 'head', right)]
    ppermute x21 -> x0, starting transfers between devices: 21.8 us -> none  [the longest x6 10.1 us: flow_spread(): coming = lax.ppermute(coming, 'head', left)]
    ppermute x12 -> x3, waiting for transfers between devices: 19.5 us -> 0.78 us  [flow_steps(): from_right = lax.ppermute(coming, 'head', left)]
    dynamic_update_slice x12 -> x0, local copies, waits for them, and re-layouts: 13.9 us -> none  [flow_spread(): whole = lax.dynamic_update_slice_in_dim(whole, piece, at, 0)]
    ppermute x12 -> x3, starting transfers between devices: 17 us -> 4.53 us  [flow_steps(): from_right = lax.ppermute(coming, 'head', left)]
  transfers between devices with their start and end apart: 51 -> 12, of which waited for: 22 -> 5; matrix products, arithmetic and copies ran while one was open for 15% -> 7% of each run, Pallas kernels for 15% -> 40%
where the time goes in v10:
time: 576 us; the launch traced here: 575 us
  Pallas kernels  419 us (73%)
  waiting for transfers between devices  63.2 us (11%)
  matrix products  33.8 us (6%)
  local copies, waits for them, and re-layouts  25.5 us (4%)
  between operations  14.4 us (2%)
  other arithmetic  12.9 us (2%)
  starting transfers between devices  6.42 us (1%)
    pallas_call x1, Pallas kernels, tail(): pl.pallas_call(functools.partial(tail_kernel, count, batches), out_shape=...  172 us
    pallas_call x1, Pallas kernels, mlp_back(): pl.pallas_call(functools.partial(mlp_kernel, count), out_shape=[jax.Shape...  100 us
    pallas_call x1, Pallas kernels, entry(): pl.pallas_call(functools.partial(entry_kernel, count, batches), out_shape...  70.3 us
    reduce_scatter x1, waiting for transfers between devices, per_device(): lax.psum_scatter(d_out_part, 'batch', scatter_dimension=1, tiled=True)  45.2 us
    pallas_call x1, Pallas kernels, spread(): pl.pallas_call(functools.partial(spread_kernel, count, batches, plans), o...  35.3 us
    dot_general x4, matrix products, rows_inner(): lax.dot_general(left, right, (((0,), (0,)), ((), ())), preferred_element_...  33.8 us
    pallas_call x2, Pallas kernels, local_call(): pl.pallas_call(kernel, out_shape=outs, in_specs=[smem] * len(scalars) + [...  20.6 us
    pallas_call x1, Pallas kernels, fold(): pl.pallas_call(functools.partial(fold_kernel, batches), out_shape=jax.Sha...  20.3 us
  transfers between devices with their start and end apart: 12, of which 5 were waited for; matrix products, arithmetic and copies ran while one was open for 7% of the time, Pallas kernels for 40%

profile of v10, /device:TPU:0, one launch (start us, length us, event | category | flops | bytes accessed | tf_op | source)
XLA Modules:
  0.0 574.8 jit_solution(337773704526508587)
XLA Ops:
  10.5 1.8 pad_maximum_fusion.1.w_ref
  12.3 70.3 %entry.1 = (bf16[1280,2048]{1,0:T(8,128)(2,1)}, bf16[1280,128]{1,0:T(8,128)(2,1)}, f32[1280,128]{1,0:T(8,128)}, bf16[5120,256]{1,0:T(8,128)(2,1)}, bf16[2048,512...) custom-call(bf16[1280,2048]{1,0:T(8,128)(2,1)} %x_hbm.1, ...), custom_call_target="tpu_custom_call" | custom-call | tf_op jit(solution)/shard_map/entry/pallas_call | solution.py:700
  85.1 8.8 %attend.1 = (f32[1280,128]{1,0:T(8,128)}, bf16[1280,128]{1,0:T(8,128)(2,1)}, f32[1,1280]{1,0:T(1,128)}) custom-call(s32[1280]{0:T(1024)} %copy-done.6, s32[1]{0:T(128)} %bitcast.3.base_sm, bf16[1280,128]{1,0:T(8,128)(2,1)} %get-tuple-element.63.q_ref, bf16[5120,256]{1,0:T(8,128)(2,1)} %get-tuple-element.64.kv_ref, s32[1,1280]{1,0:T(1,128)} %broadcast_in_dim.22.start_ref, ...), custom_call_target="tpu_custom_call" | custom-call | flops 3355443200 | bytes 8388608 | tf_op jit(solution)/shard_map/attend/pallas_call | solution.py:1145
  93.9 35.3 %spread_2.1.a_hbm = bf16[1280,1024]{1,0:T(8,128)(2,1)} custom-call(bf16[1280,128]{1,0:T(8,128)(2,1)} %get-tuple-element.67.refs_0_), custom_call_target="tpu_custom_call" | custom-call | tf_op jit(solution)/shard_map/spread_2/pallas_call | solution.py:164
  129.8 12.0 %all-gather.5.cloned.1.call-done.up_w = bf16[2048,768]{1,0:T(8,128)(2,1)} async-done(((bf16[512,768]{1,0:T(8,128)(2,1)}), bf16[2048,768]{1,0:T(8,128)(2,1)}) %all-gather.5.cloned.1.call-update) | async-done | bytes 3145744 | tf_op jit(solution)/shard_map/all_gather | solution.py:1239
  141.9 100.4 %mlp_back.1 = (bf16[1280,2048]{1,0:T(8,128)(2,1)}, bf16[1280,768]{1,0:T(8,128)(2,1)}, bf16[1280,1536]{1,0:T(8,128)(2,1)}, bf16[1280,2048]{1,0:T(8,128)(2,1)}, f3...) custom-call(bf16[1280,2048]{1,0:T(8,128)(2,1)} %x_hbm.1, ...), custom_call_target="tpu_custom_call" | custom-call | flops 29527900160 | bytes 41943040 | tf_op jit(solution)/shard_map/mlp_back/pallas_call | solution.py:470
  242.3 4.6 convolution_convert_fusion.1
  248.9 9.0 %convolution_convert_fusion.2 = bf16[768,2048]{1,0:T(8,128)(2,1)} fusion(bf16[1280,768]{1,0:T(8,128)(2,1)} %get-tuple-element.78, bf16[1280,2048]{1,0:T(8,128)(2,1)} %dy_hbm.1), kind=kOutput, calls=%fused_computation.2 | convolution fusion | flops 4028104704 | bytes 10354688 | tf_op jit(solution)/shard_map/dot_general | solution.py:1194
  262.1 1.8 collective-permute-start.3
  264.2 13.5 %convolution_convert_fusion = bf16[2048,1536]{1,0:T(8,128)(2,1)} fusion(bf16[1280,2048]{1,0:T(8,128)(2,1)} %get-tuple-element.82, bf16[1280,1536]{1,0:T(8,128)(2,1)} %get-tuple-element.83), kind=kOutput, calls=%fused_computation | convolution fusion | flops 8056209408 | bytes 15466496 | tf_op jit(solution)/shard_map/dot_general | solution.py:1194
  277.7 1.8 add_convert_fusion.1
  279.5 1.9 collective-permute-start.5
  281.6 11.8 %attend_back.1 = (bf16[1280,128]{1,0:T(8,128)(2,1)}, bf16[1280,128]{1,0:T(8,128)(2,1)}, bf16[5120,256]{1,0:T(8,128)(2,1)}) custom-call(s32[1280]{0:T(1024)} %copy-done.6, s32[1]{0:T(128)} %bitcast.3.base_sm, bf16[1280,128]{1,0:T(8,128)(2,1)} %get-tuple-element.63.q_ref, bf16[5120,256]{1,0:T(8,128)(2,1)} %get-tuple-element.64.kv_ref, ...), custom_call_target="tpu_custom_call" | custom-call | flops 8388608000 | bytes 8388608 | tf_op jit(solution)/shard_map/attend_back/pallas_call | solution.py:1145
  294.8 2.5 reduce-scatter.7.cloned.1.call-done
  297.3 2.5 convert_element_type.95
  299.8 45.2 %reduce-scatter.5.cloned.1.call-done.wout_ref = bf16[1024,512]{1,0:T(8,128)(2,1)} async-done(((bf16[1024,2048]{1,0:T(8,128)(2,1)}), bf16[1024,512]{1,0:T(8,128)(2,1)}) %reduce-scatter.5.cloned.1.call-update) | async-done | bytes 1048592 | tf_op jit(solution)/shard_map/reduce_scatter | solution.py:1273
  345.0 20.3 %fold.1 = bf16[1280,128]{1,0:T(8,128)(2,1)} custom-call(bf16[5120,256]{1,0:T(8,128)(2,1)} %get-tuple-element.94.part_ref), custom_call_target="tpu_custom_call" | custom-call | tf_op jit(solution)/shard_map/fold/pallas_call | solution.py:912
  367.4 6.6 %convolution_convert_fusion.3 = bf16[2048,384]{1,0:T(8,128)(2,1)} fusion(bf16[1280,2048]{1,0:T(8,128)(2,1)} %get-tuple-element.97, bf16[1280,384]{1,0:T(8,128)(2,1)S(1)} %pad_maximum_fusion.cat_ref), kind=kOutput, calls=%fused_computation.3 | convolution fusion | flops 2014052352 | bytes 7798784 | tf_op jit(solution)/shard_map/dot_general | solution.py:1194
  375.2 2.0 constant_dynamic-slice_fusion.x_ref
  378.2 171.7 %tail.1 = (bf16[8,160,2048]{2,1,0:T(8,128)(2,1)}, bf16[8,160,2048]{2,1,0:T(8,128)(2,1)}, f32[2,512]{1,0:T(2,128)}, f32[128,512]{1,0:T(8,128)}) custom-call(bf16[1280,384]{1,0:T(8,128)(2,1)} %copy-done.1, bf16[2048,512]{1,0:T(8,128)(2,1)} %get-tuple-element.99.w_ref, bf16[160,2048]{1,0:T(8,128)(2,1)} %constant_dynamic-slice_fusion.x_ref, f32[1,2048]{1,0:T(1,128)} %bitcast.31, ...), custom_call_target="tpu_custom_call" | custom-call | flops 2013265920 | bytes 419430400 | tf_op jit(solution)/shard_map/tail/pallas_call | solution.py:1109
  553.9 1.8 fusion.3
  555.7 3.4 fusion.2
  559.1 5.8 %copy.47 = bf16[1280,2048]{1,0:T(8,128)(2,1)} copy(bf16[1280,2048]{1,0:T(8,128)(2,1)} %bitcast.27) | data formatting | bytes 10485760
  564.9 2.4 copy.48
  (71 shorter events, 23.1 us)
Async XLA Ops:
  7.2 122.7 %all-gather.3.cloned.1.call-start = ((), (), s32[]{:S(2)}) async-start(), calls=%async_computation.4 | async-start | bytes 3932160 | tf_op jit(solution)/shard_map/all_gather | solution.py:1238
  12.3 72.1 %copy-start.5 = (s32[1280]{0:T(1024)S(1)}, s32[1280]{0:T(1024)}, u32[]{:S(2)}) copy-start(s32[1280]{0:T(1024)} %param.14) | copy-start | bytes 15364
  82.6 59.2 %all-gather.5.cloned.1.call-start = ((), (), s32[]{:S(2)}) async-start(), calls=%async_computation.5 | async-start | bytes 3932160 | tf_op jit(solution)/shard_map/all_gather | solution.py:1239
  83.4 214.0 %reduce-scatter.7.cloned.1.call-start = ((), (), s32[]{:S(2)}) async-start(), calls=%async_computation.7 | async-start | bytes 3932160 | tf_op jit(solution)/shard_map/reduce_scatter | solution.py:1276
  84.5 0.6 copy-start.6
  93.9 35.3 %copy-start.7 = (f32[4,8,128]{2,1,0:T(8,128)S(1)}, f32[4,8,128]{2,1,0:T(8,128)}, u32[]{:S(2)}) copy-start(f32[4,8,128]{2,1,0:T(8,128)} %get-tuple-element.69) | copy-start | bytes 49156
  242.3 4.6 copy-start.9
  242.3 5.4 copy-start.8
  246.9 11.8 %collective-permute-start.1 = (bf16[160,2048]{1,0:T(8,128)(2,1)S(1)}, bf16[160,2048]{1,0:T(8,128)(2,1)S(1)}, u32[]{:S(2)}, u32[]{:S(2)}) collective-permute-start(bf16[160,2048]{1,0:T(8,128)(2,1)S(1)} %copy-done.9), channel_id=1, source_target_pairs={{0,1},{2,0},{4,2},{6,4},{7,6},{5,7},{3,5},{1,3},{8,9},{10,8},{12,1... | collective-permute-start | bytes 1966088 | tf_op jit(solution)/shard_map/ppermute | solution.py:1180
  247.7 11.9 %collective-permute-start = (bf16[160,2048]{1,0:T(8,128)(2,1)S(1)}, bf16[160,2048]{1,0:T(8,128)(2,1)S(1)}, u32[]{:S(2)}, u32[]{:S(2)}) collective-permute-start(bf16[160,2048]{1,0:T(8,128)(2,1)S(1)} %copy-done.8), channel_id=1, source_target_pairs={{0,2},{2,4},{4,6},{6,7},{7,5},{5,3},{3,1},{1,0},{8,10},{10,12},{12... | collective-permute-start | bytes 1966088 | tf_op jit(solution)/shard_map/ppermute | solution.py:1179
  261.4 83.6 %reduce-scatter.5.cloned.1.call-start = ((), (), s32[]{:S(2)}) async-start(), calls=%async_computation.6 | async-start | bytes 5242880 | tf_op jit(solution)/shard_map/reduce_scatter | solution.py:1273
  262.0 289.2 %reduce-scatter.9.cloned.1.call-start = ((), (), s32[]{:S(2)}) async-start(), calls=%async_computation.8 | async-start | bytes 1966080 | tf_op jit(solution)/shard_map/reduce_scatter | solution.py:1304
  262.1 15.6 %collective-permute-start.3 = (bf16[160,2048]{1,0:T(8,128)(2,1)S(1)}, bf16[160,2048]{1,0:T(8,128)(2,1)S(1)}, u32[]{:S(2)}, u32[]{:S(2)}) collective-permute-start(bf16[160,2048]{1,0:T(8,128)(2,1)S(1)} %get-tuple-element.85), channel_id=1, source_target_pairs={{0,1},{2,0},{4,2},{6,4},{7,6},{5,7},{3,5},{1,3},{8,9},{10,8},{12,1... | collective-permute-start | bytes 1966088 | tf_op jit(solution)/shard_map/ppermute | solution.py:1180
  263.9 13.8 %collective-permute-start.2 = (bf16[160,2048]{1,0:T(8,128)(2,1)S(1)}, bf16[160,2048]{1,0:T(8,128)(2,1)S(1)}, u32[]{:S(2)}, u32[]{:S(2)}) collective-permute-start(bf16[160,2048]{1,0:T(8,128)(2,1)S(1)} %get-tuple-element.84), channel_id=1, source_target_pairs={{0,2},{2,4},{4,6},{6,7},{7,5},{5,3},{3,1},{1,0},{8,10},{10,12},{12... | collective-permute-start | bytes 1966088 | tf_op jit(solution)/shard_map/ppermute | solution.py:1179
  279.5 13.9 %collective-permute-start.5 = (bf16[160,2048]{1,0:T(8,128)(2,1)S(1)}, bf16[160,2048]{1,0:T(8,128)(2,1)S(1)}, u32[]{:S(2)}, u32[]{:S(2)}) collective-permute-start(bf16[160,2048]{1,0:T(8,128)(2,1)S(1)} %get-tuple-element.92), channel_id=1, source_target_pairs={{0,1},{2,0},{4,2},{6,4},{7,6},{5,7},{3,5},{1,3},{8,9},{10,8},{12,1... | collective-permute-start | bytes 1966088 | tf_op jit(solution)/shard_map/ppermute | solution.py:1185
  281.4 12.0 %collective-permute-start.4 = (bf16[160,2048]{1,0:T(8,128)(2,1)S(1)}, bf16[160,2048]{1,0:T(8,128)(2,1)S(1)}, u32[]{:S(2)}, u32[]{:S(2)}) collective-permute-start(bf16[160,2048]{1,0:T(8,128)(2,1)S(1)} %get-tuple-element.91), channel_id=1, source_target_pairs={{0,2},{2,4},{4,6},{6,7},{7,5},{5,3},{3,1},{1,0},{8,10},{10,12},{12... | collective-permute-start | bytes 1966088 | tf_op jit(solution)/shard_map/ppermute | solution.py:1184
  294.8 70.5 %copy-start.2 = (bf16[1280,128]{1,0:T(8,128)(2,1)S(1)}, bf16[1280,128]{1,0:T(8,128)(2,1)}, u32[]{:S(2)}) copy-start(bf16[1280,128]{1,0:T(8,128)(2,1)} %get-tuple-element.88) | copy-start | bytes 983044
  294.8 70.5 %copy-start.3 = (bf16[1280,128]{1,0:T(8,128)(2,1)S(1)}, bf16[1280,128]{1,0:T(8,128)(2,1)}, u32[]{:S(2)}) copy-start(bf16[1280,128]{1,0:T(8,128)(2,1)} %get-tuple-element.89) | copy-start | bytes 983044
  366.5 0.9 copy-start.1
  374.0 3.2 copy-start
  374.0 181.7 %reduce-scatter.11.cloned.1.call-start = ((), (), s32[]{:S(2)}) async-start(), calls=%async_computation.9 | async-start | bytes 7864320 | tf_op jit(solution)/shard_map/reduce_scatter | solution.py:1280
  555.7 9.2 %slice-start = ((s8[5242880]{0:T(1024)(128)(4,1)}), s8[4194304]{0:T(1024)(128)(4,1)S(1)}, s32[]{:S(2)}) async-start(s8[5242880]{0:T(1024)(128)(4,1)} %bitcast.24), calls=%async_computation.10 | async-start | bytes 8388608
  559.1 5.8 %slice-start.1 = ((s8[5242880]{0:T(1024)(128)(4,1)}), s8[1048576]{0:T(1024)(128)(4,1)S(1)}, s32[]{:S(2)}) async-start(s8[5242880]{0:T(1024)(128)(4,1)} %bitcast.24), calls=%async_computation.11 | async-start | bytes 2097152
  564.9 2.4 copy-start.4
Sparse Core Ops, SparseCore 0:
  82.7 29.0 all-gather.2
  113.3 28.4 all-gather.4
  261.6 35.7 reduce-scatter.6
  300.4 44.5 reduce-scatter.4
  374.1 28.1 reduce-scatter.8
  404.9 58.3 reduce-scatter.10

commit v11 on v10

--- a/solution.py
+++ b/solution.py
@@ -164,7 +164,7 @@
     return pl.pallas_call(
         functools.partial(spread_kernel, count, batches, plans),
         out_shape=[jax.ShapeDtypeStruct(shape, a.dtype) for shape, a in zip(shapes, arrays)],
-        in_specs=[hbm] * len(arrays),
+        in_specs=[pl.BlockSpec(memory_space=pltpu.VMEM)] * len(arrays),
         out_specs=[hbm] * len(arrays),
         scratch_shapes=[
             pltpu.SemaphoreType.DMA((slots,)),
@@ -504,8 +504,8 @@
 
 
 def entry_kernel(
-    count, batches, x_ref, w_ref, out_ref, gain_ref, seg_ref, down_ref,
-    n1_ref, q_ref, logit_ref, kv_ref, w_all, out_all, gain_all, seg_all, down_all,
+    count, batches, x_ref, w_ref, out_ref, gain_ref, seg_ref,
+    n1_ref, q_ref, logit_ref, kv_ref, w_all, out_all, gain_all, seg_all,
     send_sem, recv_sem, local_sem,
 ):
     steps = count // 2
@@ -642,12 +642,6 @@
     def kv_view(at):
         return kv_ref.at[part(at, rows)]
 
-    def down_view(at):
-        return down_all.at[:, part(at, down_ref.shape[1])]
-
-    down_out, down_twin = both(down_view, down_ref)
-    stay(down_ref, down_view(batch))
-
     @pl.loop(0, blocks)
     def _(at):
         here = part(at, block)
@@ -673,8 +667,6 @@
     for step in range(2, steps):
         ring(step)
     kv_passed = pass_on(kv_view, kv_out)
-    down_passed = pass_on(down_view, down_out)
-    local[-1].wait()
     for pair in flows:
         for copy in pair:
             copy.wait_recv()
@@ -682,13 +674,13 @@
     for hop in range(others):
         there = out_all.at[:, part(spots[hop] * 2 + core, wide)]
         swaps.append(go(there, there, twin))
-    for copy in (*kv_twin, *kv_passed, *swaps, *down_twin, *down_passed):
+    for copy in (*kv_twin, *kv_passed, *swaps):
         copy.wait_recv()
     for copy in copies:
         copy.wait_send()
 
 
-def entry(tokens, w_shard, w_out, gains, segments, w_down, collective_id):
+def entry(tokens, w_shard, w_out, gains, segments, collective_id):
     count = lax.axis_size("head")
     batches = lax.axis_size("batch")
     others = batches // 2
@@ -708,16 +700,15 @@
             jax.ShapeDtypeStruct((count * size, batches * wide), BF),
             jax.ShapeDtypeStruct((batches, *gains.shape), F32),
             jax.ShapeDtypeStruct((batches, *segments.shape), jnp.int32),
-            jax.ShapeDtypeStruct((w_down.shape[0], batches * w_down.shape[1]), BF),
         ],
-        in_specs=[vmem] * 6,
-        out_specs=[vmem] * 9,
+        in_specs=[vmem] * 5,
+        out_specs=[vmem] * 8,
         scratch_shapes=[sems, sems, pltpu.SemaphoreType.DMA((5,))],
         compiler_params=pltpu.CompilerParams(
             collective_id=collective_id, has_side_effects=True, vmem_limit_bytes=VMEM_LIMIT
         ),
         name="entry",
-    )(tokens, w_shard, w_out, gains, segments, w_down)
+    )(tokens, w_shard, w_out, gains, segments)
 
 
 KEY_BLOCK = 512
@@ -932,8 +923,8 @@
 
 
 def tail_kernel(
-    count, batches, cat_ref, w_ref, x_ref, gain_ref, dh1_ref, out_ref, wout_ref, second_ref,
-    out_all, tok_all, gains_ref, wout_own,
+    count, batches, cat_ref, w_ref, x_ref, gain_ref, dh1_ref, wout_ref, second_ref,
+    out_0, out_r1, out_l1, out_all, tok_all, gains_ref, wout_own,
     part_ref, tok_ref, got, wout_got, gain_own, gain_got, gain_mid, gain_heads,
     send_sem, recv_sem, local_sem,
 ):
@@ -972,7 +963,7 @@
     def gather(own, whole, step, last):
         out = []
         for flow, chunk, device in ((0, place - step, right), (1, place + step, left)):
-            if step:
+            if last:
                 last[flow].wait_recv()
             target = whole.at[lax.rem(chunk + count, count)]
             source = target if step else own
@@ -1004,12 +995,17 @@
             out.append(go(held.at[flow, step - 1], held.at[flow, step], device))
         return out
 
-    keep_out = pltpu.make_async_copy(out_ref, out_all.at[place], local_sem.at[0])
-    keep_out.start()
+    keep = []
+    for index, (piece, shift) in enumerate(
+        ((out_0, 0), (out_r1, -1), (out_l1, 1))
+    ):
+        target = out_all.at[lax.rem(place + shift + count, count)]
+        keep.append(pltpu.make_async_copy(piece, target, local_sem.at[index]))
+        keep[-1].start()
     compute(place + steps)
     sums = reduce(part_ref, got, 0, None)
-    outs = gather(out_ref, out_all, 0, None)
     wsums = reduce(wout_ref, wout_got, 0, None)
+    outs = []
 
     @pl.loop(1, count)
     def _(hop):
@@ -1018,7 +1014,10 @@
     for step in range(1, steps):
         sums = reduce(part_ref, got, step, sums)
         wsums = reduce(wout_ref, wout_got, step, wsums)
-        outs = gather(out_ref, out_all, step, outs)
+        if step == 1:
+            for copy in keep:
+                copy.wait()
+        outs = gather(None, out_all, step, outs)
     for copy in sums:
         copy.wait_recv()
 
@@ -1052,7 +1051,7 @@
         gain_own[pl.ds(1, 1), cols] = second_ref[:, cols]
         tok_ref[:, cols] = (dh1_ref[:, cols] + scale * (gain_ref[:, cols] * dn1) - x * pull).astype(BF)
 
-    keep_tok = pltpu.make_async_copy(tok_ref, tok_all.at[place], local_sem.at[1])
+    keep_tok = pltpu.make_async_copy(tok_ref, tok_all.at[place], local_sem.at[3])
     keep_tok.start()
     toks = gather(tok_ref, tok_all, 0, None)
     wide = width // batches
@@ -1091,18 +1090,16 @@
         copy.wait_recv()
     for copy in copies:
         copy.wait_send()
-    keep_out.wait()
     keep_tok.wait()
 
 
-def tail(d_cat, w_in, x_own, gain, d_resid, out_own, wout_part, second, collective_id):
+def tail(d_cat, w_in, x_own, gain, d_resid, wout_part, second, pieces, collective_id):
     count = lax.axis_size("head")
     batches = lax.axis_size("batch")
     steps = count // 2
     rows, width = x_own.shape
     size, wide = wout_part.shape[0] // count, wout_part.shape[1]
     vmem = pl.BlockSpec(memory_space=pltpu.VMEM)
-    hbm = pl.BlockSpec(memory_space=pl.ANY)
     whole = jax.ShapeDtypeStruct((count, rows, width), BF)
     sems = pltpu.SemaphoreType.DMA((5 * count + batches,))
     gains = (2, width // batches)
@@ -1114,8 +1111,8 @@
             jax.ShapeDtypeStruct(gains, F32),
             jax.ShapeDtypeStruct((size, wide), F32),
         ],
-        in_specs=[vmem] * 8,
-        out_specs=[hbm, hbm, vmem, vmem],
+        in_specs=[vmem] * 10,
+        out_specs=[vmem] * 4,
         scratch_shapes=[
             pltpu.VMEM((count * rows, width), BF),
             pltpu.VMEM((rows, width), BF),
@@ -1127,7 +1124,7 @@
             pltpu.VMEM((count, *gains), F32),
             sems,
             sems,
-            pltpu.SemaphoreType.DMA((2,)),
+            pltpu.SemaphoreType.DMA((4,)),
         ],
         compiler_params=pltpu.CompilerParams(
             collective_id=collective_id, has_side_effects=True, vmem_limit_bytes=VMEM_LIMIT
@@ -1136,7 +1133,7 @@
             flops=2 * count * rows * width * d_cat.shape[1], bytes_accessed=400 << 20, transcendentals=0
         ),
         name="tail",
-    )(d_cat, w_in, x_own, gain, d_resid, out_own, wout_part, second)
+    )(d_cat, w_in, x_own, gain, d_resid, wout_part, second, *pieces)
 
 
 def local_call(kernel, scalars, arrays, outs, scratch, flops, name):
@@ -1228,8 +1225,8 @@
 
     w_shard = jnp.concatenate([w_query, w_gate, w_key, w_value], axis=1)
     gains = jnp.concatenate([norm1_gain, norm2_gain]).reshape(-1, 128).astype(F32)
-    normed_one, queries, gate_logit, kv_all, w_in, out_full, gains, seg_all, down_full = entry(
-        tokens, w_shard, w_out, gains, segment_ids.reshape(-1, 128), w_down, 1
+    normed_one, queries, gate_logit, kv_all, w_in, out_full, gains, seg_all = entry(
+        tokens, w_shard, w_out, gains, segment_ids.reshape(-1, 128), 1
     )
     gains, w_mlp_gate, w_mlp_up = lax.optimization_barrier((gains, w_mlp_gate, w_mlp_up))
     seg_all = seg_all.reshape(-1)
@@ -1257,7 +1254,7 @@
         pair_flops,
         "attend",
     )
-    (mixed_all,) = spread([mixed], (("head", "cols"),), 2)
+    mixed_all, down_full = spread([mixed, w_down], (("head", "cols"), ("batch", "cols")), 2)
     (
         normed_two, hidden, d_pre, mlp_part, resid_own, d_resid, d_resid_low, d_gain_two, d_mixed,
         going, coming,
@@ -1273,7 +1270,6 @@
     d_out_part = lax.psum_scatter(d_out_part, "batch", scatter_dimension=1, tiled=True)
     d_down = rows_inner(hidden, out_grad).astype(BF)
     normed_two, d_down, state = hold((normed_two, d_down, state))
-    d_down = lax.psum_scatter(d_down, "batch", scatter_dimension=1, tiled=True).astype(F32)
     state = flow.send(state)
     d_mlp = rows_inner(normed_two, d_pre).astype(BF)
     d_mixed, d_mlp, state = hold((d_mixed, d_mlp, state))
@@ -1294,17 +1290,20 @@
         5 * pair_flops // 2,
         "attend_back",
     )
-    d_kv_all, state, d_out_part = hold((d_kv_all, state, d_out_part))
-    out_own = (resid_own + state).astype(BF)
+    d_kv_all, state, d_down, d_out_part = hold((d_kv_all, state, d_down, d_out_part))
+    d_down = lax.psum_scatter(d_down, "batch", scatter_dimension=1, tiled=True).astype(F32)
+    right, left = ring_routes(heads)
+    pieces = [(resid_own + state).astype(BF)]
+    pieces += [lax.ppermute(pieces[0], "head", right), lax.ppermute(pieces[0], "head", left)]
     d_kv = fold(d_kv_all, row_count, 4)
+    d_kv, *pieces = hold((d_kv, *pieces))
     d_cat = jnp.concatenate([d_queries, d_gate_logit, d_kv], axis=1)
-    d_cat, d_down = hold((d_cat, d_down))
     d_in = rows_inner(normed_one, d_cat).astype(BF)
-    d_cat, d_in = hold((d_cat, d_in))
+    d_cat, d_in, d_down = hold((d_cat, d_in, d_down))
     d_in = lax.psum_scatter(d_in, "batch", scatter_dimension=0, tiled=True).astype(F32)
     inputs_own = lax.dynamic_slice_in_dim(tokens, me * chunk, chunk, 0)
     output, d_tokens, d_gains, d_out = tail(
-        d_cat, w_in, inputs_own, gain_one[None], d_resid, out_own, d_out_part, d_gain_two, 5
+        d_cat, w_in, inputs_own, gain_one[None], d_resid, d_out_part, d_gain_two, pieces, 5
     )
     output = output.reshape(row_count, width)
     d_tokens = d_tokens.reshape(row_count, width)

time: 576 us -> 600 us (1.042)
  Pallas kernels: 419 us -> 442 us
    reduce_scatter x1, waiting for transfers between devices: 0.01 us -> 55.7 us  [per_device(): lax.psum_scatter(d_mlp, 'batch', scatter_dimension=0, tiled=True)]
    reduce_scatter x1, waiting for transfers between devices: 45.2 us -> 0.02 us  [per_device(): lax.psum_scatter(d_out_part, 'batch', scatter_dimension=1, tiled=True)]
    pallas_call x1, Pallas kernels: 35.3 us -> 65.5 us  [spread(): pl.pallas_call(functools.partial(spread_kernel, count, batches, plans), o...]
    pallas_call x1, Pallas kernels: 20.3 us -> 41.3 us  [fold(): pl.pallas_call(functools.partial(fold_kernel, batches), out_shape=jax.Sha...]
    pallas_call x1, Pallas kernels: 70.3 us -> 54.6 us  [entry(): pl.pallas_call(functools.partial(entry_kernel, count, batches), out_shape...]
    all_gather x1, waiting for transfers between devices: 12 us -> 0.02 us  [per_device(): mup_full = lax.all_gather(w_mlp_up, 'batch', axis=0, tiled=True)]
    pallas_call x1, Pallas kernels: 172 us -> 166 us  [tail(): pl.pallas_call(functools.partial(tail_kernel, count, batches), out_shape=...]
    unnamed x34 -> x42, local copies, waits for them, and re-layouts: 14.5 us -> 15.3 us
  transfers between devices with their start and end apart: 12 -> 14, of which waited for: 5 -> 4; matrix products, arithmetic and copies ran while one was open for 7% -> 8% of each run, Pallas kernels for 40% -> 49%
where the time goes in v11:
time: 600 us; the launch traced here: 598 us
  Pallas kernels  442 us (74%)
  waiting for transfers between devices  59.5 us (10%)
  matrix products  33.6 us (6%)
  local copies, waits for them, and re-layouts  28.3 us (5%)
  between operations  14.5 us (2%)
  other arithmetic  11.3 us (2%)
  starting transfers between devices  8.49 us (1%)
    pallas_call x1, Pallas kernels, tail(): pl.pallas_call(functools.partial(tail_kernel, count, batches), out_shape=...  166 us
    pallas_call x1, Pallas kernels, mlp_back(): pl.pallas_call(functools.partial(mlp_kernel, count), out_shape=[jax.Shape...  96.5 us
    pallas_call x1, Pallas kernels, spread(): pl.pallas_call(functools.partial(spread_kernel, count, batches, plans), o...  65.5 us
    reduce_scatter x1, waiting for transfers between devices, per_device(): lax.psum_scatter(d_mlp, 'batch', scatter_dimension=0, tiled=True)  55.7 us
    pallas_call x1, Pallas kernels, entry(): pl.pallas_call(functools.partial(entry_kernel, count, batches), out_shape...  54.6 us
    pallas_call x1, Pallas kernels, fold(): pl.pallas_call(functools.partial(fold_kernel, batches), out_shape=jax.Sha...  41.3 us
    dot_general x4, matrix products, rows_inner(): lax.dot_general(left, right, (((0,), (0,)), ((), ())), preferred_element_...  33.6 us
    pallas_call x2, Pallas kernels, local_call(): pl.pallas_call(kernel, out_shape=outs, in_specs=[smem] * len(scalars) + [...  18.4 us
  transfers between devices with their start and end apart: 14, of which 4 were waited for; matrix products, arithmetic and copies ran while one was open for 8% of the time, Pallas kernels for 49%

profile of v11, /device:TPU:0, one launch (start us, length us, event | category | flops | bytes accessed | tf_op | source)
XLA Modules:
  0.0 597.7 jit_solution(15891378267904574183)
XLA Ops:
  10.5 1.8 pad_maximum_fusion.w_ref
  12.3 54.6 %entry.1 = (bf16[1280,2048]{1,0:T(8,128)(2,1)}, bf16[1280,128]{1,0:T(8,128)(2,1)}, f32[1280,128]{1,0:T(8,128)}, bf16[5120,256]{1,0:T(8,128)(2,1)}, bf16[2048,512...) custom-call(bf16[1280,2048]{1,0:T(8,128)(2,1)} %x_hbm.1, ...), custom_call_target="tpu_custom_call" | custom-call | tf_op jit(solution)/shard_map/entry/pallas_call | solution.py:692
  70.7 7.6 %attend.1 = (f32[1280,128]{1,0:T(8,128)}, bf16[1280,128]{1,0:T(8,128)(2,1)}, f32[1,1280]{1,0:T(1,128)}) custom-call(s32[1280]{0:T(1024)} %copy-done.9, s32[1]{0:T(128)} %bitcast.3.base_sm, bf16[1280,128]{1,0:T(8,128)(2,1)} %get-tuple-element.68.q_ref, bf16[5120,256]{1,0:T(8,128)(2,1)} %get-tuple-element.69.kv_ref, s32[1,1280]{1,0:T(1,128)} %broadcast_in_dim.22.start_ref, ...), custom_call_target="tpu_custom_call" | custom-call | flops 3355443200 | bytes 8388608 | tf_op jit(solution)/shard_map/attend/pallas_call | solution.py:1142
  78.3 65.5 %spread_2.1 = (bf16[1280,1024]{1,0:T(8,128)(2,1)}, bf16[768,2048]{1,0:T(8,128)(2,1)}) custom-call(bf16[1280,128]{1,0:T(8,128)(2,1)} %get-tuple-element.72.refs_0_, bf16[768,512]{1,0:T(8,128)(2,1)} %refs_1_.1), custom_call_target="tpu_custom_call" | custom-call | tf_op jit(solution)/shard_map/spread_2/pallas_call | solution.py:164
  143.9 96.5 %mlp_back.1 = (bf16[1280,2048]{1,0:T(8,128)(2,1)}, bf16[1280,768]{1,0:T(8,128)(2,1)}, bf16[1280,1536]{1,0:T(8,128)(2,1)}, bf16[1280,2048]{1,0:T(8,128)(2,1)}, f3...) custom-call(bf16[1280,2048]{1,0:T(8,128)(2,1)} %x_hbm.1, ...), custom_call_target="tpu_custom_call" | custom-call | flops 29527900160 | bytes 41943040 | tf_op jit(solution)/shard_map/mlp_back/pallas_call | solution.py:470
  240.5 4.5 convolution_convert_fusion.1
  248.1 9.5 %convolution_convert_fusion.2 = bf16[768,2048]{1,0:T(8,128)(2,1)} fusion(bf16[1280,768]{1,0:T(8,128)(2,1)} %get-tuple-element.84, bf16[1280,2048]{1,0:T(8,128)(2,1)} %dy_hbm.1), kind=kOutput, calls=%fused_computation.2 | convolution fusion | flops 4028104704 | bytes 10354688 | tf_op jit(solution)/shard_map/dot_general | solution.py:1191
  258.3 2.1 add_convert_fusion.3
  260.4 1.5 collective-permute-start.3
  262.5 12.7 %convolution_convert_fusion = bf16[2048,1536]{1,0:T(8,128)(2,1)} fusion(bf16[1280,2048]{1,0:T(8,128)(2,1)} %get-tuple-element.88, bf16[1280,1536]{1,0:T(8,128)(2,1)S(1)} %copy-done.12), kind=kOutput, calls=%fused_computation | convolution fusion | flops 8056209408 | bytes 15466496 | tf_op jit(solution)/shard_map/dot_general | solution.py:1191
  275.2 1.8 add_convert_fusion.1
  277.0 1.6 collective-permute-start.5
  279.1 10.8 %attend_back.1 = (bf16[1280,128]{1,0:T(8,128)(2,1)}, bf16[1280,128]{1,0:T(8,128)(2,1)}, bf16[5120,256]{1,0:T(8,128)(2,1)}) custom-call(s32[1280]{0:T(1024)} %copy-done.9, s32[1]{0:T(128)} %bitcast.3.base_sm, bf16[1280,128]{1,0:T(8,128)(2,1)} %get-tuple-element.68.q_ref, bf16[5120,256]{1,0:T(8,128)(2,1)} %get-tuple-element.69.kv_ref, ...), custom_call_target="tpu_custom_call" | custom-call | flops 8388608000 | bytes 8388608 | tf_op jit(solution)/shard_map/attend_back/pallas_call | solution.py:1142
  295.1 41.3 %fold.1 = bf16[1280,128]{1,0:T(8,128)(2,1)} custom-call(bf16[5120,256]{1,0:T(8,128)(2,1)} %get-tuple-element.101.part_ref), custom_call_target="tpu_custom_call" | custom-call | tf_op jit(solution)/shard_map/fold/pallas_call | solution.py:903
  337.8 6.9 %convolution_convert_fusion.3 = bf16[2048,384]{1,0:T(8,128)(2,1)} fusion(bf16[1280,2048]{1,0:T(8,128)(2,1)} %get-tuple-element.105, bf16[1280,384]{1,0:T(8,128)(2,1)S(1)} %constant_dynamic-update-slice_fusion.cat_ref), kind=kOutput, calls=%fused_computation.3 | convolution fusion | flops 2014052352 | bytes 7798784 | tf_op jit(solution)/shard_map/dot_general | solution.py:1191
  344.7 1.7 reduce-scatter.7.cloned.1.call-done
  346.4 2.5 convert_element_type.97
  349.5 2.0 constant_dynamic-slice_fusion.x_ref
  351.5 55.7 %reduce-scatter.11.cloned.1.call-done = bf16[512,1536]{1,0:T(8,128)(2,1)} async-done(((bf16[2048,1536]{1,0:T(8,128)(2,1)}), bf16[512,1536]{1,0:T(8,128)(2,1)}) %reduce-scatter.11.cloned.1.call-update) | async-done | bytes 1572880 | tf_op jit(solution)/shard_map/reduce_scatter | solution.py:1276
  407.2 3.3 fusion.2
  410.4 165.6 %tail.1 = (bf16[8,160,2048]{2,1,0:T(8,128)(2,1)}, bf16[8,160,2048]{2,1,0:T(8,128)(2,1)}, f32[2,512]{1,0:T(2,128)}, f32[128,512]{1,0:T(8,128)}) custom-call(bf16[1280,384]{1,0:T(8,128)(2,1)} %copy-done.1, bf16[2048,512]{1,0:T(8,128)(2,1)} %get-tuple-element.108.w_ref, bf16[160,2048]{1,0:T(8,128)(2,1)} %constant_dynamic-slice_fusion.x_ref, ...), custom_call_target="tpu_custom_call" | custom-call | flops 2013265920 | bytes 419430400 | tf_op jit(solution)/shard_map/tail/pallas_call | solution.py:1106
  580.0 1.9 fusion.3
  581.9 5.8 copy.49
  587.7 2.4 copy.50
  (83 shorter events, 23.6 us)
Async XLA Ops:
  7.2 136.7 %all-gather.3.cloned.1.call-start = ((), (), s32[]{:S(2)}) async-start(), calls=%async_computation.4 | async-start | bytes 3932160 | tf_op jit(solution)/shard_map/all_gather | solution.py:1235
  12.3 56.4 %copy-start.8 = (s32[1280]{0:T(1024)S(1)}, s32[1280]{0:T(1024)}, u32[]{:S(2)}) copy-start(s32[1280]{0:T(1024)} %param.14) | copy-start | bytes 15364
  66.9 77.0 %all-gather.5.cloned.1.call-start = ((), (), s32[]{:S(2)}) async-start(), calls=%async_computation.5 | async-start | bytes 3932160 | tf_op jit(solution)/shard_map/all_gather | solution.py:1236
  67.6 223.7 %reduce-scatter.5.cloned.1.call-start = ((), (), s32[]{:S(2)}) async-start(), calls=%async_computation.6 | async-start | bytes 5242880 | tf_op jit(solution)/shard_map/reduce_scatter | solution.py:1270
  245.0 101.4 %reduce-scatter.7.cloned.1.call-start = ((), (), s32[]{:S(2)}) async-start(), calls=%async_computation.7 | async-start | bytes 3932160 | tf_op jit(solution)/shard_map/reduce_scatter | solution.py:1294
  246.1 11.6 %collective-permute-start.1 = (bf16[160,2048]{1,0:T(8,128)(2,1)S(1)}, bf16[160,2048]{1,0:T(8,128)(2,1)S(1)}, u32[]{:S(2)}, u32[]{:S(2)}) collective-permute-start(bf16[160,2048]{1,0:T(8,128)(2,1)S(1)} %copy-done.11), channel_id=1, source_target_pairs={{0,1},{2,0},{4,2},{6,4},{7,6},{5,7},{3,5},{1,3},{8,9},{10,8},{12,1... | collective-permute-start | bytes 1966088 | tf_op jit(solution)/shard_map/ppermute | solution.py:1177
  246.7 11.6 %collective-permute-start = (bf16[160,2048]{1,0:T(8,128)(2,1)S(1)}, bf16[160,2048]{1,0:T(8,128)(2,1)S(1)}, u32[]{:S(2)}, u32[]{:S(2)}) collective-permute-start(bf16[160,2048]{1,0:T(8,128)(2,1)S(1)} %copy-done.10), channel_id=1, source_target_pairs={{0,2},{2,4},{4,6},{6,7},{7,5},{5,3},{3,1},{1,0},{8,10},{10,12},{12... | collective-permute-start | bytes 1966088 | tf_op jit(solution)/shard_map/ppermute | solution.py:1176
  257.6 4.8 copy-start.12
  260.4 14.8 %collective-permute-start.3 = (bf16[160,2048]{1,0:T(8,128)(2,1)S(1)}, bf16[160,2048]{1,0:T(8,128)(2,1)S(1)}, u32[]{:S(2)}, u32[]{:S(2)}) collective-permute-start(bf16[160,2048]{1,0:T(8,128)(2,1)S(1)} %get-tuple-element.91), channel_id=1, source_target_pairs={{0,1},{2,0},{4,2},{6,4},{7,6},{5,7},{3,5},{1,3},{8,9},{10,8},{12,1... | collective-permute-start | bytes 1966088 | tf_op jit(solution)/shard_map/ppermute | solution.py:1177
  261.9 13.3 %collective-permute-start.2 = (bf16[160,2048]{1,0:T(8,128)(2,1)S(1)}, bf16[160,2048]{1,0:T(8,128)(2,1)S(1)}, u32[]{:S(2)}, u32[]{:S(2)}) collective-permute-start(bf16[160,2048]{1,0:T(8,128)(2,1)S(1)} %get-tuple-element.90), channel_id=1, source_target_pairs={{0,2},{2,4},{4,6},{6,7},{7,5},{5,3},{3,1},{1,0},{8,10},{10,12},{12... | collective-permute-start | bytes 1966088 | tf_op jit(solution)/shard_map/ppermute | solution.py:1176
  277.0 12.9 %collective-permute-start.5 = (bf16[160,2048]{1,0:T(8,128)(2,1)S(1)}, bf16[160,2048]{1,0:T(8,128)(2,1)S(1)}, u32[]{:S(2)}, u32[]{:S(2)}) collective-permute-start(bf16[160,2048]{1,0:T(8,128)(2,1)S(1)} %get-tuple-element.98), channel_id=1, source_target_pairs={{0,1},{2,0},{4,2},{6,4},{7,6},{5,7},{3,5},{1,3},{8,9},{10,8},{12,1... | collective-permute-start | bytes 1966088 | tf_op jit(solution)/shard_map/ppermute | solution.py:1182
  278.5 11.4 %collective-permute-start.4 = (bf16[160,2048]{1,0:T(8,128)(2,1)S(1)}, bf16[160,2048]{1,0:T(8,128)(2,1)S(1)}, u32[]{:S(2)}, u32[]{:S(2)}) collective-permute-start(bf16[160,2048]{1,0:T(8,128)(2,1)S(1)} %get-tuple-element.97), channel_id=1, source_target_pairs={{0,2},{2,4},{4,6},{6,7},{7,5},{5,3},{3,1},{1,0},{8,10},{10,12},{12... | collective-permute-start | bytes 1966088 | tf_op jit(solution)/shard_map/ppermute | solution.py:1181
  291.4 115.8 %reduce-scatter.11.cloned.1.call-start = ((), (), s32[]{:S(2)}) async-start(), calls=%async_computation.9 | async-start | bytes 7864320 | tf_op jit(solution)/shard_map/reduce_scatter | solution.py:1276
  291.9 285.4 %reduce-scatter.9.cloned.1.call-start = ((), (), s32[]{:S(2)}) async-start(), calls=%async_computation.8 | async-start | bytes 1966080 | tf_op jit(solution)/shard_map/reduce_scatter | solution.py:1303
  292.0 2.9 copy-start.6
  292.0 3.0 copy-start.5
  292.8 51.9 %copy-start = (bf16[160,2048]{1,0:T(8,128)(2,1)}, bf16[160,2048]{1,0:T(8,128)(2,1)S(1)}, u32[]{:S(2)}) copy-start(bf16[160,2048]{1,0:T(8,128)(2,1)S(1)} %add_convert_fusion.out_0) | copy-start | bytes 1966084
  292.8 43.6 %collective-permute-start.6 = (bf16[160,2048]{1,0:T(8,128)(2,1)S(1)}, bf16[160,2048]{1,0:T(8,128)(2,1)S(1)}, u32[]{:S(2)}, u32[]{:S(2)}) collective-permute-start(bf16[160,2048]{1,0:T(8,128)(2,1)S(1)} %add_convert_fusion.out_0), channel_id=1, source_target_pairs={{0,2},{2,4},{4,6},{6,7},{7,5},{5,3},{3,1},{1,0},{8,10},{10,12},{12... | collective-permute-start | bytes 1966088 | tf_op jit(solution)/shard_map/ppermute | solution.py:1297
  294.0 42.5 %collective-permute-start.7 = (bf16[160,2048]{1,0:T(8,128)(2,1)S(1)}, bf16[160,2048]{1,0:T(8,128)(2,1)S(1)}, u32[]{:S(2)}, u32[]{:S(2)}) collective-permute-start(bf16[160,2048]{1,0:T(8,128)(2,1)S(1)} %add_convert_fusion.out_0), channel_id=1, source_target_pairs={{0,1},{2,0},{4,2},{6,4},{7,6},{5,7},{3,5},{1,3},{8,9},{10,8},{12,1... | collective-permute-start | bytes 1966088 | tf_op jit(solution)/shard_map/ppermute | solution.py:1297
  336.4 8.3 %copy-start.3 = (bf16[160,2048]{1,0:T(8,128)(2,1)}, bf16[160,2048]{1,0:T(8,128)(2,1)S(1)}, u32[]{:S(2)}) copy-start(bf16[160,2048]{1,0:T(8,128)(2,1)S(1)} %collective-permute-done.6.out_r1) | copy-start | bytes 1966084
  336.4 8.3 %copy-start.4 = (bf16[160,2048]{1,0:T(8,128)(2,1)}, bf16[160,2048]{1,0:T(8,128)(2,1)S(1)}, u32[]{:S(2)}) copy-start(bf16[160,2048]{1,0:T(8,128)(2,1)S(1)} %collective-permute-done.7.out_l1) | copy-start | bytes 1966084
  337.8 6.9 %copy-start.1 = (bf16[1280,384]{1,0:T(8,128)(2,1)}, bf16[1280,384]{1,0:T(8,128)(2,1)S(1)}, u32[]{:S(2)}) copy-start(bf16[1280,384]{1,0:T(8,128)(2,1)S(1)} %constant_dynamic-update-slice_fusion.cat_ref) | copy-start | bytes 2949124
  580.0 7.7 %slice-start = ((s8[5242880]{0:T(1024)(128)(4,1)}), s8[4194304]{0:T(1024)(128)(4,1)S(1)}, s32[]{:S(2)}) async-start(s8[5242880]{0:T(1024)(128)(4,1)} %bitcast.24), calls=%async_computation.10 | async-start | bytes 8388608
  581.9 5.8 slice-start.1
  (5 other events, 8.5 us)
Sparse Core Ops, SparseCore 0:
  67.0 28.5 all-gather.2
  97.2 35.5 all-gather.4
  245.1 42.4 reduce-scatter.4
  291.5 54.8 reduce-scatter.6
  348.8 58.3 reduce-scatter.10
  410.3 28.2 reduce-scatter.8

commit v12 on v10

--- a/solution.py
+++ b/solution.py
@@ -164,7 +164,7 @@
     return pl.pallas_call(
         functools.partial(spread_kernel, count, batches, plans),
         out_shape=[jax.ShapeDtypeStruct(shape, a.dtype) for shape, a in zip(shapes, arrays)],
-        in_specs=[hbm] * len(arrays),
+        in_specs=[pl.BlockSpec(memory_space=pltpu.VMEM)] * len(arrays),
         out_specs=[hbm] * len(arrays),
         scratch_shapes=[
             pltpu.SemaphoreType.DMA((slots,)),
@@ -180,10 +180,10 @@
 
 def mlp_kernel(
     count, x_hbm, a_hbm, dy_hbm, gain_ref, out_w, gate_w, up_w, down_w,
-    n2_hbm, hid_hbm, grad_hbm, mlp_hbm, h1_ref, dh1_ref, low_ref, dgain_ref, da_ref, ahead_ref, behind_ref,
-    x_s, a_s, dy_s, n2_s, hid_s, grad_s, mlp_s, h1_s, dy_own, da_part, mlp_far, mlp_got,
-    right_part, left_part, right_got, left_got,
-    in_sem, out_sem, send_sem, recv_sem, da_send, da_recv, far_send, far_recv,
+    mlp_hbm, dmlp_hbm, ddown_hbm, h1_ref, dh1_ref, low_ref, dgain_ref, da_ref, ahead_ref, behind_ref,
+    x_s, a_s, mlp_s, h1_s, dy_all, n2_all, hid_all, grad_all, dmlp_s, ddown_s, da_part,
+    mlp_far, mlp_next, mlp_got, right_part, left_part, right_got, left_got,
+    in_sem, out_sem, grad_sem, send_sem, recv_sem, da_send, da_recv, far_send, far_recv,
 ):
     steps = count // 2
     rows = x_hbm.shape[0] // count
@@ -210,51 +210,53 @@
     def span(owner):
         return pl.ds(pl.multiple_of(owner * rows, rows), rows)
 
+    def tile_of(at, extent=tile):
+        return pl.ds(pl.multiple_of(at * extent, extent), extent)
+
     def loads(group, slot):
         return [
             pltpu.make_async_copy(
                 source.at[span(owner)],
-                target.at[slot, pl.ds(at * rows, rows)],
+                target.at[pl.ds(at * rows, rows)],
                 in_sem.at[slot, 2 * index + at],
             )
-            for index, (source, target) in enumerate(((x_hbm, x_s), (a_hbm, a_s), (dy_hbm, dy_s)))
+            for index, (source, target) in enumerate(
+                ((x_hbm, x_s.at[slot]), (a_hbm, a_s.at[slot]), (dy_hbm, dy_all.at[group]))
+            )
             for at, owner in enumerate(owners(group))
         ]
 
     def stores(group, slot):
         return [
             pltpu.make_async_copy(
-                source.at[slot, pl.ds(at * rows, rows)],
-                target.at[span(owner)],
-                out_sem.at[slot, 2 * index + at],
-            )
-            for index, (source, target) in enumerate(
-                ((n2_s, n2_hbm), (hid_s, hid_hbm), (grad_s, grad_hbm), (mlp_s, mlp_hbm))
+                mlp_s.at[slot, pl.ds(at * rows, rows)], mlp_hbm.at[span(owner)], out_sem.at[slot, at]
             )
             for at, owner in enumerate(owners(group))
         ]
 
-    def passing(source, target, flow, step, device):
+    def passing(source, target, sems, slot, device):
         return pltpu.make_async_remote_copy(
             src_ref=source,
             dst_ref=target,
-            send_sem=send_sem.at[flow * steps + step],
-            recv_sem=recv_sem.at[flow * steps + step],
+            send_sem=sems[0].at[slot],
+            recv_sem=sems[1].at[slot],
             device_id=device,
             device_id_type=MESH,
         )
 
+    ring_sems, far_sems = (send_sem, recv_sem), (far_send, far_recv)
+    ahead, behind = pl.ds(0, side), pl.ds(side, side)
+
     def first_copies():
-        ahead, behind = pl.ds(0, side), pl.ds(side, side)
         return (
-            passing(right_part.at[0, :, ahead], right_got.at[0, :, ahead], 0, 0, right),
-            passing(right_part.at[0, :, behind], left_got.at[0, :, behind], 1, 0, left),
+            passing(right_part.at[0, :, ahead], right_got.at[0, :, ahead], ring_sems, 0, right),
+            passing(right_part.at[0, :, behind], left_got.at[0, :, behind], ring_sems, steps, left),
         )
 
     def later_copies(step):
         return (
-            passing(right_part.at[step], right_got.at[step], 0, step, right),
-            passing(left_part.at[step], left_got.at[step], 1, step, left),
+            passing(right_got.at[step - 1], right_got.at[step], ring_sems, step, right),
+            passing(left_got.at[step - 1], left_got.at[step], ring_sems, steps + step, left),
         )
 
     for copy in loads(0, 0):
@@ -279,7 +281,7 @@
         mixed = a_s[slot]
 
         def residual(at, total):
-            cols = pl.ds(pl.multiple_of(at * tile, tile), tile)
+            cols = tile_of(at)
             values = x_s[slot, :, cols].astype(F32) + matmul(mixed, out_w[:, cols])
             h1_s[:, cols] = values
             return total + jnp.sum(values * values, axis=1, keepdims=True)
@@ -290,39 +292,39 @@
         @pl.when(group == 0)
         def _():
             h1_ref[...] = h1_s[pl.ds(rows, rows)]
-            dy_own[...] = dy_s[slot, pl.ds(rows, rows)]
 
         @pl.loop(0, width // tile)
         def _(at):
-            cols = pl.ds(pl.multiple_of(at * tile, tile), tile)
-            n2_s[slot, :, cols] = (h1_s[:, cols] * scale * gain_ref[:, cols]).astype(BF)
-
-        normed = n2_s[slot]
-        dy = dy_s[slot]
+            cols = tile_of(at)
+            n2_all[group, :, cols] = (h1_s[:, cols] * scale * gain_ref[:, cols]).astype(BF)
+
+        normed = n2_all[group]
+        dy = dy_all[group]
 
         @pl.loop(0, hidden // inner)
         def _(at):
-            cols = pl.ds(pl.multiple_of(at * inner, inner), inner)
+            cols = tile_of(at, inner)
             cols_up = pl.ds(pl.multiple_of(hidden + at * inner, inner), inner)
             gate = matmul(normed, gate_w[:, cols])
             up = matmul(normed, up_w[:, cols])
             d_hidden = cols_inner(dy, down_w[cols])
             sig = jax.nn.sigmoid(gate)
             silu = gate * sig
-            hid_s[slot, :, cols] = (silu * up).astype(BF)
-            grad_s[slot, :, cols] = (d_hidden * up * sig * (1.0 + gate * (1.0 - sig))).astype(BF)
-            grad_s[slot, :, cols_up] = (d_hidden * silu).astype(BF)
-
-        hid = hid_s[slot]
-        d_gate = grad_s[slot, :, :hidden]
-        d_up = grad_s[slot, :, hidden:]
+            hid_all[group, :, cols] = (silu * up).astype(BF)
+            grad_all[group, :, cols] = (d_hidden * up * sig * (1.0 + gate * (1.0 - sig))).astype(BF)
+            grad_all[group, :, cols_up] = (d_hidden * silu).astype(BF)
+
+        hid = hid_all[group]
+        d_gate = grad_all[group, :, :hidden]
+        d_up = grad_all[group, :, hidden:]
+        half = jnp.minimum(group, 1)
 
         @pl.loop(0, width // tile)
         def _(at):
-            cols = pl.ds(pl.multiple_of(at * tile, tile), tile)
+            cols = tile_of(at)
             part = (cols_inner(d_gate, gate_w[cols]) + cols_inner(d_up, up_w[cols])).astype(BF)
-            right_part[group, :, cols] = part[:rows]
-            left_part[group, :, cols] = part[rows:]
+            right_part[half, :, cols] = part[:rows]
+            left_part[half, :, cols] = part[rows:]
             mlp_s[slot, :, cols] = matmul(hid, down_w[:, cols]).astype(BF)
 
         for copy in stores(group, slot):
@@ -331,57 +333,105 @@
         @pl.when(group == 0)
         def _():
             mlp_far[...] = mlp_s[slot, pl.ds(0, rows)]
+            for copy in first_copies():
+                copy.start()
 
         @pl.when(group == 1)
+        def _():
+            mlp_next[0] = mlp_s[slot, pl.ds(0, rows)]
+            mlp_next[1] = mlp_s[slot, pl.ds(rows, rows)]
+            one, two = first_copies()
+            one.wait_recv()
+            right_got[0, :, ahead] = add_low(right_part[1, :, ahead], right_got[0, :, ahead])
+            right_got[0, :, behind] = right_part[1, :, behind]
+            two.wait_recv()
+            left_got[0, :, behind] = add_low(left_part[1, :, behind], left_got[0, :, behind])
+            left_got[0, :, ahead] = left_part[1, :, ahead]
+
+        @pl.when(group == 2)
         def _():
             ahead_ref[...] = mlp_s[slot, pl.ds(0, rows)]
             behind_ref[...] = mlp_s[slot, pl.ds(rows, rows)]
-
-        @pl.when(group == 0)
-        def _():
-            for copy in first_copies():
-                copy.start()
-
-        @pl.when(group == 1)
-        def _():
-            one, two = first_copies()
-            one.wait_recv()
-            two.wait_recv()
-            ahead, behind = pl.ds(0, side), pl.ds(side, side)
-            right_part[1, :, ahead] = add_low(right_part[1, :, ahead], right_got[0, :, ahead])
-            left_part[1, :, behind] = add_low(left_part[1, :, behind], left_got[0, :, behind])
 
         @pl.when(group >= 2)
         def _():
             one, two = later_copies(group - 1)
             one.wait_recv()
-            right_part[group] = add_low(right_part[group], right_got[group - 1])
+            right_got[group - 1] = add_low(right_part[1], right_got[group - 1])
             two.wait_recv()
-            left_part[group] = add_low(left_part[group], left_got[group - 1])
+            left_got[group - 1] = add_low(left_part[1], left_got[group - 1])
 
         @pl.when(group >= 1)
         def _():
             for copy in later_copies(group):
                 copy.start()
 
-    for copy in later_copies(steps - 1):
-        copy.wait_recv()
     far_copies = [
-        pltpu.make_async_remote_copy(
-            src_ref=mlp_far.at[:, pl.ds(flow * side, side)],
-            dst_ref=mlp_got.at[flow],
-            send_sem=far_send.at[flow],
-            recv_sem=far_recv.at[flow],
-            device_id=device,
-            device_id_type=MESH,
-        )
-        for flow, device in ((0, right), (1, left))
+        passing(mlp_far.at[:, ahead], mlp_got.at[0, :, ahead], far_sems, 0, right),
+        passing(mlp_far.at[:, behind], mlp_got.at[1, :, behind], far_sems, 1, left),
     ]
     for copy in far_copies:
         copy.start()
 
-    def tile_of(at):
-        return pl.ds(pl.multiple_of(at * tile, tile), tile)
+    every = steps * 2 * rows
+
+    def dmlp_copy(at, slot):
+        return pltpu.make_async_copy(
+            dmlp_s.at[slot], dmlp_hbm.at[tile_of(at // 2), tile_of(lax.rem(at, 2), hidden)], grad_sem.at[slot]
+        )
+
+    mlp_tiles = 2 * (width // tile)
+
+    @pl.loop(0, mlp_tiles)
+    def _(at):
+        slot = lax.rem(at, 2)
+
+        @pl.when(at >= 2)
+        def _():
+            dmlp_copy(at - 2, slot).wait()
+
+        normed = n2_all[:, :, tile_of(at // 2)].reshape(every, tile)
+        grads = grad_all[:, :, tile_of(lax.rem(at, 2), hidden)].reshape(every, hidden)
+        dmlp_s[slot] = rows_inner(normed, grads).astype(BF)
+        dmlp_copy(at, slot).start()
+
+    wide = 512
+    across = width // wide
+
+    def ddown_copy(at, slot):
+        return pltpu.make_async_copy(
+            ddown_s.at[slot],
+            ddown_hbm.at[tile_of(at // across, inner), tile_of(lax.rem(at, across), wide)],
+            grad_sem.at[2 + slot],
+        )
+
+    down_tiles = across * (hidden // inner)
+
+    @pl.loop(0, down_tiles)
+    def _(at):
+        slot = lax.rem(at, 2)
+
+        @pl.when(at >= 2)
+        def _():
+            ddown_copy(at - 2, slot).wait()
+
+        hid = hid_all[:, :, tile_of(at // across, inner)].reshape(every, inner)
+        dy = dy_all[:, :, tile_of(lax.rem(at, across), wide)].reshape(every, wide)
+        ddown_s[slot] = rows_inner(hid, dy).astype(BF)
+        ddown_copy(at, slot).start()
+
+    for copy in later_copies(steps - 1):
+        copy.wait_recv()
+    for flow, have, lack in ((0, ahead, behind), (1, behind, ahead)):
+        far_copies[flow].wait_recv()
+        mlp_got[flow, :, have] = add_low(mlp_got[flow, :, have], mlp_next[flow, :, have])
+        mlp_got[flow, :, lack] = mlp_next[flow, :, lack]
+    next_copies = [
+        passing(mlp_got.at[0], mlp_got.at[2], far_sems, 2, right),
+        passing(mlp_got.at[1], mlp_got.at[3], far_sems, 3, left),
+    ]
+    for copy in next_copies:
+        copy.start()
 
     def collect(at, state):
         squares, mean = state
@@ -406,18 +456,14 @@
         cols = tile_of(at)
         dn2, h1 = dh1_ref[:, cols], h1_ref[:, cols]
         dgain_ref[:, cols] = jnp.sum(dn2 * h1 * scale_own, axis=0, keepdims=True)
-        d_resid = dy_own[:, cols].astype(F32) + scale_own * (gain_ref[:, cols] * dn2) - h1 * pull
+        dy = dy_all[0, pl.ds(rows, rows), cols].astype(F32)
+        d_resid = dy + scale_own * (gain_ref[:, cols] * dn2) - h1 * pull
         dh1_ref[:, cols] = d_resid
         low_ref[:, cols] = d_resid.astype(BF)
 
     def da_copy(hop):
-        return pltpu.make_async_remote_copy(
-            src_ref=da_part.at[hop],
-            dst_ref=da_ref.at[span(place)],
-            send_sem=da_send.at[hop],
-            recv_sem=da_recv.at[hop],
-            device_id=member(hop)[1],
-            device_id_type=MESH,
+        return passing(
+            da_part.at[hop], da_ref.at[span(place)], (da_send, da_recv), hop, member(hop)[1]
         )
 
     low = low_ref[...]
@@ -425,12 +471,10 @@
     @pl.loop(1, count)
     def _(hop):
         spot = member(hop)[0]
-        part = cols_inner(low, out_w[pl.ds(pl.multiple_of(spot * size, size), size)])
-        da_part[hop] = part.astype(BF)
+        da_part[hop] = cols_inner(low, out_w[tile_of(spot, size)]).astype(BF)
         da_copy(hop).start()
 
-    own_w = out_w[pl.ds(pl.multiple_of(place * size, size), size)]
-    da_ref[span(place)] = cols_inner(low, own_w).astype(BF)
+    da_ref[span(place)] = cols_inner(low, out_w[tile_of(place, size)]).astype(BF)
 
     @pl.loop(1, count)
     def _(hop):
@@ -438,19 +482,19 @@
         da_copy(hop).wait_send()
 
     for flow, held in ((0, ahead_ref), (1, behind_ref)):
-        far_copies[flow].wait_recv()
-        cols = pl.ds(flow * side, side)
-        held[:, cols] = add_low(held[:, cols], mlp_got[flow])
-        far_copies[flow].wait_send()
-
-    for copy in first_copies():
+        next_copies[flow].wait_recv()
+        held[...] = add_low(held[...], mlp_got[2 + flow])
+    for copy in (*far_copies, *next_copies, *first_copies()):
         copy.wait_send()
     for step in range(1, steps):
         for copy in later_copies(step):
             copy.wait_send()
-    for group in range(max(steps - 2, 0), steps):
+    for group in range(steps - 2, steps):
         for copy in stores(group, group % 2):
             copy.wait()
+    for at in range(2):
+        dmlp_copy(mlp_tiles - 2 + at, (mlp_tiles + at) % 2).wait()
+        ddown_copy(down_tiles - 2 + at, (down_tiles + at) % 2).wait()
 
 
 def mlp_back(tokens, mixed, dy, gain, out_w, gate_w, up_w, down_w, collective_id):
@@ -459,41 +503,38 @@
     hidden = gate_w.shape[1]
     rows, steps = total // count, count // 2
     size = mixed.shape[1] // count
+    inner = 256 if hidden % 256 == 0 else 128
     vmem = pl.BlockSpec(memory_space=pltpu.VMEM)
     hbm = pl.BlockSpec(memory_space=pl.ANY)
 
-    def slots(wide, dtype=BF):
-        return pltpu.VMEM((2, 2 * rows, wide), dtype)
-
-    part = pltpu.VMEM((steps, rows, width), BF)
-    flops = 2 * total * width * (mixed.shape[1] + 6 * hidden)
+    def slots(many, tall, wide, dtype=BF):
+        return pltpu.VMEM((many, tall, wide), dtype)
+
+    def shape(*extent, dtype=BF):
+        return jax.ShapeDtypeStruct(extent, dtype)
+
+    dma = pltpu.SemaphoreType.DMA
+    flops = 2 * total * width * (mixed.shape[1] + 9 * hidden)
     return pl.pallas_call(
         functools.partial(mlp_kernel, count),
         out_shape=[
-            jax.ShapeDtypeStruct((total, width), BF),
-            jax.ShapeDtypeStruct((total, hidden), BF),
-            jax.ShapeDtypeStruct((total, 2 * hidden), BF),
-            jax.ShapeDtypeStruct((total, width), BF),
-            jax.ShapeDtypeStruct((rows, width), F32),
-            jax.ShapeDtypeStruct((rows, width), F32),
-            jax.ShapeDtypeStruct((rows, width), BF),
-            jax.ShapeDtypeStruct((1, width), F32),
-            jax.ShapeDtypeStruct((total, size), BF),
-            jax.ShapeDtypeStruct((rows, width), BF),
-            jax.ShapeDtypeStruct((rows, width), BF),
+            shape(total, width), shape(width, 2 * hidden), shape(hidden, width),
+            shape(rows, width, dtype=F32), shape(rows, width, dtype=F32), shape(rows, width),
+            shape(1, width, dtype=F32), shape(total, size), shape(rows, width), shape(rows, width),
         ],
         in_specs=[hbm] * 3 + [vmem] * 5,
-        out_specs=[hbm] * 4 + [vmem] * 7,
+        out_specs=[hbm] * 3 + [vmem] * 7,
         scratch_shapes=[
-            slots(width), slots(mixed.shape[1]), slots(width), slots(width), slots(hidden),
-            slots(2 * hidden), slots(width), pltpu.VMEM((2 * rows, width), F32),
-            pltpu.VMEM((rows, width), BF), pltpu.VMEM((count, rows, size), BF),
-            pltpu.VMEM((rows, width), BF), pltpu.VMEM((2, rows, width // 2), BF),
-            part, part, part, part,
-            pltpu.SemaphoreType.DMA((2, 6)), pltpu.SemaphoreType.DMA((2, 8)),
-            pltpu.SemaphoreType.DMA((count,)), pltpu.SemaphoreType.DMA((count,)),
-            pltpu.SemaphoreType.DMA((count,)), pltpu.SemaphoreType.DMA((count,)),
-            pltpu.SemaphoreType.DMA((2,)), pltpu.SemaphoreType.DMA((2,)),
+            slots(2, 2 * rows, width), slots(2, 2 * rows, mixed.shape[1]), slots(2, 2 * rows, width),
+            pltpu.VMEM((2 * rows, width), F32),
+            slots(steps, 2 * rows, width), slots(steps, 2 * rows, width),
+            slots(steps, 2 * rows, hidden), slots(steps, 2 * rows, 2 * hidden),
+            slots(2, 256, hidden), slots(2, inner, 512), slots(count, rows, size),
+            pltpu.VMEM((rows, width), BF), slots(2, rows, width), slots(4, rows, width),
+            slots(2, rows, width), slots(2, rows, width),
+            slots(steps, rows, width), slots(steps, rows, width),
+            dma((2, 6)), dma((2, 2)), dma((4,)), dma((count,)), dma((count,)),
+            dma((count,)), dma((count,)), dma((4,)), dma((4,)),
         ],
         compiler_params=pltpu.CompilerParams(
             collective_id=collective_id, has_side_effects=True, vmem_limit_bytes=VMEM_LIMIT
@@ -628,6 +669,12 @@
     mate_out, mate_twin = both(mate_view, mate_view(batch))
     ring(0)
 
+    def down_view(at):
+        return down_all.at[:, part(at, down_ref.shape[1])]
+
+    down_out, down_twin = both(down_view, down_ref)
+    stay(down_ref, down_view(batch))
+
     @pl.loop(middle, blocks)
     def _(at):
         normalize(at)
@@ -641,12 +688,6 @@
 
     def kv_view(at):
         return kv_ref.at[part(at, rows)]
-
-    def down_view(at):
-        return down_all.at[:, part(at, down_ref.shape[1])]
-
-    down_out, down_twin = both(down_view, down_ref)
-    stay(down_ref, down_view(batch))
 
     @pl.loop(0, blocks)
     def _(at):
@@ -672,9 +713,8 @@
 
     for step in range(2, steps):
         ring(step)
+    down_passed = pass_on(down_view, down_out)
     kv_passed = pass_on(kv_view, kv_out)
-    down_passed = pass_on(down_view, down_out)
-    local[-1].wait()
     for pair in flows:
         for copy in pair:
             copy.wait_recv()
@@ -932,8 +972,8 @@
 
 
 def tail_kernel(
-    count, batches, cat_ref, w_ref, x_ref, gain_ref, dh1_ref, out_ref, wout_ref, second_ref,
-    out_all, tok_all, gains_ref, wout_own,
+    count, batches, cat_ref, w_ref, x_ref, gain_ref, dh1_ref, wout_ref, second_ref,
+    out_0, out_all, tok_all, gains_ref, wout_own,
     part_ref, tok_ref, got, wout_got, gain_own, gain_got, gain_mid, gain_heads,
     send_sem, recv_sem, local_sem,
 ):
@@ -972,7 +1012,7 @@
     def gather(own, whole, step, last):
         out = []
         for flow, chunk, device in ((0, place - step, right), (1, place + step, left)):
-            if step:
+            if last:
                 last[flow].wait_recv()
             target = whole.at[lax.rem(chunk + count, count)]
             source = target if step else own
@@ -1004,12 +1044,12 @@
             out.append(go(held.at[flow, step - 1], held.at[flow, step], device))
         return out
 
-    keep_out = pltpu.make_async_copy(out_ref, out_all.at[place], local_sem.at[0])
+    keep_out = pltpu.make_async_copy(out_0, out_all.at[place], local_sem.at[0])
     keep_out.start()
     compute(place + steps)
     sums = reduce(part_ref, got, 0, None)
-    outs = gather(out_ref, out_all, 0, None)
     wsums = reduce(wout_ref, wout_got, 0, None)
+    outs = gather(out_0, out_all, 0, None)
 
     @pl.loop(1, count)
     def _(hop):
@@ -1018,7 +1058,7 @@
     for step in range(1, steps):
         sums = reduce(part_ref, got, step, sums)
         wsums = reduce(wout_ref, wout_got, step, wsums)
-        outs = gather(out_ref, out_all, step, outs)
+        outs = gather(out_0, out_all, step, outs)
     for copy in sums:
         copy.wait_recv()
 
@@ -1095,14 +1135,13 @@
     keep_tok.wait()
 
 
-def tail(d_cat, w_in, x_own, gain, d_resid, out_own, wout_part, second, collective_id):
+def tail(d_cat, w_in, x_own, gain, d_resid, wout_part, second, pieces, collective_id):
     count = lax.axis_size("head")
     batches = lax.axis_size("batch")
     steps = count // 2
     rows, width = x_own.shape
     size, wide = wout_part.shape[0] // count, wout_part.shape[1]
     vmem = pl.BlockSpec(memory_space=pltpu.VMEM)
-    hbm = pl.BlockSpec(memory_space=pl.ANY)
     whole = jax.ShapeDtypeStruct((count, rows, width), BF)
     sems = pltpu.SemaphoreType.DMA((5 * count + batches,))
     gains = (2, width // batches)
@@ -1115,7 +1154,7 @@
             jax.ShapeDtypeStruct((size, wide), F32),
         ],
         in_specs=[vmem] * 8,
-        out_specs=[hbm, hbm, vmem, vmem],
+        out_specs=[vmem] * 4,
         scratch_shapes=[
             pltpu.VMEM((count * rows, width), BF),
             pltpu.VMEM((rows, width), BF),
@@ -1136,7 +1175,7 @@
             flops=2 * count * rows * width * d_cat.shape[1], bytes_accessed=400 << 20, transcendentals=0
         ),
         name="tail",
-    )(d_cat, w_in, x_own, gain, d_resid, out_own, wout_part, second)
+    )(d_cat, w_in, x_own, gain, d_resid, wout_part, second, *pieces)
 
 
 def local_call(kernel, scalars, arrays, outs, scratch, flops, name):
@@ -1175,7 +1214,7 @@
     def mine(owner):
         return lax.dynamic_slice_in_dim(part, lax.rem(owner + count, count) * rows, rows, 0)
 
-    for step in range(1, steps - 1):
+    for step in range(2, steps - 1):
         from_left = lax.ppermute(going, "head", right)
         from_right = lax.ppermute(coming, "head", left)
         going = add_low(from_left, mine(place + steps - 1 - step))
@@ -1259,8 +1298,7 @@
     )
     (mixed_all,) = spread([mixed], (("head", "cols"),), 2)
     (
-        normed_two, hidden, d_pre, mlp_part, resid_own, d_resid, d_resid_low, d_gain_two, d_mixed,
-        going, coming,
+        mlp_part, d_mlp, d_down, resid_own, d_resid, d_resid_low, d_gain_two, d_mixed, going, coming,
     ) = mlp_back(
         tokens, mixed_all, out_grad, gain_two[None], out_full, mgate_full, mup_full, down_full, 3
     )
@@ -1269,17 +1307,7 @@
     flow = flow_steps(mlp_part, going, coming)
     state = next(flow)
     d_out_part = rows_inner(mixed_own, d_resid_low).astype(BF)
-    hidden, d_out_part = hold((hidden, d_out_part))
     d_out_part = lax.psum_scatter(d_out_part, "batch", scatter_dimension=1, tiled=True)
-    d_down = rows_inner(hidden, out_grad).astype(BF)
-    normed_two, d_down, state = hold((normed_two, d_down, state))
-    d_down = lax.psum_scatter(d_down, "batch", scatter_dimension=1, tiled=True).astype(F32)
-    state = flow.send(state)
-    d_mlp = rows_inner(normed_two, d_pre).astype(BF)
-    d_mixed, d_mlp, state = hold((d_mixed, d_mlp, state))
-    d_mlp = lax.psum_scatter(d_mlp, "batch", scatter_dimension=0, tiled=True).astype(F32)
-    while isinstance(state, tuple):
-        state = flow.send(state)
 
     d_queries, d_gate_logit, d_kv_all = local_call(
         functools.partial(attend_back_kernel, scale_factor),
@@ -1294,18 +1322,24 @@
         5 * pair_flops // 2,
         "attend_back",
     )
-    d_kv_all, state, d_out_part = hold((d_kv_all, state, d_out_part))
+    d_kv_all, state = hold((d_kv_all, state))
+    while isinstance(state, tuple):
+        state = flow.send(state)
+    d_kv = fold(d_kv_all, row_count, 4)
+    d_kv, state, d_out_part, d_down, d_mlp = hold((d_kv, state, d_out_part, d_down, d_mlp))
     out_own = (resid_own + state).astype(BF)
-    d_kv = fold(d_kv_all, row_count, 4)
+    d_down = lax.psum_scatter(d_down, "batch", scatter_dimension=1, tiled=True)
+    d_mlp = lax.psum_scatter(d_mlp, "batch", scatter_dimension=0, tiled=True)
     d_cat = jnp.concatenate([d_queries, d_gate_logit, d_kv], axis=1)
-    d_cat, d_down = hold((d_cat, d_down))
     d_in = rows_inner(normed_one, d_cat).astype(BF)
     d_cat, d_in = hold((d_cat, d_in))
-    d_in = lax.psum_scatter(d_in, "batch", scatter_dimension=0, tiled=True).astype(F32)
+    d_in = lax.psum_scatter(d_in, "batch", scatter_dimension=0, tiled=True)
     inputs_own = lax.dynamic_slice_in_dim(tokens, me * chunk, chunk, 0)
     output, d_tokens, d_gains, d_out = tail(
-        d_cat, w_in, inputs_own, gain_one[None], d_resid, out_own, d_out_part, d_gain_two, 5
+        d_cat, w_in, inputs_own, gain_one[None], d_resid, d_out_part, d_gain_two, [out_own], 5
     )
+    d_tokens, d_in, d_mlp, d_down = hold((d_tokens, d_in, d_mlp, d_down))
+    d_in, d_mlp, d_down = d_in.astype(F32), d_mlp.astype(F32), d_down.astype(F32)
     output = output.reshape(row_count, width)
     d_tokens = d_tokens.reshape(row_count, width)
     hidden_own = w_mlp_gate.shape[1]

time: 576 us -> 525 us (0.911)
  waiting for transfers between devices: 63.2 us -> 14.2 us
  Pallas kernels: 419 us -> 445 us
  matrix products: 33.8 us -> 11.3 us
    reduce_scatter x1, waiting for transfers between devices: 45.2 us -> 0.02 us  [per_device(): lax.psum_scatter(d_out_part, 'batch', scatter_dimension=1, tiled=True)]
    dot_general x4 -> x2, matrix products: 33.8 us -> 11.3 us  [rows_inner(): lax.dot_general(left, right, (((0,), (0,)), ((), ())), preferred_element_...]
    pallas_call x1, Pallas kernels: 20.3 us -> 34.4 us  [fold(): pl.pallas_call(functools.partial(fold_kernel, batches), out_shape=jax.Sha...]
    pallas_call x1, Pallas kernels: 100 us -> 114 us  [mlp_back(): pl.pallas_call(functools.partial(mlp_kernel, count), out_shape=[shape(tot...]
    unnamed x34 -> x40, local copies, waits for them, and re-layouts: 14.5 us -> 16.4 us
  transfers between devices with their start and end apart: 12 -> 10, of which waited for: 5 -> 1; matrix products, arithmetic and copies ran while one was open for 7% -> 2% of each run, Pallas kernels for 40% -> 51%
where the time goes in v12:
time: 525 us
  Pallas kernels  445 us (85%)
  local copies, waits for them, and re-layouts  26.7 us (5%)
  between operations  14.4 us (3%)
  waiting for transfers between devices  14.2 us (3%)
  matrix products  11.3 us (2%)
  other arithmetic  8.96 us (2%)
    pallas_call x1, Pallas kernels, tail(): pl.pallas_call(functools.partial(tail_kernel, count, batches), out_shape=...  174 us
    pallas_call x1, Pallas kernels, mlp_back(): pl.pallas_call(functools.partial(mlp_kernel, count), out_shape=[shape(tot...  114 us
    pallas_call x1, Pallas kernels, entry(): pl.pallas_call(functools.partial(entry_kernel, count, batches), out_shape...  65.1 us
    pallas_call x1, Pallas kernels, spread(): pl.pallas_call(functools.partial(spread_kernel, count, batches, plans), o...  35.6 us
    pallas_call x1, Pallas kernels, fold(): pl.pallas_call(functools.partial(fold_kernel, batches), out_shape=jax.Sha...  34.4 us
    pallas_call x2, Pallas kernels, local_call(): pl.pallas_call(kernel, out_shape=outs, in_specs=[smem] * len(scalars) + [...  21.2 us
    unnamed x40, local copies, waits for them, and re-layouts  16.4 us
    all_gather x1, waiting for transfers between devices, per_device(): mup_full = lax.all_gather(w_mlp_up, 'batch', axis=0, tiled=True)  12.3 us
  transfers between devices with their start and end apart: 10, of which 1 were waited for; matrix products, arithmetic and copies ran while one was open for 2% of the time, Pallas kernels for 51%

profile of v12, /device:TPU:0, one launch (start us, length us, event | category | flops | bytes accessed | tf_op | source)
XLA Modules:
  0.0 524.8 jit_solution(6938201042228909847)
XLA Ops:
  9.2 1.3 maximum_convert_fusion.gain_ref
  10.5 1.8 pad_maximum_fusion.w_ref
  12.3 65.1 %entry.1 = (bf16[1280,2048]{1,0:T(8,128)(2,1)}, bf16[1280,128]{1,0:T(8,128)(2,1)}, f32[1280,128]{1,0:T(8,128)}, bf16[5120,256]{1,0:T(8,128)(2,1)}, bf16[2048,512...) custom-call(bf16[1280,2048]{1,0:T(8,128)(2,1)} %x_hbm.1, ...), custom_call_target="tpu_custom_call" | custom-call | tf_op jit(solution)/shard_map/entry/pallas_call | solution.py:740
  79.9 8.8 %attend.1 = (f32[1280,128]{1,0:T(8,128)}, bf16[1280,128]{1,0:T(8,128)(2,1)}, f32[1,1280]{1,0:T(1,128)}) custom-call(s32[1280]{0:T(1024)} %copy-done.8, s32[1]{0:T(128)} %bitcast.3.base_sm, bf16[1280,128]{1,0:T(8,128)(2,1)} %get-tuple-element.59.q_ref, bf16[5120,256]{1,0:T(8,128)(2,1)} %get-tuple-element.60.kv_ref, s32[1,1280]{1,0:T(1,128)} %broadcast_in_dim.22.start_ref, ...), custom_call_target="tpu_custom_call" | custom-call | flops 3355443200 | bytes 8388608 | tf_op jit(solution)/shard_map/attend/pallas_call | solution.py:1184
  88.6 35.6 %spread_2.1.a_hbm = bf16[1280,1024]{1,0:T(8,128)(2,1)} custom-call(bf16[1280,128]{1,0:T(8,128)(2,1)} %get-tuple-element.63.refs_0_), custom_call_target="tpu_custom_call" | custom-call | tf_op jit(solution)/shard_map/spread_2/pallas_call | solution.py:164
  124.9 12.3 %all-gather.5.cloned.1.call-done.up_w = bf16[2048,768]{1,0:T(8,128)(2,1)} async-done(((bf16[512,768]{1,0:T(8,128)(2,1)}), bf16[2048,768]{1,0:T(8,128)(2,1)}) %all-gather.5.cloned.1.call-update) | async-done | bytes 3145744 | tf_op jit(solution)/shard_map/all_gather | solution.py:1278
  137.2 114.4 %mlp_back.1 = (bf16[1280,2048]{1,0:T(8,128)(2,1)}, bf16[2048,1536]{1,0:T(8,128)(2,1)}, bf16[768,2048]{1,0:T(8,128)(2,1)}, f32[160,2048]{1,0:T(8,128)}, f32[160,2...) custom-call(bf16[1280,2048]{1,0:T(8,128)(2,1)} %x_hbm.1, ...), custom_call_target="tpu_custom_call" | custom-call | flops 41607495680 | bytes 41943040 | tf_op jit(solution)/shard_map/mlp_back/pallas_call | solution.py:518
  251.6 4.5 convolution_convert_fusion
  257.9 1.3 collective-permute-start
  259.2 12.4 %attend_back.1 = (bf16[1280,128]{1,0:T(8,128)(2,1)}, bf16[1280,128]{1,0:T(8,128)(2,1)}, bf16[5120,256]{1,0:T(8,128)(2,1)}) custom-call(s32[1280]{0:T(1024)} %copy-done.8, s32[1]{0:T(128)} %bitcast.3.base_sm, bf16[1280,128]{1,0:T(8,128)(2,1)} %get-tuple-element.59.q_ref, bf16[5120,256]{1,0:T(8,128)(2,1)} %get-tuple-element.60.kv_ref, ...), custom_call_target="tpu_custom_call" | custom-call | flops 8388608000 | bytes 8388608 | tf_op jit(solution)/shard_map/attend_back/pallas_call | solution.py:1184
  271.7 1.8 add_convert_fusion.1
  274.1 1.4 collective-permute-start.2
  277.1 34.4 %fold.1 = bf16[1280,128]{1,0:T(8,128)(2,1)} custom-call(bf16[5120,256]{1,0:T(8,128)(2,1)} %get-tuple-element.78.part_ref), custom_call_target="tpu_custom_call" | custom-call | tf_op jit(solution)/shard_map/fold/pallas_call | solution.py:952
  311.5 1.4 convert_add_fusion
  313.8 6.8 %convolution_convert_fusion.1 = bf16[2048,384]{1,0:T(8,128)(2,1)} fusion(bf16[1280,2048]{1,0:T(8,128)(2,1)} %get-tuple-element.85, bf16[1280,384]{1,0:T(8,128)(2,1)} %constant_dynamic-update-slice_fusion.cat_ref), kind=kOutput, calls=%fused_computation.1 | convolution fusion | flops 2014052352 | bytes 7798784 | tf_op jit(solution)/shard_map/dot_general | solution.py:1233
  322.4 2.0 constant_dynamic-slice_fusion.x_ref
  325.4 174.2 %tail.1 = (bf16[8,160,2048]{2,1,0:T(8,128)(2,1)}, bf16[8,160,2048]{2,1,0:T(8,128)(2,1)}, f32[2,512]{1,0:T(2,128)}, f32[128,512]{1,0:T(8,128)}) custom-call(bf16[1280,384]{1,0:T(8,128)(2,1)} %constant_dynamic-update-slice_fusion.cat_ref, bf16[2048,512]{1,0:T(8,128)(2,1)} %get-tuple-element.87.w_ref, bf16[160,2048]{1,0:T(8,128)(2,1)} %constant_dynamic-slice_fusion.x_ref, ...), custom_call_target="tpu_custom_call" | custom-call | flops 2013265920 | bytes 419430400 | tf_op jit(solution)/shard_map/tail/pallas_call | solution.py:1148
  499.6 1.3 fusion.5
  501.0 1.9 fusion.3
  502.9 1.1 fusion.4
  505.5 1.9 fusion.2
  507.4 1.4 convert_element_type.67
  508.8 6.2 %copy.49 = bf16[1280,2048]{1,0:T(8,128)(2,1)} copy(bf16[1280,2048]{1,0:T(8,128)(2,1)} %bitcast.23) | data formatting | bytes 10485760
  514.9 2.4 copy.50
  (70 shorter events, 14.8 us)
Async XLA Ops:
  7.2 117.7 %all-gather.3.cloned.1.call-start = ((), (), s32[]{:S(2)}) async-start(), calls=%async_computation.4 | async-start | bytes 3932160 | tf_op jit(solution)/shard_map/all_gather | solution.py:1277
  12.3 66.9 %copy-start.7 = (s32[1280]{0:T(1024)S(1)}, s32[1280]{0:T(1024)}, u32[]{:S(2)}) copy-start(s32[1280]{0:T(1024)} %param.14) | copy-start | bytes 15364
  77.4 59.8 %all-gather.5.cloned.1.call-start = ((), (), s32[]{:S(2)}) async-start(), calls=%async_computation.5 | async-start | bytes 3932160 | tf_op jit(solution)/shard_map/all_gather | solution.py:1278
  78.2 234.8 %reduce-scatter.5.cloned.1.call-start = ((), (), s32[]{:S(2)}) async-start(), calls=%async_computation.6 | async-start | bytes 5242880 | tf_op jit(solution)/shard_map/reduce_scatter | solution.py:1310
  79.2 0.6 copy-start.8
  88.6 35.6 %copy-start.9 = (f32[4,8,128]{2,1,0:T(8,128)S(1)}, f32[4,8,128]{2,1,0:T(8,128)}, u32[]{:S(2)}) copy-start(f32[4,8,128]{2,1,0:T(8,128)} %get-tuple-element.65) | copy-start | bytes 49156
  256.1 1.1 copy-start.11
  256.1 1.9 copy-start.10
  256.1 244.8 %reduce-scatter.7.cloned.1.call-start = ((), (), s32[]{:S(2)}) async-start(), calls=%async_computation.7 | async-start | bytes 1966080 | tf_op jit(solution)/shard_map/reduce_scatter | solution.py:1336
  257.2 14.5 %collective-permute-start.1 = (bf16[160,2048]{1,0:T(8,128)(2,1)S(1)}, bf16[160,2048]{1,0:T(8,128)(2,1)S(1)}, u32[]{:S(2)}, u32[]{:S(2)}) collective-permute-start(bf16[160,2048]{1,0:T(8,128)(2,1)S(1)} %copy-done.11), channel_id=1, source_target_pairs={{0,1},{2,0},{4,2},{6,4},{7,6},{5,7},{3,5},{1,3},{8,9},{10,8},{12,1... | collective-permute-start | bytes 1966088 | tf_op jit(solution)/shard_map/ppermute | solution.py:1219
  257.9 13.7 %collective-permute-start = (bf16[160,2048]{1,0:T(8,128)(2,1)S(1)}, bf16[160,2048]{1,0:T(8,128)(2,1)S(1)}, u32[]{:S(2)}, u32[]{:S(2)}) collective-permute-start(bf16[160,2048]{1,0:T(8,128)(2,1)S(1)} %copy-done.10), channel_id=1, source_target_pairs={{0,2},{2,4},{4,6},{6,7},{7,5},{5,3},{3,1},{1,0},{8,10},{10,12},{12... | collective-permute-start | bytes 1966088 | tf_op jit(solution)/shard_map/ppermute | solution.py:1218
  271.6 3.9 copy-start.5
  271.6 4.7 copy-start.4
  273.5 38.0 %collective-permute-start.3 = (bf16[160,2048]{1,0:T(8,128)(2,1)S(1)}, bf16[160,2048]{1,0:T(8,128)(2,1)S(1)}, u32[]{:S(2)}, u32[]{:S(2)}) collective-permute-start(bf16[160,2048]{1,0:T(8,128)(2,1)S(1)} %get-tuple-element.80), channel_id=1, source_target_pairs={{0,1},{2,0},{4,2},{6,4},{7,6},{5,7},{3,5},{1,3},{8,9},{10,8},{12,1... | collective-permute-start | bytes 1966088 | tf_op jit(solution)/shard_map/ppermute | solution.py:1224
  274.1 37.4 %collective-permute-start.2 = (bf16[160,2048]{1,0:T(8,128)(2,1)S(1)}, bf16[160,2048]{1,0:T(8,128)(2,1)S(1)}, u32[]{:S(2)}, u32[]{:S(2)}) collective-permute-start(bf16[160,2048]{1,0:T(8,128)(2,1)S(1)} %get-tuple-element.79), channel_id=1, source_target_pairs={{0,2},{2,4},{4,6},{6,7},{7,5},{5,3},{3,1},{1,0},{8,10},{10,12},{12... | collective-permute-start | bytes 1966088 | tf_op jit(solution)/shard_map/ppermute | solution.py:1223
  311.5 1.5 copy-start.2
  320.6 180.3 %reduce-scatter.11.cloned.1.call-start = ((), (), s32[]{:S(2)}) async-start(), calls=%async_computation.9 | async-start | bytes 3932160 | tf_op jit(solution)/shard_map/reduce_scatter | solution.py:1331
  321.2 3.2 copy-start.1
  321.2 179.7 %reduce-scatter.9.cloned.1.call-start = ((), (), s32[]{:S(2)}) async-start(), calls=%async_computation.8 | async-start | bytes 7864320 | tf_op jit(solution)/shard_map/reduce_scatter | solution.py:1332
  501.0 4.6 copy-start
  505.5 1.9 copy-start.3
  507.4 7.5 %slice-start = ((s8[5242880]{0:T(1024)(128)(4,1)}), s8[4194304]{0:T(1024)(128)(4,1)S(1)}, s32[]{:S(2)}) async-start(s8[5242880]{0:T(1024)(128)(4,1)} %bitcast.20), calls=%async_computation.10 | async-start | bytes 8388608
  508.8 6.2 %slice-start.1 = ((s8[5242880]{0:T(1024)(128)(4,1)}), s8[1048576]{0:T(1024)(128)(4,1)S(1)}, s32[]{:S(2)}) async-start(s8[5242880]{0:T(1024)(128)(4,1)} %bitcast.20), calls=%async_computation.11 | async-start | bytes 2097152
  514.9 2.4 copy-start.6
Sparse Core Ops, SparseCore 0:
  77.5 29.4 all-gather.2
  108.6 28.6 all-gather.4
  256.2 46.0 reduce-scatter.4
  320.7 28.3 reduce-scatter.6
  351.5 37.9 reduce-scatter.10
  392.1 58.5 reduce-scatter.8

commit v13 on v12

--- a/solution.py
+++ b/solution.py
@@ -172,7 +172,7 @@
             pltpu.SemaphoreType.DMA((len(arrays),)),
         ],
         compiler_params=pltpu.CompilerParams(
-            collective_id=collective_id, has_side_effects=True, vmem_limit_bytes=VMEM_LIMIT
+            collective_id=collective_id, has_side_effects=True, vmem_limit_bytes=8 << 20
         ),
         name=f"spread_{collective_id}",
     )(*arrays)
@@ -754,7 +754,7 @@
         out_specs=[vmem] * 9,
         scratch_shapes=[sems, sems, pltpu.SemaphoreType.DMA((5,))],
         compiler_params=pltpu.CompilerParams(
-            collective_id=collective_id, has_side_effects=True, vmem_limit_bytes=VMEM_LIMIT
+            collective_id=collective_id, has_side_effects=True, vmem_limit_bytes=44 << 20
         ),
         name="entry",
     )(tokens, w_shard, w_out, gains, segments, w_down)
@@ -965,16 +965,18 @@
             sems,
         ],
         compiler_params=pltpu.CompilerParams(
-            collective_id=collective_id, has_side_effects=True, vmem_limit_bytes=VMEM_LIMIT
+            collective_id=collective_id, has_side_effects=True, vmem_limit_bytes=20 << 20
         ),
         name="fold",
     )(part)
 
 
 def tail_kernel(
-    count, batches, cat_ref, w_ref, x_ref, gain_ref, dh1_ref, wout_ref, second_ref,
-    out_0, out_all, tok_all, gains_ref, wout_own,
+    count, batches, cat_ref, w_ref, x_ref, gain_ref, dh1_ref, second_ref,
+    n1_ref, mixed_ref, low_ref, out_0,
+    out_all, tok_all, gains_ref, wout_own, din_ref,
     part_ref, tok_ref, got, wout_got, gain_own, gain_got, gain_mid, gain_heads,
+    din_s, din_got, din_x, wout_s, wout_twin, wout_x, wout_part,
     send_sem, recv_sem, local_sem,
 ):
     steps = count // 2
@@ -996,6 +998,45 @@
         slot += 1
         copies.append(copy)
         return copy
+
+    across, core = batch // 2, lax.rem(batch, 2)
+    spots = [lax.rem(across + hop, batches // 2) for hop in range(batches // 2)]
+    order = list(range(1, batches // 2)) + [0]
+    twin = (across * 2 + 1 - core, head)
+
+    def scatter_swap(view, held):
+        return [go(view(2 * spots[hop] + 1 - core), held.at[spots[hop]], twin) for hop in order]
+
+    def add_tiles(target, one, other):
+        @pl.loop(0, target.shape[0] // 128)
+        def _(at):
+            lines = pl.ds(pl.multiple_of(at * 128, 128), 128)
+            total = one[lines].astype(F32) + other[lines].astype(F32)
+            target[lines] = total.astype(target.dtype)
+
+    def scatter_cross(view, held, crossed, arriving):
+        out = []
+        for copy, hop in zip(arriving, order):
+            copy.wait_recv()
+            spot = spots[hop]
+            add_tiles(held.at[spot], held.at[spot], view(2 * spot + core))
+            if hop:
+                out.append(go(held.at[spot], crossed.at[hop - 1], (spot * 2 + core, head)))
+        return out
+
+    def scatter_end(held, crossed, arriving, target):
+        for hop, copy in enumerate(arriving):
+            copy.wait_recv()
+            last = hop == len(arriving) - 1
+            add_tiles(target if last else held.at[across], held.at[across], crossed.at[hop])
+
+    def wout_view(at):
+        wide = wout_part.shape[1]
+        return wout_s.at[:, pl.ds(pl.multiple_of(at * wide, wide), wide)]
+
+    def din_view(at):
+        tall = din_ref.shape[0]
+        return din_s.at[pl.ds(pl.multiple_of(at * tall, tall), tall)]
 
     def span(owner, extent):
         return pl.ds(pl.multiple_of(lax.rem(owner + count, count) * extent, extent), extent)
@@ -1048,17 +1089,31 @@
     keep_out.start()
     compute(place + steps)
     sums = reduce(part_ref, got, 0, None)
-    wsums = reduce(wout_ref, wout_got, 0, None)
     outs = gather(out_0, out_all, 0, None)
 
     @pl.loop(1, count)
     def _(hop):
         compute(place + steps + hop)
 
+    @pl.loop(0, width // tile)
+    def _(at):
+        cols = pl.ds(pl.multiple_of(at * tile, tile), tile)
+        wout_s[:, cols] = rows_inner(mixed_ref[...], low_ref[:, cols]).astype(BF)
+
+    wouts = scatter_swap(wout_view, wout_twin)
+
+    @pl.loop(0, width // tile)
+    def _(at):
+        cols = pl.ds(pl.multiple_of(at * tile, tile), tile)
+        din_s[cols] = rows_inner(n1_ref[:, cols], cat_ref[...]).astype(BF)
+
+    dins = scatter_swap(din_view, din_got)
     for step in range(1, steps):
         sums = reduce(part_ref, got, step, sums)
-        wsums = reduce(wout_ref, wout_got, step, wsums)
         outs = gather(out_0, out_all, step, outs)
+        if step == 1:
+            wouts = scatter_cross(wout_view, wout_twin, wout_x, wouts)
+            dins = scatter_cross(din_view, din_got, din_x, dins)
     for copy in sums:
         copy.wait_recv()
 
@@ -1095,6 +1150,9 @@
     keep_tok = pltpu.make_async_copy(tok_ref, tok_all.at[place], local_sem.at[1])
     keep_tok.start()
     toks = gather(tok_ref, tok_all, 0, None)
+    scatter_end(wout_twin, wout_x, wouts, wout_part)
+    wsums = reduce(wout_part, wout_got, 0, None)
+    scatter_end(din_got, din_x, dins, din_ref)
     wide = width // batches
 
     def slice_of(at):
@@ -1105,6 +1163,7 @@
         for hop, other in enumerate(others)
     ]
     toks = gather(tok_ref, tok_all, 1, toks)
+    wsums = reduce(wout_part, wout_got, 1, wsums)
     middle = gain_own[:, slice_of(batch)]
     for hop, copy in enumerate(gains):
         copy.wait_recv()
@@ -1114,6 +1173,7 @@
     gains = [go(gain_mid, gain_heads.at[place], member) for member in members]
     for step in range(2, steps):
         toks = gather(tok_ref, tok_all, step, toks)
+        wsums = reduce(wout_part, wout_got, step, wsums)
     for copy in gains:
         copy.wait_recv()
     middle = gain_heads[0]
@@ -1123,7 +1183,7 @@
     for copy in (*wsums, *outs):
         copy.wait_recv()
     wout_own[...] = (
-        wout_ref[span(place, wout_own.shape[0])].astype(F32)
+        wout_part[span(place, wout_own.shape[0])].astype(F32)
         + wout_got[0, steps - 1].astype(F32)
         + wout_got[1, steps - 1].astype(F32)
     )
@@ -1135,15 +1195,17 @@
     keep_tok.wait()
 
 
-def tail(d_cat, w_in, x_own, gain, d_resid, wout_part, second, pieces, collective_id):
+def tail(d_cat, w_in, x_own, gain, d_resid, second, normed, mixed, low, out_own, collective_id):
     count = lax.axis_size("head")
     batches = lax.axis_size("batch")
     steps = count // 2
     rows, width = x_own.shape
-    size, wide = wout_part.shape[0] // count, wout_part.shape[1]
+    others = batches // 2
+    size, wide = mixed.shape[1] // count, width // batches
+    depth = d_cat.shape[1]
     vmem = pl.BlockSpec(memory_space=pltpu.VMEM)
     whole = jax.ShapeDtypeStruct((count, rows, width), BF)
-    sems = pltpu.SemaphoreType.DMA((5 * count + batches,))
+    sems = pltpu.SemaphoreType.DMA((5 * count + 3 * batches,))
     gains = (2, width // batches)
     return pl.pallas_call(
         functools.partial(tail_kernel, count, batches),
@@ -1152,9 +1214,10 @@
             whole,
             jax.ShapeDtypeStruct(gains, F32),
             jax.ShapeDtypeStruct((size, wide), F32),
+            jax.ShapeDtypeStruct((wide, depth), F32),
         ],
-        in_specs=[vmem] * 8,
-        out_specs=[vmem] * 4,
+        in_specs=[vmem] * 10,
+        out_specs=[vmem] * 5,
         scratch_shapes=[
             pltpu.VMEM((count * rows, width), BF),
             pltpu.VMEM((rows, width), BF),
@@ -1164,18 +1227,25 @@
             pltpu.VMEM((batches - 1, *gains), F32),
             pltpu.VMEM(gains, F32),
             pltpu.VMEM((count, *gains), F32),
+            pltpu.VMEM((width, depth), BF),
+            pltpu.VMEM((others, wide, depth), BF),
+            pltpu.VMEM((others - 1, wide, depth), BF),
+            pltpu.VMEM((count * size, width), BF),
+            pltpu.VMEM((others, count * size, wide), BF),
+            pltpu.VMEM((others - 1, count * size, wide), BF),
+            pltpu.VMEM((count * size, wide), BF),
             sems,
             sems,
             pltpu.SemaphoreType.DMA((2,)),
         ],
         compiler_params=pltpu.CompilerParams(
-            collective_id=collective_id, has_side_effects=True, vmem_limit_bytes=VMEM_LIMIT
+            collective_id=collective_id, has_side_effects=True, vmem_limit_bytes=52 << 20
         ),
         cost_estimate=pl.CostEstimate(
             flops=2 * count * rows * width * d_cat.shape[1], bytes_accessed=400 << 20, transcendentals=0
         ),
         name="tail",
-    )(d_cat, w_in, x_own, gain, d_resid, wout_part, second, *pieces)
+    )(d_cat, w_in, x_own, gain, d_resid, second, normed, mixed, low, out_own)
 
 
 def local_call(kernel, scalars, arrays, outs, scratch, flops, name):
@@ -1187,7 +1257,7 @@
         in_specs=[smem] * len(scalars) + [vmem] * len(arrays),
         out_specs=[vmem] * len(outs),
         scratch_shapes=scratch,
-        compiler_params=pltpu.CompilerParams(vmem_limit_bytes=VMEM_LIMIT),
+        compiler_params=pltpu.CompilerParams(vmem_limit_bytes=36 << 20),
         cost_estimate=pl.CostEstimate(flops=flops, bytes_accessed=8 << 20, transcendentals=0),
         name=name,
     )(*scalars, *arrays)
@@ -1306,8 +1376,6 @@
     mixed_own = lax.dynamic_slice_in_dim(mixed_all, me * chunk, chunk, 0)
     flow = flow_steps(mlp_part, going, coming)
     state = next(flow)
-    d_out_part = rows_inner(mixed_own, d_resid_low).astype(BF)
-    d_out_part = lax.psum_scatter(d_out_part, "batch", scatter_dimension=1, tiled=True)
 
     d_queries, d_gate_logit, d_kv_all = local_call(
         functools.partial(attend_back_kernel, scale_factor),
@@ -1326,20 +1394,18 @@
     while isinstance(state, tuple):
         state = flow.send(state)
     d_kv = fold(d_kv_all, row_count, 4)
-    d_kv, state, d_out_part, d_down, d_mlp = hold((d_kv, state, d_out_part, d_down, d_mlp))
+    d_kv, state, d_down, d_mlp = hold((d_kv, state, d_down, d_mlp))
     out_own = (resid_own + state).astype(BF)
     d_down = lax.psum_scatter(d_down, "batch", scatter_dimension=1, tiled=True)
     d_mlp = lax.psum_scatter(d_mlp, "batch", scatter_dimension=0, tiled=True)
     d_cat = jnp.concatenate([d_queries, d_gate_logit, d_kv], axis=1)
-    d_in = rows_inner(normed_one, d_cat).astype(BF)
-    d_cat, d_in = hold((d_cat, d_in))
-    d_in = lax.psum_scatter(d_in, "batch", scatter_dimension=0, tiled=True)
     inputs_own = lax.dynamic_slice_in_dim(tokens, me * chunk, chunk, 0)
-    output, d_tokens, d_gains, d_out = tail(
-        d_cat, w_in, inputs_own, gain_one[None], d_resid, d_out_part, d_gain_two, [out_own], 5
+    output, d_tokens, d_gains, d_out, d_in = tail(
+        d_cat, w_in, inputs_own, gain_one[None], d_resid, d_gain_two, normed_one, mixed_own,
+        d_resid_low, out_own, 5,
     )
-    d_tokens, d_in, d_mlp, d_down = hold((d_tokens, d_in, d_mlp, d_down))
-    d_in, d_mlp, d_down = d_in.astype(F32), d_mlp.astype(F32), d_down.astype(F32)
+    d_tokens, d_mlp, d_down = hold((d_tokens, d_mlp, d_down))
+    d_mlp, d_down = d_mlp.astype(F32), d_down.astype(F32)
     output = output.reshape(row_count, width)
     d_tokens = d_tokens.reshape(row_count, width)
     hidden_own = w_mlp_gate.shape[1]

time: 525 us -> 512 us (0.975)
  Pallas kernels: 445 us -> 432 us
  matrix products: 11.3 us -> 0 us
  local copies, waits for them, and re-layouts: 26.7 us -> 36.5 us
    unnamed x40 -> x62, local copies, waits for them, and re-layouts: 16.4 us -> 28.2 us
    dot_general x2 -> x0, matrix products: 11.3 us -> none  [rows_inner(): lax.dot_general(left, right, (((0,), (0,)), ((), ())), preferred_element_...]
    pallas_call x2, Pallas kernels: 21.2 us -> 15 us  [local_call(): pl.pallas_call(kernel, out_shape=outs, in_specs=[smem] * len(scalars) + [...]
  transfers between devices with their start and end apart: 10 -> 8, of which waited for: 1 -> 1; matrix products, arithmetic and copies ran while one was open for 2% -> 2% of each run, Pallas kernels for 51% -> 50%
where the time goes in v13:
time: 512 us
  Pallas kernels  432 us (84%)
  local copies, waits for them, and re-layouts  36.5 us (7%)
  waiting for transfers between devices  15.6 us (3%)
  between operations  14.1 us (3%)
  other arithmetic  10.2 us (2%)
    pallas_call x1, Pallas kernels, tail(): pl.pallas_call(functools.partial(tail_kernel, count, batches), out_shape=...  172 us
    pallas_call x1, Pallas kernels, mlp_back(): pl.pallas_call(functools.partial(mlp_kernel, count), out_shape=[shape(tot...  115 us
    pallas_call x1, Pallas kernels, entry(): pl.pallas_call(functools.partial(entry_kernel, count, batches), out_shape...  62 us
    pallas_call x1, Pallas kernels, fold(): pl.pallas_call(functools.partial(fold_kernel, batches), out_shape=jax.Sha...  34.4 us
    pallas_call x1, Pallas kernels, spread(): pl.pallas_call(functools.partial(spread_kernel, count, batches, plans), o...  33.7 us
    unnamed x62, local copies, waits for them, and re-layouts  28.2 us
    pallas_call x2, Pallas kernels, local_call(): pl.pallas_call(kernel, out_shape=outs, in_specs=[smem] * len(scalars) + [...  15 us
    all_gather x1, waiting for transfers between devices, per_device(): mup_full = lax.all_gather(w_mlp_up, 'batch', axis=0, tiled=True)  14.3 us
  transfers between devices with their start and end apart: 8, of which 1 were waited for; matrix products, arithmetic and copies ran while one was open for 2% of the time, Pallas kernels for 50%

profile of v13, /device:TPU:0, one launch (start us, length us, event | category | flops | bytes accessed | tf_op | source)
XLA Modules:
  0.0 512.3 jit_solution(10077048325087749532)
XLA Ops:
  11.0 1.1 copy-done.2
  13.7 62.0 %entry.1 = (bf16[1280,2048]{1,0:T(8,128)(2,1)}, bf16[1280,128]{1,0:T(8,128)(2,1)S(1)}, f32[1280,128]{1,0:T(8,128)S(1)}, bf16[5120,256]{1,0:T(8,128)(2,1)S(1)}, b...) custom-call(bf16[1280,2048]{1,0:T(8,128)(2,1)} %x_hbm.1, ...), custom_call_target="tpu_custom_call" | custom-call | tf_op jit(solution)/shard_map/entry/pallas_call | solution.py:740
  75.7 1.3 copy-done.1
  77.0 1.7 copy-done.10
  81.8 6.5 %attend.1 = (f32[1280,128]{1,0:T(8,128)S(1)}, bf16[1280,128]{1,0:T(8,128)(2,1)S(1)}, f32[1,1280]{1,0:T(1,128)S(1)}) custom-call(s32[1280]{0:T(1024)S(1)} %select_reduce_fusion.start_sm, s32[1]{0:T(128)} %bitcast.3.base_sm, bf16[1280,128]{1,0:T(8,128)(2,1)S(1)} %get-tuple-element.56.q_ref, bf16[5120,256]{1,0:T(8,128)(2,1)S(1)} %get-tuple-element.57.kv_ref, ...), custom_call_target="tpu_custom_call" | custom-call | flops 3355443200 | bytes 8388608 | tf_op jit(solution)/shard_map/attend/pallas_call | solution.py:1254
  89.1 33.7 %spread_2.1.a_hbm = bf16[1280,1024]{1,0:T(8,128)(2,1)S(1)} custom-call(bf16[1280,128]{1,0:T(8,128)(2,1)S(1)} %get-tuple-element.60.refs_0_), custom_call_target="tpu_custom_call" | custom-call | tf_op jit(solution)/shard_map/spread_2/pallas_call | solution.py:164
  122.8 1.4 copy-done
  124.9 14.3 %all-gather.5.cloned.1.call-done.up_w = bf16[2048,768]{1,0:T(8,128)(2,1)} async-done(((bf16[512,768]{1,0:T(8,128)(2,1)}), bf16[2048,768]{1,0:T(8,128)(2,1)}) %all-gather.5.cloned.1.call-update) | async-done | bytes 3145744 | tf_op jit(solution)/shard_map/all_gather | solution.py:1348
  139.3 114.6 %mlp_back.1 = (bf16[1280,2048]{1,0:T(8,128)(2,1)}, bf16[2048,1536]{1,0:T(8,128)(2,1)}, bf16[768,2048]{1,0:T(8,128)(2,1)}, f32[160,2048]{1,0:T(8,128)}, f32[160,2...) custom-call(bf16[1280,2048]{1,0:T(8,128)(2,1)} %x_hbm.1, ...), custom_call_target="tpu_custom_call" | custom-call | flops 41607495680 | bytes 41943040 | tf_op jit(solution)/shard_map/mlp_back/pallas_call | solution.py:518
  254.7 1.3 collective-permute-start
  256.0 1.7 copy-done.12
  260.9 8.5 %attend_back.1 = (bf16[1280,128]{1,0:T(8,128)(2,1)S(1)}, bf16[1280,128]{1,0:T(8,128)(2,1)S(1)}, bf16[5120,256]{1,0:T(8,128)(2,1)S(1)}) custom-call(s32[1280]{0:T(1024)S(1)} %select_reduce_fusion.start_sm, s32[1]{0:T(128)} %bitcast.3.base_sm, bf16[1280,128]{1,0:T(8,128)(2,1)S(1)} %copy-done.17, bf16[5120,256]{1,0:T(8,128)(2,1)S(1)} %copy-done.12, ...), custom_call_target="tpu_custom_call" | custom-call | flops 8388608000 | bytes 8388608 | tf_op jit(solution)/shard_map/attend_back/pallas_call | solution.py:1254
  269.4 2.9 add_convert_fusion.1
  273.1 1.3 collective-permute-start.2
  274.4 34.4 %fold.1 = bf16[1280,128]{1,0:T(8,128)(2,1)S(1)} custom-call(bf16[5120,256]{1,0:T(8,128)(2,1)S(1)} %get-tuple-element.75.part_ref), custom_call_target="tpu_custom_call" | custom-call | tf_op jit(solution)/shard_map/fold/pallas_call | solution.py:952
  308.8 1.8 convert_add_fusion
  311.3 1.1 constant_dynamic-slice_fusion.1.mixed_ref
  312.4 1.1 constant_dynamic-slice_fusion.x_ref
  315.7 171.9 %tail.1 = (bf16[8,160,2048]{2,1,0:T(8,128)(2,1)}, bf16[8,160,2048]{2,1,0:T(8,128)(2,1)}, f32[2,512]{1,0:T(2,128)S(1)}, f32[128,512]{1,0:T(8,128)S(1)}, f32[512,384]{1,0:T(8,128)}) custom-call(bf16[1280,384]{1,0:T(8,128)(2,1)} %pad_maximum_fusion.cat_ref, bf16[2048,512]{1,0:T(8,128)(2,1)} %copy-done.1, ...), custom_call_target="tpu_custom_call" | custom-call | flops 2013265920 | bytes 419430400 | tf_op jit(solution)/shard_map/tail/pallas_call | solution.py:1210
  487.7 1.2 fusion.2
  491.9 3.3 fusion
  495.2 1.4 convert_element_type.55
  496.6 6.2 %copy.47 = bf16[1280,2048]{1,0:T(8,128)(2,1)} copy(bf16[1280,2048]{1,0:T(8,128)(2,1)} %bitcast.22) | data formatting | bytes 10485760
  502.7 2.4 copy.48
  (85 shorter events, 20.9 us)
Async XLA Ops:
  7.2 117.8 %all-gather.3.cloned.1.call-start = ((), (), s32[]{:S(2)}) async-start(), calls=%async_computation.2 | async-start | bytes 3932160 | tf_op jit(solution)/shard_map/all_gather | solution.py:1347
  10.9 1.1 copy-start.2
  13.7 66.9 %copy-start.8 = (s32[1280]{0:T(1024)S(1)}, s32[1280]{0:T(1024)}, u32[]{:S(2)}) copy-start(s32[1280]{0:T(1024)} %param.14) | copy-start | bytes 15364
  75.7 1.3 copy-start.1
  77.0 1.7 copy-start.10
  79.5 8.7 %copy-start.11 = (bf16[5120,256]{1,0:T(8,128)(2,1)}, bf16[5120,256]{1,0:T(8,128)(2,1)S(1)}, u32[]{:S(2)}) copy-start(bf16[5120,256]{1,0:T(8,128)(2,1)S(1)} %get-tuple-element.57.kv_ref) | copy-start | bytes 7864324
  79.5 8.7 %copy-start.16 = (bf16[1280,128]{1,0:T(8,128)(2,1)}, bf16[1280,128]{1,0:T(8,128)(2,1)S(1)}, u32[]{:S(2)}) copy-start(bf16[1280,128]{1,0:T(8,128)(2,1)S(1)} %get-tuple-element.56.q_ref) | copy-start | bytes 983044
  79.6 59.7 %all-gather.5.cloned.1.call-start = ((), (), s32[]{:S(2)}) async-start(), calls=%async_computation.3 | async-start | bytes 3932160 | tf_op jit(solution)/shard_map/all_gather | solution.py:1348
  80.3 411.5 %reduce-scatter.5.cloned.1.call-start = ((), (), s32[]{:S(2)}) async-start(), calls=%async_computation.5 | async-start | bytes 3932160 | tf_op jit(solution)/shard_map/reduce_scatter | solution.py:1399
  122.8 1.5 copy-start
  139.3 116.7 %copy-start.17 = (bf16[1280,128]{1,0:T(8,128)(2,1)S(1)}, bf16[1280,128]{1,0:T(8,128)(2,1)}, u32[]{:S(2)}) copy-start(bf16[1280,128]{1,0:T(8,128)(2,1)} %copy-done.16) | copy-start | bytes 983044
  253.9 15.5 %collective-permute-start.1 = (bf16[160,2048]{1,0:T(8,128)(2,1)}, bf16[160,2048]{1,0:T(8,128)(2,1)S(1)}, u32[]{:S(2)}, u32[]{:S(2)}) collective-permute-start(bf16[160,2048]{1,0:T(8,128)(2,1)} %get-tuple-element.74), channel_id=1, source_target_pairs={{0,1},{2,0},{4,2},{6,4},{7,6},{5,7},{3,5},{1,3},{8,9},{10,8},{12,1... | collective-permute-start | bytes 1966088 | tf_op jit(solution)/shard_map/ppermute | solution.py:1289
  254.7 14.8 %collective-permute-start = (bf16[160,2048]{1,0:T(8,128)(2,1)}, bf16[160,2048]{1,0:T(8,128)(2,1)S(1)}, u32[]{:S(2)}, u32[]{:S(2)}) collective-permute-start(bf16[160,2048]{1,0:T(8,128)(2,1)} %get-tuple-element.72), channel_id=1, source_target_pairs={{0,2},{2,4},{4,6},{6,7},{7,5},{5,3},{3,1},{1,0},{8,10},{10,12},{12... | collective-permute-start | bytes 1966088 | tf_op jit(solution)/shard_map/ppermute | solution.py:1288
  256.0 1.7 copy-start.12
  269.4 3.0 copy-start.4
  272.4 36.4 %collective-permute-start.3 = (bf16[160,2048]{1,0:T(8,128)(2,1)}, bf16[160,2048]{1,0:T(8,128)(2,1)}, u32[]{:S(2)}, u32[]{:S(2)}) collective-permute-start(bf16[160,2048]{1,0:T(8,128)(2,1)} %get-tuple-element.77), channel_id=1, source_target_pairs={{0,1},{2,0},{4,2},{6,4},{7,6},{5,7},{3,5},{1,3},{8,9},{10,8},{12,1... | collective-permute-start | bytes 1966088 | tf_op jit(solution)/shard_map/ppermute | solution.py:1294
  273.1 35.7 %collective-permute-start.2 = (bf16[160,2048]{1,0:T(8,128)(2,1)}, bf16[160,2048]{1,0:T(8,128)(2,1)}, u32[]{:S(2)}, u32[]{:S(2)}) collective-permute-start(bf16[160,2048]{1,0:T(8,128)(2,1)} %get-tuple-element.76), channel_id=1, source_target_pairs={{0,2},{2,4},{4,6},{6,7},{7,5},{5,3},{3,1},{1,0},{8,10},{10,12},{12... | collective-permute-start | bytes 1966088 | tf_op jit(solution)/shard_map/ppermute | solution.py:1293
  310.7 181.2 %reduce-scatter.3.cloned.1.call-start = ((), (), s32[]{:S(2)}) async-start(), calls=%async_computation.4 | async-start | bytes 7864320 | tf_op jit(solution)/shard_map/reduce_scatter | solution.py:1400
  311.2 2.3 copy-start.5
  311.3 3.4 copy-start.22
  487.6 3.4 copy-start.21
  491.9 3.3 copy-start.23
  495.2 7.5 %slice-start = ((s8[5242880]{0:T(1024)(128)(4,1)}), s8[4194304]{0:T(1024)(128)(4,1)S(1)}, s32[]{:S(2)}) async-start(s8[5242880]{0:T(1024)(128)(4,1)} %bitcast.19), calls=%async_computation.6 | async-start | bytes 8388608
  496.6 6.2 %slice-start.1 = ((s8[5242880]{0:T(1024)(128)(4,1)}), s8[1048576]{0:T(1024)(128)(4,1)S(1)}, s32[]{:S(2)}) async-start(s8[5242880]{0:T(1024)(128)(4,1)} %bitcast.19), calls=%async_computation.7 | async-start | bytes 2097152
  (10 other events, 9.7 us)
Sparse Core Ops, SparseCore 0:
  79.7 29.4 all-gather.2
  110.7 28.4 all-gather.4
  310.8 35.5 reduce-scatter.4
  349.0 65.4 reduce-scatter.2

commit v14 on v13

--- a/solution.py
+++ b/solution.py
@@ -99,19 +99,32 @@
         waiting.append(copy)
         return copy
 
-    onward = []
+    stages = []
     for index, (axis, form) in enumerate(plans):
         own, whole = own_refs[index], all_refs[index]
         spot = place if axis == "head" else batch
-        mine = place_of(whole, own, spot, form)
-        copy = pltpu.make_async_copy(own, mine, local_sem.at[index])
+        copy = pltpu.make_async_copy(own, place_of(whole, own, spot, form), local_sem.at[index])
         copy.start()
         local.append(copy)
         if axis == "batch":
+            stages.append(index)
+    onward = []
+
+    def stage():
+        for copy, block in onward:
+            copy.wait_recv()
+            arriving.append(go(block, block, twin))
+        onward.clear()
+        if stages:
+            index = stages.pop(0)
+            own, whole, form = own_refs[index], all_refs[index], plans[index][1]
+            mine = place_of(whole, own, batch, form)
             for hop, peer in enumerate(peers, 1):
                 source = lax.rem(across + others - hop, others) * 2 + core
                 onward.append((go(own, mine, peer), place_of(whole, own, source, form)))
             arriving.append(go(own, mine, twin))
+
+    stage()
     copies = [None] * (2 * arrays)
     for step in range(steps):
         for index, (axis, form) in enumerate(plans):
@@ -130,11 +143,10 @@
                     source = source.at[part]
                     target = target.at[part]
                 copies[at] = go(source, target, device)
-        if step == 0 or not ring:
-            for copy, block in onward:
-                copy.wait_recv()
-                arriving.append(go(block, block, twin))
-            onward = []
+        if step == steps // 2:
+            stage()
+    while stages or onward:
+        stage()
     for copy in copies:
         if copy is not None:
             arriving.append(copy)
@@ -191,6 +203,7 @@
     hidden = gate_w.shape[1]
     side = width // 2
     tile = 256
+    broad = 1024
     inner = 256 if hidden % 256 == 0 else 128
     size = da_ref.shape[1]
     place, right, left = ring_setup(count)
@@ -281,12 +294,12 @@
         mixed = a_s[slot]
 
         def residual(at, total):
-            cols = tile_of(at)
+            cols = tile_of(at, broad)
             values = x_s[slot, :, cols].astype(F32) + matmul(mixed, out_w[:, cols])
             h1_s[:, cols] = values
             return total + jnp.sum(values * values, axis=1, keepdims=True)
 
-        total = lax.fori_loop(0, width // tile, residual, jnp.zeros((2 * rows, 1), F32))
+        total = lax.fori_loop(0, width // broad, residual, jnp.zeros((2 * rows, 1), F32))
         scale = lax.rsqrt(total / width + EPSILON)
 
         @pl.when(group == 0)
@@ -319,9 +332,9 @@
         d_up = grad_all[group, :, hidden:]
         half = jnp.minimum(group, 1)
 
-        @pl.loop(0, width // tile)
+        @pl.loop(0, width // broad)
         def _(at):
-            cols = tile_of(at)
+            cols = tile_of(at, broad)
             part = (cols_inner(d_gate, gate_w[cols]) + cols_inner(d_up, up_w[cols])).astype(BF)
             right_part[half, :, cols] = part[:rows]
             left_part[half, :, cols] = part[rows:]
@@ -545,8 +558,8 @@
 
 
 def entry_kernel(
-    count, batches, x_ref, w_ref, out_ref, gain_ref, seg_ref, down_ref,
-    n1_ref, q_ref, logit_ref, kv_ref, w_all, out_all, gain_all, seg_all, down_all,
+    count, batches, x_ref, w_ref, out_ref, gain_ref, seg_ref,
+    n1_ref, q_ref, logit_ref, kv_ref, w_all, out_all, gain_all, seg_all,
     send_sem, recv_sem, local_sem,
 ):
     steps = count // 2
@@ -669,12 +682,6 @@
     mate_out, mate_twin = both(mate_view, mate_view(batch))
     ring(0)
 
-    def down_view(at):
-        return down_all.at[:, part(at, down_ref.shape[1])]
-
-    down_out, down_twin = both(down_view, down_ref)
-    stay(down_ref, down_view(batch))
-
     @pl.loop(middle, blocks)
     def _(at):
         normalize(at)
@@ -713,7 +720,6 @@
 
     for step in range(2, steps):
         ring(step)
-    down_passed = pass_on(down_view, down_out)
     kv_passed = pass_on(kv_view, kv_out)
     for pair in flows:
         for copy in pair:
@@ -722,13 +728,13 @@
     for hop in range(others):
         there = out_all.at[:, part(spots[hop] * 2 + core, wide)]
         swaps.append(go(there, there, twin))
-    for copy in (*kv_twin, *kv_passed, *swaps, *down_twin, *down_passed):
+    for copy in (*kv_twin, *kv_passed, *swaps):
         copy.wait_recv()
     for copy in copies:
         copy.wait_send()
 
 
-def entry(tokens, w_shard, w_out, gains, segments, w_down, collective_id):
+def entry(tokens, w_shard, w_out, gains, segments, collective_id):
     count = lax.axis_size("head")
     batches = lax.axis_size("batch")
     others = batches // 2
@@ -748,16 +754,15 @@
             jax.ShapeDtypeStruct((count * size, batches * wide), BF),
             jax.ShapeDtypeStruct((batches, *gains.shape), F32),
             jax.ShapeDtypeStruct((batches, *segments.shape), jnp.int32),
-            jax.ShapeDtypeStruct((w_down.shape[0], batches * w_down.shape[1]), BF),
         ],
-        in_specs=[vmem] * 6,
-        out_specs=[vmem] * 9,
+        in_specs=[vmem] * 5,
+        out_specs=[vmem] * 8,
         scratch_shapes=[sems, sems, pltpu.SemaphoreType.DMA((5,))],
         compiler_params=pltpu.CompilerParams(
             collective_id=collective_id, has_side_effects=True, vmem_limit_bytes=44 << 20
         ),
         name="entry",
-    )(tokens, w_shard, w_out, gains, segments, w_down)
+    )(tokens, w_shard, w_out, gains, segments)
 
 
 KEY_BLOCK = 512
@@ -1204,14 +1209,14 @@
     size, wide = mixed.shape[1] // count, width // batches
     depth = d_cat.shape[1]
     vmem = pl.BlockSpec(memory_space=pltpu.VMEM)
-    whole = jax.ShapeDtypeStruct((count, rows, width), BF)
+    whole = (count, rows, width)
     sems = pltpu.SemaphoreType.DMA((5 * count + 3 * batches,))
     gains = (2, width // batches)
     return pl.pallas_call(
         functools.partial(tail_kernel, count, batches),
         out_shape=[
-            whole,
-            whole,
+            jax.ShapeDtypeStruct(whole, BF),
+            jax.ShapeDtypeStruct(whole, BF),
             jax.ShapeDtypeStruct(gains, F32),
             jax.ShapeDtypeStruct((size, wide), F32),
             jax.ShapeDtypeStruct((wide, depth), F32),
@@ -1239,7 +1244,7 @@
             pltpu.SemaphoreType.DMA((2,)),
         ],
         compiler_params=pltpu.CompilerParams(
-            collective_id=collective_id, has_side_effects=True, vmem_limit_bytes=52 << 20
+            collective_id=collective_id, has_side_effects=True, vmem_limit_bytes=(32 << 20) + 4 * count * size * width
         ),
         cost_estimate=pl.CostEstimate(
             flops=2 * count * rows * width * d_cat.shape[1], bytes_accessed=400 << 20, transcendentals=0
@@ -1337,15 +1342,14 @@
 
     w_shard = jnp.concatenate([w_query, w_gate, w_key, w_value], axis=1)
     gains = jnp.concatenate([norm1_gain, norm2_gain]).reshape(-1, 128).astype(F32)
-    normed_one, queries, gate_logit, kv_all, w_in, out_full, gains, seg_all, down_full = entry(
-        tokens, w_shard, w_out, gains, segment_ids.reshape(-1, 128), w_down, 1
+    normed_one, queries, gate_logit, kv_all, w_in, out_full, gains, seg_all = entry(
+        tokens, w_shard, w_out, gains, segment_ids.reshape(-1, 128), 1
     )
-    gains, w_mlp_gate, w_mlp_up = lax.optimization_barrier((gains, w_mlp_gate, w_mlp_up))
+    gains, w_mlp_gate = lax.optimization_barrier((gains, w_mlp_gate))
     seg_all = seg_all.reshape(-1)
     gains = gains.reshape(batches, 2, -1).transpose(1, 0, 2).reshape(2, width)
     gain_one, gain_two = gains[0], gains[1]
     mgate_full = lax.all_gather(w_mlp_gate, "batch", axis=0, tiled=True)
-    mup_full = lax.all_gather(w_mlp_up, "batch", axis=0, tiled=True)
 
     base = lax.axis_index("batch") * row_count
     ids = jnp.arange(DOCUMENTS, dtype=jnp.int32)
@@ -1366,7 +1370,9 @@
         pair_flops,
         "attend",
     )
-    (mixed_all,) = spread([mixed], (("head", "cols"),), 2)
+    mixed_all, down_full, mup_full = spread(
+        [mixed, w_down, w_mlp_up], (("head", "cols"), ("batch", "cols"), ("batch", "rows")), 2
+    )
     (
         mlp_part, d_mlp, d_down, resid_own, d_resid, d_resid_low, d_gain_two, d_mixed, going, coming,
     ) = mlp_back(

time: 512 us -> 502 us (0.980)
  waiting for transfers between devices: 15.6 us -> 0.73 us
  Pallas kernels: 432 us -> 439 us
    pallas_call x1, Pallas kernels: 33.7 us -> 56.8 us  [spread(): pl.pallas_call(functools.partial(spread_kernel, count, batches, plans), o...]
    all_gather x1 -> x0, waiting for transfers between devices: 14.3 us -> none  [per_device(): mup_full = lax.all_gather(w_mlp_up, 'batch', axis=0, tiled=True)]
    pallas_call x1, Pallas kernels: 62 us -> 53 us  [entry(): pl.pallas_call(functools.partial(entry_kernel, count, batches), out_shape...]
    pallas_call x1, Pallas kernels: 115 us -> 108 us  [mlp_back(): pl.pallas_call(functools.partial(mlp_kernel, count), out_shape=[shape(tot...]
    unnamed x62 -> x74, local copies, waits for them, and re-layouts: 28.2 us -> 31 us
  transfers between devices with their start and end apart: 8 -> 7, of which waited for: 1 -> 0; matrix products, arithmetic and copies ran while one was open for 2% -> 1% of each run, Pallas kernels for 50% -> 55%
where the time goes in v14:
time: 502 us; the launch traced here: 505 us
  Pallas kernels  439 us (87%)
  local copies, waits for them, and re-layouts  38.2 us (8%)
  between operations  14.2 us (3%)
  other arithmetic  8.38 us (2%)
    pallas_call x1, Pallas kernels, tail(): pl.pallas_call(functools.partial(tail_kernel, count, batches), out_shape=...  169 us
    pallas_call x1, Pallas kernels, mlp_back(): pl.pallas_call(functools.partial(mlp_kernel, count), out_shape=[shape(tot...  108 us
    pallas_call x1, Pallas kernels, spread(): pl.pallas_call(functools.partial(spread_kernel, count, batches, plans), o...  56.8 us
    pallas_call x1, Pallas kernels, entry(): pl.pallas_call(functools.partial(entry_kernel, count, batches), out_shape...  53 us
    pallas_call x1, Pallas kernels, fold(): pl.pallas_call(functools.partial(fold_kernel, batches), out_shape=jax.Sha...  37.5 us
    unnamed x74, local copies, waits for them, and re-layouts  31 us
    pallas_call x2, Pallas kernels, local_call(): pl.pallas_call(kernel, out_shape=outs, in_specs=[smem] * len(scalars) + [...  15 us
  transfers between devices with their start and end apart: 7, of which 0 were waited for; matrix products, arithmetic and copies ran while one was open for 1% of the time, Pallas kernels for 55%

profile of v14, /device:TPU:0, one launch (start us, length us, event | category | flops | bytes accessed | tf_op | source)
XLA Modules:
  0.0 505.0 jit_solution(16398561308217029375)
XLA Ops:
  12.5 53.0 %entry.1 = (bf16[1280,2048]{1,0:T(8,128)(2,1)}, bf16[1280,128]{1,0:T(8,128)(2,1)S(1)}, f32[1280,128]{1,0:T(8,128)S(1)}, bf16[5120,256]{1,0:T(8,128)(2,1)S(1)}, b...) custom-call(bf16[1280,2048]{1,0:T(8,128)(2,1)} %x_hbm.1, ...), custom_call_target="tpu_custom_call" | custom-call | tf_op jit(solution)/shard_map/entry/pallas_call | solution.py:746
  65.6 1.3 copy-done.1
  69.1 1.1 copy-done.19
  70.2 6.5 %attend.1 = (f32[1280,128]{1,0:T(8,128)S(1)}, bf16[1280,128]{1,0:T(8,128)(2,1)S(1)}, f32[1,1280]{1,0:T(1,128)S(1)}) custom-call(s32[1280]{0:T(1024)S(1)} %select_reduce_fusion.start_sm, s32[1]{0:T(128)} %bitcast.3.base_sm, bf16[1280,128]{1,0:T(8,128)(2,1)S(1)} %get-tuple-element.57.q_ref, bf16[5120,256]{1,0:T(8,128)(2,1)S(1)} %get-tuple-element.58.kv_ref, ...), custom_call_target="tpu_custom_call" | custom-call | flops 3355443200 | bytes 8388608 | tf_op jit(solution)/shard_map/attend/pallas_call | solution.py:1259
  77.6 56.8 %spread_2.1 = (bf16[1280,1024]{1,0:T(8,128)(2,1)S(1)}, bf16[768,2048]{1,0:T(8,128)(2,1)S(1)}, bf16[2048,768]{1,0:T(8,128)(2,1)S(1)}) custom-call(bf16[1280,128]{1,0:T(8,128)(2,1)S(1)} %get-tuple-element.61.refs_0_, bf16[768,512]{1,0:T(8,128)(2,1)S(1)} %copy-done.4, bf16[512,768]{1,0:T(8,128)(2,1)S(1)} %copy-done.5), custom_call_target="tpu_custom_call" | custom-call | tf_op jit(solution)/shard_map/spread_2/pallas_call | solution.py:176
  134.4 1.6 copy-done.10
  136.0 1.7 copy-done.14
  137.6 1.7 copy-done.15
  139.3 108.0 %mlp_back.1 = (bf16[1280,2048]{1,0:T(8,128)(2,1)}, bf16[2048,1536]{1,0:T(8,128)(2,1)}, bf16[768,2048]{1,0:T(8,128)(2,1)}, f32[160,2048]{1,0:T(8,128)}, f32[160,2...) custom-call(bf16[1280,2048]{1,0:T(8,128)(2,1)} %x_hbm.1, ...), custom_call_target="tpu_custom_call" | custom-call | flops 41607495680 | bytes 41943040 | tf_op jit(solution)/shard_map/mlp_back/pallas_call | solution.py:531
  249.4 1.7 copy-done.17
  251.1 1.1 copy-done.20
  252.2 1.1 copy-done.24
  254.3 8.5 %attend_back.1 = (bf16[1280,128]{1,0:T(8,128)(2,1)S(1)}, bf16[1280,128]{1,0:T(8,128)(2,1)S(1)}, bf16[5120,256]{1,0:T(8,128)(2,1)S(1)}) custom-call(s32[1280]{0:T(1024)S(1)} %select_reduce_fusion.start_sm, s32[1]{0:T(128)} %bitcast.3.base_sm, bf16[1280,128]{1,0:T(8,128)(2,1)S(1)} %copy-done.22, bf16[5120,256]{1,0:T(8,128)(2,1)S(1)} %copy-done.17, ...), custom_call_target="tpu_custom_call" | custom-call | flops 8388608000 | bytes 8388608 | tf_op jit(solution)/shard_map/attend_back/pallas_call | solution.py:1259
  262.8 2.9 add_convert_fusion.1
  267.8 37.5 %fold.1 = bf16[1280,128]{1,0:T(8,128)(2,1)S(1)} custom-call(bf16[5120,256]{1,0:T(8,128)(2,1)S(1)} %get-tuple-element.77.part_ref), custom_call_target="tpu_custom_call" | custom-call | tf_op jit(solution)/shard_map/fold/pallas_call | solution.py:957
  305.3 1.8 convert_add_fusion
  307.9 1.1 constant_dynamic-slice_fusion.1.mixed_ref
  309.0 1.1 constant_dynamic-slice_fusion.x_ref
  312.4 169.0 %tail.1 = (bf16[8,160,2048]{2,1,0:T(8,128)(2,1)S(1)}, bf16[8,160,2048]{2,1,0:T(8,128)(2,1)}, f32[2,512]{1,0:T(2,128)S(1)}, f32[128,512]{1,0:T(8,128)S(1)}, f32[512,384]{1,0:T(8,128)S(1)}) custom-call(bf16[1280,384]{1,0:T(8,128)(2,1)S(1)} %pad_maximum_fusion.cat_ref, bf16[2048,512]{1,0:T(8,128)(2,1)S(1)} %copy-done.2, ...), custom_call_target="tpu_custom_call" | custom-call | flops 2013265920 | bytes 419430400 | tf_op jit(solution)/shard_map/tail/pallas_call | solution.py:1215
  481.4 2.3 copy-done
  486.9 3.4 fusion
  490.3 1.4 convert_element_type.55
  491.7 2.7 copy.47
  495.4 2.4 copy.48
  (95 shorter events, 21.2 us)
Async XLA Ops:
  7.2 132.1 %all-gather.2.cloned.1.call-start = ((), (), s32[]{:S(2)}) async-start(), calls=%async_computation.2 | async-start | bytes 3932160 | tf_op jit(solution)/shard_map/all_gather | solution.py:1352
  12.5 55.5 %copy-start.12 = (s32[1280]{0:T(1024)S(1)}, s32[1280]{0:T(1024)}, u32[]{:S(2)}) copy-start(s32[1280]{0:T(1024)} %param.14) | copy-start | bytes 15364
  67.7 9.0 %copy-start.16 = (bf16[5120,256]{1,0:T(8,128)(2,1)}, bf16[5120,256]{1,0:T(8,128)(2,1)S(1)}, u32[]{:S(2)}) copy-start(bf16[5120,256]{1,0:T(8,128)(2,1)S(1)} %get-tuple-element.58.kv_ref) | copy-start | bytes 7864324
  67.7 9.0 %copy-start.21 = (bf16[1280,128]{1,0:T(8,128)(2,1)}, bf16[1280,128]{1,0:T(8,128)(2,1)S(1)}, u32[]{:S(2)}) copy-start(bf16[1280,128]{1,0:T(8,128)(2,1)S(1)} %get-tuple-element.57.q_ref) | copy-start | bytes 983044
  67.7 419.1 %reduce-scatter.5.cloned.1.call-start = ((), (), s32[]{:S(2)}) async-start(), calls=%async_computation.4 | async-start | bytes 3932160 | tf_op jit(solution)/shard_map/reduce_scatter | solution.py:1405
  70.2 7.4 %copy-start.4 = (bf16[768,512]{1,0:T(8,128)(2,1)S(1)}, bf16[768,512]{1,0:T(8,128)(2,1)}, u32[]{:S(2)}) copy-start(bf16[768,512]{1,0:T(8,128)(2,1)} %refs_1_.1) | copy-start | bytes 2359300
  70.2 7.4 %copy-start.5 = (bf16[512,768]{1,0:T(8,128)(2,1)S(1)}, bf16[512,768]{1,0:T(8,128)(2,1)}, u32[]{:S(2)}) copy-start(bf16[512,768]{1,0:T(8,128)(2,1)} %refs_2_.1) | copy-start | bytes 2359300
  139.3 110.1 %copy-start.22 = (bf16[1280,128]{1,0:T(8,128)(2,1)S(1)}, bf16[1280,128]{1,0:T(8,128)(2,1)}, u32[]{:S(2)}) copy-start(bf16[1280,128]{1,0:T(8,128)(2,1)} %copy-done.21) | copy-start | bytes 983044
  247.3 15.5 %collective-permute-start.1 = (bf16[160,2048]{1,0:T(8,128)(2,1)}, bf16[160,2048]{1,0:T(8,128)(2,1)S(1)}, u32[]{:S(2)}, u32[]{:S(2)}) collective-permute-start(bf16[160,2048]{1,0:T(8,128)(2,1)} %get-tuple-element.76), channel_id=1, source_target_pairs={{0,1},{2,0},{4,2},{6,4},{7,6},{5,7},{3,5},{1,3},{8,9},{10,8},{12,1... | collective-permute-start | bytes 1966088 | tf_op jit(solution)/shard_map/ppermute | solution.py:1294
  248.3 14.5 %collective-permute-start = (bf16[160,2048]{1,0:T(8,128)(2,1)}, bf16[160,2048]{1,0:T(8,128)(2,1)S(1)}, u32[]{:S(2)}, u32[]{:S(2)}) collective-permute-start(bf16[160,2048]{1,0:T(8,128)(2,1)} %get-tuple-element.74), channel_id=1, source_target_pairs={{0,2},{2,4},{4,6},{6,7},{7,5},{5,3},{3,1},{1,0},{8,10},{10,12},{12... | collective-permute-start | bytes 1966088 | tf_op jit(solution)/shard_map/ppermute | solution.py:1293
  262.8 3.0 copy-start.7
  265.8 39.5 %collective-permute-start.3 = (bf16[160,2048]{1,0:T(8,128)(2,1)}, bf16[160,2048]{1,0:T(8,128)(2,1)}, u32[]{:S(2)}, u32[]{:S(2)}) collective-permute-start(bf16[160,2048]{1,0:T(8,128)(2,1)} %get-tuple-element.79), channel_id=1, source_target_pairs={{0,1},{2,0},{4,2},{6,4},{7,6},{5,7},{3,5},{1,3},{8,9},{10,8},{12,1... | collective-permute-start | bytes 1966088 | tf_op jit(solution)/shard_map/ppermute | solution.py:1299
  266.7 38.5 %collective-permute-start.2 = (bf16[160,2048]{1,0:T(8,128)(2,1)}, bf16[160,2048]{1,0:T(8,128)(2,1)}, u32[]{:S(2)}, u32[]{:S(2)}) collective-permute-start(bf16[160,2048]{1,0:T(8,128)(2,1)} %get-tuple-element.78), channel_id=1, source_target_pairs={{0,2},{2,4},{4,6},{6,7},{7,5},{5,3},{3,1},{1,0},{8,10},{10,12},{12... | collective-permute-start | bytes 1966088 | tf_op jit(solution)/shard_map/ppermute | solution.py:1298
  307.1 179.8 %reduce-scatter.3.cloned.1.call-start = ((), (), s32[]{:S(2)}) async-start(), calls=%async_computation.3 | async-start | bytes 7864320 | tf_op jit(solution)/shard_map/reduce_scatter | solution.py:1406
  307.8 2.3 copy-start.8
  307.9 2.5 copy-start.26
  310.3 2.0 copy-start.6
  310.3 2.0 copy-start.13
  481.4 2.4 copy-start
  486.0 5.6 %slice-start = ((s8[5242880]{0:T(1024)(128)(4,1)}), s8[1048576]{0:T(1024)(128)(4,1)S(1)}, s32[]{:S(2)}) async-start(s8[5242880]{0:T(1024)(128)(4,1)} %bitcast.17), calls=%async_computation.5 | async-start | bytes 2097152
  486.9 3.4 copy-start.27
  486.9 4.8 slice-start.1
  490.3 4.0 slice-start.2
  491.7 3.8 slice-start.3
  (15 other events, 18.8 us)
Sparse Core Ops, SparseCore 0:
  67.9 28.4 all-gather.1
  307.2 35.6 reduce-scatter.4
  345.6 64.0 reduce-scatter.2

commit v15 on v14

--- a/solution.py
+++ b/solution.py
@@ -184,23 +184,30 @@
             pltpu.SemaphoreType.DMA((len(arrays),)),
         ],
         compiler_params=pltpu.CompilerParams(
-            collective_id=collective_id, has_side_effects=True, vmem_limit_bytes=8 << 20
+            collective_id=collective_id, has_side_effects=True, vmem_limit_bytes=VMEM_LIMIT
         ),
         name=f"spread_{collective_id}",
     )(*arrays)
 
 
 def mlp_kernel(
-    count, x_hbm, a_hbm, dy_hbm, gain_ref, out_w, gate_w, up_w, down_w,
+    count, x_hbm, a_hbm, dy_hbm, gain_ref, out_hbm, gate_hbm, up_hbm, down_hbm,
     mlp_hbm, dmlp_hbm, ddown_hbm, h1_ref, dh1_ref, low_ref, dgain_ref, da_ref, ahead_ref, behind_ref,
     x_s, a_s, mlp_s, h1_s, dy_all, n2_all, hid_all, grad_all, dmlp_s, ddown_s, da_part,
     mlp_far, mlp_next, mlp_got, right_part, left_part, right_got, left_got,
-    in_sem, out_sem, grad_sem, send_sem, recv_sem, da_send, da_recv, far_send, far_recv,
+    out_w, gate_w, up_w, down_w, in_sem, out_sem, grad_sem, weight_sem,
+    send_sem, recv_sem, da_send, da_recv, far_send, far_recv,
 ):
     steps = count // 2
     rows = x_hbm.shape[0] // count
     width = x_hbm.shape[1]
     hidden = gate_w.shape[1]
+    weights = [
+        pltpu.make_async_copy(source, target, weight_sem.at[index])
+        for index, (source, target) in enumerate(
+            ((out_hbm, out_w), (gate_hbm, gate_w), (up_hbm, up_w), (down_hbm, down_w))
+        )
+    ]
     side = width // 2
     tile = 256
     broad = 1024
@@ -211,8 +218,6 @@
     def member(hop):
         spot = lax.rem(place + hop, count)
         return spot, (lax.axis_index("batch"), ring_head(spot, count))
-
-    greet([member(hop)[1] for hop in range(1, count)])
 
     def owners(group):
         first = jnp.where(group == 0, 1, 0)
@@ -272,8 +277,10 @@
             passing(left_got.at[step - 1], left_got.at[step], ring_sems, steps + step, left),
         )
 
-    for copy in loads(0, 0):
+    for copy in (*loads(0, 0), *weights):
         copy.start()
+    greet([member(hop)[1] for hop in range(1, count)])
+    weights[0].wait()
 
     @pl.loop(0, steps)
     def _(group):
@@ -305,6 +312,8 @@
         @pl.when(group == 0)
         def _():
             h1_ref[...] = h1_s[pl.ds(rows, rows)]
+            for copy in weights[1:]:
+                copy.wait()
 
         @pl.loop(0, width // tile)
         def _(at):
@@ -535,7 +544,7 @@
             shape(rows, width, dtype=F32), shape(rows, width, dtype=F32), shape(rows, width),
             shape(1, width, dtype=F32), shape(total, size), shape(rows, width), shape(rows, width),
         ],
-        in_specs=[hbm] * 3 + [vmem] * 5,
+        in_specs=[hbm] * 3 + [vmem] + [hbm] * 4,
         out_specs=[hbm] * 3 + [vmem] * 7,
         scratch_shapes=[
             slots(2, 2 * rows, width), slots(2, 2 * rows, mixed.shape[1]), slots(2, 2 * rows, width),
@@ -546,7 +555,8 @@
             pltpu.VMEM((rows, width), BF), slots(2, rows, width), slots(4, rows, width),
             slots(2, rows, width), slots(2, rows, width),
             slots(steps, rows, width), slots(steps, rows, width),
-            dma((2, 6)), dma((2, 2)), dma((4,)), dma((count,)), dma((count,)),
+            *[pltpu.VMEM(weight.shape, BF) for weight in (out_w, gate_w, up_w, down_w)],
+            dma((2, 6)), dma((2, 2)), dma((4,)), dma((4,)), dma((count,)), dma((count,)),
             dma((count,)), dma((count,)), dma((4,)), dma((4,)),
         ],
         compiler_params=pltpu.CompilerParams(
@@ -759,7 +769,7 @@
         out_specs=[vmem] * 8,
         scratch_shapes=[sems, sems, pltpu.SemaphoreType.DMA((5,))],
         compiler_params=pltpu.CompilerParams(
-            collective_id=collective_id, has_side_effects=True, vmem_limit_bytes=44 << 20
+            collective_id=collective_id, has_side_effects=True, vmem_limit_bytes=VMEM_LIMIT
         ),
         name="entry",
     )(tokens, w_shard, w_out, gains, segments)
@@ -970,7 +980,7 @@
             sems,
         ],
         compiler_params=pltpu.CompilerParams(
-            collective_id=collective_id, has_side_effects=True, vmem_limit_bytes=20 << 20
+            collective_id=collective_id, has_side_effects=True, vmem_limit_bytes=VMEM_LIMIT
         ),
         name="fold",
     )(part)
@@ -1262,7 +1272,7 @@
         in_specs=[smem] * len(scalars) + [vmem] * len(arrays),
         out_specs=[vmem] * len(outs),
         scratch_shapes=scratch,
-        compiler_params=pltpu.CompilerParams(vmem_limit_bytes=36 << 20),
+        compiler_params=pltpu.CompilerParams(vmem_limit_bytes=VMEM_LIMIT),
         cost_estimate=pl.CostEstimate(flops=flops, bytes_accessed=8 << 20, transcendentals=0),
         name=name,
     )(*scalars, *arrays)

time: 502 us -> 491 us (0.978); the launches traced: 505 us -> 487 us
  local copies, waits for them, and re-layouts: 38.2 us -> 24.8 us
    unnamed x74 -> x42, local copies, waits for them, and re-layouts: 31 us -> 15.4 us
  transfers between devices with their start and end apart: 7 -> 7, of which waited for: 0 -> 0; matrix products, arithmetic and copies ran while one was open for 1% -> 2% of each run, Pallas kernels for 55% -> 56%
where the time goes in v15:
time: 491 us; the launch traced here: 487 us
  Pallas kernels  434 us (88%)
  local copies, waits for them, and re-layouts  24.8 us (5%)
  between operations  14.1 us (3%)
  other arithmetic  8.2 us (2%)
  starting transfers between devices  5.12 us (1%)
    pallas_call x1, Pallas kernels, tail(): pl.pallas_call(functools.partial(tail_kernel, count, batches), out_shape=...  168 us
    pallas_call x1, Pallas kernels, mlp_back(): pl.pallas_call(functools.partial(mlp_kernel, count), out_shape=[shape(tot...  106 us
    pallas_call x1, Pallas kernels, entry(): pl.pallas_call(functools.partial(entry_kernel, count, batches), out_shape...  54.6 us
    pallas_call x1, Pallas kernels, spread(): pl.pallas_call(functools.partial(spread_kernel, count, batches, plans), o...  53 us
    pallas_call x1, Pallas kernels, fold(): pl.pallas_call(functools.partial(fold_kernel, batches), out_shape=jax.Sha...  33.2 us
    pallas_call x2, Pallas kernels, local_call(): pl.pallas_call(kernel, out_shape=outs, in_specs=[smem] * len(scalars) + [...  18.4 us
    unnamed x42, local copies, waits for them, and re-layouts  15.4 us
  transfers between devices with their start and end apart: 7, of which 0 were waited for; matrix products, arithmetic and copies ran while one was open for 2% of the time, Pallas kernels for 56%

profile of v15, /device:TPU:0, one launch (start us, length us, event | category | flops | bytes accessed | tf_op | source)
XLA Modules:
  0.0 486.5 jit_solution(17795410215044757237)
XLA Ops:
  7.2 1.0 copy.36
  8.2 1.0 copy.35
  9.2 1.3 maximum_convert_fusion.gain_ref
  10.5 1.8 pad_maximum_fusion.1.w_ref
  12.3 54.6 %entry.1 = (bf16[1280,2048]{1,0:T(8,128)(2,1)}, bf16[1280,128]{1,0:T(8,128)(2,1)}, f32[1280,128]{1,0:T(8,128)}, bf16[5120,256]{1,0:T(8,128)(2,1)}, bf16[2048,512...) custom-call(bf16[1280,2048]{1,0:T(8,128)(2,1)} %x_hbm.1, ...), custom_call_target="tpu_custom_call" | custom-call | tf_op jit(solution)/shard_map/entry/pallas_call | solution.py:756
  70.0 7.6 %attend.1 = (f32[1280,128]{1,0:T(8,128)}, bf16[1280,128]{1,0:T(8,128)(2,1)}, f32[1,1280]{1,0:T(1,128)}) custom-call(s32[1280]{0:T(1024)} %copy-done.11, s32[1]{0:T(128)} %bitcast.3.base_sm, bf16[1280,128]{1,0:T(8,128)(2,1)} %get-tuple-element.57.q_ref, bf16[5120,256]{1,0:T(8,128)(2,1)} %get-tuple-element.58.kv_ref, s32[1,1280]{1,0:T(1,128)} %broadcast_in_dim.22.start_ref, ...), custom_call_target="tpu_custom_call" | custom-call | flops 3355443200 | bytes 8388608 | tf_op jit(solution)/shard_map/attend/pallas_call | solution.py:1269
  77.6 53.0 %spread_2.1 = (bf16[1280,1024]{1,0:T(8,128)(2,1)}, bf16[768,2048]{1,0:T(8,128)(2,1)}, bf16[2048,768]{1,0:T(8,128)(2,1)}) custom-call(bf16[1280,128]{1,0:T(8,128)(2,1)} %get-tuple-element.61.refs_0_, bf16[768,512]{1,0:T(8,128)(2,1)} %refs_1_.1, bf16[512,768]{1,0:T(8,128)(2,1)} %refs_2_.1), custom_call_target="tpu_custom_call" | custom-call | tf_op jit(solution)/shard_map/spread_2/pallas_call | solution.py:176
  130.7 106.5 %mlp_back.1 = (bf16[1280,2048]{1,0:T(8,128)(2,1)}, bf16[2048,1536]{1,0:T(8,128)(2,1)}, bf16[768,2048]{1,0:T(8,128)(2,1)}, f32[160,2048]{1,0:T(8,128)}, f32[160,2...) custom-call(bf16[1280,2048]{1,0:T(8,128)(2,1)} %x_hbm.1, ...), custom_call_target="tpu_custom_call" | custom-call | flops 41607495680 | bytes 41943040 | tf_op jit(solution)/shard_map/mlp_back/pallas_call | solution.py:540
  237.3 1.9 collective-permute-start
  239.2 10.8 %attend_back.1 = (bf16[1280,128]{1,0:T(8,128)(2,1)}, bf16[1280,128]{1,0:T(8,128)(2,1)}, bf16[5120,256]{1,0:T(8,128)(2,1)}) custom-call(s32[1280]{0:T(1024)} %copy-done.11, s32[1]{0:T(128)} %bitcast.3.base_sm, bf16[1280,128]{1,0:T(8,128)(2,1)} %get-tuple-element.57.q_ref, bf16[5120,256]{1,0:T(8,128)(2,1)} %get-tuple-element.58.kv_ref, ...), custom_call_target="tpu_custom_call" | custom-call | flops 8388608000 | bytes 8388608 | tf_op jit(solution)/shard_map/attend_back/pallas_call | solution.py:1269
  250.0 1.8 add_convert_fusion.1
  251.8 2.9 collective-permute-start.3
  254.7 33.2 %fold.1 = bf16[1280,128]{1,0:T(8,128)(2,1)} custom-call(bf16[5120,256]{1,0:T(8,128)(2,1)} %get-tuple-element.77.part_ref), custom_call_target="tpu_custom_call" | custom-call | tf_op jit(solution)/shard_map/fold/pallas_call | solution.py:967
  287.9 1.4 convert_add_fusion
  290.1 1.1 constant_dynamic-slice_fusion.1.mixed_ref
  291.3 1.1 constant_dynamic-slice_fusion.x_ref
  292.8 1.3 copy-done.2
  295.0 168.0 %tail.1 = (bf16[8,160,2048]{2,1,0:T(8,128)(2,1)S(1)}, bf16[8,160,2048]{2,1,0:T(8,128)(2,1)}, f32[2,512]{1,0:T(2,128)S(1)}, f32[128,512]{1,0:T(8,128)S(1)}, f32[512,384]{1,0:T(8,128)S(1)}) custom-call(bf16[1280,384]{1,0:T(8,128)(2,1)S(1)} %pad_maximum_fusion.cat_ref, bf16[2048,512]{1,0:T(8,128)(2,1)S(1)} %copy-done.1, ...), custom_call_target="tpu_custom_call" | custom-call | flops 2013265920 | bytes 419430400 | tf_op jit(solution)/shard_map/tail/pallas_call | solution.py:1225
  462.9 2.3 copy-done
  468.4 3.4 fusion
  471.8 1.4 convert_element_type.55
  473.2 2.7 copy.47
  475.9 1.1 slice-done.3
  476.9 2.4 copy.48
  (63 shorter events, 9.0 us)
Async XLA Ops:
  7.2 123.5 %all-gather.2.cloned.1.call-start = ((), (), s32[]{:S(2)}) async-start(), calls=%async_computation.2 | async-start | bytes 3932160 | tf_op jit(solution)/shard_map/all_gather | solution.py:1362
  12.3 55.7 %copy-start.10 = (s32[1280]{0:T(1024)S(1)}, s32[1280]{0:T(1024)}, u32[]{:S(2)}) copy-start(s32[1280]{0:T(1024)} %param.14) | copy-start | bytes 15364
  66.9 401.5 %reduce-scatter.5.cloned.1.call-start = ((), (), s32[]{:S(2)}) async-start(), calls=%async_computation.4 | async-start | bytes 3932160 | tf_op jit(solution)/shard_map/reduce_scatter | solution.py:1415
  68.0 2.0 copy-start.11
  237.1 12.9 %collective-permute-start.1 = (bf16[160,2048]{1,0:T(8,128)(2,1)}, bf16[160,2048]{1,0:T(8,128)(2,1)S(1)}, u32[]{:S(2)}, u32[]{:S(2)}) collective-permute-start(bf16[160,2048]{1,0:T(8,128)(2,1)} %get-tuple-element.76), channel_id=1, source_target_pairs={{0,1},{2,0},{4,2},{6,4},{7,6},{5,7},{3,5},{1,3},{8,9},{10,8},{12,1... | collective-permute-start | bytes 1966088 | tf_op jit(solution)/shard_map/ppermute | solution.py:1304
  237.3 12.7 %collective-permute-start = (bf16[160,2048]{1,0:T(8,128)(2,1)}, bf16[160,2048]{1,0:T(8,128)(2,1)S(1)}, u32[]{:S(2)}, u32[]{:S(2)}) collective-permute-start(bf16[160,2048]{1,0:T(8,128)(2,1)} %get-tuple-element.74), channel_id=1, source_target_pairs={{0,2},{2,4},{4,6},{6,7},{7,5},{5,3},{3,1},{1,0},{8,10},{10,12},{12... | collective-permute-start | bytes 1966088 | tf_op jit(solution)/shard_map/ppermute | solution.py:1303
  251.8 36.1 %collective-permute-start.3 = (bf16[160,2048]{1,0:T(8,128)(2,1)S(1)}, bf16[160,2048]{1,0:T(8,128)(2,1)S(1)}, u32[]{:S(2)}, u32[]{:S(2)}) collective-permute-start(bf16[160,2048]{1,0:T(8,128)(2,1)S(1)} %get-tuple-element.79), channel_id=1, source_target_pairs={{0,1},{2,0},{4,2},{6,4},{7,6},{5,7},{3,5},{1,3},{8,9},{10,8},{12,1... | collective-permute-start | bytes 1966088 | tf_op jit(solution)/shard_map/ppermute | solution.py:1309
  254.7 33.2 %collective-permute-start.2 = (bf16[160,2048]{1,0:T(8,128)(2,1)S(1)}, bf16[160,2048]{1,0:T(8,128)(2,1)S(1)}, u32[]{:S(2)}, u32[]{:S(2)}) collective-permute-start(bf16[160,2048]{1,0:T(8,128)(2,1)S(1)} %get-tuple-element.78), channel_id=1, source_target_pairs={{0,2},{2,4},{4,6},{6,7},{7,5},{5,3},{3,1},{1,0},{8,10},{10,12},{12... | collective-permute-start | bytes 1966088 | tf_op jit(solution)/shard_map/ppermute | solution.py:1308
  289.3 179.1 %reduce-scatter.3.cloned.1.call-start = ((), (), s32[]{:S(2)}) async-start(), calls=%async_computation.3 | async-start | bytes 7864320 | tf_op jit(solution)/shard_map/reduce_scatter | solution.py:1416
  290.0 2.4 copy-start.6
  290.1 2.4 copy-start.8
  290.1 2.4 copy-start.9
  290.1 2.5 copy-start.5
  292.4 1.7 copy-start.2
  292.6 2.2 copy-start.1
  292.6 2.4 copy-start.3
  292.6 2.4 copy-start.4
  462.9 2.4 copy-start
  467.6 5.6 %slice-start = ((s8[5242880]{0:T(1024)(128)(4,1)}), s8[1048576]{0:T(1024)(128)(4,1)S(1)}, s32[]{:S(2)}) async-start(s8[5242880]{0:T(1024)(128)(4,1)} %bitcast.17), calls=%async_computation.5 | async-start | bytes 2097152
  468.4 3.4 copy-start.7
  468.4 4.8 slice-start.1
  471.8 4.0 slice-start.2
  473.2 3.8 slice-start.3
Sparse Core Ops, SparseCore 0:
  67.0 28.4 all-gather.1
  289.4 36.7 reduce-scatter.4
  329.0 61.8 reduce-scatter.2

commit v16 on v15

--- a/solution.py
+++ b/solution.py
@@ -892,111 +892,19 @@
         dkv_ref[keys, size:] = jnp.concatenate([dk[:, half:], dv[:, half:]], axis=1)
 
 
-def fold_kernel(
-    batches, part_ref, own_ref, core_got, x_first, x_second, y_first, y_second, held, send_sem, recv_sem
-):
-    rows, size = own_ref.shape
-    half = rows // 2
-    others = batches // 2
-    head = lax.axis_index("head")
-    batch = lax.axis_index("batch")
-    across, core, low = batch // 2, lax.rem(batch, 2), lax.rem(head, 2)
-    twin = (across * 2 + 1 - core, head)
-    mate = (batch, head + 1 - 2 * low)
-    spots = [lax.rem(across + hop, others) for hop in range(others)]
-    peers = [(spot * 2 + core, head) for spot in spots]
-    greet((twin, mate, *peers[1:]))
-    sems = (send_sem, recv_sem)
-    slot = 0
-    copies = []
-    mine = pl.ds(pl.multiple_of(low * size, size), size)
-    given = pl.ds(pl.multiple_of((1 - low) * size, size), size)
-    top, bottom = pl.ds(0, half), pl.ds(half, half)
-
-    def block(at, side):
-        return pl.ds(pl.multiple_of((2 * at + side) * rows, rows), rows)
-
-    def go(source, target, device):
-        nonlocal slot
-        copy = send(source, target, sems, slot, device)
-        slot += 1
-        copies.append(copy)
-        return copy
-
-    order = list(range(1, others)) + [0]
-    first = [go(part_ref.at[block(spots[hop], 1 - core)], core_got.at[spots[hop]], twin) for hop in order]
-    tops, bottoms = [], []
-    for copy, hop in zip(first, order):
-        copy.wait_recv()
-        spot = spots[hop]
-        core_got[spot] = add_low(core_got[spot], part_ref[block(spot, core)])
-        bottoms.append(go(core_got.at[spot, bottom, given], y_first.at[spot], mate))
-        if hop:
-            tops.append(go(core_got.at[spot, top], x_first.at[hop - 1], peers[hop]))
-    total = core_got[across, top].astype(F32)
-    for hop in range(1, others):
-        tops[hop - 1].wait_recv()
-        total = total + x_first[hop - 1].astype(F32)
-    held[...] = total.astype(BF)
-    last = go(held.at[:, given], y_second, mate)
-    ends = []
-    for copy, hop in zip(bottoms, order):
-        copy.wait_recv()
-        spot = spots[hop]
-        y_first[spot] = add_low(y_first[spot], core_got[spot, bottom, mine])
-        if hop:
-            ends.append(go(y_first.at[spot], x_second.at[hop - 1], peers[hop]))
-    last.wait_recv()
-    own_ref[top] = add_low(held[:, mine], y_second[...])
-    total = y_first[across].astype(F32)
-    for hop in range(1, others):
-        ends[hop - 1].wait_recv()
-        total = total + x_second[hop - 1].astype(F32)
-    own_ref[bottom] = total.astype(BF)
-    for copy in copies:
-        copy.wait_send()
-
-
-def fold(part, rows, collective_id):
-    batches = lax.axis_size("batch")
-    others = batches // 2
-    size = part.shape[1] // 2
-    half = rows // 2
-    vmem = pl.BlockSpec(memory_space=pltpu.VMEM)
-    sems = pltpu.SemaphoreType.DMA((4 * others,))
-    return pl.pallas_call(
-        functools.partial(fold_kernel, batches),
-        out_shape=jax.ShapeDtypeStruct((rows, size), BF),
-        in_specs=[vmem],
-        out_specs=vmem,
-        scratch_shapes=[
-            pltpu.VMEM((others, rows, 2 * size), BF),
-            pltpu.VMEM((others - 1, half, 2 * size), BF),
-            pltpu.VMEM((others - 1, half, size), BF),
-            pltpu.VMEM((others, half, size), BF),
-            pltpu.VMEM((half, size), BF),
-            pltpu.VMEM((half, 2 * size), BF),
-            sems,
-            sems,
-        ],
-        compiler_params=pltpu.CompilerParams(
-            collective_id=collective_id, has_side_effects=True, vmem_limit_bytes=VMEM_LIMIT
-        ),
-        name="fold",
-    )(part)
-
-
 def tail_kernel(
-    count, batches, cat_ref, w_ref, x_ref, gain_ref, dh1_ref, second_ref,
-    n1_ref, mixed_ref, low_ref, out_0,
+    count, batches, dq_ref, dg_ref, dkv_ref, w_ref, x_ref, gain_ref, dh1_ref, second_ref,
+    n1_ref, mixed_ref, low_ref, base_ref, ahead_ref, behind_ref,
     out_all, tok_all, gains_ref, wout_own, din_ref,
     part_ref, tok_ref, got, wout_got, gain_own, gain_got, gain_mid, gain_heads,
-    din_s, din_got, din_x, wout_s, wout_twin, wout_x, wout_part,
+    din_s, din_got, din_x, wout_s, wout_twin, wout_x,
+    cat_ref, out_s, out_got, core_got, x_first, x_second, y_first, y_second, held, n1_s,
     send_sem, recv_sem, local_sem,
 ):
     steps = count // 2
     rows, width = x_ref.shape
     depth = cat_ref.shape[1]
+    tall, size = dq_ref.shape
     tile = 256
     place, right, left = ring_setup(count)
     batch, head = lax.axis_index("batch"), lax.axis_index("head")
@@ -1046,7 +954,7 @@
             add_tiles(target if last else held.at[across], held.at[across], crossed.at[hop])
 
     def wout_view(at):
-        wide = wout_part.shape[1]
+        wide = width // batches
         return wout_s.at[:, pl.ds(pl.multiple_of(at * wide, wide), wide)]
 
     def din_view(at):
@@ -1100,32 +1008,95 @@
             out.append(go(held.at[flow, step - 1], held.at[flow, step], device))
         return out
 
-    keep_out = pltpu.make_async_copy(out_0, out_all.at[place], local_sem.at[0])
-    keep_out.start()
-    compute(place + steps)
-    sums = reduce(part_ref, got, 0, None)
-    outs = gather(out_0, out_all, 0, None)
-
-    @pl.loop(1, count)
-    def _(hop):
-        compute(place + steps + hop)
+    low = lax.rem(head, 2)
+    mate = (batch, head + 1 - 2 * low)
+    peers = [(spot * 2 + core, head) for spot in spots]
+    mine = pl.ds(pl.multiple_of(low * size, size), size)
+    given = pl.ds(pl.multiple_of((1 - low) * size, size), size)
+    top, bottom = pl.ds(0, tall // 2), pl.ds(tall // 2, tall // 2)
+    fresh = pl.ds(2 * size, size)
+
+    def keys_of(at):
+        return dkv_ref.at[pl.ds(pl.multiple_of(at * tall, tall), tall)]
+
+    def normed_copy(at, slot):
+        cols = pl.ds(pl.multiple_of(at * tile, tile), tile)
+        return pltpu.make_async_copy(n1_ref.at[:, cols], n1_s.at[slot], local_sem.at[2 + slot])
+
+    for at in range(2):
+        normed_copy(at, at).start()
+    last_sums = [go(ahead_ref, out_got.at[0], right), go(behind_ref, out_got.at[1], left)]
+    swaps = scatter_swap(keys_of, core_got)
+    cat_ref[:, pl.ds(0, size)] = dq_ref[...]
+    cat_ref[:, pl.ds(size, size)] = dg_ref[...]
 
     @pl.loop(0, width // tile)
     def _(at):
         cols = pl.ds(pl.multiple_of(at * tile, tile), tile)
         wout_s[:, cols] = rows_inner(mixed_ref[...], low_ref[:, cols]).astype(BF)
 
+    tops, bottoms = [], []
+    for copy, hop in zip(swaps, order):
+        copy.wait_recv()
+        spot = spots[hop]
+        add_tiles(core_got.at[spot], core_got.at[spot], keys_of(2 * spot + core))
+        bottoms.append(go(core_got.at[spot, bottom, given], y_first.at[spot], mate))
+        if hop:
+            tops.append(go(core_got.at[spot, top], x_first.at[hop - 1], peers[hop]))
     wouts = scatter_swap(wout_view, wout_twin)
+    for copy in last_sums:
+        copy.wait_recv()
+    out_s[...] = (
+        base_ref[...] + out_got[0].astype(F32) + out_got[1].astype(F32)
+    ).astype(BF)
+    keep_out = pltpu.make_async_copy(out_s, out_all.at[place], local_sem.at[0])
+    keep_out.start()
+    outs = gather(out_s, out_all, 0, None)
+    total = core_got[across, top].astype(F32)
+    for hop, copy in enumerate(tops):
+        copy.wait_recv()
+        total = total + x_first[hop].astype(F32)
+    held[...] = total.astype(BF)
+    last = go(held.at[:, given], y_second, mate)
+    ends = []
+    for copy, hop in zip(bottoms, order):
+        copy.wait_recv()
+        spot = spots[hop]
+        y_first[spot] = add_low(y_first[spot], core_got[spot, bottom, mine])
+        if hop:
+            ends.append(go(y_first.at[spot], x_second.at[hop - 1], peers[hop]))
+    last.wait_recv()
+    cat_ref[top, fresh] = add_low(held[:, mine], y_second[...])
+    total = y_first[across].astype(F32)
+    for hop, copy in enumerate(ends):
+        copy.wait_recv()
+        total = total + x_second[hop].astype(F32)
+    cat_ref[bottom, fresh] = total.astype(BF)
+
+    compute(place + steps)
+    sums = reduce(part_ref, got, 0, None)
+    outs = gather(out_s, out_all, 1, outs)
+
+    @pl.loop(1, count)
+    def _(hop):
+        compute(place + steps + hop)
 
     @pl.loop(0, width // tile)
     def _(at):
+        slot = lax.rem(at, 2)
+        normed_copy(at, slot).wait()
         cols = pl.ds(pl.multiple_of(at * tile, tile), tile)
-        din_s[cols] = rows_inner(n1_ref[:, cols], cat_ref[...]).astype(BF)
+        din_s[cols] = rows_inner(n1_s[slot], cat_ref[...]).astype(BF)
+
+        @pl.when(at + 2 < width // tile)
+        def _():
+            normed_copy(at + 2, slot).start()
 
     dins = scatter_swap(din_view, din_got)
     for step in range(1, steps):
         sums = reduce(part_ref, got, step, sums)
-        outs = gather(out_0, out_all, step, outs)
+        if step + 1 < steps:
+            outs = gather(out_s, out_all, step + 1, outs)
         if step == 1:
             wouts = scatter_cross(wout_view, wout_twin, wout_x, wouts)
             dins = scatter_cross(din_view, din_got, din_x, dins)
@@ -1165,6 +1136,7 @@
     keep_tok = pltpu.make_async_copy(tok_ref, tok_all.at[place], local_sem.at[1])
     keep_tok.start()
     toks = gather(tok_ref, tok_all, 0, None)
+    wout_part = wout_twin.at[across]
     scatter_end(wout_twin, wout_x, wouts, wout_part)
     wsums = reduce(wout_part, wout_got, 0, None)
     scatter_end(din_got, din_x, dins, din_ref)
@@ -1210,17 +1182,19 @@
     keep_tok.wait()
 
 
-def tail(d_cat, w_in, x_own, gain, d_resid, second, normed, mixed, low, out_own, collective_id):
+def tail(arrays, collective_id):
+    d_queries, _, d_keys, _, x_own, *_, mixed, _, _, _, _ = arrays
     count = lax.axis_size("head")
     batches = lax.axis_size("batch")
     steps = count // 2
     rows, width = x_own.shape
     others = batches // 2
     size, wide = mixed.shape[1] // count, width // batches
-    depth = d_cat.shape[1]
+    tall, head_size = d_queries.shape
+    depth = 3 * head_size
     vmem = pl.BlockSpec(memory_space=pltpu.VMEM)
     whole = (count, rows, width)
-    sems = pltpu.SemaphoreType.DMA((5 * count + 3 * batches,))
+    sems = pltpu.SemaphoreType.DMA((6 * count + 6 * batches,))
     gains = (2, width // batches)
     return pl.pallas_call(
         functools.partial(tail_kernel, count, batches),
@@ -1231,7 +1205,7 @@
             jax.ShapeDtypeStruct((size, wide), F32),
             jax.ShapeDtypeStruct((wide, depth), F32),
         ],
-        in_specs=[vmem] * 10,
+        in_specs=[vmem] * 8 + [pl.BlockSpec(memory_space=pl.ANY)] + [vmem] * 5,
         out_specs=[vmem] * 5,
         scratch_shapes=[
             pltpu.VMEM((count * rows, width), BF),
@@ -1248,19 +1222,28 @@
             pltpu.VMEM((count * size, width), BF),
             pltpu.VMEM((others, count * size, wide), BF),
             pltpu.VMEM((others - 1, count * size, wide), BF),
-            pltpu.VMEM((count * size, wide), BF),
+            pltpu.VMEM((tall, depth), BF),
+            pltpu.VMEM((rows, width), BF),
+            pltpu.VMEM((2, rows, width), BF),
+            pltpu.VMEM((others, tall, 2 * head_size), BF),
+            pltpu.VMEM((others - 1, tall // 2, 2 * head_size), BF),
+            pltpu.VMEM((others - 1, tall // 2, head_size), BF),
+            pltpu.VMEM((others, tall // 2, head_size), BF),
+            pltpu.VMEM((tall // 2, head_size), BF),
+            pltpu.VMEM((tall // 2, 2 * head_size), BF),
+            pltpu.VMEM((2, tall, 256), BF),
             sems,
             sems,
-            pltpu.SemaphoreType.DMA((2,)),
+            pltpu.SemaphoreType.DMA((4,)),
         ],
         compiler_params=pltpu.CompilerParams(
-            collective_id=collective_id, has_side_effects=True, vmem_limit_bytes=(32 << 20) + 4 * count * size * width
+            collective_id=collective_id, has_side_effects=True, vmem_limit_bytes=(36 << 20) + 6 * count * size * width
         ),
         cost_estimate=pl.CostEstimate(
-            flops=2 * count * rows * width * d_cat.shape[1], bytes_accessed=400 << 20, transcendentals=0
+            flops=4 * count * rows * width * depth, bytes_accessed=400 << 20, transcendentals=0
         ),
         name="tail",
-    )(d_cat, w_in, x_own, gain, d_resid, second, normed, mixed, low, out_own)
+    )(*arrays)
 
 
 def local_call(kernel, scalars, arrays, outs, scratch, flops, name):
@@ -1305,9 +1288,6 @@
         going = add_low(from_left, mine(place + steps - 1 - step))
         coming = add_low(from_right, mine(place - steps + 1 + step))
         going, coming = yield going, coming
-    from_left = lax.ppermute(going, "head", right)
-    from_right = lax.ppermute(coming, "head", left)
-    yield mine(place).astype(F32) + from_left.astype(F32) + from_right.astype(F32)
 
 
 def matmul(left, right):
@@ -1406,19 +1386,18 @@
         5 * pair_flops // 2,
         "attend_back",
     )
-    d_kv_all, state = hold((d_kv_all, state))
-    while isinstance(state, tuple):
+    for _ in range(3, heads // 2 - 1):
         state = flow.send(state)
-    d_kv = fold(d_kv_all, row_count, 4)
-    d_kv, state, d_down, d_mlp = hold((d_kv, state, d_down, d_mlp))
-    out_own = (resid_own + state).astype(BF)
     d_down = lax.psum_scatter(d_down, "batch", scatter_dimension=1, tiled=True)
     d_mlp = lax.psum_scatter(d_mlp, "batch", scatter_dimension=0, tiled=True)
-    d_cat = jnp.concatenate([d_queries, d_gate_logit, d_kv], axis=1)
     inputs_own = lax.dynamic_slice_in_dim(tokens, me * chunk, chunk, 0)
+    base_own = resid_own + lax.dynamic_slice_in_dim(mlp_part, me * chunk, chunk, 0).astype(F32)
     output, d_tokens, d_gains, d_out, d_in = tail(
-        d_cat, w_in, inputs_own, gain_one[None], d_resid, d_gain_two, normed_one, mixed_own,
-        d_resid_low, out_own, 5,
+        (
+            d_queries, d_gate_logit, d_kv_all, w_in, inputs_own, gain_one[None], d_resid, d_gain_two,
+            normed_one, mixed_own, d_resid_low, base_own, *state,
+        ),
+        5,
     )
     d_tokens, d_mlp, d_down = hold((d_tokens, d_mlp, d_down))
     d_mlp, d_down = d_mlp.astype(F32), d_down.astype(F32)

time: 491 us -> 496 us (1.010)
  Pallas kernels: 434 us -> 448 us
    pallas_call x1, Pallas kernels: 168 us -> 212 us  [tail(): pl.pallas_call(functools.partial(tail_kernel, count, batches), out_shape=...]
    pallas_call x1 -> x0, Pallas kernels: 33.2 us -> none  [fold(): pl.pallas_call(functools.partial(fold_kernel, batches), out_shape=jax.Sha...]
    unnamed x42 -> x32, local copies, waits for them, and re-layouts: 15.4 us -> 13.4 us
  transfers between devices with their start and end apart: 7 -> 5, of which waited for: 0 -> 0; matrix products, arithmetic and copies ran while one was open for 2% -> 2% of each run, Pallas kernels for 56% -> 58%
where the time goes in v16:
time: 496 us
  Pallas kernels  448 us (90%)
  local copies, waits for them, and re-layouts  22.5 us (5%)
  between operations  14 us (3%)
  other arithmetic  8.48 us (2%)
    pallas_call x1, Pallas kernels, tail(): pl.pallas_call(functools.partial(tail_kernel, count, batches), out_shape=...  212 us
    pallas_call x1, Pallas kernels, mlp_back(): pl.pallas_call(functools.partial(mlp_kernel, count), out_shape=[shape(tot...  105 us
    pallas_call x1, Pallas kernels, spread(): pl.pallas_call(functools.partial(spread_kernel, count, batches, plans), o...  57.6 us
    pallas_call x1, Pallas kernels, entry(): pl.pallas_call(functools.partial(entry_kernel, count, batches), out_shape...  54.6 us
    pallas_call x2, Pallas kernels, local_call(): pl.pallas_call(kernel, out_shape=outs, in_specs=[smem] * len(scalars) + [...  18.9 us
    unnamed x32, local copies, waits for them, and re-layouts  13.4 us
  transfers between devices with their start and end apart: 5, of which 0 were waited for; matrix products, arithmetic and copies ran while one was open for 2% of the time, Pallas kernels for 58%

profile of v16, /device:TPU:0, one launch (start us, length us, event | category | flops | bytes accessed | tf_op | source)
XLA Modules:
  0.0 495.5 jit_solution(18089923540627590778)
XLA Ops:
  7.2 1.0 copy.36
  8.2 1.0 copy.35
  9.2 1.3 maximum_convert_fusion.gain_ref
  10.5 1.8 pad_maximum_fusion.w_ref
  12.3 54.6 %entry.1 = (bf16[1280,2048]{1,0:T(8,128)(2,1)}, bf16[1280,128]{1,0:T(8,128)(2,1)}, f32[1280,128]{1,0:T(8,128)}, bf16[5120,256]{1,0:T(8,128)(2,1)}, bf16[2048,512...) custom-call(bf16[1280,2048]{1,0:T(8,128)(2,1)} %x_hbm.1, ...), custom_call_target="tpu_custom_call" | custom-call | tf_op jit(solution)/shard_map/entry/pallas_call | solution.py:756
  67.0 0.8 lt.34
  68.6 0.7 reshape.50
  70.0 7.6 %attend.1 = (f32[1280,128]{1,0:T(8,128)}, bf16[1280,128]{1,0:T(8,128)(2,1)}, f32[1,1280]{1,0:T(1,128)}) custom-call(s32[1280]{0:T(1024)} %copy-done.8, s32[1]{0:T(128)} %bitcast.3.base_sm, bf16[1280,128]{1,0:T(8,128)(2,1)} %get-tuple-element.50.q_ref, bf16[5120,256]{1,0:T(8,128)(2,1)} %get-tuple-element.51.kv_ref, s32[1,1280]{1,0:T(1,128)} %broadcast_in_dim.22.start_ref, ...), custom_call_target="tpu_custom_call" | custom-call | flops 3355443200 | bytes 8388608 | tf_op jit(solution)/shard_map/attend/pallas_call | solution.py:1252
  77.6 57.6 %spread_2.1 = (bf16[1280,1024]{1,0:T(8,128)(2,1)}, bf16[768,2048]{1,0:T(8,128)(2,1)}, bf16[2048,768]{1,0:T(8,128)(2,1)}) custom-call(bf16[1280,128]{1,0:T(8,128)(2,1)} %get-tuple-element.54.refs_0_, bf16[768,512]{1,0:T(8,128)(2,1)} %refs_1_.1, bf16[512,768]{1,0:T(8,128)(2,1)} %refs_2_.1), custom_call_target="tpu_custom_call" | custom-call | tf_op jit(solution)/shard_map/spread_2/pallas_call | solution.py:176
  135.3 104.9 %mlp_back.1 = (bf16[1280,2048]{1,0:T(8,128)(2,1)}, bf16[2048,1536]{1,0:T(8,128)(2,1)}, bf16[768,2048]{1,0:T(8,128)(2,1)}, f32[160,2048]{1,0:T(8,128)}, f32[160,2...) custom-call(bf16[1280,2048]{1,0:T(8,128)(2,1)} %x_hbm.1, ...), custom_call_target="tpu_custom_call" | custom-call | flops 41607495680 | bytes 41943040 | tf_op jit(solution)/shard_map/mlp_back/pallas_call | solution.py:540
  241.1 1.0 constant_dynamic-slice_fusion.mixed_ref
  242.1 1.1 constant_dynamic-slice_fusion.1.x_ref
  243.8 1.5 collective-permute-start
  245.3 11.3 %attend_back.1 = (bf16[1280,128]{1,0:T(8,128)(2,1)}, bf16[1280,128]{1,0:T(8,128)(2,1)}, bf16[5120,256]{1,0:T(8,128)(2,1)}) custom-call(s32[1280]{0:T(1024)} %copy-done.8, s32[1]{0:T(128)} %bitcast.3.base_sm, bf16[1280,128]{1,0:T(8,128)(2,1)} %get-tuple-element.50.q_ref, bf16[5120,256]{1,0:T(8,128)(2,1)} %get-tuple-element.51.kv_ref, ...), custom_call_target="tpu_custom_call" | custom-call | flops 8388608000 | bytes 8388608 | tf_op jit(solution)/shard_map/attend_back/pallas_call | solution.py:1252
  256.6 3.8 add_convert_fusion
  260.4 211.5 %tail.1 = (bf16[8,160,2048]{2,1,0:T(8,128)(2,1)}, bf16[8,160,2048]{2,1,0:T(8,128)(2,1)}, f32[2,512]{1,0:T(2,128)S(1)}, f32[128,512]{1,0:T(8,128)S(1)}, f32[512,384]{1,0:T(8,128)S(1)}) custom-call(bf16[1280,128]{1,0:T(8,128)(2,1)S(1)} %copy-done.2, bf16[1280,128]{1,0:T(8,128)(2,1)S(1)} %copy-done.3, bf16[5120,256]{1,0:T(8,128)(2,1)} %get-tuple-element.66.dkv_ref, ...), custom_call_target="tpu_custom_call" | custom-call | flops 4026531840 | bytes 419430400 | tf_op jit(solution)/shard_map/tail/pallas_call | solution.py:1199
  472.1 0.8 copy.38
  472.9 0.8 copy.39
  474.2 0.8 fusion.1
  475.0 3.3 fusion
  478.4 1.4 convert_element_type.43
  479.8 6.2 %copy.47 = bf16[1280,2048]{1,0:T(8,128)(2,1)} copy(bf16[1280,2048]{1,0:T(8,128)(2,1)} %bitcast.21) | data formatting | bytes 10485760
  485.9 2.4 copy.48
  488.3 0.7 copy.49
  (44 shorter events, 3.7 us)
Async XLA Ops:
  7.2 128.1 %all-gather.2.cloned.1.call-start = ((), (), s32[]{:S(2)}) async-start(), calls=%async_computation.2 | async-start | bytes 3932160 | tf_op jit(solution)/shard_map/all_gather | solution.py:1342
  12.3 55.6 %copy-start.7 = (s32[1280]{0:T(1024)S(1)}, s32[1280]{0:T(1024)}, u32[]{:S(2)}) copy-start(s32[1280]{0:T(1024)} %param.14) | copy-start | bytes 15364
  66.9 408.1 %reduce-scatter.5.cloned.1.call-start = ((), (), s32[]{:S(2)}) async-start(), calls=%async_computation.4 | async-start | bytes 3932160 | tf_op jit(solution)/shard_map/reduce_scatter | solution.py:1391
  68.0 2.0 copy-start.8
  240.2 234.8 %reduce-scatter.3.cloned.1.call-start = ((), (), s32[]{:S(2)}) async-start(), calls=%async_computation.3 | async-start | bytes 7864320 | tf_op jit(solution)/shard_map/reduce_scatter | solution.py:1392
  243.2 13.3 %collective-permute-start.1 = (bf16[160,2048]{1,0:T(8,128)(2,1)}, bf16[160,2048]{1,0:T(8,128)(2,1)S(1)}, u32[]{:S(2)}, u32[]{:S(2)}) collective-permute-start(bf16[160,2048]{1,0:T(8,128)(2,1)} %get-tuple-element.75), channel_id=1, source_target_pairs={{0,1},{2,0},{4,2},{6,4},{7,6},{5,7},{3,5},{1,3},{8,9},{10,8},{12,1... | collective-permute-start | bytes 1966088 | tf_op jit(solution)/shard_map/ppermute | solution.py:1287
  243.8 12.8 %collective-permute-start = (bf16[160,2048]{1,0:T(8,128)(2,1)}, bf16[160,2048]{1,0:T(8,128)(2,1)S(1)}, u32[]{:S(2)}, u32[]{:S(2)}) collective-permute-start(bf16[160,2048]{1,0:T(8,128)(2,1)} %get-tuple-element.74), channel_id=1, source_target_pairs={{0,2},{2,4},{4,6},{6,7},{7,5},{5,3},{3,1},{1,0},{8,10},{10,12},{12... | collective-permute-start | bytes 1966088 | tf_op jit(solution)/shard_map/ppermute | solution.py:1286
  245.3 11.3 %copy-start.5 = (f32[160,2048]{1,0:T(8,128)S(1)}, f32[160,2048]{1,0:T(8,128)}, u32[]{:S(2)}) copy-start(f32[160,2048]{1,0:T(8,128)} %get-tuple-element.72) | copy-start | bytes 3932164
  256.6 3.8 copy-start
  256.6 3.8 copy-start.1
  256.6 3.8 copy-start.2
  256.6 3.8 copy-start.3
  256.6 3.8 copy-start.4
  475.0 3.3 copy-start.6
  478.4 7.5 %slice-start = ((s8[5242880]{0:T(1024)(128)(4,1)}), s8[4194304]{0:T(1024)(128)(4,1)S(1)}, s32[]{:S(2)}) async-start(s8[5242880]{0:T(1024)(128)(4,1)} %bitcast.18), calls=%async_computation.5 | async-start | bytes 8388608
  479.8 6.2 %slice-start.1 = ((s8[5242880]{0:T(1024)(128)(4,1)}), s8[1048576]{0:T(1024)(128)(4,1)S(1)}, s32[]{:S(2)}) async-start(s8[5242880]{0:T(1024)(128)(4,1)} %bitcast.18), calls=%async_computation.6 | async-start | bytes 2097152
Sparse Core Ops, SparseCore 0:
  67.0 28.4 all-gather.1
  240.4 37.1 reduce-scatter.4
  280.3 58.3 reduce-scatter.2

commit v17 on v16

--- a/solution.py
+++ b/solution.py
@@ -893,13 +893,13 @@
 
 
 def tail_kernel(
-    count, batches, dq_ref, dg_ref, dkv_ref, w_ref, x_ref, gain_ref, dh1_ref, second_ref,
-    n1_ref, mixed_ref, low_ref, base_ref, ahead_ref, behind_ref,
+    count, batches, dq_ref, dg_ref, dkv_ref, w_ref, gain_ref, dh1_ref, second_ref,
+    low_ref, h1_ref, ahead_ref, behind_ref, n1_ref, x_hbm, mixed_hbm, mlp_hbm,
     out_all, tok_all, gains_ref, wout_own, din_ref,
     part_ref, tok_ref, got, wout_got, gain_own, gain_got, gain_mid, gain_heads,
     din_s, din_got, din_x, wout_s, wout_twin, wout_x,
     cat_ref, out_s, out_got, core_got, x_first, x_second, y_first, y_second, held, n1_s,
-    send_sem, recv_sem, local_sem,
+    x_ref, mixed_ref, mlp_ref, send_sem, recv_sem, local_sem,
 ):
     steps = count // 2
     rows, width = x_ref.shape
@@ -1023,12 +1023,23 @@
         cols = pl.ds(pl.multiple_of(at * tile, tile), tile)
         return pltpu.make_async_copy(n1_ref.at[:, cols], n1_s.at[slot], local_sem.at[2 + slot])
 
+    own_rows = pl.ds(pl.multiple_of(place * rows, rows), rows)
+    fetches = [
+        pltpu.make_async_copy(source.at[own_rows], target, local_sem.at[4 + index])
+        for index, (source, target) in enumerate(
+            ((mixed_hbm, mixed_ref), (mlp_hbm, mlp_ref), (x_hbm, x_ref))
+        )
+    ]
+    for copy in fetches:
+        copy.start()
     for at in range(2):
         normed_copy(at, at).start()
     last_sums = [go(ahead_ref, out_got.at[0], right), go(behind_ref, out_got.at[1], left)]
     swaps = scatter_swap(keys_of, core_got)
     cat_ref[:, pl.ds(0, size)] = dq_ref[...]
     cat_ref[:, pl.ds(size, size)] = dg_ref[...]
+    for copy in fetches:
+        copy.wait()
 
     @pl.loop(0, width // tile)
     def _(at):
@@ -1047,7 +1058,7 @@
     for copy in last_sums:
         copy.wait_recv()
     out_s[...] = (
-        base_ref[...] + out_got[0].astype(F32) + out_got[1].astype(F32)
+        h1_ref[...] + mlp_ref[...].astype(F32) + out_got[0].astype(F32) + out_got[1].astype(F32)
     ).astype(BF)
     keep_out = pltpu.make_async_copy(out_s, out_all.at[place], local_sem.at[0])
     keep_out.start()
@@ -1183,16 +1194,17 @@
 
 
 def tail(arrays, collective_id):
-    d_queries, _, d_keys, _, x_own, *_, mixed, _, _, _, _ = arrays
+    d_queries, tokens, mixed = arrays[0], arrays[-3], arrays[-2]
     count = lax.axis_size("head")
     batches = lax.axis_size("batch")
     steps = count // 2
-    rows, width = x_own.shape
+    rows, width = tokens.shape[0] // count, tokens.shape[1]
     others = batches // 2
     size, wide = mixed.shape[1] // count, width // batches
     tall, head_size = d_queries.shape
     depth = 3 * head_size
     vmem = pl.BlockSpec(memory_space=pltpu.VMEM)
+    hbm = pl.BlockSpec(memory_space=pl.ANY)
     whole = (count, rows, width)
     sems = pltpu.SemaphoreType.DMA((6 * count + 6 * batches,))
     gains = (2, width // batches)
@@ -1205,8 +1217,8 @@
             jax.ShapeDtypeStruct((size, wide), F32),
             jax.ShapeDtypeStruct((wide, depth), F32),
         ],
-        in_specs=[vmem] * 8 + [pl.BlockSpec(memory_space=pl.ANY)] + [vmem] * 5,
-        out_specs=[vmem] * 5,
+        in_specs=[vmem] * 11 + [hbm] * 4,
+        out_specs=[hbm] * 2 + [vmem] * 3,
         scratch_shapes=[
             pltpu.VMEM((count * rows, width), BF),
             pltpu.VMEM((rows, width), BF),
@@ -1232,18 +1244,53 @@
             pltpu.VMEM((tall // 2, head_size), BF),
             pltpu.VMEM((tall // 2, 2 * head_size), BF),
             pltpu.VMEM((2, tall, 256), BF),
+            pltpu.VMEM((rows, width), BF),
+            pltpu.VMEM((rows, mixed.shape[1]), BF),
+            pltpu.VMEM((rows, width), BF),
             sems,
             sems,
-            pltpu.SemaphoreType.DMA((4,)),
+            pltpu.SemaphoreType.DMA((7,)),
         ],
         compiler_params=pltpu.CompilerParams(
-            collective_id=collective_id, has_side_effects=True, vmem_limit_bytes=(36 << 20) + 6 * count * size * width
+            collective_id=collective_id, has_side_effects=True, vmem_limit_bytes=VMEM_LIMIT
         ),
         cost_estimate=pl.CostEstimate(
             flops=4 * count * rows * width * depth, bytes_accessed=400 << 20, transcendentals=0
         ),
         name="tail",
     )(*arrays)
+
+
+def finish_kernel(out_ref, tok_ref, gate_ref, up_ref, down_ref, *results):
+    for source, target in zip((out_ref, tok_ref, gate_ref, up_ref, down_ref), results):
+        value = source[...]
+        target[...] = value.reshape(target.shape).astype(target.dtype)
+
+
+def finish(output, d_tokens, d_mlp, d_down):
+    count, rows, width = output.shape
+    tall, hidden = d_mlp.shape[0], d_mlp.shape[1] // 2
+    down_rows, wide = d_down.shape
+    whole_in = pl.BlockSpec((1, rows, width), lambda i: (i, 0, 0))
+    whole_out = pl.BlockSpec((rows, width), lambda i: (i, 0))
+    gate = pl.BlockSpec((tall // count, hidden), lambda i: (i, 0))
+    up = pl.BlockSpec((tall // count, hidden), lambda i: (i, 1))
+    down = pl.BlockSpec((down_rows // count, wide), lambda i: (i, 0))
+    return pl.pallas_call(
+        finish_kernel,
+        grid=(count,),
+        out_shape=[
+            jax.ShapeDtypeStruct((count * rows, width), BF),
+            jax.ShapeDtypeStruct((count * rows, width), BF),
+            jax.ShapeDtypeStruct((tall, hidden), F32),
+            jax.ShapeDtypeStruct((tall, hidden), F32),
+            jax.ShapeDtypeStruct((down_rows, wide), F32),
+        ],
+        in_specs=[whole_in, whole_in, gate, up, down],
+        out_specs=[whole_out, whole_out, gate, gate, down],
+        compiler_params=pltpu.CompilerParams(vmem_limit_bytes=VMEM_LIMIT),
+        name="finish",
+    )(output, d_tokens, d_mlp, d_mlp, d_down)
 
 
 def local_call(kernel, scalars, arrays, outs, scratch, flops, name):
@@ -1369,7 +1416,6 @@
         tokens, mixed_all, out_grad, gain_two[None], out_full, mgate_full, mup_full, down_full, 3
     )
     hold = lax.optimization_barrier
-    mixed_own = lax.dynamic_slice_in_dim(mixed_all, me * chunk, chunk, 0)
     flow = flow_steps(mlp_part, going, coming)
     state = next(flow)
 
@@ -1390,20 +1436,14 @@
         state = flow.send(state)
     d_down = lax.psum_scatter(d_down, "batch", scatter_dimension=1, tiled=True)
     d_mlp = lax.psum_scatter(d_mlp, "batch", scatter_dimension=0, tiled=True)
-    inputs_own = lax.dynamic_slice_in_dim(tokens, me * chunk, chunk, 0)
-    base_own = resid_own + lax.dynamic_slice_in_dim(mlp_part, me * chunk, chunk, 0).astype(F32)
     output, d_tokens, d_gains, d_out, d_in = tail(
         (
-            d_queries, d_gate_logit, d_kv_all, w_in, inputs_own, gain_one[None], d_resid, d_gain_two,
-            normed_one, mixed_own, d_resid_low, base_own, *state,
+            d_queries, d_gate_logit, d_kv_all, w_in, gain_one[None], d_resid, d_gain_two,
+            d_resid_low, resid_own, *state, normed_one, tokens, mixed_all, mlp_part,
         ),
         5,
     )
-    d_tokens, d_mlp, d_down = hold((d_tokens, d_mlp, d_down))
-    d_mlp, d_down = d_mlp.astype(F32), d_down.astype(F32)
-    output = output.reshape(row_count, width)
-    d_tokens = d_tokens.reshape(row_count, width)
-    hidden_own = w_mlp_gate.shape[1]
+    output, d_tokens, d_mgate, d_mup, d_down = finish(output, d_tokens, d_mlp, d_down)
     return (
         output,
         d_tokens,
@@ -1414,8 +1454,8 @@
         d_in[:, head_size : 2 * head_size],
         d_out,
         d_gains[1],
-        d_mlp[:, :hidden_own],
-        d_mlp[:, hidden_own:],
+        d_mgate,
+        d_mup,
         d_down,
     )
 

time: 496 us -> 494 us (level)
  local copies, waits for them, and re-layouts: 22.5 us -> 11.9 us
  Pallas kernels: 448 us -> 458 us
    pallas_call x0 -> x1, Pallas kernels: none -> 11.8 us  [finish(): pl.pallas_call(finish_kernel, grid=(count,), out_shape=[jax.ShapeDtypeStr...]
    unnamed x32 -> x18, local copies, waits for them, and re-layouts: 13.4 us -> 5.41 us
  transfers between devices with their start and end apart: 5 -> 5, of which waited for: 0 -> 1; matrix products, arithmetic and copies ran while one was open for 2% -> 3% of each run, Pallas kernels for 58% -> 58%
where the time goes in v17:
time: 494 us; the launch traced here: 493 us
  Pallas kernels  458 us (93%)
  between operations  13.9 us (3%)
  local copies, waits for them, and re-layouts  11.9 us (2%)
  other arithmetic  6.24 us (1%)
    pallas_call x1, Pallas kernels, tail(): pl.pallas_call(functools.partial(tail_kernel, count, batches), out_shape=...  210 us
    pallas_call x1, Pallas kernels, mlp_back(): pl.pallas_call(functools.partial(mlp_kernel, count), out_shape=[shape(tot...  105 us
    pallas_call x1, Pallas kernels, spread(): pl.pallas_call(functools.partial(spread_kernel, count, batches, plans), o...  57.6 us
    pallas_call x1, Pallas kernels, entry(): pl.pallas_call(functools.partial(entry_kernel, count, batches), out_shape...  54.7 us
    pallas_call x2, Pallas kernels, local_call(): pl.pallas_call(kernel, out_shape=outs, in_specs=[smem] * len(scalars) + [...  18.9 us
    pallas_call x1, Pallas kernels, finish(): pl.pallas_call(finish_kernel, grid=(count,), out_shape=[jax.ShapeDtypeStr...  11.8 us
  transfers between devices with their start and end apart: 5, of which 1 were waited for; matrix products, arithmetic and copies ran while one was open for 3% of the time, Pallas kernels for 58%

profile of v17, /device:TPU:0, one launch (start us, length us, event | category | flops | bytes accessed | tf_op | source)
XLA Modules:
  0.0 492.7 jit_solution(537969708039306064)
XLA Ops:
  7.2 1.0 copy.35
  8.2 1.0 copy.36
  9.2 1.3 maximum_convert_fusion.gain_ref
  10.5 1.8 pad_maximum_fusion.w_ref
  12.3 54.7 %entry.1 = (bf16[1280,2048]{1,0:T(8,128)(2,1)}, bf16[1280,128]{1,0:T(8,128)(2,1)}, f32[1280,128]{1,0:T(8,128)}, bf16[5120,256]{1,0:T(8,128)(2,1)}, bf16[2048,512...) custom-call(bf16[1280,2048]{1,0:T(8,128)(2,1)} %x_hbm.3, ...), custom_call_target="tpu_custom_call" | custom-call | tf_op jit(solution)/shard_map/entry/pallas_call | solution.py:756
  67.1 0.8 lt.27
  68.7 0.7 reshape.44
  69.4 0.6 copy.40
  70.1 7.6 %attend.1 = (f32[1280,128]{1,0:T(8,128)}, bf16[1280,128]{1,0:T(8,128)(2,1)}, f32[1,1280]{1,0:T(1,128)}) custom-call(s32[1280]{0:T(1024)} %copy-done.2, s32[1]{0:T(128)} %bitcast.3.base_sm, bf16[1280,128]{1,0:T(8,128)(2,1)} %get-tuple-element.52.q_ref, bf16[5120,256]{1,0:T(8,128)(2,1)} %get-tuple-element.53.kv_ref, s32[1,1280]{1,0:T(1,128)} %broadcast_in_dim.22.start_ref, ...), custom_call_target="tpu_custom_call" | custom-call | flops 3355443200 | bytes 8388608 | tf_op jit(solution)/shard_map/attend/pallas_call | solution.py:1299
  77.7 57.6 %spread_2.1 = (bf16[1280,1024]{1,0:T(8,128)(2,1)}, bf16[768,2048]{1,0:T(8,128)(2,1)}, bf16[2048,768]{1,0:T(8,128)(2,1)}) custom-call(bf16[1280,128]{1,0:T(8,128)(2,1)} %get-tuple-element.56.refs_0_, bf16[768,512]{1,0:T(8,128)(2,1)} %refs_1_.1, bf16[512,768]{1,0:T(8,128)(2,1)} %refs_2_.1), custom_call_target="tpu_custom_call" | custom-call | tf_op jit(solution)/shard_map/spread_2/pallas_call | solution.py:176
  135.4 105.0 %mlp_back.1 = (bf16[1280,2048]{1,0:T(8,128)(2,1)}, bf16[2048,1536]{1,0:T(8,128)(2,1)}, bf16[768,2048]{1,0:T(8,128)(2,1)}, f32[160,2048]{1,0:T(8,128)}, f32[160,2...) custom-call(bf16[1280,2048]{1,0:T(8,128)(2,1)} %x_hbm.3, ...), custom_call_target="tpu_custom_call" | custom-call | flops 41607495680 | bytes 41943040 | tf_op jit(solution)/shard_map/mlp_back/pallas_call | solution.py:540
  240.4 0.7 reduce-scatter.3.cloned.1.call-update
  241.7 1.0 collective-permute-start
  242.7 1.0 collective-permute-start.1
  243.8 11.3 %attend_back.1 = (bf16[1280,128]{1,0:T(8,128)(2,1)}, bf16[1280,128]{1,0:T(8,128)(2,1)}, bf16[5120,256]{1,0:T(8,128)(2,1)}) custom-call(s32[1280]{0:T(1024)} %copy-done.2, s32[1]{0:T(128)} %bitcast.3.base_sm, bf16[1280,128]{1,0:T(8,128)(2,1)} %get-tuple-element.52.q_ref, bf16[5120,256]{1,0:T(8,128)(2,1)} %get-tuple-element.53.kv_ref, ...), custom_call_target="tpu_custom_call" | custom-call | flops 8388608000 | bytes 8388608 | tf_op jit(solution)/shard_map/attend_back/pallas_call | solution.py:1299
  255.2 2.9 add_convert_fusion
  258.0 209.7 %tail.1 = (bf16[8,160,2048]{2,1,0:T(8,128)(2,1)}, bf16[8,160,2048]{2,1,0:T(8,128)(2,1)}, f32[2,512]{1,0:T(2,128)}, f32[128,512]{1,0:T(8,128)}, f32[512,384]{1,0:T(8,128)}) custom-call(bf16[1280,128]{1,0:T(8,128)(2,1)} %get-tuple-element.66.dq_ref, bf16[1280,128]{1,0:T(8,128)(2,1)} %get-tuple-element.67.dg_ref, bf16[5120,256]{1,0:T(8,128)(2,1)} %get-tuple-element.68.dkv_ref, ...), custom_call_target="tpu_custom_call" | custom-call | flops 4026531840 | bytes 419430400 | tf_op jit(solution)/shard_map/tail/pallas_call | solution.py:1211
  467.8 1.2 fusion.1
  468.9 0.8 copy.38
  469.7 0.8 copy.39
  470.5 1.3 fusion.2
  471.8 1.9 fusion
  473.7 11.8 %finish.1 = (bf16[1280,2048]{1,0:T(8,128)(2,1)}, bf16[1280,2048]{1,0:T(8,128)(2,1)}, f32[512,768]{1,0:T(8,128)}, f32[512,768]{1,0:T(8,128)}, f32[768,512]{1,0:T(8,128)}) custom-call(bf16[8,160,2048]{2,1,0:T(8,128)(2,1)} %get-tuple-element.78.out_ref, bf16[8,160,2048]{2,1,0:T(8,128)(2,1)} %get-tuple-element.79.tok_ref, ...), custom_call_target="tpu_custom_call" | custom-call | tf_op jit(solution)/shard_map/finish/pallas_call | solution.py:1279
  485.5 0.7 copy.45
  (26 shorter events, 1.8 us)
Async XLA Ops:
  7.2 128.2 %all-gather.2.cloned.1.call-start = ((), (), s32[]{:S(2)}) async-start(), calls=%async_computation.2 | async-start | bytes 3932160 | tf_op jit(solution)/shard_map/all_gather | solution.py:1389
  12.3 55.7 %copy-start.1 = (s32[1280]{0:T(1024)S(1)}, s32[1280]{0:T(1024)}, u32[]{:S(2)}) copy-start(s32[1280]{0:T(1024)} %param.14) | copy-start | bytes 15364
  67.0 406.7 %reduce-scatter.5.cloned.1.call-start = ((), (), s32[]{:S(2)}) async-start(), calls=%async_computation.4 | async-start | bytes 3932160 | tf_op jit(solution)/shard_map/reduce_scatter | solution.py:1437
  68.1 2.0 copy-start.2
  240.3 233.4 %reduce-scatter.3.cloned.1.call-start = ((), (), s32[]{:S(2)}) async-start(), calls=%async_computation.3 | async-start | bytes 7864320 | tf_op jit(solution)/shard_map/reduce_scatter | solution.py:1438
  240.4 1.3 copy-start.4
  240.4 2.3 copy-start.3
  241.7 13.3 %collective-permute-start = (bf16[160,2048]{1,0:T(8,128)(2,1)S(1)}, bf16[160,2048]{1,0:T(8,128)(2,1)S(1)}, u32[]{:S(2)}, u32[]{:S(2)}) collective-permute-start(bf16[160,2048]{1,0:T(8,128)(2,1)S(1)} %copy-done.4), channel_id=1, source_target_pairs={{0,2},{2,4},{4,6},{6,7},{7,5},{5,3},{3,1},{1,0},{8,10},{10,12},{12... | collective-permute-start | bytes 1966088 | tf_op jit(solution)/shard_map/ppermute | solution.py:1333
  242.7 12.4 %collective-permute-start.1 = (bf16[160,2048]{1,0:T(8,128)(2,1)S(1)}, bf16[160,2048]{1,0:T(8,128)(2,1)S(1)}, u32[]{:S(2)}, u32[]{:S(2)}) collective-permute-start(bf16[160,2048]{1,0:T(8,128)(2,1)S(1)} %copy-done.3), channel_id=1, source_target_pairs={{0,1},{2,0},{4,2},{6,4},{7,6},{5,7},{3,5},{1,3},{8,9},{10,8},{12,1... | collective-permute-start | bytes 1966088 | tf_op jit(solution)/shard_map/ppermute | solution.py:1334
  473.7 11.8 %copy-start = (f32[128,512]{1,0:T(8,128)S(1)}, f32[128,512]{1,0:T(8,128)}, u32[]{:S(2)}) copy-start(f32[128,512]{1,0:T(8,128)} %get-tuple-element.155) | copy-start | bytes 786436
Sparse Core Ops, SparseCore 0:
  67.1 28.4 all-gather.1
  240.5 37.1 reduce-scatter.4
  280.4 58.3 reduce-scatter.2

commit v18 on v17

--- a/solution.py
+++ b/solution.py
@@ -347,21 +347,14 @@
             part = (cols_inner(d_gate, gate_w[cols]) + cols_inner(d_up, up_w[cols])).astype(BF)
             right_part[half, :, cols] = part[:rows]
             left_part[half, :, cols] = part[rows:]
-            mlp_s[slot, :, cols] = matmul(hid, down_w[:, cols]).astype(BF)
-
-        for copy in stores(group, slot):
-            copy.start()
 
         @pl.when(group == 0)
         def _():
-            mlp_far[...] = mlp_s[slot, pl.ds(0, rows)]
             for copy in first_copies():
                 copy.start()
 
         @pl.when(group == 1)
         def _():
-            mlp_next[0] = mlp_s[slot, pl.ds(0, rows)]
-            mlp_next[1] = mlp_s[slot, pl.ds(rows, rows)]
             one, two = first_copies()
             one.wait_recv()
             right_got[0, :, ahead] = add_low(right_part[1, :, ahead], right_got[0, :, ahead])
@@ -370,11 +363,6 @@
             left_got[0, :, behind] = add_low(left_part[1, :, behind], left_got[0, :, behind])
             left_got[0, :, ahead] = left_part[1, :, ahead]
 
-        @pl.when(group == 2)
-        def _():
-            ahead_ref[...] = mlp_s[slot, pl.ds(0, rows)]
-            behind_ref[...] = mlp_s[slot, pl.ds(rows, rows)]
-
         @pl.when(group >= 2)
         def _():
             one, two = later_copies(group - 1)
@@ -387,6 +375,28 @@
         def _():
             for copy in later_copies(group):
                 copy.start()
+
+        @pl.loop(0, width // broad)
+        def _(at):
+            cols = tile_of(at, broad)
+            mlp_s[slot, :, cols] = matmul(hid, down_w[:, cols]).astype(BF)
+
+        for copy in stores(group, slot):
+            copy.start()
+
+        @pl.when(group == 0)
+        def _():
+            mlp_far[...] = mlp_s[slot, pl.ds(0, rows)]
+
+        @pl.when(group == 1)
+        def _():
+            mlp_next[0] = mlp_s[slot, pl.ds(0, rows)]
+            mlp_next[1] = mlp_s[slot, pl.ds(rows, rows)]
+
+        @pl.when(group == 2)
+        def _():
+            ahead_ref[...] = mlp_s[slot, pl.ds(0, rows)]
+            behind_ref[...] = mlp_s[slot, pl.ds(rows, rows)]
 
     far_copies = [
         passing(mlp_far.at[:, ahead], mlp_got.at[0, :, ahead], far_sems, 0, right),
@@ -776,7 +786,7 @@
 
 
 KEY_BLOCK = 512
-QUERY_BLOCK = 256
+QUERY_BLOCK = 640
 
 
 def key_range(start_ref, base, query_block):
@@ -1106,8 +1116,8 @@
     dins = scatter_swap(din_view, din_got)
     for step in range(1, steps):
         sums = reduce(part_ref, got, step, sums)
-        if step + 1 < steps:
-            outs = gather(out_s, out_all, step + 1, outs)
+        if 2 <= step < steps - 1:
+            outs = gather(out_s, out_all, step, outs)
         if step == 1:
             wouts = scatter_cross(wout_view, wout_twin, wout_x, wouts)
             dins = scatter_cross(din_view, din_got, din_x, dins)
@@ -1147,6 +1157,7 @@
     keep_tok = pltpu.make_async_copy(tok_ref, tok_all.at[place], local_sem.at[1])
     keep_tok.start()
     toks = gather(tok_ref, tok_all, 0, None)
+    outs = gather(out_s, out_all, steps - 1, outs)
     wout_part = wout_twin.at[across]
     scatter_end(wout_twin, wout_x, wouts, wout_part)
     wsums = reduce(wout_part, wout_got, 0, None)
@@ -1261,36 +1272,58 @@
     )(*arrays)
 
 
-def finish_kernel(out_ref, tok_ref, gate_ref, up_ref, down_ref, *results):
-    for source, target in zip((out_ref, tok_ref, gate_ref, up_ref, down_ref), results):
-        value = source[...]
-        target[...] = value.reshape(target.shape).astype(target.dtype)
-
-
-def finish(output, d_tokens, d_mlp, d_down):
+def finish_kernel(out_ref, tok_ref, mgate_ref, mup_ref, down_ref, in_ref, gains_ref, *results):
+    for source, target in zip((out_ref, tok_ref, mgate_ref, mup_ref, down_ref), results):
+        target[...] = source[...].reshape(target.shape).astype(target.dtype)
+    query, gate, key, value, first, second = results[5:]
+    size, half = query.shape[1], key.shape[1]
+    query[...] = in_ref[:, :size]
+    gate[...] = in_ref[:, size : 2 * size]
+    key[...] = in_ref[:, 2 * size : 2 * size + half]
+    value[...] = in_ref[:, 2 * size + half :]
+    first[...] = gains_ref[pl.ds(0, 1)]
+    second[...] = gains_ref[pl.ds(1, 1)]
+
+
+def finish(output, d_tokens, d_mlp, d_down, d_in, gains):
     count, rows, width = output.shape
     tall, hidden = d_mlp.shape[0], d_mlp.shape[1] // 2
     down_rows, wide = d_down.shape
-    whole_in = pl.BlockSpec((1, rows, width), lambda i: (i, 0, 0))
-    whole_out = pl.BlockSpec((rows, width), lambda i: (i, 0))
-    gate = pl.BlockSpec((tall // count, hidden), lambda i: (i, 0))
-    up = pl.BlockSpec((tall // count, hidden), lambda i: (i, 1))
-    down = pl.BlockSpec((down_rows // count, wide), lambda i: (i, 0))
+    depth = d_in.shape[1]
+    size = depth // 3
+
+    def strip(high, across, at=0):
+        return pl.BlockSpec((high // count, across), lambda i: (i, at))
+
+    def held(*shape):
+        return pl.BlockSpec(shape, lambda i: (0, 0))
+
+    def shape(*extent, dtype=F32):
+        return jax.ShapeDtypeStruct(extent, dtype)
+
+    whole = pl.BlockSpec((1, rows, width), lambda i: (i, 0, 0))
     return pl.pallas_call(
         finish_kernel,
         grid=(count,),
         out_shape=[
-            jax.ShapeDtypeStruct((count * rows, width), BF),
-            jax.ShapeDtypeStruct((count * rows, width), BF),
-            jax.ShapeDtypeStruct((tall, hidden), F32),
-            jax.ShapeDtypeStruct((tall, hidden), F32),
-            jax.ShapeDtypeStruct((down_rows, wide), F32),
+            shape(count * rows, width, dtype=BF), shape(count * rows, width, dtype=BF),
+            shape(tall, hidden), shape(tall, hidden), shape(down_rows, wide),
+            shape(tall, size), shape(tall, size), shape(tall, size // 2), shape(tall, size // 2),
+            shape(1, wide), shape(1, wide),
         ],
-        in_specs=[whole_in, whole_in, gate, up, down],
-        out_specs=[whole_out, whole_out, gate, gate, down],
+        in_specs=[
+            whole, whole, strip(tall, hidden), strip(tall, hidden, 1), strip(down_rows, wide),
+            strip(tall, depth), held(2, wide),
+        ],
+        out_specs=[
+            strip(count * rows, width), strip(count * rows, width),
+            strip(tall, hidden), strip(tall, hidden), strip(down_rows, wide),
+            strip(tall, size), strip(tall, size), strip(tall, size // 2), strip(tall, size // 2),
+            held(1, wide), held(1, wide),
+        ],
         compiler_params=pltpu.CompilerParams(vmem_limit_bytes=VMEM_LIMIT),
         name="finish",
-    )(output, d_tokens, d_mlp, d_mlp, d_down)
+    )(output, d_tokens, d_mlp, d_mlp, d_down, d_in, gains)
 
 
 def local_call(kernel, scalars, arrays, outs, scratch, flops, name):
@@ -1443,17 +1476,19 @@
         ),
         5,
     )
-    output, d_tokens, d_mgate, d_mup, d_down = finish(output, d_tokens, d_mlp, d_down)
+    (
+        output, d_tokens, d_mgate, d_mup, d_down, d_query, d_gate, d_key, d_value, d_one, d_two,
+    ) = finish(output, d_tokens, d_mlp, d_down, d_in, d_gains)
     return (
         output,
         d_tokens,
-        d_gains[0],
-        d_in[:, :head_size],
-        d_in[:, 2 * head_size : 2 * head_size + half],
-        d_in[:, 2 * head_size + half :],
-        d_in[:, head_size : 2 * head_size],
+        d_one.reshape(-1),
+        d_query,
+        d_key,
+        d_value,
+        d_gate,
         d_out,
-        d_gains[1],
+        d_two.reshape(-1),
         d_mgate,
         d_mup,
         d_down,

time: 494 us -> 489 us (0.990)
  transfers between devices with their start and end apart: 5 -> 5, of which waited for: 1 -> 0; matrix products, arithmetic and copies ran while one was open for 3% -> 1% of each run, Pallas kernels for 58% -> 58%
where the time goes in v18:
time: 489 us
  Pallas kernels  456 us (93%)
  between operations  13.9 us (3%)
  local copies, waits for them, and re-layouts  9.4 us (2%)
  other arithmetic  6.58 us (1%)
    pallas_call x1, Pallas kernels, tail(): pl.pallas_call(functools.partial(tail_kernel, count, batches), out_shape=...  209 us
    pallas_call x1, Pallas kernels, mlp_back(): pl.pallas_call(functools.partial(mlp_kernel, count), out_shape=[shape(tot...  104 us
    pallas_call x1, Pallas kernels, spread(): pl.pallas_call(functools.partial(spread_kernel, count, batches, plans), o...  55.3 us
    pallas_call x1, Pallas kernels, entry(): pl.pallas_call(functools.partial(entry_kernel, count, batches), out_shape...  54.7 us
    pallas_call x2, Pallas kernels, local_call(): pl.pallas_call(kernel, out_shape=outs, in_specs=[smem] * len(scalars) + [...  20.8 us
    pallas_call x1, Pallas kernels, finish(): pl.pallas_call(finish_kernel, grid=(count,), out_shape=[shape(count * row...  12.2 us
  transfers between devices with their start and end apart: 5, of which 0 were waited for; matrix products, arithmetic and copies ran while one was open for 1% of the time, Pallas kernels for 58%

profile of v18, /device:TPU:0, one launch (start us, length us, event | category | flops | bytes accessed | tf_op | source)
XLA Modules:
  0.0 489.0 jit_solution(14552984578023249447)
XLA Ops:
  7.2 1.0 copy.35
  8.2 1.0 copy.36
  9.2 1.3 maximum_convert_fusion.gain_ref
  10.5 1.8 pad_maximum_fusion.w_ref
  12.3 54.7 %entry.1 = (bf16[1280,2048]{1,0:T(8,128)(2,1)}, bf16[1280,128]{1,0:T(8,128)(2,1)}, f32[1280,128]{1,0:T(8,128)}, bf16[5120,256]{1,0:T(8,128)(2,1)}, bf16[2048,512...) custom-call(bf16[1280,2048]{1,0:T(8,128)(2,1)} %x_hbm.3, ...), custom_call_target="tpu_custom_call" | custom-call | tf_op jit(solution)/shard_map/entry/pallas_call | solution.py:766
  67.1 0.8 lt.27
  67.8 0.2 convert_reduce_fusion
  68.1 0.6 broadcast_in_dim.22.start_ref
  68.7 0.7 reshape.50
  69.4 0.6 copy.40
  70.1 8.2 %attend.1 = (f32[1280,128]{1,0:T(8,128)}, bf16[1280,128]{1,0:T(8,128)(2,1)}, f32[1,1280]{1,0:T(1,128)}) custom-call(s32[1280]{0:T(1024)} %copy-done.2, s32[1]{0:T(128)} %bitcast.3.base_sm, bf16[1280,128]{1,0:T(8,128)(2,1)} %get-tuple-element.58.q_ref, bf16[5120,256]{1,0:T(8,128)(2,1)} %get-tuple-element.59.kv_ref, s32[1,1280]{1,0:T(1,128)} %broadcast_in_dim.22.start_ref, ...), custom_call_target="tpu_custom_call" | custom-call | flops 3355443200 | bytes 8388608 | tf_op jit(solution)/shard_map/attend/pallas_call | solution.py:1332
  78.3 55.3 %spread_2.1 = (bf16[1280,1024]{1,0:T(8,128)(2,1)}, bf16[768,2048]{1,0:T(8,128)(2,1)}, bf16[2048,768]{1,0:T(8,128)(2,1)}) custom-call(bf16[1280,128]{1,0:T(8,128)(2,1)} %get-tuple-element.62.refs_0_, bf16[768,512]{1,0:T(8,128)(2,1)} %refs_1_.1, bf16[512,768]{1,0:T(8,128)(2,1)} %refs_2_.1), custom_call_target="tpu_custom_call" | custom-call | tf_op jit(solution)/shard_map/spread_2/pallas_call | solution.py:176
  133.6 104.5 %mlp_back.1 = (bf16[1280,2048]{1,0:T(8,128)(2,1)}, bf16[2048,1536]{1,0:T(8,128)(2,1)}, bf16[768,2048]{1,0:T(8,128)(2,1)}, f32[160,2048]{1,0:T(8,128)}, f32[160,2...) custom-call(bf16[1280,2048]{1,0:T(8,128)(2,1)} %x_hbm.3, ...), custom_call_target="tpu_custom_call" | custom-call | flops 41607495680 | bytes 41943040 | tf_op jit(solution)/shard_map/mlp_back/pallas_call | solution.py:550
  238.2 0.7 reduce-scatter.3.cloned.1.call-update
  238.9 0.6 copy.41
  239.6 1.0 collective-permute-start
  240.6 1.0 collective-permute-start.1
  241.6 12.5 %attend_back.1 = (bf16[1280,128]{1,0:T(8,128)(2,1)}, bf16[1280,128]{1,0:T(8,128)(2,1)}, bf16[5120,256]{1,0:T(8,128)(2,1)}) custom-call(s32[1280]{0:T(1024)} %copy-done.2, s32[1]{0:T(128)} %bitcast.3.base_sm, bf16[1280,128]{1,0:T(8,128)(2,1)} %get-tuple-element.58.q_ref, bf16[5120,256]{1,0:T(8,128)(2,1)} %get-tuple-element.59.kv_ref, ...), custom_call_target="tpu_custom_call" | custom-call | flops 8388608000 | bytes 8388608 | tf_op jit(solution)/shard_map/attend_back/pallas_call | solution.py:1332
  254.1 3.2 add_convert_fusion
  257.3 208.6 %tail.1 = (bf16[8,160,2048]{2,1,0:T(8,128)(2,1)}, bf16[8,160,2048]{2,1,0:T(8,128)(2,1)}, f32[2,512]{1,0:T(2,128)}, f32[128,512]{1,0:T(8,128)}, f32[512,384]{1,0:T(8,128)}) custom-call(bf16[1280,128]{1,0:T(8,128)(2,1)} %get-tuple-element.72.dq_ref, bf16[1280,128]{1,0:T(8,128)(2,1)} %get-tuple-element.73.dg_ref, bf16[5120,256]{1,0:T(8,128)(2,1)} %get-tuple-element.74.dkv_ref, ...), custom_call_target="tpu_custom_call" | custom-call | flops 4026531840 | bytes 419430400 | tf_op jit(solution)/shard_map/tail/pallas_call | solution.py:1222
  466.1 12.2 %finish.1 = (bf16[1280,2048]{1,0:T(8,128)(2,1)}, bf16[1280,2048]{1,0:T(8,128)(2,1)}, f32[512,768]{1,0:T(8,128)}, f32[512,768]{1,0:T(8,128)}, f32[768,512]{1,0:T(...) custom-call(bf16[8,160,2048]{2,1,0:T(8,128)(2,1)} %get-tuple-element, ...), custom_call_target="tpu_custom_call" | custom-call | tf_op jit(solution)/shard_map/finish/pallas_call | solution.py:1305
  478.3 1.7 copy.38
  480.0 1.7 copy.39
  481.7 0.7 copy.45
  (23 shorter events, 0.3 us)
Async XLA Ops:
  7.2 126.4 %all-gather.2.cloned.1.call-start = ((), (), s32[]{:S(2)}) async-start(), calls=%async_computation.2 | async-start | bytes 3932160 | tf_op jit(solution)/shard_map/all_gather | solution.py:1422
  12.3 55.7 %copy-start.1 = (s32[1280]{0:T(1024)S(1)}, s32[1280]{0:T(1024)}, u32[]{:S(2)}) copy-start(s32[1280]{0:T(1024)} %param.14) | copy-start | bytes 15364
  67.0 399.0 %reduce-scatter.5.cloned.1.call-start = ((), (), s32[]{:S(2)}) async-start(), calls=%async_computation.4 | async-start | bytes 3932160 | tf_op jit(solution)/shard_map/reduce_scatter | solution.py:1470
  68.1 2.0 copy-start.2
  238.2 227.9 %reduce-scatter.3.cloned.1.call-start = ((), (), s32[]{:S(2)}) async-start(), calls=%async_computation.3 | async-start | bytes 7864320 | tf_op jit(solution)/shard_map/reduce_scatter | solution.py:1471
  238.2 1.3 copy-start.4
  238.2 2.3 copy-start.3
  239.6 14.6 %collective-permute-start = (bf16[160,2048]{1,0:T(8,128)(2,1)S(1)}, bf16[160,2048]{1,0:T(8,128)(2,1)S(1)}, u32[]{:S(2)}, u32[]{:S(2)}) collective-permute-start(bf16[160,2048]{1,0:T(8,128)(2,1)S(1)} %copy-done.4), channel_id=1, source_target_pairs={{0,2},{2,4},{4,6},{6,7},{7,5},{5,3},{3,1},{1,0},{8,10},{10,12},{12... | collective-permute-start | bytes 1966088 | tf_op jit(solution)/shard_map/ppermute | solution.py:1366
  240.6 13.6 %collective-permute-start.1 = (bf16[160,2048]{1,0:T(8,128)(2,1)S(1)}, bf16[160,2048]{1,0:T(8,128)(2,1)S(1)}, u32[]{:S(2)}, u32[]{:S(2)}) collective-permute-start(bf16[160,2048]{1,0:T(8,128)(2,1)S(1)} %copy-done.3), channel_id=1, source_target_pairs={{0,1},{2,0},{4,2},{6,4},{7,6},{5,7},{3,5},{1,3},{8,9},{10,8},{12,1... | collective-permute-start | bytes 1966088 | tf_op jit(solution)/shard_map/ppermute | solution.py:1367
  466.1 15.7 %copy-start = (f32[128,512]{1,0:T(8,128)S(1)}, f32[128,512]{1,0:T(8,128)}, u32[]{:S(2)}) copy-start(f32[128,512]{1,0:T(8,128)} %get-tuple-element.161) | copy-start | bytes 786436
Sparse Core Ops, SparseCore 0:
  67.1 28.4 all-gather.1
  238.3 36.8 reduce-scatter.4
  277.9 58.3 reduce-scatter.2

commit v19 on v18

--- a/solution.py
+++ b/solution.py
@@ -191,7 +191,7 @@
 
 
 def mlp_kernel(
-    count, x_hbm, a_hbm, dy_hbm, gain_ref, out_hbm, gate_hbm, up_hbm, down_hbm,
+    count, x_hbm, a_hbm, dy_hbm, gain_ref, out_hbm, gate_hbm, up_hbm, top_hbm, low_hbm,
     mlp_hbm, dmlp_hbm, ddown_hbm, h1_ref, dh1_ref, low_ref, dgain_ref, da_ref, ahead_ref, behind_ref,
     x_s, a_s, mlp_s, h1_s, dy_all, n2_all, hid_all, grad_all, dmlp_s, ddown_s, da_part,
     mlp_far, mlp_next, mlp_got, right_part, left_part, right_got, left_got,
@@ -202,10 +202,14 @@
     rows = x_hbm.shape[0] // count
     width = x_hbm.shape[1]
     hidden = gate_w.shape[1]
+    middle = hidden // 2
     weights = [
         pltpu.make_async_copy(source, target, weight_sem.at[index])
         for index, (source, target) in enumerate(
-            ((out_hbm, out_w), (gate_hbm, gate_w), (up_hbm, up_w), (down_hbm, down_w))
+            (
+                (out_hbm, out_w), (gate_hbm, gate_w), (up_hbm, up_w),
+                (top_hbm, down_w.at[pl.ds(0, middle)]), (low_hbm, down_w.at[pl.ds(middle, middle)]),
+            )
         )
     ]
     side = width // 2
@@ -529,7 +533,7 @@
         ddown_copy(down_tiles - 2 + at, (down_tiles + at) % 2).wait()
 
 
-def mlp_back(tokens, mixed, dy, gain, out_w, gate_w, up_w, down_w, collective_id):
+def mlp_back(tokens, mixed, dy, gain, out_w, gate_w, up_w, down_top, down_low, collective_id):
     count = lax.axis_size("head")
     total, width = tokens.shape
     hidden = gate_w.shape[1]
@@ -554,7 +558,7 @@
             shape(rows, width, dtype=F32), shape(rows, width, dtype=F32), shape(rows, width),
             shape(1, width, dtype=F32), shape(total, size), shape(rows, width), shape(rows, width),
         ],
-        in_specs=[hbm] * 3 + [vmem] + [hbm] * 4,
+        in_specs=[hbm] * 3 + [vmem] + [hbm] * 5,
         out_specs=[hbm] * 3 + [vmem] * 7,
         scratch_shapes=[
             slots(2, 2 * rows, width), slots(2, 2 * rows, mixed.shape[1]), slots(2, 2 * rows, width),
@@ -565,8 +569,9 @@
             pltpu.VMEM((rows, width), BF), slots(2, rows, width), slots(4, rows, width),
             slots(2, rows, width), slots(2, rows, width),
             slots(steps, rows, width), slots(steps, rows, width),
-            *[pltpu.VMEM(weight.shape, BF) for weight in (out_w, gate_w, up_w, down_w)],
-            dma((2, 6)), dma((2, 2)), dma((4,)), dma((4,)), dma((count,)), dma((count,)),
+            *[pltpu.VMEM(weight.shape, BF) for weight in (out_w, gate_w, up_w)],
+            pltpu.VMEM((hidden, width), BF),
+            dma((2, 6)), dma((2, 2)), dma((4,)), dma((5,)), dma((count,)), dma((count,)),
             dma((count,)), dma((count,)), dma((4,)), dma((4,)),
         ],
         compiler_params=pltpu.CompilerParams(
@@ -574,13 +579,13 @@
         ),
         cost_estimate=pl.CostEstimate(flops=flops, bytes_accessed=40 << 20, transcendentals=0),
         name="mlp_back",
-    )(tokens, mixed, dy, gain, out_w, gate_w, up_w, down_w)
+    )(tokens, mixed, dy, gain, out_w, gate_w, up_w, down_top, down_low)
 
 
 def entry_kernel(
-    count, batches, x_ref, w_ref, out_ref, gain_ref, seg_ref,
-    n1_ref, q_ref, logit_ref, kv_ref, w_all, out_all, gain_all, seg_all,
-    send_sem, recv_sem, local_sem,
+    count, batches, x_ref, w_ref, out_ref, gain_ref, seg_ref, down_ref,
+    n1_hbm, q_ref, logit_ref, kv_ref, w_all, out_all, gain_all, seg_all, down_all,
+    x_s, n1_ref, send_sem, recv_sem, local_sem, x_sem, n1_sem,
 ):
     steps = count // 2
     others = batches // 2
@@ -588,6 +593,18 @@
     depth = w_ref.shape[0]
     size, wide = out_ref.shape
     block = 256
+    blocks = rows // block
+
+    def x_copy(at):
+        here = pl.ds(pl.multiple_of(at * block, block), block)
+        return pltpu.make_async_copy(x_ref.at[here], x_s.at[here], x_sem.at[at])
+
+    def n1_copy(at):
+        here = pl.ds(pl.multiple_of(at * block, block), block)
+        return pltpu.make_async_copy(n1_ref.at[here], n1_hbm.at[here], n1_sem.at[at])
+
+    for at in range(blocks):
+        x_copy(at).start()
     place, right, left = ring_setup(count)
     head = lax.axis_index("head")
     batch = lax.axis_index("batch")
@@ -676,9 +693,10 @@
 
     def normalize(at):
         here = part(at, block)
+        x_copy(at).wait()
 
         def squares(tile, total):
-            values = x_ref[here, part(tile, 256)].astype(F32)
+            values = x_s[here, part(tile, 256)].astype(F32)
             return total + jnp.sum(values * values, axis=1, keepdims=True)
 
         total = lax.fori_loop(0, width // 256, squares, jnp.zeros((block, 1), F32))
@@ -688,10 +706,11 @@
         def _(owner):
             for tile in range(depth // 128):
                 cols = pl.ds(pl.multiple_of(owner * depth + tile * 128, 128), 128)
-                values = x_ref[here, cols].astype(F32) * scale
+                values = x_s[here, cols].astype(F32) * scale
                 n1_ref[here, cols] = (values * gain_all[owner, pl.ds(tile, 1)]).astype(BF)
 
-    blocks = rows // block
+        n1_copy(at).start()
+
     middle = blocks // 2
 
     @pl.loop(0, middle)
@@ -701,6 +720,12 @@
     from_mate.wait_recv()
     mate_out, mate_twin = both(mate_view, mate_view(batch))
     ring(0)
+
+    def down_view(at):
+        return down_all.at[:, part(at, down_ref.shape[1])]
+
+    down_out, down_twin = both(down_view, down_ref)
+    stay(down_ref, down_view(batch))
 
     @pl.loop(middle, blocks)
     def _(at):
@@ -740,6 +765,7 @@
 
     for step in range(2, steps):
         ring(step)
+    down_passed = pass_on(down_view, down_out)
     kv_passed = pass_on(kv_view, kv_out)
     for pair in flows:
         for copy in pair:
@@ -748,19 +774,22 @@
     for hop in range(others):
         there = out_all.at[:, part(spots[hop] * 2 + core, wide)]
         swaps.append(go(there, there, twin))
-    for copy in (*kv_twin, *kv_passed, *swaps):
+    for copy in (*kv_twin, *kv_passed, *swaps, *down_twin, *down_passed):
         copy.wait_recv()
     for copy in copies:
         copy.wait_send()
-
-
-def entry(tokens, w_shard, w_out, gains, segments, collective_id):
+    for at in range(blocks):
+        n1_copy(at).wait()
+
+
+def entry(tokens, w_shard, w_out, gains, segments, w_down, collective_id):
     count = lax.axis_size("head")
     batches = lax.axis_size("batch")
     others = batches // 2
     rows, width = tokens.shape
     size, wide = w_out.shape
     vmem = pl.BlockSpec(memory_space=pltpu.VMEM)
+    hbm = pl.BlockSpec(memory_space=pl.ANY)
     slots = 6 * batches + others * (count + 3)
     sems = pltpu.SemaphoreType.DMA((slots,))
     return pl.pallas_call(
@@ -774,15 +803,20 @@
             jax.ShapeDtypeStruct((count * size, batches * wide), BF),
             jax.ShapeDtypeStruct((batches, *gains.shape), F32),
             jax.ShapeDtypeStruct((batches, *segments.shape), jnp.int32),
+            jax.ShapeDtypeStruct((w_down.shape[0], batches * w_down.shape[1]), BF),
         ],
-        in_specs=[vmem] * 5,
-        out_specs=[vmem] * 8,
-        scratch_shapes=[sems, sems, pltpu.SemaphoreType.DMA((5,))],
+        in_specs=[hbm] + [vmem] * 5,
+        out_specs=[hbm] + [vmem] * 4 + [hbm] + [vmem] * 2 + [hbm],
+        scratch_shapes=[
+            pltpu.VMEM((rows, width), BF), pltpu.VMEM((rows, width), BF),
+            sems, sems, pltpu.SemaphoreType.DMA((5,)),
+            pltpu.SemaphoreType.DMA((rows // 256,)), pltpu.SemaphoreType.DMA((rows // 256,)),
+        ],
         compiler_params=pltpu.CompilerParams(
             collective_id=collective_id, has_side_effects=True, vmem_limit_bytes=VMEM_LIMIT
         ),
         name="entry",
-    )(tokens, w_shard, w_out, gains, segments)
+    )(tokens, w_shard, w_out, gains, segments, w_down)
 
 
 KEY_BLOCK = 512
@@ -905,7 +939,7 @@
 def tail_kernel(
     count, batches, dq_ref, dg_ref, dkv_ref, w_ref, gain_ref, dh1_ref, second_ref,
     low_ref, h1_ref, ahead_ref, behind_ref, n1_ref, x_hbm, mixed_hbm, mlp_hbm,
-    out_all, tok_all, gains_ref, wout_own, din_ref,
+    out_all, tok_all, gains_ref, wout_own, din_ref, key_ref, value_ref,
     part_ref, tok_ref, got, wout_got, gain_own, gain_got, gain_mid, gain_heads,
     din_s, din_got, din_x, wout_s, wout_twin, wout_x,
     cat_ref, out_s, out_got, core_got, x_first, x_second, y_first, y_second, held, n1_s,
@@ -1162,6 +1196,9 @@
     scatter_end(wout_twin, wout_x, wouts, wout_part)
     wsums = reduce(wout_part, wout_got, 0, None)
     scatter_end(din_got, din_x, dins, din_ref)
+    narrow = din_ref[:, pl.ds(2 * size, size)].T
+    key_ref[...] = narrow[: size // 2]
+    value_ref[...] = narrow[size // 2 :]
     wide = width // batches
 
     def slice_of(at):
@@ -1227,9 +1264,11 @@
             jax.ShapeDtypeStruct(gains, F32),
             jax.ShapeDtypeStruct((size, wide), F32),
             jax.ShapeDtypeStruct((wide, depth), F32),
+            jax.ShapeDtypeStruct((size // 2, wide), F32),
+            jax.ShapeDtypeStruct((size // 2, wide), F32),
         ],
         in_specs=[vmem] * 11 + [hbm] * 4,
-        out_specs=[hbm] * 2 + [vmem] * 3,
+        out_specs=[hbm] * 2 + [vmem] * 5,
         scratch_shapes=[
             pltpu.VMEM((count * rows, width), BF),
             pltpu.VMEM((rows, width), BF),
@@ -1272,28 +1311,33 @@
     )(*arrays)
 
 
-def finish_kernel(out_ref, tok_ref, mgate_ref, mup_ref, down_ref, in_ref, gains_ref, *results):
+def finish_kernel(
+    out_ref, tok_ref, mgate_ref, mup_ref, down_ref, in_ref, gains_ref, key_ref, value_ref, wout_ref, *results
+):
     for source, target in zip((out_ref, tok_ref, mgate_ref, mup_ref, down_ref), results):
         target[...] = source[...].reshape(target.shape).astype(target.dtype)
-    query, gate, key, value, first, second = results[5:]
-    size, half = query.shape[1], key.shape[1]
+    query, gate, first, second, key, value, wout = results[5:]
+    key[...] = key_ref[...]
+    value[...] = value_ref[...]
+    wout[...] = wout_ref[...]
+    size = query.shape[1]
     query[...] = in_ref[:, :size]
     gate[...] = in_ref[:, size : 2 * size]
-    key[...] = in_ref[:, 2 * size : 2 * size + half]
-    value[...] = in_ref[:, 2 * size + half :]
     first[...] = gains_ref[pl.ds(0, 1)]
     second[...] = gains_ref[pl.ds(1, 1)]
 
 
-def finish(output, d_tokens, d_mlp, d_down, d_in, gains):
+def finish(output, d_tokens, d_mlp, d_down, d_in, gains, *rest):
     count, rows, width = output.shape
     tall, hidden = d_mlp.shape[0], d_mlp.shape[1] // 2
     down_rows, wide = d_down.shape
     depth = d_in.shape[1]
     size = depth // 3
+    parts = max(1, 16 // count)
+    grid = count * parts
 
     def strip(high, across, at=0):
-        return pl.BlockSpec((high // count, across), lambda i: (i, at))
+        return pl.BlockSpec((high // grid, across), lambda i: (i, at))
 
     def held(*shape):
         return pl.BlockSpec(shape, lambda i: (0, 0))
@@ -1301,29 +1345,29 @@
     def shape(*extent, dtype=F32):
         return jax.ShapeDtypeStruct(extent, dtype)
 
-    whole = pl.BlockSpec((1, rows, width), lambda i: (i, 0, 0))
+    whole = pl.BlockSpec((1, rows // parts, width), lambda i: (i // parts, i % parts, 0))
     return pl.pallas_call(
         finish_kernel,
-        grid=(count,),
+        grid=(grid,),
         out_shape=[
             shape(count * rows, width, dtype=BF), shape(count * rows, width, dtype=BF),
             shape(tall, hidden), shape(tall, hidden), shape(down_rows, wide),
-            shape(tall, size), shape(tall, size), shape(tall, size // 2), shape(tall, size // 2),
-            shape(1, wide), shape(1, wide),
+            shape(tall, size), shape(tall, size),
+            shape(1, wide), shape(1, wide), *[shape(*a.shape) for a in rest],
         ],
         in_specs=[
             whole, whole, strip(tall, hidden), strip(tall, hidden, 1), strip(down_rows, wide),
-            strip(tall, depth), held(2, wide),
+            strip(tall, depth), held(2, wide), *[held(*a.shape) for a in rest],
         ],
         out_specs=[
             strip(count * rows, width), strip(count * rows, width),
             strip(tall, hidden), strip(tall, hidden), strip(down_rows, wide),
-            strip(tall, size), strip(tall, size), strip(tall, size // 2), strip(tall, size // 2),
-            held(1, wide), held(1, wide),
+            strip(tall, size), strip(tall, size),
+            held(1, wide), held(1, wide), *[held(*a.shape) for a in rest],
         ],
         compiler_params=pltpu.CompilerParams(vmem_limit_bytes=VMEM_LIMIT),
         name="finish",
-    )(output, d_tokens, d_mlp, d_mlp, d_down, d_in, gains)
+    )(output, d_tokens, d_mlp, d_mlp, d_down, d_in, gains, *rest)
 
 
 def local_call(kernel, scalars, arrays, outs, scratch, flops, name):
@@ -1410,10 +1454,11 @@
     me = ring_place(lax.axis_index("head"), heads)
     scale_factor = 1.0 / math.sqrt(head_size)
 
+    down_parts = jnp.split(w_down, 2, axis=0)
     w_shard = jnp.concatenate([w_query, w_gate, w_key, w_value], axis=1)
     gains = jnp.concatenate([norm1_gain, norm2_gain]).reshape(-1, 128).astype(F32)
-    normed_one, queries, gate_logit, kv_all, w_in, out_full, gains, seg_all = entry(
-        tokens, w_shard, w_out, gains, segment_ids.reshape(-1, 128), 1
+    normed_one, queries, gate_logit, kv_all, w_in, out_full, gains, seg_all, down_top = entry(
+        tokens, w_shard, w_out, gains, segment_ids.reshape(-1, 128), down_parts[0], 1
     )
     gains, w_mlp_gate = lax.optimization_barrier((gains, w_mlp_gate))
     seg_all = seg_all.reshape(-1)
@@ -1440,13 +1485,13 @@
         pair_flops,
         "attend",
     )
-    mixed_all, down_full, mup_full = spread(
-        [mixed, w_down, w_mlp_up], (("head", "cols"), ("batch", "cols"), ("batch", "rows")), 2
+    mixed_all, down_low, mup_full = spread(
+        [mixed, down_parts[1], w_mlp_up], (("head", "cols"), ("batch", "cols"), ("batch", "rows")), 2
     )
     (
         mlp_part, d_mlp, d_down, resid_own, d_resid, d_resid_low, d_gain_two, d_mixed, going, coming,
     ) = mlp_back(
-        tokens, mixed_all, out_grad, gain_two[None], out_full, mgate_full, mup_full, down_full, 3
+        tokens, mixed_all, out_grad, gain_two[None], out_full, mgate_full, mup_full, down_top, down_low, 3
     )
     hold = lax.optimization_barrier
     flow = flow_steps(mlp_part, going, coming)
@@ -1469,7 +1514,7 @@
         state = flow.send(state)
     d_down = lax.psum_scatter(d_down, "batch", scatter_dimension=1, tiled=True)
     d_mlp = lax.psum_scatter(d_mlp, "batch", scatter_dimension=0, tiled=True)
-    output, d_tokens, d_gains, d_out, d_in = tail(
+    output, d_tokens, d_gains, d_out, d_in, d_key, d_value = tail(
         (
             d_queries, d_gate_logit, d_kv_all, w_in, gain_one[None], d_resid, d_gain_two,
             d_resid_low, resid_own, *state, normed_one, tokens, mixed_all, mlp_part,
@@ -1477,15 +1522,16 @@
         5,
     )
     (
-        output, d_tokens, d_mgate, d_mup, d_down, d_query, d_gate, d_key, d_value, d_one, d_two,
-    ) = finish(output, d_tokens, d_mlp, d_down, d_in, d_gains)
+        output, d_tokens, d_mgate, d_mup, d_down, d_query, d_gate, d_one, d_two,
+        d_key, d_value, d_out,
+    ) = finish(output, d_tokens, d_mlp, d_down, d_in, d_gains, d_key, d_value, d_out)
     return (
         output,
         d_tokens,
         d_one.reshape(-1),
         d_query,
-        d_key,
-        d_value,
+        d_key.T,
+        d_value.T,
         d_gate,
         d_out,
         d_two.reshape(-1),

time: 489 us -> 480 us (0.982)
  Pallas kernels: 456 us -> 447 us
    pallas_call x1, Pallas kernels: 209 us -> 202 us  [tail(): pl.pallas_call(functools.partial(tail_kernel, count, batches), out_shape=...]
  transfers between devices with their start and end apart: 5 -> 5, of which waited for: 0 -> 1; matrix products, arithmetic and copies ran while one was open for 1% -> 1% of each run, Pallas kernels for 58% -> 57%
where the time goes in v19:
time: 480 us; the launch traced here: 479 us
  Pallas kernels  447 us (93%)
  between operations  13.9 us (3%)
  local copies, waits for them, and re-layouts  7.29 us (2%)
  other arithmetic  6.59 us (1%)
    pallas_call x1, Pallas kernels, tail(): pl.pallas_call(functools.partial(tail_kernel, count, batches), out_shape=...  202 us
    pallas_call x1, Pallas kernels, mlp_back(): pl.pallas_call(functools.partial(mlp_kernel, count), out_shape=[shape(tot...  105 us
    pallas_call x1, Pallas kernels, spread(): pl.pallas_call(functools.partial(spread_kernel, count, batches, plans), o...  54.1 us
    pallas_call x1, Pallas kernels, entry(): pl.pallas_call(functools.partial(entry_kernel, count, batches), out_shape...  52.1 us
    pallas_call x2, Pallas kernels, local_call(): pl.pallas_call(kernel, out_shape=outs, in_specs=[smem] * len(scalars) + [...  18.3 us
    pallas_call x1, Pallas kernels, finish(): pl.pallas_call(finish_kernel, grid=(grid,), out_shape=[shape(count * rows...  15.8 us
  transfers between devices with their start and end apart: 5, of which 1 were waited for; matrix products, arithmetic and copies ran while one was open for 1% of the time, Pallas kernels for 57%

profile of v19, /device:TPU:0, one launch (start us, length us, event | category | flops | bytes accessed | tf_op | source)
XLA Modules:
  0.0 479.1 jit_solution(1397564653482258498)
XLA Ops:
  7.2 2.0 fusion
  9.3 1.0 copy.31
  10.2 1.0 copy.32
  11.2 1.3 maximum_convert_fusion.gain_ref
  12.5 1.8 pad_maximum_fusion.w_ref
  14.3 52.1 %entry.1 = (bf16[1280,2048]{1,0:T(8,128)(2,1)}, bf16[1280,128]{1,0:T(8,128)(2,1)}, f32[1280,128]{1,0:T(8,128)}, bf16[5120,256]{1,0:T(8,128)(2,1)}, bf16[2048,512...) custom-call(bf16[1280,2048]{1,0:T(8,128)(2,1)} %x_hbm.3, ...), custom_call_target="tpu_custom_call" | custom-call | tf_op jit(solution)/shard_map/entry/pallas_call | solution.py:795
  66.5 0.2 reduce-scatter.5.cloned.1.call-start
  66.7 0.8 lt.27
  67.5 0.2 convert_reduce_fusion
  67.7 0.6 broadcast_in_dim.22.start_ref
  68.3 0.7 reshape.50
  69.1 0.6 copy.34
  69.7 7.3 %attend.1 = (f32[1280,128]{1,0:T(8,128)}, bf16[1280,128]{1,0:T(8,128)(2,1)}, f32[1,1280]{1,0:T(1,128)}) custom-call(s32[1280]{0:T(1024)} %copy-done.1, s32[1]{0:T(128)} %bitcast.3.base_sm, bf16[1280,128]{1,0:T(8,128)(2,1)} %get-tuple-element.62.q_ref, bf16[5120,256]{1,0:T(8,128)(2,1)} %get-tuple-element.63.kv_ref, s32[1,1280]{1,0:T(1,128)} %broadcast_in_dim.22.start_ref, ...), custom_call_target="tpu_custom_call" | custom-call | flops 3355443200 | bytes 8388608 | tf_op jit(solution)/shard_map/attend/pallas_call | solution.py:1376
  77.0 54.1 %spread_2.1 = (bf16[1280,1024]{1,0:T(8,128)(2,1)}, bf16[384,2048]{1,0:T(8,128)(2,1)}, bf16[2048,768]{1,0:T(8,128)(2,1)}) custom-call(bf16[1280,128]{1,0:T(8,128)(2,1)} %get-tuple-element.66.refs_0_, bf16[384,512]{1,0:T(8,128)(2,1)} %get-tuple-element.112.refs_1_, bf16[512,768]{1,0:T(8,128)(2,1)} %refs_2_.1), custom_call_target="tpu_custom_call" | custom-call | tf_op jit(solution)/shard_map/spread_2/pallas_call | solution.py:176
  131.2 105.0 %mlp_back.1 = (bf16[1280,2048]{1,0:T(8,128)(2,1)}, bf16[2048,1536]{1,0:T(8,128)(2,1)}, bf16[768,2048]{1,0:T(8,128)(2,1)}, f32[160,2048]{1,0:T(8,128)}, f32[160,2...) custom-call(bf16[1280,2048]{1,0:T(8,128)(2,1)} %x_hbm.3, ...), custom_call_target="tpu_custom_call" | custom-call | flops 41607495680 | bytes 41943040 | tf_op jit(solution)/shard_map/mlp_back/pallas_call | solution.py:554
  236.3 0.7 reduce-scatter.3.cloned.1.call-update
  237.0 0.6 copy.35
  237.6 1.0 collective-permute-start
  238.6 1.0 collective-permute-start.1
  239.7 11.0 %attend_back.1 = (bf16[1280,128]{1,0:T(8,128)(2,1)}, bf16[1280,128]{1,0:T(8,128)(2,1)}, bf16[5120,256]{1,0:T(8,128)(2,1)}) custom-call(s32[1280]{0:T(1024)} %copy-done.1, s32[1]{0:T(128)} %bitcast.3.base_sm, bf16[1280,128]{1,0:T(8,128)(2,1)} %get-tuple-element.62.q_ref, bf16[5120,256]{1,0:T(8,128)(2,1)} %get-tuple-element.63.kv_ref, ...), custom_call_target="tpu_custom_call" | custom-call | flops 8388608000 | bytes 8388608 | tf_op jit(solution)/shard_map/attend_back/pallas_call | solution.py:1376
  250.7 0.8 collective-permute-done.1
  251.5 3.2 add_convert_fusion
  254.7 202.0 %tail.1 = (bf16[8,160,2048]{2,1,0:T(8,128)(2,1)}, bf16[8,160,2048]{2,1,0:T(8,128)(2,1)}, f32[2,512]{1,0:T(2,128)}, f32[128,512]{1,0:T(8,128)}, f32[512,384]{1,0:...) custom-call(bf16[1280,128]{1,0:T(8,128)(2,1)} %get-tuple-element.77.dq_ref, bf16[1280,128]{1,0:T(8,128)(2,1)} %get-tuple-element.78.dg_ref, ...), custom_call_target="tpu_custom_call" | custom-call | flops 4026531840 | bytes 419430400 | tf_op jit(solution)/shard_map/tail/pallas_call | solution.py:1259
  456.8 15.8 %finish.1 = (bf16[1280,2048]{1,0:T(8,128)(2,1)}, bf16[1280,2048]{1,0:T(8,128)(2,1)}, f32[512,768]{1,0:T(8,128)}, f32[512,768]{1,0:T(8,128)}, f32[768,512]{1,0:T(...) custom-call(bf16[8,160,2048]{2,1,0:T(8,128)(2,1)} %get-tuple-element, ...), custom_call_target="tpu_custom_call" | custom-call | tf_op jit(solution)/shard_map/finish/pallas_call | solution.py:1349
  (19 shorter events, 0.3 us)
Async XLA Ops:
  7.2 124.0 %all-gather.2.cloned.1.call-start = ((), (), s32[]{:S(2)}) async-start(), calls=%async_computation.2 | async-start | bytes 3932160 | tf_op jit(solution)/shard_map/all_gather | solution.py:1467
  14.3 53.3 %copy-start = (s32[1280]{0:T(1024)S(1)}, s32[1280]{0:T(1024)}, u32[]{:S(2)}) copy-start(s32[1280]{0:T(1024)} %param.14) | copy-start | bytes 15364
  66.5 390.3 %reduce-scatter.5.cloned.1.call-start = ((), (), s32[]{:S(2)}) async-start(), calls=%async_computation.4 | async-start | bytes 3932160 | tf_op jit(solution)/shard_map/reduce_scatter | solution.py:1515
  67.7 2.0 copy-start.1
  236.2 220.6 %reduce-scatter.3.cloned.1.call-start = ((), (), s32[]{:S(2)}) async-start(), calls=%async_computation.3 | async-start | bytes 7864320 | tf_op jit(solution)/shard_map/reduce_scatter | solution.py:1516
  236.3 1.3 copy-start.3
  236.3 2.3 copy-start.2
  237.6 13.1 %collective-permute-start = (bf16[160,2048]{1,0:T(8,128)(2,1)S(1)}, bf16[160,2048]{1,0:T(8,128)(2,1)S(1)}, u32[]{:S(2)}, u32[]{:S(2)}) collective-permute-start(bf16[160,2048]{1,0:T(8,128)(2,1)S(1)} %copy-done.3), channel_id=1, source_target_pairs={{0,2},{2,4},{4,6},{6,7},{7,5},{5,3},{3,1},{1,0},{8,10},{10,12},{12... | collective-permute-start | bytes 1966088 | tf_op jit(solution)/shard_map/ppermute | solution.py:1410
  238.6 12.9 %collective-permute-start.1 = (bf16[160,2048]{1,0:T(8,128)(2,1)S(1)}, bf16[160,2048]{1,0:T(8,128)(2,1)S(1)}, u32[]{:S(2)}, u32[]{:S(2)}) collective-permute-start(bf16[160,2048]{1,0:T(8,128)(2,1)S(1)} %copy-done.2), channel_id=1, source_target_pairs={{0,1},{2,0},{4,2},{6,4},{7,6},{5,7},{3,5},{1,3},{8,9},{10,8},{12,1... | collective-permute-start | bytes 1966088 | tf_op jit(solution)/shard_map/ppermute | solution.py:1411
Sparse Core Ops, SparseCore 0:
  66.6 30.1 all-gather.1
  236.3 37.1 reduce-scatter.4
  276.3 70.6 reduce-scatter.2

commit v20 on v19

--- a/solution.py
+++ b/solution.py
@@ -76,7 +76,11 @@
 def spread_kernel(count, batches, plans, *refs):
     steps = count // 2
     arrays = len(plans)
-    own_refs, all_refs = refs[:arrays], refs[arrays : 2 * arrays]
+    own_refs, all_refs = list(refs[:arrays]), refs[arrays : 2 * arrays]
+    for index, (_, form) in enumerate(plans):
+        if form == "low":
+            half = own_refs[index].shape[0] // 2
+            own_refs[index] = own_refs[index].at[pl.ds(half, half)]
     send_sem, recv_sem, local_sem = refs[2 * arrays :]
     place, right, left = ring_setup(count)
     head = lax.axis_index("head")
@@ -171,7 +175,8 @@
         elif form == "rows":
             shapes.append((many * array.shape[0], array.shape[1]))
         else:
-            shapes.append((array.shape[0], many * array.shape[1]))
+            tall = array.shape[0] // (2 if form == "low" else 1)
+            shapes.append((tall, many * array.shape[1]))
     hbm = pl.BlockSpec(memory_space=pl.ANY)
     return pl.pallas_call(
         functools.partial(spread_kernel, count, batches, plans),
@@ -724,8 +729,9 @@
     def down_view(at):
         return down_all.at[:, part(at, down_ref.shape[1])]
 
-    down_out, down_twin = both(down_view, down_ref)
-    stay(down_ref, down_view(batch))
+    down_own = down_ref.at[pl.ds(0, down_ref.shape[0] // 2)]
+    down_out, down_twin = both(down_view, down_own)
+    stay(down_own, down_view(batch))
 
     @pl.loop(middle, blocks)
     def _(at):
@@ -803,7 +809,7 @@
             jax.ShapeDtypeStruct((count * size, batches * wide), BF),
             jax.ShapeDtypeStruct((batches, *gains.shape), F32),
             jax.ShapeDtypeStruct((batches, *segments.shape), jnp.int32),
-            jax.ShapeDtypeStruct((w_down.shape[0], batches * w_down.shape[1]), BF),
+            jax.ShapeDtypeStruct((w_down.shape[0] // 2, batches * w_down.shape[1]), BF),
         ],
         in_specs=[hbm] + [vmem] * 5,
         out_specs=[hbm] + [vmem] * 4 + [hbm] + [vmem] * 2 + [hbm],
@@ -943,7 +949,7 @@
     part_ref, tok_ref, got, wout_got, gain_own, gain_got, gain_mid, gain_heads,
     din_s, din_got, din_x, wout_s, wout_twin, wout_x,
     cat_ref, out_s, out_got, core_got, x_first, x_second, y_first, y_second, held, n1_s,
-    x_ref, mixed_ref, mlp_ref, send_sem, recv_sem, local_sem,
+    x_ref, mixed_ref, mlp_ref, mlp_next, send_sem, recv_sem, local_sem,
 ):
     steps = count // 2
     rows, width = x_ref.shape
@@ -1074,12 +1080,20 @@
             ((mixed_hbm, mixed_ref), (mlp_hbm, mlp_ref), (x_hbm, x_ref))
         )
     ]
-    for copy in fetches:
+    nexts = [
+        pltpu.make_async_copy(mlp_hbm.at[span(place + shift, rows)], mlp_next.at[at], local_sem.at[7 + at])
+        for at, shift in enumerate((1, -1))
+    ]
+    for copy in (*nexts, *fetches):
         copy.start()
     for at in range(2):
         normed_copy(at, at).start()
-    last_sums = [go(ahead_ref, out_got.at[0], right), go(behind_ref, out_got.at[1], left)]
     swaps = scatter_swap(keys_of, core_got)
+    last_sums = []
+    for at, (held_part, device) in enumerate(((ahead_ref, right), (behind_ref, left))):
+        nexts[at].wait()
+        mlp_next[at] = add_low(mlp_next[at], held_part[...])
+        last_sums.append(go(mlp_next.at[at], out_got.at[at], device))
     cat_ref[:, pl.ds(0, size)] = dq_ref[...]
     cat_ref[:, pl.ds(size, size)] = dg_ref[...]
     for copy in fetches:
@@ -1297,9 +1311,10 @@
             pltpu.VMEM((rows, width), BF),
             pltpu.VMEM((rows, mixed.shape[1]), BF),
             pltpu.VMEM((rows, width), BF),
+            pltpu.VMEM((2, rows, width), BF),
             sems,
             sems,
-            pltpu.SemaphoreType.DMA((7,)),
+            pltpu.SemaphoreType.DMA((9,)),
         ],
         compiler_params=pltpu.CompilerParams(
             collective_id=collective_id, has_side_effects=True, vmem_limit_bytes=VMEM_LIMIT
@@ -1312,62 +1327,67 @@
 
 
 def finish_kernel(
-    out_ref, tok_ref, mgate_ref, mup_ref, down_ref, in_ref, gains_ref, key_ref, value_ref, wout_ref, *results
+    out_hbm, tok_hbm, mlp_ref, down_ref, in_ref, gains_ref, key_ref, value_ref, wout_ref,
+    output, d_tokens, mgate, mup, down, query, gate, first, second, key, value, wout, sem,
 ):
-    for source, target in zip((out_ref, tok_ref, mgate_ref, mup_ref, down_ref), results):
-        target[...] = source[...].reshape(target.shape).astype(target.dtype)
-    query, gate, first, second, key, value, wout = results[5:]
+    count, rows = out_hbm.shape[:2]
+    moves = [
+        pltpu.make_async_copy(source.at[at], target.at[pl.ds(at * rows, rows)], sem.at[index * count + at])
+        for index, (source, target) in enumerate(((out_hbm, output), (tok_hbm, d_tokens)))
+        for at in range(count)
+    ]
+    for copy in moves:
+        copy.start()
+    hidden = mgate.shape[1]
+    size = query.shape[1]
+
+    def convert(target, source, start):
+        tall = 32
+
+        @pl.loop(0, target.shape[0] // tall)
+        def _(at):
+            lines = pl.ds(pl.multiple_of(at * tall, tall), tall)
+            target[lines] = source[lines, pl.ds(start, target.shape[1])].astype(target.dtype)
+
+    convert(mgate, mlp_ref, 0)
+    convert(mup, mlp_ref, hidden)
+    convert(down, down_ref, 0)
+    convert(query, in_ref, 0)
+    convert(gate, in_ref, size)
     key[...] = key_ref[...]
     value[...] = value_ref[...]
     wout[...] = wout_ref[...]
-    size = query.shape[1]
-    query[...] = in_ref[:, :size]
-    gate[...] = in_ref[:, size : 2 * size]
     first[...] = gains_ref[pl.ds(0, 1)]
     second[...] = gains_ref[pl.ds(1, 1)]
+    for copy in moves:
+        copy.wait()
 
 
 def finish(output, d_tokens, d_mlp, d_down, d_in, gains, *rest):
     count, rows, width = output.shape
     tall, hidden = d_mlp.shape[0], d_mlp.shape[1] // 2
     down_rows, wide = d_down.shape
-    depth = d_in.shape[1]
-    size = depth // 3
-    parts = max(1, 16 // count)
-    grid = count * parts
-
-    def strip(high, across, at=0):
-        return pl.BlockSpec((high // grid, across), lambda i: (i, at))
-
-    def held(*shape):
-        return pl.BlockSpec(shape, lambda i: (0, 0))
+    size = d_in.shape[1] // 3
+    vmem = pl.BlockSpec(memory_space=pltpu.VMEM)
+    hbm = pl.BlockSpec(memory_space=pl.ANY)
 
     def shape(*extent, dtype=F32):
         return jax.ShapeDtypeStruct(extent, dtype)
 
-    whole = pl.BlockSpec((1, rows // parts, width), lambda i: (i // parts, i % parts, 0))
     return pl.pallas_call(
         finish_kernel,
-        grid=(grid,),
         out_shape=[
             shape(count * rows, width, dtype=BF), shape(count * rows, width, dtype=BF),
             shape(tall, hidden), shape(tall, hidden), shape(down_rows, wide),
             shape(tall, size), shape(tall, size),
             shape(1, wide), shape(1, wide), *[shape(*a.shape) for a in rest],
         ],
-        in_specs=[
-            whole, whole, strip(tall, hidden), strip(tall, hidden, 1), strip(down_rows, wide),
-            strip(tall, depth), held(2, wide), *[held(*a.shape) for a in rest],
-        ],
-        out_specs=[
-            strip(count * rows, width), strip(count * rows, width),
-            strip(tall, hidden), strip(tall, hidden), strip(down_rows, wide),
-            strip(tall, size), strip(tall, size),
-            held(1, wide), held(1, wide), *[held(*a.shape) for a in rest],
-        ],
+        in_specs=[hbm] * 2 + [vmem] * 7,
+        out_specs=[hbm] * 2 + [vmem] * 10,
+        scratch_shapes=[pltpu.SemaphoreType.DMA((2 * count,))],
         compiler_params=pltpu.CompilerParams(vmem_limit_bytes=VMEM_LIMIT),
         name="finish",
-    )(output, d_tokens, d_mlp, d_mlp, d_down, d_in, gains, *rest)
+    )(output, d_tokens, d_mlp, d_down, d_in, gains, *rest)
 
 
 def local_call(kernel, scalars, arrays, outs, scratch, flops, name):
@@ -1407,11 +1427,12 @@
         return lax.dynamic_slice_in_dim(part, lax.rem(owner + count, count) * rows, rows, 0)
 
     for step in range(2, steps - 1):
-        from_left = lax.ppermute(going, "head", right)
-        from_right = lax.ppermute(coming, "head", left)
-        going = add_low(from_left, mine(place + steps - 1 - step))
-        coming = add_low(from_right, mine(place - steps + 1 + step))
-        going, coming = yield going, coming
+        going = lax.ppermute(going, "head", right)
+        coming = lax.ppermute(coming, "head", left)
+        if step < steps - 2:
+            going = add_low(going, mine(place + steps - 1 - step))
+            coming = add_low(coming, mine(place - steps + 1 + step))
+    return going, coming
 
 
 def matmul(left, right):
@@ -1454,11 +1475,10 @@
     me = ring_place(lax.axis_index("head"), heads)
     scale_factor = 1.0 / math.sqrt(head_size)
 
-    down_parts = jnp.split(w_down, 2, axis=0)
     w_shard = jnp.concatenate([w_query, w_gate, w_key, w_value], axis=1)
     gains = jnp.concatenate([norm1_gain, norm2_gain]).reshape(-1, 128).astype(F32)
     normed_one, queries, gate_logit, kv_all, w_in, out_full, gains, seg_all, down_top = entry(
-        tokens, w_shard, w_out, gains, segment_ids.reshape(-1, 128), down_parts[0], 1
+        tokens, w_shard, w_out, gains, segment_ids.reshape(-1, 128), w_down, 1
     )
     gains, w_mlp_gate = lax.optimization_barrier((gains, w_mlp_gate))
     seg_all = seg_all.reshape(-1)
@@ -1486,7 +1506,7 @@
         "attend",
     )
     mixed_all, down_low, mup_full = spread(
-        [mixed, down_parts[1], w_mlp_up], (("head", "cols"), ("batch", "cols"), ("batch", "rows")), 2
+        [mixed, w_down, w_mlp_up], (("head", "cols"), ("batch", "low"), ("batch", "rows")), 2
     )
     (
         mlp_part, d_mlp, d_down, resid_own, d_resid, d_resid_low, d_gain_two, d_mixed, going, coming,
@@ -1494,8 +1514,7 @@
         tokens, mixed_all, out_grad, gain_two[None], out_full, mgate_full, mup_full, down_top, down_low, 3
     )
     hold = lax.optimization_barrier
-    flow = flow_steps(mlp_part, going, coming)
-    state = next(flow)
+    state = flow_steps(mlp_part, going, coming)
 
     d_queries, d_gate_logit, d_kv_all = local_call(
         functools.partial(attend_back_kernel, scale_factor),
@@ -1510,8 +1529,6 @@
         5 * pair_flops // 2,
         "attend_back",
     )
-    for _ in range(3, heads // 2 - 1):
-        state = flow.send(state)
     d_down = lax.psum_scatter(d_down, "batch", scatter_dimension=1, tiled=True)
     d_mlp = lax.psum_scatter(d_mlp, "batch", scatter_dimension=0, tiled=True)
     output, d_tokens, d_gains, d_out, d_in, d_key, d_value = tail(

time: 480 us -> 786 us (1.64)
  Pallas kernels: 447 us -> 757 us
    pallas_call x1, Pallas kernels: 15.8 us -> 323 us  [finish(): pl.pallas_call(finish_kernel, out_shape=[shape(count * rows, width, dtype...]
  transfers between devices with their start and end apart: 5 -> 5, of which waited for: 1 -> 1; matrix products, arithmetic and copies ran while one was open for 1% -> 0% of each run, Pallas kernels for 57% -> 35%
where the time goes in v20:
time: 786 us; the launch traced here: 785 us
  Pallas kernels  757 us (96%)
  between operations  13.9 us (2%)
    pallas_call x1, Pallas kernels, finish(): pl.pallas_call(finish_kernel, out_shape=[shape(count * rows, width, dtype...  323 us
    pallas_call x1, Pallas kernels, tail(): pl.pallas_call(functools.partial(tail_kernel, count, batches), out_shape=...  204 us
    pallas_call x1, Pallas kernels, mlp_back(): pl.pallas_call(functools.partial(mlp_kernel, count), out_shape=[shape(tot...  105 us
    pallas_call x1, Pallas kernels, spread(): pl.pallas_call(functools.partial(spread_kernel, count, batches, plans), o...  54.2 us
    pallas_call x1, Pallas kernels, entry(): pl.pallas_call(functools.partial(entry_kernel, count, batches), out_shape...  52.2 us
    pallas_call x2, Pallas kernels, local_call(): pl.pallas_call(kernel, out_shape=outs, in_specs=[smem] * len(scalars) + [...  18.4 us
  transfers between devices with their start and end apart: 5, of which 1 were waited for; matrix products, arithmetic and copies ran while one was open for 0% of the time, Pallas kernels for 35%

profile of v20, /device:TPU:0, one launch (start us, length us, event | category | flops | bytes accessed | tf_op | source)
XLA Modules:
  0.0 784.5 jit_solution(6837893198304864241)
XLA Ops:
  7.2 1.0 copy.31
  8.2 1.0 copy.32
  9.2 1.3 maximum_convert_fusion.gain_ref
  10.5 1.8 pad_maximum_fusion.w_ref
  12.3 52.2 %entry.1 = (bf16[1280,2048]{1,0:T(8,128)(2,1)}, bf16[1280,128]{1,0:T(8,128)(2,1)}, f32[1280,128]{1,0:T(8,128)}, bf16[5120,256]{1,0:T(8,128)(2,1)}, bf16[2048,512...) custom-call(bf16[1280,2048]{1,0:T(8,128)(2,1)} %x_hbm.3, ...), custom_call_target="tpu_custom_call" | custom-call | tf_op jit(solution)/shard_map/entry/pallas_call | solution.py:801
  64.6 0.2 reduce-scatter.5.cloned.1.call-start
  64.8 0.8 lt.15
  65.6 0.7 reshape.50
  66.3 0.2 convert_reduce_fusion
  66.5 0.1 select_reduce_fusion.start_sm
  66.6 0.6 broadcast_in_dim.22.start_ref
  67.2 0.6 copy.34
  67.8 7.3 attend.1
  75.1 54.2 %spread_2.1 = (bf16[1280,1024]{1,0:T(8,128)(2,1)}, bf16[384,2048]{1,0:T(8,128)(2,1)}, bf16[2048,768]{1,0:T(8,128)(2,1)}) custom-call(bf16[1280,128]{1,0:T(8,128)(2,1)} %get-tuple-element.66.refs_0_, bf16[768,512]{1,0:T(8,128)(2,1)} %refs_1_.1, bf16[512,768]{1,0:T(8,128)(2,1)} %refs_2_.1), custom_call_target="tpu_custom_call" | custom-call | tf_op jit(solution)/shard_map/spread_2/pallas_call | solution.py:181
  129.4 105.0 %mlp_back.1 = (bf16[1280,2048]{1,0:T(8,128)(2,1)}, bf16[2048,1536]{1,0:T(8,128)(2,1)}, bf16[768,2048]{1,0:T(8,128)(2,1)}, f32[160,2048]{1,0:T(8,128)}, f32[160,2...) custom-call(bf16[1280,2048]{1,0:T(8,128)(2,1)} %x_hbm.3, ...), custom_call_target="tpu_custom_call" | custom-call | flops 41607495680 | bytes 41943040 | tf_op jit(solution)/shard_map/mlp_back/pallas_call | solution.py:559
  234.5 0.7 reduce-scatter.3.cloned.1.call-update
  235.2 0.6 copy.35
  235.8 1.0 collective-permute-start
  236.8 1.0 collective-permute-start.1
  237.8 11.1 %attend_back.1 = (bf16[1280,128]{1,0:T(8,128)(2,1)}, bf16[1280,128]{1,0:T(8,128)(2,1)}, bf16[5120,256]{1,0:T(8,128)(2,1)}) custom-call(s32[1280]{0:T(1024)} %copy-done.3, s32[1]{0:T(128)} %bitcast.3.base_sm, bf16[1280,128]{1,0:T(8,128)(2,1)} %get-tuple-element.62.q_ref, bf16[5120,256]{1,0:T(8,128)(2,1)} %get-tuple-element.63.kv_ref, ...), custom_call_target="tpu_custom_call" | custom-call | flops 8388608000 | bytes 8388608 | tf_op jit(solution)/shard_map/attend_back/pallas_call | solution.py:1396
  248.9 0.7 collective-permute-done.1.behind_ref
  249.7 0.7 copy-done.1
  250.5 204.0 %tail.1 = (bf16[8,160,2048]{2,1,0:T(8,128)(2,1)}, bf16[8,160,2048]{2,1,0:T(8,128)(2,1)}, f32[2,512]{1,0:T(2,128)}, f32[128,512]{1,0:T(8,128)}, f32[512,384]{1,0:...) custom-call(bf16[1280,128]{1,0:T(8,128)(2,1)} %get-tuple-element.77.dq_ref, bf16[1280,128]{1,0:T(8,128)(2,1)} %get-tuple-element.78.dg_ref, ...), custom_call_target="tpu_custom_call" | custom-call | flops 4026531840 | bytes 419430400 | tf_op jit(solution)/shard_map/tail/pallas_call | solution.py:1273
  454.6 323.4 %finish.1 = (bf16[1280,2048]{1,0:T(8,128)(2,1)}, bf16[1280,2048]{1,0:T(8,128)(2,1)}, f32[512,768]{1,0:T(8,128)}, f32[512,768]{1,0:T(8,128)}, f32[768,512]{1,0:T(...) custom-call(bf16[8,160,2048]{2,1,0:T(8,128)(2,1)} %get-tuple-element, ...), custom_call_target="tpu_custom_call" | custom-call | tf_op jit(solution)/shard_map/finish/pallas_call | solution.py:1377
  (21 shorter events, 0.3 us)
Async XLA Ops:
  7.2 122.2 %all-gather.2.cloned.1.call-start = ((), (), s32[]{:S(2)}) async-start(), calls=%async_computation.2 | async-start | bytes 3932160 | tf_op jit(solution)/shard_map/all_gather | solution.py:1487
  12.3 54.2 %copy-start.2 = (s32[1280]{0:T(1024)S(1)}, s32[1280]{0:T(1024)}, u32[]{:S(2)}) copy-start(s32[1280]{0:T(1024)} %param.14) | copy-start | bytes 15364
  64.6 390.0 %reduce-scatter.5.cloned.1.call-start = ((), (), s32[]{:S(2)}) async-start(), calls=%async_computation.4 | async-start | bytes 3932160 | tf_op jit(solution)/shard_map/reduce_scatter | solution.py:1532
  66.5 1.2 copy-start.3
  234.4 220.1 %reduce-scatter.3.cloned.1.call-start = ((), (), s32[]{:S(2)}) async-start(), calls=%async_computation.3 | async-start | bytes 7864320 | tf_op jit(solution)/shard_map/reduce_scatter | solution.py:1533
  234.5 1.3 copy-start.5
  234.5 2.3 copy-start.4
  235.8 13.1 %collective-permute-start = (bf16[160,2048]{1,0:T(8,128)(2,1)S(1)}, bf16[160,2048]{1,0:T(8,128)(2,1)S(1)}, u32[]{:S(2)}, u32[]{:S(2)}) collective-permute-start(bf16[160,2048]{1,0:T(8,128)(2,1)S(1)} %copy-done.5), channel_id=1, source_target_pairs={{0,2},{2,4},{4,6},{6,7},{7,5},{5,3},{3,1},{1,0},{8,10},{10,12},{12... | collective-permute-start | bytes 1966088 | tf_op jit(solution)/shard_map/ppermute | solution.py:1430
  236.8 12.8 %collective-permute-start.1 = (bf16[160,2048]{1,0:T(8,128)(2,1)S(1)}, bf16[160,2048]{1,0:T(8,128)(2,1)S(1)}, u32[]{:S(2)}, u32[]{:S(2)}) collective-permute-start(bf16[160,2048]{1,0:T(8,128)(2,1)S(1)} %copy-done.4), channel_id=1, source_target_pairs={{0,1},{2,0},{4,2},{6,4},{7,6},{5,7},{3,5},{1,3},{8,9},{10,8},{12,1... | collective-permute-start | bytes 1966088 | tf_op jit(solution)/shard_map/ppermute | solution.py:1431
  248.9 0.8 copy-start
  249.6 0.8 copy-start.1
Sparse Core Ops, SparseCore 0:
  64.7 30.0 all-gather.1
  234.5 38.7 reduce-scatter.4
  276.0 72.7 reduce-scatter.2

commit v21 on v20

--- a/solution.py
+++ b/solution.py
@@ -1328,15 +1328,21 @@
 
 def finish_kernel(
     out_hbm, tok_hbm, mlp_ref, down_ref, in_ref, gains_ref, key_ref, value_ref, wout_ref,
-    output, d_tokens, mgate, mup, down, query, gate, first, second, key, value, wout, sem,
+    output, d_tokens, mgate, mup, down, query, gate, first, second, key, value, wout,
+    held, load_sem, store_sem,
 ):
     count, rows = out_hbm.shape[:2]
-    moves = [
-        pltpu.make_async_copy(source.at[at], target.at[pl.ds(at * rows, rows)], sem.at[index * count + at])
-        for index, (source, target) in enumerate(((out_hbm, output), (tok_hbm, d_tokens)))
-        for at in range(count)
-    ]
-    for copy in moves:
+    loads, stores = [], []
+    for index, (source, target) in enumerate(((out_hbm, output), (tok_hbm, d_tokens))):
+        for at in range(count):
+            slot = index * count + at
+            loads.append(pltpu.make_async_copy(source.at[at], held.at[slot], load_sem.at[slot]))
+            stores.append(
+                pltpu.make_async_copy(
+                    held.at[slot], target.at[pl.ds(at * rows, rows)], store_sem.at[slot]
+                )
+            )
+    for copy in loads:
         copy.start()
     hidden = mgate.shape[1]
     size = query.shape[1]
@@ -1349,6 +1355,9 @@
             lines = pl.ds(pl.multiple_of(at * tall, tall), tall)
             target[lines] = source[lines, pl.ds(start, target.shape[1])].astype(target.dtype)
 
+    for load, store in zip(loads, stores):
+        load.wait()
+        store.start()
     convert(mgate, mlp_ref, 0)
     convert(mup, mlp_ref, hidden)
     convert(down, down_ref, 0)
@@ -1359,7 +1368,7 @@
     wout[...] = wout_ref[...]
     first[...] = gains_ref[pl.ds(0, 1)]
     second[...] = gains_ref[pl.ds(1, 1)]
-    for copy in moves:
+    for copy in stores:
         copy.wait()
 
 
@@ -1384,7 +1393,11 @@
         ],
         in_specs=[hbm] * 2 + [vmem] * 7,
         out_specs=[hbm] * 2 + [vmem] * 10,
-        scratch_shapes=[pltpu.SemaphoreType.DMA((2 * count,))],
+        scratch_shapes=[
+            pltpu.VMEM((2 * count, rows, width), BF),
+            pltpu.SemaphoreType.DMA((2 * count,)),
+            pltpu.SemaphoreType.DMA((2 * count,)),
+        ],
         compiler_params=pltpu.CompilerParams(vmem_limit_bytes=VMEM_LIMIT),
         name="finish",
     )(output, d_tokens, d_mlp, d_down, d_in, gains, *rest)

time: 786 us -> 476 us (0.61)
  Pallas kernels: 757 us -> 450 us
    pallas_call x1, Pallas kernels: 323 us -> 12.6 us  [finish(): pl.pallas_call(finish_kernel, out_shape=[shape(count * rows, width, dtype...]
  transfers between devices with their start and end apart: 5 -> 5, of which waited for: 1 -> 0; matrix products, arithmetic and copies ran while one was open for 0% -> 1% of each run, Pallas kernels for 35% -> 59%
where the time goes in v21:
time: 476 us
  Pallas kernels  450 us (95%)
  between operations  13.9 us (3%)
  local copies, waits for them, and re-layouts  6.28 us (1%)
    pallas_call x1, Pallas kernels, tail(): pl.pallas_call(functools.partial(tail_kernel, count, batches), out_shape=...  204 us
    pallas_call x1, Pallas kernels, mlp_back(): pl.pallas_call(functools.partial(mlp_kernel, count), out_shape=[shape(tot...  105 us
    pallas_call x1, Pallas kernels, spread(): pl.pallas_call(functools.partial(spread_kernel, count, batches, plans), o...  54.6 us
    pallas_call x1, Pallas kernels, entry(): pl.pallas_call(functools.partial(entry_kernel, count, batches), out_shape...  52.2 us
    pallas_call x2, Pallas kernels, local_call(): pl.pallas_call(kernel, out_shape=outs, in_specs=[smem] * len(scalars) + [...  20.4 us
    pallas_call x1, Pallas kernels, finish(): pl.pallas_call(finish_kernel, out_shape=[shape(count * rows, width, dtype...  12.6 us
  transfers between devices with their start and end apart: 5, of which 0 were waited for; matrix products, arithmetic and copies ran while one was open for 1% of the time, Pallas kernels for 59%

profile of v21, /device:TPU:0, one launch (start us, length us, event | category | flops | bytes accessed | tf_op | source)
XLA Modules:
  0.0 476.3 jit_solution(2980597687516672799)
XLA Ops:
  7.2 1.0 copy.31
  8.2 1.0 copy.32
  9.2 1.3 maximum_convert_fusion.gain_ref
  10.5 1.8 pad_maximum_fusion.w_ref
  12.3 52.2 %entry.1 = (bf16[1280,2048]{1,0:T(8,128)(2,1)}, bf16[1280,128]{1,0:T(8,128)(2,1)}, f32[1280,128]{1,0:T(8,128)}, bf16[5120,256]{1,0:T(8,128)(2,1)}, bf16[2048,512...) custom-call(bf16[1280,2048]{1,0:T(8,128)(2,1)} %x_hbm.3, ...), custom_call_target="tpu_custom_call" | custom-call | tf_op jit(solution)/shard_map/entry/pallas_call | solution.py:801
  64.6 0.2 reduce-scatter.5.cloned.1.call-start
  64.8 0.8 lt.15
  65.6 0.7 reshape.50
  66.3 0.2 convert_reduce_fusion
  66.5 0.1 select_reduce_fusion.start_sm
  66.6 0.6 broadcast_in_dim.22.start_ref
  67.2 0.6 copy.34
  67.8 8.2 %attend.1 = (f32[1280,128]{1,0:T(8,128)}, bf16[1280,128]{1,0:T(8,128)(2,1)}, f32[1,1280]{1,0:T(1,128)}) custom-call(s32[1280]{0:T(1024)} %copy-done.3, s32[1]{0:T(128)} %bitcast.3.base_sm, bf16[1280,128]{1,0:T(8,128)(2,1)} %get-tuple-element.62.q_ref, bf16[5120,256]{1,0:T(8,128)(2,1)} %get-tuple-element.63.kv_ref, s32[1,1280]{1,0:T(1,128)} %broadcast_in_dim.22.start_ref, ...), custom_call_target="tpu_custom_call" | custom-call | flops 3355443200 | bytes 8388608 | tf_op jit(solution)/shard_map/attend/pallas_call | solution.py:1409
  76.0 54.6 %spread_2.1 = (bf16[1280,1024]{1,0:T(8,128)(2,1)}, bf16[384,2048]{1,0:T(8,128)(2,1)}, bf16[2048,768]{1,0:T(8,128)(2,1)}) custom-call(bf16[1280,128]{1,0:T(8,128)(2,1)} %get-tuple-element.66.refs_0_, bf16[768,512]{1,0:T(8,128)(2,1)} %refs_1_.1, bf16[512,768]{1,0:T(8,128)(2,1)} %refs_2_.1), custom_call_target="tpu_custom_call" | custom-call | tf_op jit(solution)/shard_map/spread_2/pallas_call | solution.py:181
  130.6 105.5 %mlp_back.1 = (bf16[1280,2048]{1,0:T(8,128)(2,1)}, bf16[2048,1536]{1,0:T(8,128)(2,1)}, bf16[768,2048]{1,0:T(8,128)(2,1)}, f32[160,2048]{1,0:T(8,128)}, f32[160,2...) custom-call(bf16[1280,2048]{1,0:T(8,128)(2,1)} %x_hbm.3, ...), custom_call_target="tpu_custom_call" | custom-call | flops 41607495680 | bytes 41943040 | tf_op jit(solution)/shard_map/mlp_back/pallas_call | solution.py:559
  236.2 0.7 reduce-scatter.3.cloned.1.call-update
  236.9 0.6 copy.35
  237.5 1.0 collective-permute-start
  238.5 1.0 collective-permute-start.1
  239.5 12.2 %attend_back.1 = (bf16[1280,128]{1,0:T(8,128)(2,1)}, bf16[1280,128]{1,0:T(8,128)(2,1)}, bf16[5120,256]{1,0:T(8,128)(2,1)}) custom-call(s32[1280]{0:T(1024)} %copy-done.3, s32[1]{0:T(128)} %bitcast.3.base_sm, bf16[1280,128]{1,0:T(8,128)(2,1)} %get-tuple-element.62.q_ref, bf16[5120,256]{1,0:T(8,128)(2,1)} %get-tuple-element.63.kv_ref, ...), custom_call_target="tpu_custom_call" | custom-call | flops 8388608000 | bytes 8388608 | tf_op jit(solution)/shard_map/attend_back/pallas_call | solution.py:1409
  251.7 0.8 copy-done
  252.5 0.2 copy-done.1
  252.7 204.3 %tail.1 = (bf16[8,160,2048]{2,1,0:T(8,128)(2,1)}, bf16[8,160,2048]{2,1,0:T(8,128)(2,1)}, f32[2,512]{1,0:T(2,128)}, f32[128,512]{1,0:T(8,128)}, f32[512,384]{1,0:...) custom-call(bf16[1280,128]{1,0:T(8,128)(2,1)} %get-tuple-element.77.dq_ref, bf16[1280,128]{1,0:T(8,128)(2,1)} %get-tuple-element.78.dg_ref, ...), custom_call_target="tpu_custom_call" | custom-call | flops 4026531840 | bytes 419430400 | tf_op jit(solution)/shard_map/tail/pallas_call | solution.py:1273
  457.1 12.6 %finish.1 = (bf16[1280,2048]{1,0:T(8,128)(2,1)}, bf16[1280,2048]{1,0:T(8,128)(2,1)}, f32[512,768]{1,0:T(8,128)}, f32[512,768]{1,0:T(8,128)}, f32[768,512]{1,0:T(...) custom-call(bf16[8,160,2048]{2,1,0:T(8,128)(2,1)} %get-tuple-element, ...), custom_call_target="tpu_custom_call" | custom-call | tf_op jit(solution)/shard_map/finish/pallas_call | solution.py:1386
  (21 shorter events, 0.2 us)
Async XLA Ops:
  7.2 123.4 %all-gather.2.cloned.1.call-start = ((), (), s32[]{:S(2)}) async-start(), calls=%async_computation.2 | async-start | bytes 3932160 | tf_op jit(solution)/shard_map/all_gather | solution.py:1500
  12.3 54.2 %copy-start.2 = (s32[1280]{0:T(1024)S(1)}, s32[1280]{0:T(1024)}, u32[]{:S(2)}) copy-start(s32[1280]{0:T(1024)} %param.14) | copy-start | bytes 15364
  64.6 392.5 %reduce-scatter.5.cloned.1.call-start = ((), (), s32[]{:S(2)}) async-start(), calls=%async_computation.4 | async-start | bytes 3932160 | tf_op jit(solution)/shard_map/reduce_scatter | solution.py:1545
  66.5 1.2 copy-start.3
  236.1 221.0 %reduce-scatter.3.cloned.1.call-start = ((), (), s32[]{:S(2)}) async-start(), calls=%async_computation.3 | async-start | bytes 7864320 | tf_op jit(solution)/shard_map/reduce_scatter | solution.py:1546
  236.2 1.3 copy-start.5
  236.2 2.3 copy-start.4
  237.5 14.2 %collective-permute-start = (bf16[160,2048]{1,0:T(8,128)(2,1)S(1)}, bf16[160,2048]{1,0:T(8,128)(2,1)S(1)}, u32[]{:S(2)}, u32[]{:S(2)}) collective-permute-start(bf16[160,2048]{1,0:T(8,128)(2,1)S(1)} %copy-done.5), channel_id=1, source_target_pairs={{0,2},{2,4},{4,6},{6,7},{7,5},{5,3},{3,1},{1,0},{8,10},{10,12},{12... | collective-permute-start | bytes 1966088 | tf_op jit(solution)/shard_map/ppermute | solution.py:1443
  238.5 13.2 %collective-permute-start.1 = (bf16[160,2048]{1,0:T(8,128)(2,1)S(1)}, bf16[160,2048]{1,0:T(8,128)(2,1)S(1)}, u32[]{:S(2)}, u32[]{:S(2)}) collective-permute-start(bf16[160,2048]{1,0:T(8,128)(2,1)S(1)} %copy-done.4), channel_id=1, source_target_pairs={{0,1},{2,0},{4,2},{6,4},{7,6},{5,7},{3,5},{1,3},{8,9},{10,8},{12,1... | collective-permute-start | bytes 1966088 | tf_op jit(solution)/shard_map/ppermute | solution.py:1444
  251.7 0.8 copy-start
  251.7 1.0 copy-start.1
Sparse Core Ops, SparseCore 0:
  64.7 28.9 all-gather.1
  236.2 38.6 reduce-scatter.4
  277.6 72.8 reduce-scatter.2

commit v22 on v21

--- a/solution.py
+++ b/solution.py
@@ -1023,18 +1023,23 @@
             cols = pl.ds(pl.multiple_of(at * tile, tile), tile)
             part_ref[here, cols] = cols_inner(values, w_ref[cols, pl.ds(0, depth)]).astype(BF)
 
-    def gather(own, whole, step, last):
+    def gather(own, whole, step, last, start=0, many=1):
         out = []
+        span_wide = width // many
         for flow, chunk, device in ((0, place - step, right), (1, place + step, left)):
             if last:
                 last[flow].wait_recv()
             target = whole.at[lax.rem(chunk + count, count)]
             source = target if step else own
+            cut = (slice(None), pl.ds(start, span_wide))
             if step == steps - 1:
-                cut = (slice(None), pl.ds(flow * (width // 2), width // 2))
-                source, target = source.at[cut], target.at[cut]
-            out.append(go(source, target, device))
+                cut = (slice(None), pl.ds(start + flow * (span_wide // 2), span_wide // 2))
+            out.append(go(source.at[cut], target.at[cut], device))
         return out
+
+    def gather_halves(own, whole, step, last):
+        last = last or (None, None)
+        return [gather(own, whole, step, last[at], at * (width // 2), 2) for at in range(2)]
 
     def reduce(parts, held, step, last):
         extent, side = held.shape[2], held.shape[3] // 2
@@ -1204,7 +1209,7 @@
 
     keep_tok = pltpu.make_async_copy(tok_ref, tok_all.at[place], local_sem.at[1])
     keep_tok.start()
-    toks = gather(tok_ref, tok_all, 0, None)
+    toks = gather_halves(tok_ref, tok_all, 0, None)
     outs = gather(out_s, out_all, steps - 1, outs)
     wout_part = wout_twin.at[across]
     scatter_end(wout_twin, wout_x, wouts, wout_part)
@@ -1222,7 +1227,7 @@
         go(gain_own.at[:, slice_of(other)], gain_got.at[hop], (other, head))
         for hop, other in enumerate(others)
     ]
-    toks = gather(tok_ref, tok_all, 1, toks)
+    toks = gather_halves(tok_ref, tok_all, 1, toks)
     wsums = reduce(wout_part, wout_got, 1, wsums)
     middle = gain_own[:, slice_of(batch)]
     for hop, copy in enumerate(gains):
@@ -1232,7 +1237,7 @@
     gain_heads[place] = middle
     gains = [go(gain_mid, gain_heads.at[place], member) for member in members]
     for step in range(2, steps):
-        toks = gather(tok_ref, tok_all, step, toks)
+        toks = gather_halves(tok_ref, tok_all, step, toks)
         wsums = reduce(wout_part, wout_got, step, wsums)
     for copy in gains:
         copy.wait_recv()
@@ -1247,7 +1252,7 @@
         + wout_got[0, steps - 1].astype(F32)
         + wout_got[1, steps - 1].astype(F32)
     )
-    for copy in toks:
+    for copy in (*toks[0], *toks[1]):
         copy.wait_recv()
     for copy in copies:
         copy.wait_send()

time: 476 us -> 476 us (level)
  transfers between devices with their start and end apart: 5 -> 5, of which waited for: 0 -> 1; matrix products, arithmetic and copies ran while one was open for 1% -> 1% of each run, Pallas kernels for 59% -> 58%
where the time goes in v22:
time: 476 us; the launch traced here: 474 us
  Pallas kernels  447 us (94%)
  between operations  13.9 us (3%)
  local copies, waits for them, and re-layouts  6.09 us (1%)
    pallas_call x1, Pallas kernels, tail(): pl.pallas_call(functools.partial(tail_kernel, count, batches), out_shape=...  204 us
    pallas_call x1, Pallas kernels, mlp_back(): pl.pallas_call(functools.partial(mlp_kernel, count), out_shape=[shape(tot...  105 us
    pallas_call x1, Pallas kernels, spread(): pl.pallas_call(functools.partial(spread_kernel, count, batches, plans), o...  54.2 us
    pallas_call x1, Pallas kernels, entry(): pl.pallas_call(functools.partial(entry_kernel, count, batches), out_shape...  52.2 us
    pallas_call x2, Pallas kernels, local_call(): pl.pallas_call(kernel, out_shape=outs, in_specs=[smem] * len(scalars) + [...  18.4 us
    pallas_call x1, Pallas kernels, finish(): pl.pallas_call(finish_kernel, out_shape=[shape(count * rows, width, dtype...  12.6 us
  transfers between devices with their start and end apart: 5, of which 1 were waited for; matrix products, arithmetic and copies ran while one was open for 1% of the time, Pallas kernels for 58%

profile of v22, /device:TPU:0, one launch (start us, length us, event | category | flops | bytes accessed | tf_op | source)
XLA Modules:
  0.0 473.7 jit_solution(10401281744158800527)
XLA Ops:
  7.2 1.0 copy.31
  8.2 1.0 copy.32
  9.2 1.3 maximum_convert_fusion.gain_ref
  10.5 1.8 pad_maximum_fusion.w_ref
  12.3 52.2 %entry.1 = (bf16[1280,2048]{1,0:T(8,128)(2,1)}, bf16[1280,128]{1,0:T(8,128)(2,1)}, f32[1280,128]{1,0:T(8,128)}, bf16[5120,256]{1,0:T(8,128)(2,1)}, bf16[2048,512...) custom-call(bf16[1280,2048]{1,0:T(8,128)(2,1)} %x_hbm.3, ...), custom_call_target="tpu_custom_call" | custom-call | tf_op jit(solution)/shard_map/entry/pallas_call | solution.py:801
  64.6 0.2 reduce-scatter.5.cloned.1.call-start
  64.8 0.8 lt.15
  65.6 0.7 reshape.50
  66.3 0.2 convert_reduce_fusion
  66.5 0.1 select_reduce_fusion.start_sm
  66.6 0.6 broadcast_in_dim.22.start_ref
  67.2 0.6 copy.34
  67.8 7.3 %attend.1 = (f32[1280,128]{1,0:T(8,128)}, bf16[1280,128]{1,0:T(8,128)(2,1)}, f32[1,1280]{1,0:T(1,128)}) custom-call(s32[1280]{0:T(1024)} %copy-done.3, s32[1]{0:T(128)} %bitcast.3.base_sm, bf16[1280,128]{1,0:T(8,128)(2,1)} %get-tuple-element.62.q_ref, bf16[5120,256]{1,0:T(8,128)(2,1)} %get-tuple-element.63.kv_ref, s32[1,1280]{1,0:T(1,128)} %broadcast_in_dim.22.start_ref, ...), custom_call_target="tpu_custom_call" | custom-call | flops 3355443200 | bytes 8388608 | tf_op jit(solution)/shard_map/attend/pallas_call | solution.py:1414
  75.1 54.2 %spread_2.1 = (bf16[1280,1024]{1,0:T(8,128)(2,1)}, bf16[384,2048]{1,0:T(8,128)(2,1)}, bf16[2048,768]{1,0:T(8,128)(2,1)}) custom-call(bf16[1280,128]{1,0:T(8,128)(2,1)} %get-tuple-element.66.refs_0_, bf16[768,512]{1,0:T(8,128)(2,1)} %refs_1_.1, bf16[512,768]{1,0:T(8,128)(2,1)} %refs_2_.1), custom_call_target="tpu_custom_call" | custom-call | tf_op jit(solution)/shard_map/spread_2/pallas_call | solution.py:181
  129.4 105.0 %mlp_back.1 = (bf16[1280,2048]{1,0:T(8,128)(2,1)}, bf16[2048,1536]{1,0:T(8,128)(2,1)}, bf16[768,2048]{1,0:T(8,128)(2,1)}, f32[160,2048]{1,0:T(8,128)}, f32[160,2...) custom-call(bf16[1280,2048]{1,0:T(8,128)(2,1)} %x_hbm.3, ...), custom_call_target="tpu_custom_call" | custom-call | flops 41607495680 | bytes 41943040 | tf_op jit(solution)/shard_map/mlp_back/pallas_call | solution.py:559
  234.5 0.7 reduce-scatter.3.cloned.1.call-update
  235.2 0.6 copy.35
  235.8 1.0 collective-permute-start
  236.8 1.0 collective-permute-start.1
  237.8 11.1 %attend_back.1 = (bf16[1280,128]{1,0:T(8,128)(2,1)}, bf16[1280,128]{1,0:T(8,128)(2,1)}, bf16[5120,256]{1,0:T(8,128)(2,1)}) custom-call(s32[1280]{0:T(1024)} %copy-done.3, s32[1]{0:T(128)} %bitcast.3.base_sm, bf16[1280,128]{1,0:T(8,128)(2,1)} %get-tuple-element.62.q_ref, bf16[5120,256]{1,0:T(8,128)(2,1)} %get-tuple-element.63.kv_ref, ...), custom_call_target="tpu_custom_call" | custom-call | flops 8388608000 | bytes 8388608 | tf_op jit(solution)/shard_map/attend_back/pallas_call | solution.py:1414
  248.9 0.7 collective-permute-done.1.behind_ref
  249.7 0.7 copy-done.1
  250.5 204.1 %tail.1 = (bf16[8,160,2048]{2,1,0:T(8,128)(2,1)}, bf16[8,160,2048]{2,1,0:T(8,128)(2,1)}, f32[2,512]{1,0:T(2,128)}, f32[128,512]{1,0:T(8,128)}, f32[512,384]{1,0:...) custom-call(bf16[1280,128]{1,0:T(8,128)(2,1)} %get-tuple-element.77.dq_ref, bf16[1280,128]{1,0:T(8,128)(2,1)} %get-tuple-element.78.dg_ref, ...), custom_call_target="tpu_custom_call" | custom-call | flops 4026531840 | bytes 419430400 | tf_op jit(solution)/shard_map/tail/pallas_call | solution.py:1278
  454.6 12.6 %finish.1 = (bf16[1280,2048]{1,0:T(8,128)(2,1)}, bf16[1280,2048]{1,0:T(8,128)(2,1)}, f32[512,768]{1,0:T(8,128)}, f32[512,768]{1,0:T(8,128)}, f32[768,512]{1,0:T(...) custom-call(bf16[8,160,2048]{2,1,0:T(8,128)(2,1)} %get-tuple-element, ...), custom_call_target="tpu_custom_call" | custom-call | tf_op jit(solution)/shard_map/finish/pallas_call | solution.py:1391
  (21 shorter events, 0.3 us)
Async XLA Ops:
  7.2 122.2 %all-gather.2.cloned.1.call-start = ((), (), s32[]{:S(2)}) async-start(), calls=%async_computation.2 | async-start | bytes 3932160 | tf_op jit(solution)/shard_map/all_gather | solution.py:1505
  12.3 54.2 %copy-start.2 = (s32[1280]{0:T(1024)S(1)}, s32[1280]{0:T(1024)}, u32[]{:S(2)}) copy-start(s32[1280]{0:T(1024)} %param.14) | copy-start | bytes 15364
  64.6 390.0 %reduce-scatter.5.cloned.1.call-start = ((), (), s32[]{:S(2)}) async-start(), calls=%async_computation.4 | async-start | bytes 3932160 | tf_op jit(solution)/shard_map/reduce_scatter | solution.py:1550
  66.5 1.2 copy-start.3
  234.4 220.1 %reduce-scatter.3.cloned.1.call-start = ((), (), s32[]{:S(2)}) async-start(), calls=%async_computation.3 | async-start | bytes 7864320 | tf_op jit(solution)/shard_map/reduce_scatter | solution.py:1551
  234.5 1.3 copy-start.5
  234.5 2.3 copy-start.4
  235.8 13.1 %collective-permute-start = (bf16[160,2048]{1,0:T(8,128)(2,1)S(1)}, bf16[160,2048]{1,0:T(8,128)(2,1)S(1)}, u32[]{:S(2)}, u32[]{:S(2)}) collective-permute-start(bf16[160,2048]{1,0:T(8,128)(2,1)S(1)} %copy-done.5), channel_id=1, source_target_pairs={{0,2},{2,4},{4,6},{6,7},{7,5},{5,3},{3,1},{1,0},{8,10},{10,12},{12... | collective-permute-start | bytes 1966088 | tf_op jit(solution)/shard_map/ppermute | solution.py:1448
  236.8 12.8 %collective-permute-start.1 = (bf16[160,2048]{1,0:T(8,128)(2,1)S(1)}, bf16[160,2048]{1,0:T(8,128)(2,1)S(1)}, u32[]{:S(2)}, u32[]{:S(2)}) collective-permute-start(bf16[160,2048]{1,0:T(8,128)(2,1)S(1)} %copy-done.4), channel_id=1, source_target_pairs={{0,1},{2,0},{4,2},{6,4},{7,6},{5,7},{3,5},{1,3},{8,9},{10,8},{12,1... | collective-permute-start | bytes 1966088 | tf_op jit(solution)/shard_map/ppermute | solution.py:1449
  248.9 0.8 copy-start
  249.6 0.8 copy-start.1
Sparse Core Ops, SparseCore 0:
  64.7 30.0 all-gather.1
  234.5 38.7 reduce-scatter.4
  276.0 72.7 reduce-scatter.2

commit v23 on v21

--- a/solution.py
+++ b/solution.py
@@ -1327,9 +1327,9 @@
 
 
 def finish_kernel(
-    out_hbm, tok_hbm, mlp_ref, down_ref, in_ref, gains_ref, key_ref, value_ref, wout_ref,
-    output, d_tokens, mgate, mup, down, query, gate, first, second, key, value, wout,
-    held, load_sem, store_sem,
+    out_hbm, tok_hbm, mlp_hbm, down_hbm, in_ref, gains_ref, key_ref, value_ref, wout_ref,
+    output, d_tokens, mgate_hbm, mup_hbm, d_down_hbm, query, gate, first, second, key, value, wout,
+    held, mlp_ref, down_ref, mgate, mup, down, load_sem, store_sem, grad_sem,
 ):
     count, rows = out_hbm.shape[:2]
     loads, stores = [], []
@@ -1342,7 +1342,16 @@
                     held.at[slot], target.at[pl.ds(at * rows, rows)], store_sem.at[slot]
                 )
             )
-    for copy in loads:
+    grads = [
+        pltpu.make_async_copy(source, target, grad_sem.at[index])
+        for index, (source, target) in enumerate(
+            (
+                (mlp_hbm, mlp_ref), (down_hbm, down_ref),
+                (mgate, mgate_hbm), (mup, mup_hbm), (down, d_down_hbm),
+            )
+        )
+    ]
+    for copy in (*grads[:2], *loads):
         copy.start()
     hidden = mgate.shape[1]
     size = query.shape[1]
@@ -1355,12 +1364,17 @@
             lines = pl.ds(pl.multiple_of(at * tall, tall), tall)
             target[lines] = source[lines, pl.ds(start, target.shape[1])].astype(target.dtype)
 
+    grads[0].wait()
+    convert(mgate, mlp_ref, 0)
+    grads[2].start()
+    convert(mup, mlp_ref, hidden)
+    grads[3].start()
     for load, store in zip(loads, stores):
         load.wait()
         store.start()
-    convert(mgate, mlp_ref, 0)
-    convert(mup, mlp_ref, hidden)
+    grads[1].wait()
     convert(down, down_ref, 0)
+    grads[4].start()
     convert(query, in_ref, 0)
     convert(gate, in_ref, size)
     key[...] = key_ref[...]
@@ -1368,7 +1382,7 @@
     wout[...] = wout_ref[...]
     first[...] = gains_ref[pl.ds(0, 1)]
     second[...] = gains_ref[pl.ds(1, 1)]
-    for copy in stores:
+    for copy in (*stores, *grads[2:]):
         copy.wait()
 
 
@@ -1391,12 +1405,16 @@
             shape(tall, size), shape(tall, size),
             shape(1, wide), shape(1, wide), *[shape(*a.shape) for a in rest],
         ],
-        in_specs=[hbm] * 2 + [vmem] * 7,
-        out_specs=[hbm] * 2 + [vmem] * 10,
+        in_specs=[hbm] * 4 + [vmem] * 5,
+        out_specs=[hbm] * 5 + [vmem] * 7,
         scratch_shapes=[
             pltpu.VMEM((2 * count, rows, width), BF),
+            pltpu.VMEM(d_mlp.shape, BF), pltpu.VMEM(d_down.shape, BF),
+            pltpu.VMEM((tall, hidden), F32), pltpu.VMEM((tall, hidden), F32),
+            pltpu.VMEM(d_down.shape, F32),
             pltpu.SemaphoreType.DMA((2 * count,)),
             pltpu.SemaphoreType.DMA((2 * count,)),
+            pltpu.SemaphoreType.DMA((5,)),
         ],
         compiler_params=pltpu.CompilerParams(vmem_limit_bytes=VMEM_LIMIT),
         name="finish",

time: 476 us -> 476 us (level)
  no operation moved by 1% of the time
where the time goes in v23:
time: 476 us
  Pallas kernels  450 us (95%)
  between operations  13.9 us (3%)
  local copies, waits for them, and re-layouts  6.28 us (1%)
    pallas_call x1, Pallas kernels, tail(): pl.pallas_call(functools.partial(tail_kernel, count, batches), out_shape=...  204 us
    pallas_call x1, Pallas kernels, mlp_back(): pl.pallas_call(functools.partial(mlp_kernel, count), out_shape=[shape(tot...  105 us
    pallas_call x1, Pallas kernels, spread(): pl.pallas_call(functools.partial(spread_kernel, count, batches, plans), o...  54.6 us
    pallas_call x1, Pallas kernels, entry(): pl.pallas_call(functools.partial(entry_kernel, count, batches), out_shape...  52.2 us
    pallas_call x2, Pallas kernels, local_call(): pl.pallas_call(kernel, out_shape=outs, in_specs=[smem] * len(scalars) + [...  20.4 us
    pallas_call x1, Pallas kernels, finish(): pl.pallas_call(finish_kernel, out_shape=[shape(count * rows, width, dtype...  12.5 us
  transfers between devices with their start and end apart: 5, of which 0 were waited for; matrix products, arithmetic and copies ran while one was open for 1% of the time, Pallas kernels for 59%

profile of v23, /device:TPU:0, one launch (start us, length us, event | category | flops | bytes accessed | tf_op | source)
XLA Modules:
  0.0 476.2 jit_solution(17921300156858198590)
XLA Ops:
  7.2 1.0 copy.31
  8.2 1.0 copy.32
  9.2 1.3 maximum_convert_fusion.gain_ref
  10.5 1.8 pad_maximum_fusion.w_ref
  12.3 52.2 %entry.1 = (bf16[1280,2048]{1,0:T(8,128)(2,1)}, bf16[1280,128]{1,0:T(8,128)(2,1)}, f32[1280,128]{1,0:T(8,128)}, bf16[5120,256]{1,0:T(8,128)(2,1)}, bf16[2048,512...) custom-call(bf16[1280,2048]{1,0:T(8,128)(2,1)} %x_hbm.3, ...), custom_call_target="tpu_custom_call" | custom-call | tf_op jit(solution)/shard_map/entry/pallas_call | solution.py:801
  64.6 0.2 reduce-scatter.5.cloned.1.call-start
  64.8 0.8 lt.15
  65.6 0.7 reshape.50
  66.3 0.2 convert_reduce_fusion
  66.5 0.1 select_reduce_fusion.start_sm
  66.6 0.6 broadcast_in_dim.22.start_ref
  67.2 0.6 copy.34
  67.8 8.2 %attend.1 = (f32[1280,128]{1,0:T(8,128)}, bf16[1280,128]{1,0:T(8,128)(2,1)}, f32[1,1280]{1,0:T(1,128)}) custom-call(s32[1280]{0:T(1024)} %copy-done.3, s32[1]{0:T(128)} %bitcast.3.base_sm, bf16[1280,128]{1,0:T(8,128)(2,1)} %get-tuple-element.62.q_ref, bf16[5120,256]{1,0:T(8,128)(2,1)} %get-tuple-element.63.kv_ref, s32[1,1280]{1,0:T(1,128)} %broadcast_in_dim.22.start_ref, ...), custom_call_target="tpu_custom_call" | custom-call | flops 3355443200 | bytes 8388608 | tf_op jit(solution)/shard_map/attend/pallas_call | solution.py:1427
  76.0 54.6 %spread_2.1 = (bf16[1280,1024]{1,0:T(8,128)(2,1)}, bf16[384,2048]{1,0:T(8,128)(2,1)}, bf16[2048,768]{1,0:T(8,128)(2,1)}) custom-call(bf16[1280,128]{1,0:T(8,128)(2,1)} %get-tuple-element.66.refs_0_, bf16[768,512]{1,0:T(8,128)(2,1)} %refs_1_.1, bf16[512,768]{1,0:T(8,128)(2,1)} %refs_2_.1), custom_call_target="tpu_custom_call" | custom-call | tf_op jit(solution)/shard_map/spread_2/pallas_call | solution.py:181
  130.6 105.5 %mlp_back.1 = (bf16[1280,2048]{1,0:T(8,128)(2,1)}, bf16[2048,1536]{1,0:T(8,128)(2,1)}, bf16[768,2048]{1,0:T(8,128)(2,1)}, f32[160,2048]{1,0:T(8,128)}, f32[160,2...) custom-call(bf16[1280,2048]{1,0:T(8,128)(2,1)} %x_hbm.3, ...), custom_call_target="tpu_custom_call" | custom-call | flops 41607495680 | bytes 41943040 | tf_op jit(solution)/shard_map/mlp_back/pallas_call | solution.py:559
  236.2 0.7 reduce-scatter.3.cloned.1.call-update
  236.9 0.6 copy.35
  237.5 1.0 collective-permute-start
  238.5 1.0 collective-permute-start.1
  239.5 12.2 %attend_back.1 = (bf16[1280,128]{1,0:T(8,128)(2,1)}, bf16[1280,128]{1,0:T(8,128)(2,1)}, bf16[5120,256]{1,0:T(8,128)(2,1)}) custom-call(s32[1280]{0:T(1024)} %copy-done.3, s32[1]{0:T(128)} %bitcast.3.base_sm, bf16[1280,128]{1,0:T(8,128)(2,1)} %get-tuple-element.62.q_ref, bf16[5120,256]{1,0:T(8,128)(2,1)} %get-tuple-element.63.kv_ref, ...), custom_call_target="tpu_custom_call" | custom-call | flops 8388608000 | bytes 8388608 | tf_op jit(solution)/shard_map/attend_back/pallas_call | solution.py:1427
  251.7 0.8 copy-done
  252.5 0.2 copy-done.1
  252.7 204.3 %tail.1 = (bf16[8,160,2048]{2,1,0:T(8,128)(2,1)}, bf16[8,160,2048]{2,1,0:T(8,128)(2,1)}, f32[2,512]{1,0:T(2,128)}, f32[128,512]{1,0:T(8,128)}, f32[512,384]{1,0:...) custom-call(bf16[1280,128]{1,0:T(8,128)(2,1)} %get-tuple-element.77.dq_ref, bf16[1280,128]{1,0:T(8,128)(2,1)} %get-tuple-element.78.dg_ref, ...), custom_call_target="tpu_custom_call" | custom-call | flops 4026531840 | bytes 419430400 | tf_op jit(solution)/shard_map/tail/pallas_call | solution.py:1273
  457.1 12.5 %finish.1 = (bf16[1280,2048]{1,0:T(8,128)(2,1)}, bf16[1280,2048]{1,0:T(8,128)(2,1)}, f32[512,768]{1,0:T(8,128)}, f32[512,768]{1,0:T(8,128)}, f32[768,512]{1,0:T(...) custom-call(bf16[8,160,2048]{2,1,0:T(8,128)(2,1)} %get-tuple-element, ...), custom_call_target="tpu_custom_call" | custom-call | tf_op jit(solution)/shard_map/finish/pallas_call | solution.py:1400
  (21 shorter events, 0.2 us)
Async XLA Ops:
  7.2 123.4 %all-gather.2.cloned.1.call-start = ((), (), s32[]{:S(2)}) async-start(), calls=%async_computation.2 | async-start | bytes 3932160 | tf_op jit(solution)/shard_map/all_gather | solution.py:1518
  12.3 54.2 %copy-start.2 = (s32[1280]{0:T(1024)S(1)}, s32[1280]{0:T(1024)}, u32[]{:S(2)}) copy-start(s32[1280]{0:T(1024)} %param.14) | copy-start | bytes 15364
  64.6 392.5 %reduce-scatter.5.cloned.1.call-start = ((), (), s32[]{:S(2)}) async-start(), calls=%async_computation.4 | async-start | bytes 3932160 | tf_op jit(solution)/shard_map/reduce_scatter | solution.py:1563
  66.5 1.2 copy-start.3
  236.1 221.0 %reduce-scatter.3.cloned.1.call-start = ((), (), s32[]{:S(2)}) async-start(), calls=%async_computation.3 | async-start | bytes 7864320 | tf_op jit(solution)/shard_map/reduce_scatter | solution.py:1564
  236.2 1.3 copy-start.5
  236.2 2.3 copy-start.4
  237.5 14.2 %collective-permute-start = (bf16[160,2048]{1,0:T(8,128)(2,1)S(1)}, bf16[160,2048]{1,0:T(8,128)(2,1)S(1)}, u32[]{:S(2)}, u32[]{:S(2)}) collective-permute-start(bf16[160,2048]{1,0:T(8,128)(2,1)S(1)} %copy-done.5), channel_id=1, source_target_pairs={{0,2},{2,4},{4,6},{6,7},{7,5},{5,3},{3,1},{1,0},{8,10},{10,12},{12... | collective-permute-start | bytes 1966088 | tf_op jit(solution)/shard_map/ppermute | solution.py:1461
  238.5 13.2 %collective-permute-start.1 = (bf16[160,2048]{1,0:T(8,128)(2,1)S(1)}, bf16[160,2048]{1,0:T(8,128)(2,1)S(1)}, u32[]{:S(2)}, u32[]{:S(2)}) collective-permute-start(bf16[160,2048]{1,0:T(8,128)(2,1)S(1)} %copy-done.4), channel_id=1, source_target_pairs={{0,1},{2,0},{4,2},{6,4},{7,6},{5,7},{3,5},{1,3},{8,9},{10,8},{12,1... | collective-permute-start | bytes 1966088 | tf_op jit(solution)/shard_map/ppermute | solution.py:1462
  251.7 0.8 copy-start
  251.7 1.0 copy-start.1
Sparse Core Ops, SparseCore 0:
  64.7 28.9 all-gather.1
  236.2 38.6 reduce-scatter.4
  277.6 72.8 reduce-scatter.2
